TPU v7x, 32 devices: a whole 2x2x4 slice. The times are simulated.
32 devices in a mesh: slab: 8 (over y, x, core), rep: 4 (over z).
Axes of the slice: x: 2, y: 2, z: 4, core: 2. Of those that a mesh axis runs over, the one named last changes fastest.
Arguments:
- features: bfloat16 [4, 4096, 256], P('rep', 'slab'), may hold values from -6 to 6
- cotangent: bfloat16 [4, 4096, 256], P('rep', 'slab'), may hold values from -6 to 6
- frac_pos: float32 [4, 3, 4096], P('rep', None, 'slab'), may hold values from 0 to 1
- k_vectors: int32 [3, 1024], replicated, may hold values from -6 to 6
- k_filter: float32 [1024, 256], replicated, may hold values from -4 to 4
- w_out: bfloat16 [256, 256], replicated, may hold values from -0.375 to 0.375
- w_short: bfloat16 [256, 256], replicated, may hold values from -0.375 to 0.375
- edge_src: int32 [4, 32768], P('rep', 'slab'), may hold values from 0 to 1023
- edge_dst: int32 [4, 32768], P('rep', 'slab'), may hold values from 0 to 511
- distance: float32 [4, 32768], P('rep', 'slab'), may hold values from 0.5 to 6
- halo_idx: int32 [4, 16, 256], P('rep', 'slab'), may hold values from 0 to 511
Outputs:
- grad_features: bfloat16 [4, 4096, 256], P('rep', 'slab')
- grad_wout: float32 [256, 256], replicated
- grad_wshort: float32 [256, 256], replicated
- grad_filter: float32 [1024, 256], P('slab')
Inputs may be any that keep to these rules, and one draw needn't show every extreme that they name: `edge_src`: edge sources index the slab's extended rows: its 512 atoms, then 256 lower rim rows, then 256 upper rim rows. `edge_dst`: edge targets are atoms of the slab that holds the slot. `halo_idx`: row numbers within the sending slab; list 2s goes from slab s to slab s-1, list 2s+1 to slab s+1, cyclically; repeats may occur.
All inputs are finite; a program needn't handle non-finite values.
Results may differ from a plain program's by a relative error of at most 0.0059.
Values may be sent and summed in bfloat16 or wider, within the bound.
No kernel may reach another device: no remote copies, remote signals or barrier semaphores. Data moves between devices by JAX's collectives and lax.ppermute only.
A program may use at most 64 MiB of HBM per device.

v0:
```python
import functools
import math

import jax
import jax.numpy as jnp
from jax import lax
from jax.experimental import pallas as pl
from jax.experimental.pallas import tpu as pltpu
from jax.sharding import PartitionSpec as P

cutoff_radius = 5.0
f32, bf16 = jnp.float32, jnp.bfloat16

sin_coefs = (3.1415926401307073, -5.167710083507895, 2.550077523214559, -0.5982912856198396, 0.0776576603038396)
cos_coefs = (0.9999999532476077, -4.934792830619641, 4.058411352862562, -1.331876568080612, 0.21968961109715823)

VMEM = pl.BlockSpec(memory_space=pltpu.VMEM)
SMEM = pl.BlockSpec(memory_space=pltpu.SMEM)


def params():
    return pltpu.CompilerParams(vmem_limit_bytes=48 * 1024 * 1024)


def xor_permute(value, axis, bits):
    count = lax.axis_size(axis)
    return lax.ppermute(value, axis, [(source, source ^ bits) for source in range(count)])


def shifted(value, axis, steps):
    count = lax.axis_size(axis)
    return lax.ppermute(value, axis, [(source, (source + steps) % count) for source in range(count)])


def exchange_groups(count):
    groups, base = [], 1
    while base < count:
        width = 2 if base == 1 else min(4, count // base)
        groups.append([base * g for g in range(width)])
        base *= width
    return groups


def horner(coefs, z):
    total = coefs[-1]
    for c in coefs[-2::-1]:
        total = total * z + c
    return total


def dot(left, right, left_dim=1, right_dim=0):
    return lax.dot_general(left, right, (((left_dim,), (right_dim,)), ((), ())), preferred_element_type=f32)


def tables_kernel(order, slab_ref, kv_ref, pos_ref, rows_ref, cot_ref, table_ref, part_ref, k_rows, k_cols, p_rows):
    share = table_ref.shape[0] // (2 * len(order))
    channels = rows_ref.shape[1]
    slab = slab_ref[0]
    pos = pos_ref[...]
    high = pos.astype(bf16).astype(f32)
    middle = (pos - high).astype(bf16).astype(f32)
    low = pos - high - middle
    kv = kv_ref[...].astype(f32)
    k_rows[...] = jnp.zeros_like(k_rows)
    p_rows[...] = jnp.zeros_like(p_rows)
    for i, piece in enumerate((high, middle, low)):
        k_rows[3 * i : 3 * i + 3, :] = kv
        p_rows[3 * i : 3 * i + 3, :] = piece
    k_cols[...] = k_rows[...].T
    positions = p_rows[...].astype(bf16)

    def block(place, owner):
        k_block = k_cols[pl.ds(pl.multiple_of(owner * share, 8), share), :].astype(bf16)
        turns = dot(k_block, positions)
        r = turns - jnp.floor(turns + 0.5)
        z = r * r
        s = r * horner(sin_coefs, z)
        c = horner(cos_coefs, z)
        cos = 1.0 - 2.0 * s * s
        sin = 2.0 * s * c
        table = jnp.concatenate([cos, sin], axis=0).astype(bf16)
        at = pl.ds(place * 2 * share, 2 * share)
        table_ref[at, :] = table
        part_ref[at, :channels] = dot(table, rows_ref[...]).astype(bf16)
        part_ref[at, channels:] = dot(table, cot_ref[...]).astype(bf16)

    for place, offset in enumerate(order):
        block(place, slab ^ offset)


def tables(order, slab, k_vectors, positions, rows, cotan, share):
    atoms, channels = rows.shape
    kcount = k_vectors.shape[1]
    height = 2 * share * len(order)
    return pl.pallas_call(
        functools.partial(tables_kernel, order),
        name="tables",
        out_shape=(
            jax.ShapeDtypeStruct((height, atoms), bf16),
            jax.ShapeDtypeStruct((height, 2 * channels), bf16),
        ),
        in_specs=[SMEM, VMEM, VMEM, VMEM, VMEM],
        out_specs=(VMEM, VMEM),
        scratch_shapes=[
            pltpu.VMEM((16, kcount), f32),
            pltpu.VMEM((kcount, 16), f32),
            pltpu.VMEM((16, atoms), f32),
        ],
        compiler_params=params(),
        cost_estimate=pl.CostEstimate(
            flops=2 * height * atoms * 2 * channels, bytes_accessed=4 * height * atoms, transcendentals=0
        ),
    )(slab, k_vectors, positions, rows, cotan)


def edge_kernel(block, src_ref, dst_ref, dist_ref, cot_ref, own_ref, low_ref, up_ref, total):
    atoms, _ = cot_ref.shape
    rim = low_ref.shape[0]
    edges = src_ref.shape[1]
    cot_t = cot_ref[...].T
    for start in range(0, edges, block):
        at = slice(start, start + block)
        source, target = src_ref[:, at], dst_ref[:, at]
        weight = jnp.maximum(1.0 - dist_ref[:, at] / cutoff_radius, 0.0)
        weight = weight * weight
        pick = lax.broadcasted_iota(jnp.int32, (atoms, block), 0) == target
        taken = dot(cot_t, pick.astype(f32).astype(bf16))
        weighted = (taken * weight).astype(bf16)
        put = lax.broadcasted_iota(jnp.int32, (total.shape[0], block), 0) == source
        part = dot(put.astype(f32).astype(bf16), weighted, 1, 1)
        total[...] = part if start == 0 else total[...] + part
    own_ref[...] = total[:atoms, :]
    low_ref[...] = total[atoms : atoms + rim, :].astype(bf16)
    up_ref[...] = total[atoms + rim :, :].astype(bf16)


def edge_rows(sources, targets, lengths, cotan, rim):
    atoms, channels = cotan.shape
    edges = sources.shape[1]
    rows = atoms + 2 * rim
    block = math.gcd(edges, 512)
    return pl.pallas_call(
        functools.partial(edge_kernel, block),
        name="edges",
        out_shape=(
            jax.ShapeDtypeStruct((atoms, channels), f32),
            jax.ShapeDtypeStruct((rim, channels), bf16),
            jax.ShapeDtypeStruct((rim, channels), bf16),
        ),
        in_specs=[VMEM] * 4,
        out_specs=(VMEM,) * 3,
        scratch_shapes=[pltpu.VMEM((rows, channels), f32)],
        compiler_params=params(),
        cost_estimate=pl.CostEstimate(
            flops=2 * edges * (rows + atoms) * channels, bytes_accessed=edges * 12, transcendentals=0
        ),
    )(sources, targets, lengths, cotan)


def short_kernel(own_ref, above_ref, below_ref, lists_ref, rows_ref, cot_ref, w_ref, base_ref, grad_ref):
    atoms = own_ref.shape[0]
    lists = lists_ref[...]
    shape = (atoms, lists.shape[1])
    row_at = lax.broadcasted_iota(jnp.int32, shape, 0)
    to_lower = (row_at == lists[0:1, :]).astype(f32).astype(bf16)
    to_upper = (row_at == lists[1:2, :]).astype(f32).astype(bf16)
    owned = own_ref[...] + dot(to_upper, above_ref[...]) + dot(to_lower, below_ref[...])
    owned = owned.astype(bf16)
    base_ref[...] = cot_ref[...].astype(f32) + dot(owned, w_ref[...], 1, 1)
    grad_ref[...] = dot(rows_ref[...], owned, 0, 0)


def short_range(own, above, below, lists, rows, cotan, w_short):
    atoms, channels = rows.shape
    return pl.pallas_call(
        short_kernel,
        name="short",
        out_shape=(
            jax.ShapeDtypeStruct((atoms, channels), f32),
            jax.ShapeDtypeStruct((channels, channels), f32),
        ),
        in_specs=[VMEM] * 7,
        out_specs=(VMEM, VMEM),
        compiler_params=params(),
        cost_estimate=pl.CostEstimate(
            flops=8 * atoms * channels * channels, bytes_accessed=8 * atoms * channels, transcendentals=0
        ),
    )(own, above, below, lists, rows, cotan, w_short)


def share_kernel(order, norm, count, slab_ref, filter_ref, w_ref, short_ref, own_ref, *refs):
    parts, (adj_ref, gfilter_ref, send_ref, keep_ref, full) = refs[:count], refs[count:]
    channels = w_ref.shape[0]
    height = 2 * channels // len(order)
    slab = slab_ref[0]
    total = own_ref[...].astype(f32)
    for part in parts:
        total = total + part[...].astype(f32)
    structure = total[:, :channels]
    moved = total[:, channels:].astype(bf16)
    response = dot(moved, w_ref[...], 1, 1)
    k_filter = filter_ref[...]
    double = jnp.concatenate([k_filter, k_filter], axis=0) * norm
    filtered = (structure * double).astype(bf16)
    full[:channels, :] = dot(filtered, moved, 0, 0)
    full[channels:, :] = short_ref[...]
    half = len(order) // 2
    for place, offset in enumerate(order):
        ref = send_ref if place < half else keep_ref
        at = (place % half) * height
        rows = pl.ds(pl.multiple_of((slab ^ offset) * height, height), height)
        ref[at : at + height, :] = full[rows, :].astype(ref.dtype)
    adj_ref[...] = (response * double).T.astype(bf16)
    product = structure * response
    share = k_filter.shape[0]
    gfilter_ref[...] = norm * (product[:share] + product[share:])


def own_share(order, norm, slab, k_filter, w_out, short_grad, own, parts):
    height, channels = own.shape[0], w_out.shape[0]
    share = height // 2
    whole = lambda shape: pl.BlockSpec(shape, lambda i, slab_ref: (0, 0))
    grid_spec = pltpu.PrefetchScalarGridSpec(
        num_scalar_prefetch=1,
        grid=(1,),
        in_specs=[
            pl.BlockSpec((share, channels), lambda i, slab_ref: (slab_ref[0], 0)),
            whole(w_out.shape),
            whole(short_grad.shape),
            whole(own.shape),
        ]
        + [whole(own.shape)] * len(parts),
        out_specs=(
            whole((channels, height)),
            whole((share, channels)),
            whole((channels, channels)),
            whole((channels, channels)),
        ),
        scratch_shapes=[pltpu.VMEM((2 * channels, channels), f32)],
    )
    return pl.pallas_call(
        functools.partial(share_kernel, order, norm, len(parts)),
        name="share",
        out_shape=(
            jax.ShapeDtypeStruct((channels, height), bf16),
            jax.ShapeDtypeStruct((share, channels), f32),
            jax.ShapeDtypeStruct((channels, channels), bf16),
            jax.ShapeDtypeStruct((channels, channels), f32),
        ),
        grid_spec=grid_spec,
        compiler_params=params(),
        cost_estimate=pl.CostEstimate(
            flops=4 * height * channels * channels, bytes_accessed=16 * height * channels, transcendentals=0
        ),
    )(slab, k_filter, w_out, short_grad, own, *parts)


def back_kernel(base_ref, even_ref, odd_ref, even_adj_ref, odd_adj_ref, out_ref):
    total = None
    for table_ref, adj_ref in ((even_ref, even_adj_ref), (odd_ref, odd_adj_ref)):
        count, _, width = adj_ref.shape
        for i in range(count):
            part = dot(adj_ref[i], table_ref[i * width : (i + 1) * width, :])
            total = part if total is None else total + part
    out_ref[...] = (base_ref[...] + total.T).astype(bf16)


def back_project(base, even, odd, even_adj, odd_adj):
    atoms, channels = base.shape
    return pl.pallas_call(
        back_kernel,
        name="back",
        out_shape=jax.ShapeDtypeStruct((atoms, channels), bf16),
        in_specs=[VMEM] * 5,
        out_specs=VMEM,
        compiler_params=params(),
        cost_estimate=pl.CostEstimate(
            flops=4 * even.shape[0] * atoms * channels, bytes_accessed=4 * even.shape[0] * atoms, transcendentals=0
        ),
    )(base, even, odd, even_adj, odd_adj)


def place_kernel(order, scale, slab_ref, even_ref, odd_ref, wout_ref, wshort_ref, full):
    channels = wout_ref.shape[0]
    height = 2 * channels // len(order)
    slab = slab_ref[0]
    half = len(order) // 2
    for place, offset in enumerate(order):
        ref = odd_ref if place < half else even_ref
        at = (place % half) * height
        rows = pl.ds(pl.multiple_of((slab ^ offset) * height, height), height)
        full[rows, :] = ref[at : at + height, :].astype(f32) * scale
    wout_ref[...] = full[:channels, :]
    wshort_ref[...] = full[channels:, :]


def place_grads(order, scale, slab, even, odd):
    channels = even.shape[1]
    return pl.pallas_call(
        functools.partial(place_kernel, order, scale),
        name="place",
        out_shape=(jax.ShapeDtypeStruct((channels, channels), f32),) * 2,
        in_specs=[SMEM, VMEM, VMEM],
        out_specs=(VMEM, VMEM),
        scratch_shapes=[pltpu.VMEM((2 * channels, channels), f32)],
        compiler_params=params(),
    )(slab, even, odd)


def scatter_blocks(blocks, groups):
    parts = []
    for group in groups:
        if parts:
            blocks = sum((part.astype(f32) for part in parts), blocks.astype(f32))
        width = len(group)
        split = blocks.reshape(-1, width, *blocks.shape[1:])
        parts = [xor_permute(split[:, g].astype(bf16), "slab", group[g]) for g in range(1, width)]
        blocks = split[:, 0]
    return blocks, parts


def gather_blocks(block, groups):
    blocks, order = block[None], [0]
    for group in reversed(groups):
        pieces = [blocks] + [xor_permute(blocks, "slab", offset) for offset in group[1:]]
        blocks = jnp.concatenate(pieces, axis=0)
        order = [offset ^ held for offset in group for held in order]
    return blocks, order


def sum_replicas(value):
    count = lax.axis_size("rep")
    sent = value.astype(bf16)
    terms = [sent] + [xor_permute(sent, "rep", offset) for offset in range(1, count)]
    terms = [term.astype(f32) for term in terms]
    while len(terms) > 1:
        terms = [terms[i] + terms[i + 1] for i in range(0, len(terms), 2)]
    return terms[0]


def body(
    features,
    cotangent,
    frac_pos,
    k_vectors,
    k_filter,
    w_out,
    w_short,
    edge_src,
    edge_dst,
    distance,
    halo_idx,
):
    rows = features[0]
    cotan = cotangent[0]
    atoms, channels = rows.shape
    kcount = k_filter.shape[0]
    count = lax.axis_size("slab")
    replicas = lax.axis_size("rep")
    norm = 1.0 / math.sqrt(kcount * atoms * count)
    scale = 1.0 / math.sqrt(replicas * atoms * count)
    share = kcount // count
    slab = lax.axis_index("slab").astype(jnp.int32)[None]
    pair, *rest = exchange_groups(count)

    even = [0]
    for group in reversed(rest):
        even = [offset ^ held for offset in group for held in even]
    keep_order = sorted(even)
    odd = [offset ^ 1 for offset in keep_order]
    order = odd + keep_order

    odd_table, odd_part = tables(tuple(odd), slab, k_vectors, frac_pos[0], rows, cotan, share)
    from_pair = xor_permute(odd_part, "slab", 1)
    even_table, even_part = tables(tuple(keep_order), slab, k_vectors, frac_pos[0], rows, cotan, share)

    own_rows, lower, upper = edge_rows(edge_src, edge_dst, distance, cotan, halo_idx.shape[2])
    from_above = shifted(lower, "slab", -1)
    from_below = shifted(upper, "slab", 1)
    base, short_grad = short_range(own_rows, from_above, from_below, halo_idx[0], rows, cotan, w_short)

    half = count // 2
    paired = even_part.astype(f32) + from_pair.astype(f32)
    own, parts = scatter_blocks(paired.reshape(half, 2 * share, 2 * channels), rest)
    adj, gfilter, send, keep = own_share(
        tuple(order), norm, slab, k_filter, w_out, short_grad, own[0], [part[0] for part in parts]
    )

    summed = keep + xor_permute(send, "slab", 1).astype(f32)
    own_grad, grad_parts = scatter_blocks(summed.reshape(half, -1, channels), rest)
    own_grad = sum((part.astype(f32) for part in grad_parts), own_grad)[0]

    adj_even, held = gather_blocks(adj, rest)
    place_of = [held.index(offset) for offset in keep_order]
    if place_of != list(range(half)):
        adj_even = jnp.stack([adj_even[i] for i in place_of])
    adj_odd = xor_permute(adj_even, "slab", 1)
    grad_features = back_project(base, even_table, odd_table, adj_even, adj_odd)

    own_grad = sum_replicas(own_grad).astype(bf16)
    grad_filter = sum_replicas(gfilter) / replicas
    grad_even, _ = gather_blocks(own_grad, rest)
    if place_of != list(range(half)):
        grad_even = jnp.stack([grad_even[i] for i in place_of])
    grad_even = grad_even.reshape(-1, channels)
    grad_odd = xor_permute(grad_even, "slab", 1)
    grad_wout, grad_wshort = place_grads(tuple(order), scale, slab, grad_even, grad_odd)
    return (grad_features[None], grad_wout, grad_wshort, grad_filter)


def solution(mesh):
    return jax.shard_map(
        body,
        mesh=mesh,
        in_specs=(
            P("rep", "slab", None),
            P("rep", "slab", None),
            P("rep", None, "slab"),
            P(),
            P(),
            P(),
            P(),
            P("rep", "slab"),
            P("rep", "slab"),
            P("rep", "slab"),
            P("rep", "slab", None),
        ),
        out_specs=(P("rep", "slab", None), P(), P(), P("slab", None)),
        check_vma=False,
    )
```

profile of v0, /device:TPU:0, one launch (start us, length us, event | category | flops | bytes accessed | tf_op | source)
XLA Modules:
  0.0 70.5 jit_solution(8486108014393246901)
XLA Ops:
  0.6 0.7 copy.17
  1.3 0.9 %copy-done.1 = bf16[1,512,256]{2,1,0:T(8,128)(2,1)S(1)} copy-done((bf16[1,512,256]{2,1,0:T(8,128)(2,1)S(1)}, bf16[1,512,256]{2,1,0:T(8,128)(2,1)}, u32[]{:S(2)}) %copy-start.1) | copy-done | bytes 262168
  2.3 0.9 %copy-done.4 = bf16[1,512,256]{2,1,0:T(8,128)(2,1)S(1)} copy-done((bf16[1,512,256]{2,1,0:T(8,128)(2,1)S(1)}, bf16[1,512,256]{2,1,0:T(8,128)(2,1)}, u32[]{:S(2)}) %copy-start.4) | copy-done | bytes 262168
  3.2 0.7 %copy-done.12 = s32[3,1024]{1,0:T(4,128)S(1)} copy-done((s32[3,1024]{1,0:T(4,128)S(1)}, s32[3,1024]{1,0:T(4,128)}, u32[]{:S(2)}) %copy-start.12) | copy-done | bytes 12312
  3.9 2.0 %tables.3 = (bf16[1024,512]{1,0:T(8,128)(2,1)S(1)}, bf16[1024,512]{1,0:T(8,128)(2,1)S(1)}) custom-call(s32[1]{0:T(128)} %bitcast.3.slab_ref, s32[3,1024]{1,0:T(4,128)S(1)} %copy-done.12, f32[3,512]{1,0:T(4,128)S(1)} %bitcast.61, bf16[512,256]{1,0:T(8,128)(2,1)S(1)} %bitcast.54, bf16[512,256]{1,0:T(8,128)(2,1)S(1)} %bitcast.50), custom_call_target="tpu_custom_call" | custom-call | flops 536870912 | bytes 2097152 | tf_op jit(solution)/shard_map/tables/pallas_call | solution.py:95
  5.9 0.6 collective-permute-start.2
  6.5 0.9 %copy-done.2 = bf16[1,512,256]{2,1,0:T(8,128)(2,1)S(1)} copy-done((bf16[1,512,256]{2,1,0:T(8,128)(2,1)S(1)}, bf16[1,512,256]{2,1,0:T(8,128)(2,1)}, u32[]{:S(2)}) %copy-start.2) | copy-done | bytes 262168
  7.5 0.7 %copy-done.9 = s32[1,4096]{1,0:T(1,128)S(1)} copy-done((s32[1,4096]{1,0:T(1,128)S(1)}, s32[1,4096]{1,0:T(1,128)}, u32[]{:S(2)}) %copy-start.9) | copy-done | bytes 16408
  8.2 0.7 %copy-done.10 = s32[1,4096]{1,0:T(1,128)S(1)} copy-done((s32[1,4096]{1,0:T(1,128)S(1)}, s32[1,4096]{1,0:T(1,128)}, u32[]{:S(2)}) %copy-start.10) | copy-done | bytes 16408
  8.9 0.7 %copy-done.11 = f32[1,4096]{1,0:T(1,128)S(1)} copy-done((f32[1,4096]{1,0:T(1,128)S(1)}, f32[1,4096]{1,0:T(1,128)}, u32[]{:S(2)}) %copy-start.11) | copy-done | bytes 16408
  9.6 5.2 %edges.1 = (f32[512,256]{1,0:T(8,128)S(1)}, bf16[256,256]{1,0:T(8,128)(2,1)S(1)}, bf16[256,256]{1,0:T(8,128)(2,1)S(1)}) custom-call(s32[1,4096]{1,0:T(1,128)S(1)} %copy-done.9, s32[1,4096]{1,0:T(1,128)S(1)} %copy-done.10, f32[1,4096]{1,0:T(1,128)S(1)} %copy-done.11, bf16[512,256]{1,0:T(8,128)(2,1)S(1)} %bitcast.51), custom_call_target="tpu_custom_call" | custom-call | flops 3221225472 | bytes 49152 | tf_op jit(solution)/shard_map/edges/pallas_call | solution.py:142
  14.8 3.6 %collective-permute-start = (bf16[256,256]{1,0:T(8,128)(2,1)S(1)}, bf16[256,256]{1,0:T(8,128)(2,1)S(1)}, u32[]{:S(2)}, u32[]{:S(2)}) collective-permute-start(bf16[256,256]{1,0:T(8,128)(2,1)S(1)} %get-tuple-element.20), channel_id=1, source_target_pairs={{0,28},{4,0},{8,4},{12,8},{16,12},{20,16},{24,20},{28,24},{1,29},{... | collective-permute-start | bytes 393224 | tf_op jit(solution)/shard_map/ppermute | solution.py:32
  18.4 0.0 collective-permute-start.1
  18.4 2.0 %tables.2 = (bf16[1024,512]{1,0:T(8,128)(2,1)S(1)}, bf16[1024,512]{1,0:T(8,128)(2,1)S(1)}) custom-call(s32[1]{0:T(128)} %bitcast.3.slab_ref, s32[3,1024]{1,0:T(4,128)S(1)} %copy-done.12, f32[3,512]{1,0:T(4,128)S(1)} %bitcast.62, bf16[512,256]{1,0:T(8,128)(2,1)S(1)} %bitcast.55, bf16[512,256]{1,0:T(8,128)(2,1)S(1)} %bitcast.52), custom_call_target="tpu_custom_call" | custom-call | flops 536870912 | bytes 2097152 | tf_op jit(solution)/shard_map/tables/pallas_call | solution.py:95
  20.4 0.0 collective-permute-done.2
  20.4 0.3 convert_add_fusion
  20.8 0.0 copy-start.7
  20.8 0.0 copy-start.8
  20.8 0.1 convert.10
  20.9 0.0 copy-start
  20.9 0.0 copy-start.6
  20.9 0.1 slice_bitcast_fusion.1
  21.0 0.6 collective-permute-start.5
  21.6 1.4 %collective-permute-start.3 = (bf16[1,256,512]{2,1,0:T(8,128)(2,1)S(1)}, bf16[1,256,512]{2,1,0:T(8,128)(2,1)S(1)}, u32[]{:S(2)}, u32[]{:S(2)}) collective-permute-start(bf16[1,256,512]{2,1,0:T(8,128)(2,1)S(1)} %get-tuple-element.36), channel_id=1, source_target_pairs={{0,8},{4,12},{8,0},{12,4},{16,24},{20,28},{24,16},{28,20},{1,9},{5... | collective-permute-start | bytes 786440 | tf_op jit(solution)/shard_map/ppermute | solution.py:27
  23.0 1.5 %collective-permute-start.4 = (bf16[1,256,512]{2,1,0:T(8,128)(2,1)S(1)}, bf16[1,256,512]{2,1,0:T(8,128)(2,1)S(1)}, u32[]{:S(2)}, u32[]{:S(2)}) collective-permute-start(bf16[1,256,512]{2,1,0:T(8,128)(2,1)S(1)} %get-tuple-element.35), channel_id=1, source_target_pairs={{0,16},{4,20},{8,24},{12,28},{16,0},{20,4},{24,8},{28,12},{1,17},{... | collective-permute-start | bytes 786440 | tf_op jit(solution)/shard_map/ppermute | solution.py:27
  24.6 0.0 collective-permute-done.above_ref
  24.6 0.0 collective-permute-done.1.below_ref
  24.6 0.7 short.1
  25.3 5.9 %collective-permute-done.5 = bf16[1,256,512]{2,1,0:T(8,128)(2,1)S(1)} collective-permute-done((bf16[1,256,512]{2,1,0:T(8,128)(2,1)S(1)}, bf16[1,256,512]{2,1,0:T(8,128)(2,1)S(1)}, u32[]{:S(2)}, u32[]{:S(2)}) %collective-permute-start.5) | collective-permute-done | bytes 262176 | tf_op jit(solution)/shard_map/ppermute | solution.py:27
  31.2 4.4 %collective-permute-done.3 = bf16[1,256,512]{2,1,0:T(8,128)(2,1)S(1)} collective-permute-done((bf16[1,256,512]{2,1,0:T(8,128)(2,1)S(1)}, bf16[1,256,512]{2,1,0:T(8,128)(2,1)S(1)}, u32[]{:S(2)}, u32[]{:S(2)}) %collective-permute-start.3) | collective-permute-done | bytes 262176 | tf_op jit(solution)/shard_map/ppermute | solution.py:27
  35.6 0.6 collective-permute-done.4
  36.2 0.4 share.1
  36.6 0.2 collective-permute-start.10
  36.7 1.2 %collective-permute-done.10 = bf16[256,256]{1,0:T(8,128)(2,1)S(1)} collective-permute-done((bf16[256,256]{1,0:T(8,128)(2,1)S(1)}, bf16[256,256]{1,0:T(8,128)(2,1)S(1)}, u32[]{:S(2)}, u32[]{:S(2)}) %collective-permute-start.10) | collective-permute-done | bytes 131104 | tf_op jit(solution)/shard_map/ppermute | solution.py:27
  38.1 0.1 collective-permute-start.11
  38.2 1.6 %collective-permute-start.12 = (bf16[1,64,256]{2,1,0:T(8,128)(2,1)S(1)}, bf16[1,64,256]{2,1,0:T(8,128)(2,1)S(1)}, u32[]{:S(2)}, u32[]{:S(2)}) collective-permute-start(bf16[1,64,256]{2,1,0:T(8,128)(2,1)S(1)} %get-tuple-element.39), channel_id=1, source_target_pairs={{0,16},{4,20},{8,24},{12,28},{16,0},{20,4},{24,8},{28,12},{1,17},{... | collective-permute-start | bytes 98312 | tf_op jit(solution)/shard_map/ppermute | solution.py:27
  39.8 1.9 %collective-permute-start.13 = (bf16[1,64,256]{2,1,0:T(8,128)(2,1)S(1)}, bf16[1,64,256]{2,1,0:T(8,128)(2,1)S(1)}, u32[]{:S(2)}, u32[]{:S(2)}) collective-permute-start(bf16[1,64,256]{2,1,0:T(8,128)(2,1)S(1)} %get-tuple-element.38), channel_id=1, source_target_pairs={{0,24},{4,28},{8,16},{12,20},{16,8},{20,12},{24,0},{28,4},{1,25},{... | collective-permute-start | bytes 98312 | tf_op jit(solution)/shard_map/ppermute | solution.py:27
  41.6 0.1 collective-permute-start.6
  41.7 1.5 %collective-permute-start.7 = (bf16[1,256,256]{2,1,0:T(8,128)(2,1)S(1)}, bf16[1,256,256]{2,1,0:T(8,128)(2,1)S(1)}, u32[]{:S(2)}, u32[]{:S(2)}) collective-permute-start(bf16[1,256,256]{2,1,0:T(8,128)(2,1)S(1)} %bitcast.58), channel_id=1, source_target_pairs={{0,16},{4,20},{8,24},{12,28},{16,0},{20,4},{24,8},{28,12},{1,17},{... | collective-permute-start | bytes 393224 | tf_op jit(solution)/shard_map/ppermute | solution.py:27
  43.3 1.9 %collective-permute-start.8 = (bf16[1,256,256]{2,1,0:T(8,128)(2,1)S(1)}, bf16[1,256,256]{2,1,0:T(8,128)(2,1)S(1)}, u32[]{:S(2)}, u32[]{:S(2)}) collective-permute-start(bf16[1,256,256]{2,1,0:T(8,128)(2,1)S(1)} %bitcast.59), channel_id=1, source_target_pairs={{0,24},{4,28},{8,16},{12,20},{16,8},{20,12},{24,0},{28,4},{1,25},{... | collective-permute-start | bytes 393224 | tf_op jit(solution)/shard_map/ppermute | solution.py:27
  45.1 0.0 collective-permute-done.12
  45.2 1.6 %collective-permute-start.14 = (bf16[64,256]{1,0:T(8,128)(2,1)S(1)}, bf16[64,256]{1,0:T(8,128)(2,1)S(1)}, u32[]{:S(2)}, u32[]{:S(2)}) collective-permute-start(bf16[64,256]{1,0:T(8,128)(2,1)S(1)} %fusion.5), channel_id=1, source_target_pairs={{0,1},{1,0},{2,3},{3,2},{4,5},{5,4},{6,7},{7,6},{8,9},{9,8},{10,11... | collective-permute-start | bytes 98312 | tf_op jit(solution)/shard_map/ppermute | solution.py:27
  46.8 2.6 %collective-permute-start.15 = (bf16[64,256]{1,0:T(8,128)(2,1)S(1)}, bf16[64,256]{1,0:T(8,128)(2,1)S(1)}, u32[]{:S(2)}, u32[]{:S(2)}) collective-permute-start(bf16[64,256]{1,0:T(8,128)(2,1)S(1)} %fusion.5), channel_id=1, source_target_pairs={{0,2},{1,3},{2,0},{3,1},{4,6},{5,7},{6,4},{7,5},{8,10},{9,11},{10,... | collective-permute-start | bytes 98312 | tf_op jit(solution)/shard_map/ppermute | solution.py:27
  49.4 0.0 collective-permute-done.6
  49.4 2.0 %collective-permute-start.16 = (bf16[64,256]{1,0:T(8,128)(2,1)S(1)}, bf16[64,256]{1,0:T(8,128)(2,1)S(1)}, u32[]{:S(2)}, u32[]{:S(2)}) collective-permute-start(bf16[64,256]{1,0:T(8,128)(2,1)S(1)} %fusion.5), channel_id=1, source_target_pairs={{0,3},{1,2},{2,1},{3,0},{4,7},{5,6},{6,5},{7,4},{8,11},{9,10},{10,... | collective-permute-start | bytes 98312 | tf_op jit(solution)/shard_map/ppermute | solution.py:27
  51.4 0.1 pad_maximum_fusion.even_adj_ref
  51.5 0.1 collective-permute-start.9
  51.6 0.6 collective-permute-done.15
  52.2 2.9 %collective-permute-done.16 = bf16[64,256]{1,0:T(8,128)(2,1)S(1)} collective-permute-done((bf16[64,256]{1,0:T(8,128)(2,1)S(1)}, bf16[64,256]{1,0:T(8,128)(2,1)S(1)}, u32[]{:S(2)}, u32[]{:S(2)}) %collective-permute-start.16) | collective-permute-done | bytes 32800 | tf_op jit(solution)/shard_map/ppermute | solution.py:27
  55.1 1.1 %collective-permute-start.17 = (bf16[1,64,256]{2,1,0:T(8,128)(2,1)S(1)}, bf16[1,64,256]{2,1,0:T(8,128)(2,1)S(1)}, u32[]{:S(2)}, u32[]{:S(2)}) collective-permute-start(bf16[1,64,256]{2,1,0:T(8,128)(2,1)S(1)} %fusion.4), channel_id=1, source_target_pairs={{0,8},{4,12},{8,0},{12,4},{16,24},{20,28},{24,16},{28,20},{1,9},{5... | collective-permute-start | bytes 98312 | tf_op jit(solution)/shard_map/ppermute | solution.py:27
  56.2 1.2 %collective-permute-start.18 = (bf16[1,64,256]{2,1,0:T(8,128)(2,1)S(1)}, bf16[1,64,256]{2,1,0:T(8,128)(2,1)S(1)}, u32[]{:S(2)}, u32[]{:S(2)}) collective-permute-start(bf16[1,64,256]{2,1,0:T(8,128)(2,1)S(1)} %fusion.4), channel_id=1, source_target_pairs={{0,16},{4,20},{8,24},{12,28},{16,0},{20,4},{24,8},{28,12},{1,17},{... | collective-permute-start | bytes 98312 | tf_op jit(solution)/shard_map/ppermute | solution.py:27
  57.4 1.3 %collective-permute-start.19 = (bf16[1,64,256]{2,1,0:T(8,128)(2,1)S(1)}, bf16[1,64,256]{2,1,0:T(8,128)(2,1)S(1)}, u32[]{:S(2)}, u32[]{:S(2)}) collective-permute-start(bf16[1,64,256]{2,1,0:T(8,128)(2,1)S(1)} %fusion.4), channel_id=1, source_target_pairs={{0,24},{4,28},{8,16},{12,20},{16,8},{20,12},{24,0},{28,4},{1,25},{... | collective-permute-start | bytes 98312 | tf_op jit(solution)/shard_map/ppermute | solution.py:27
  58.7 0.1 collective-permute-start.21
  58.8 0.3 collective-permute-done.17
  59.1 2.2 %collective-permute-start.22 = (bf16[128,256]{1,0:T(8,128)(2,1)S(1)}, bf16[128,256]{1,0:T(8,128)(2,1)S(1)}, u32[]{:S(2)}, u32[]{:S(2)}) collective-permute-start(bf16[128,256]{1,0:T(8,128)(2,1)S(1)} %convert_element_type.145), channel_id=1, source_target_pairs={{0,2},{1,3},{2,0},{3,1},{4,6},{5,7},{6,4},{7,5},{8,10},{9,11},{10,... | collective-permute-start | bytes 196616 | tf_op jit(solution)/shard_map/ppermute | solution.py:27
  61.3 0.0 collective-permute-done.18
  61.3 1.8 %collective-permute-start.23 = (bf16[128,256]{1,0:T(8,128)(2,1)S(1)}, bf16[128,256]{1,0:T(8,128)(2,1)S(1)}, u32[]{:S(2)}, u32[]{:S(2)}) collective-permute-start(bf16[128,256]{1,0:T(8,128)(2,1)S(1)} %convert_element_type.145), channel_id=1, source_target_pairs={{0,3},{1,2},{2,1},{3,0},{4,7},{5,6},{6,5},{7,4},{8,11},{9,10},{10,... | collective-permute-start | bytes 196616 | tf_op jit(solution)/shard_map/ppermute | solution.py:27
  63.2 0.1 collective-permute-start.20
  63.3 0.0 collective-permute-done.21
  63.3 1.0 %collective-permute-done.22 = bf16[128,256]{1,0:T(8,128)(2,1)S(1)} collective-permute-done((bf16[128,256]{1,0:T(8,128)(2,1)S(1)}, bf16[128,256]{1,0:T(8,128)(2,1)S(1)}, u32[]{:S(2)}, u32[]{:S(2)}) %collective-permute-start.22) | collective-permute-done | bytes 65568 | tf_op jit(solution)/shard_map/ppermute | solution.py:27
  64.3 3.1 %collective-permute-done.23 = bf16[128,256]{1,0:T(8,128)(2,1)S(1)} collective-permute-done((bf16[128,256]{1,0:T(8,128)(2,1)S(1)}, bf16[128,256]{1,0:T(8,128)(2,1)S(1)}, u32[]{:S(2)}, u32[]{:S(2)}) %collective-permute-start.23) | collective-permute-done | bytes 65568 | tf_op jit(solution)/shard_map/ppermute | solution.py:27
  67.4 0.7 add_multiply_fusion
  68.1 0.8 %place.1 = (f32[256,256]{1,0:T(8,128)}, f32[256,256]{1,0:T(8,128)}) custom-call(s32[1]{0:T(128)} %bitcast.3.slab_ref, bf16[256,256]{1,0:T(8,128)(2,1)S(1)} %bitcast.46, bf16[256,256]{1,0:T(8,128)(2,1)S(1)} %collective-permute-done.20.odd_ref), custom_call_target="tpu_custom_call" | custom-call | tf_op jit(solution)/shard_map/place/pallas_call | solution.py:299
  69.0 1.5 %back.1 = bf16[512,256]{1,0:T(8,128)(2,1)} custom-call(f32[512,256]{1,0:T(8,128)S(1)} %get-tuple-element.22.base_ref, bf16[1024,512]{1,0:T(8,128)(2,1)S(1)} %get-tuple-element.23.even_ref, bf16[1024,512]{1,0:T(8,128)(2,1)S(1)} %get-tuple-element.24.odd_ref, bf16[4,256,256]{2,1,0:T(8,128)(2,1)S(1)} %pad_maximum_fusion.even_adj_ref, ...), custom_call_target="tpu_custom_call" | custom-call | flops 536870912 | bytes 2097152 | tf_op jit(solution)/shard_map/back/pallas_call | solution.py:270
  (31 shorter events, 0.2 us)
Async XLA Ops:
  1.3 0.9 %copy-start.1 = (bf16[1,512,256]{2,1,0:T(8,128)(2,1)S(1)}, bf16[1,512,256]{2,1,0:T(8,128)(2,1)}, u32[]{:S(2)}) copy-start(bf16[1,512,256]{2,1,0:T(8,128)(2,1)} %param.12) | copy-start | bytes 786436
  2.3 0.9 %copy-start.4 = (bf16[1,512,256]{2,1,0:T(8,128)(2,1)S(1)}, bf16[1,512,256]{2,1,0:T(8,128)(2,1)}, u32[]{:S(2)}) copy-start(bf16[1,512,256]{2,1,0:T(8,128)(2,1)} %param.11) | copy-start | bytes 786436
  3.2 0.7 %copy-start.12 = (s32[3,1024]{1,0:T(4,128)S(1)}, s32[3,1024]{1,0:T(4,128)}, u32[]{:S(2)}) copy-start(s32[3,1024]{1,0:T(4,128)} %kv_ref.3) | copy-start | bytes 36868
  5.9 14.5 %collective-permute-start.2 = (bf16[1024,512]{1,0:T(8,128)(2,1)S(1)}, bf16[1024,512]{1,0:T(8,128)(2,1)S(1)}, u32[]{:S(2)}, u32[]{:S(2)}) collective-permute-start(bf16[1024,512]{1,0:T(8,128)(2,1)S(1)} %get-tuple-element.27), channel_id=1, source_target_pairs={{0,4},{4,0},{8,12},{12,8},{16,20},{20,16},{24,28},{28,24},{1,5},{5... | collective-permute-start | bytes 3145736 | tf_op jit(solution)/shard_map/ppermute | solution.py:27
  6.5 0.9 %copy-start.2 = (bf16[1,512,256]{2,1,0:T(8,128)(2,1)S(1)}, bf16[1,512,256]{2,1,0:T(8,128)(2,1)}, u32[]{:S(2)}) copy-start(bf16[1,512,256]{2,1,0:T(8,128)(2,1)} %param.12) | copy-start | bytes 786436
  7.5 0.7 %copy-start.9 = (s32[1,4096]{1,0:T(1,128)S(1)}, s32[1,4096]{1,0:T(1,128)}, u32[]{:S(2)}) copy-start(s32[1,4096]{1,0:T(1,128)} %src_ref.1) | copy-start | bytes 49156
  8.2 0.7 %copy-start.10 = (s32[1,4096]{1,0:T(1,128)S(1)}, s32[1,4096]{1,0:T(1,128)}, u32[]{:S(2)}) copy-start(s32[1,4096]{1,0:T(1,128)} %dst_ref.1) | copy-start | bytes 49156
  8.9 0.7 %copy-start.11 = (f32[1,4096]{1,0:T(1,128)S(1)}, f32[1,4096]{1,0:T(1,128)}, u32[]{:S(2)}) copy-start(f32[1,4096]{1,0:T(1,128)} %dist_ref.1) | copy-start | bytes 49156
  9.6 8.8 %copy-start.3 = (bf16[1,512,256]{2,1,0:T(8,128)(2,1)S(1)}, bf16[1,512,256]{2,1,0:T(8,128)(2,1)}, u32[]{:S(2)}) copy-start(bf16[1,512,256]{2,1,0:T(8,128)(2,1)} %param.12) | copy-start | bytes 786436
  9.6 8.8 %copy-start.5 = (bf16[1,512,256]{2,1,0:T(8,128)(2,1)S(1)}, bf16[1,512,256]{2,1,0:T(8,128)(2,1)}, u32[]{:S(2)}) copy-start(bf16[1,512,256]{2,1,0:T(8,128)(2,1)} %param.11) | copy-start | bytes 786436
  14.8 9.8 %collective-permute-start = (bf16[256,256]{1,0:T(8,128)(2,1)S(1)}, bf16[256,256]{1,0:T(8,128)(2,1)S(1)}, u32[]{:S(2)}, u32[]{:S(2)}) collective-permute-start(bf16[256,256]{1,0:T(8,128)(2,1)S(1)} %get-tuple-element.20), channel_id=1, source_target_pairs={{0,28},{4,0},{8,4},{12,8},{16,12},{20,16},{24,20},{28,24},{1,29},{... | collective-permute-start | bytes 393224 | tf_op jit(solution)/shard_map/ppermute | solution.py:32
  18.4 6.2 %collective-permute-start.1 = (bf16[256,256]{1,0:T(8,128)(2,1)S(1)}, bf16[256,256]{1,0:T(8,128)(2,1)S(1)}, u32[]{:S(2)}, u32[]{:S(2)}) collective-permute-start(bf16[256,256]{1,0:T(8,128)(2,1)S(1)} %get-tuple-element.21), channel_id=1, source_target_pairs={{0,4},{4,8},{8,12},{12,16},{16,20},{20,24},{24,28},{28,0},{1,5},{5... | collective-permute-start | bytes 393224 | tf_op jit(solution)/shard_map/ppermute | solution.py:32
  20.8 3.8 %copy-start.7 = (bf16[256,256]{1,0:T(8,128)(2,1)S(1)}, bf16[256,256]{1,0:T(8,128)(2,1)}, u32[]{:S(2)}) copy-start(bf16[256,256]{1,0:T(8,128)(2,1)} %w_ref.2) | copy-start | bytes 393220
  20.8 3.8 %copy-start.8 = (s32[1,2,256]{2,1,0:T(2,128)S(1)}, s32[1,2,256]{2,1,0:T(2,128)}, u32[]{:S(2)}) copy-start(s32[1,2,256]{2,1,0:T(2,128)} %param.21) | copy-start | bytes 6148
  20.9 15.3 %copy-start = (f32[1024,256]{1,0:T(8,128)S(1)}, f32[1024,256]{1,0:T(8,128)}, u32[]{:S(2)}) copy-start(f32[1024,256]{1,0:T(8,128)} %filter_ref.1) | copy-start | bytes 3145732
  20.9 15.3 %copy-start.6 = (bf16[256,256]{1,0:T(8,128)(2,1)S(1)}, bf16[256,256]{1,0:T(8,128)(2,1)}, u32[]{:S(2)}) copy-start(bf16[256,256]{1,0:T(8,128)(2,1)} %w_ref.3) | copy-start | bytes 393220
  21.0 10.2 %collective-permute-start.5 = (bf16[1,256,512]{2,1,0:T(8,128)(2,1)S(1)}, bf16[1,256,512]{2,1,0:T(8,128)(2,1)S(1)}, u32[]{:S(2)}, u32[]{:S(2)}) collective-permute-start(bf16[1,256,512]{2,1,0:T(8,128)(2,1)S(1)} %get-tuple-element.34), channel_id=1, source_target_pairs={{0,24},{4,28},{8,16},{12,20},{16,8},{20,12},{24,0},{28,4},{1,25},{... | collective-permute-start | bytes 786440 | tf_op jit(solution)/shard_map/ppermute | solution.py:27
  21.6 14.0 %collective-permute-start.3 = (bf16[1,256,512]{2,1,0:T(8,128)(2,1)S(1)}, bf16[1,256,512]{2,1,0:T(8,128)(2,1)S(1)}, u32[]{:S(2)}, u32[]{:S(2)}) collective-permute-start(bf16[1,256,512]{2,1,0:T(8,128)(2,1)S(1)} %get-tuple-element.36), channel_id=1, source_target_pairs={{0,8},{4,12},{8,0},{12,4},{16,24},{20,28},{24,16},{28,20},{1,9},{5... | collective-permute-start | bytes 786440 | tf_op jit(solution)/shard_map/ppermute | solution.py:27
  23.0 13.1 %collective-permute-start.4 = (bf16[1,256,512]{2,1,0:T(8,128)(2,1)S(1)}, bf16[1,256,512]{2,1,0:T(8,128)(2,1)S(1)}, u32[]{:S(2)}, u32[]{:S(2)}) collective-permute-start(bf16[1,256,512]{2,1,0:T(8,128)(2,1)S(1)} %get-tuple-element.35), channel_id=1, source_target_pairs={{0,16},{4,20},{8,24},{12,28},{16,0},{20,4},{24,8},{28,12},{1,17},{... | collective-permute-start | bytes 786440 | tf_op jit(solution)/shard_map/ppermute | solution.py:27
  36.6 1.4 %collective-permute-start.10 = (bf16[256,256]{1,0:T(8,128)(2,1)S(1)}, bf16[256,256]{1,0:T(8,128)(2,1)S(1)}, u32[]{:S(2)}, u32[]{:S(2)}) collective-permute-start(bf16[256,256]{1,0:T(8,128)(2,1)S(1)} %get-tuple-element.30), channel_id=1, source_target_pairs={{0,4},{4,0},{8,12},{12,8},{16,20},{20,16},{24,28},{28,24},{1,5},{5... | collective-permute-start | bytes 393224 | tf_op jit(solution)/shard_map/ppermute | solution.py:27
  38.1 5.2 %collective-permute-start.11 = (bf16[1,64,256]{2,1,0:T(8,128)(2,1)S(1)}, bf16[1,64,256]{2,1,0:T(8,128)(2,1)S(1)}, u32[]{:S(2)}, u32[]{:S(2)}) collective-permute-start(bf16[1,64,256]{2,1,0:T(8,128)(2,1)S(1)} %get-tuple-element.37), channel_id=1, source_target_pairs={{0,8},{4,12},{8,0},{12,4},{16,24},{20,28},{24,16},{28,20},{1,9},{5... | collective-permute-start | bytes 98312 | tf_op jit(solution)/shard_map/ppermute | solution.py:27
  38.2 7.0 %collective-permute-start.12 = (bf16[1,64,256]{2,1,0:T(8,128)(2,1)S(1)}, bf16[1,64,256]{2,1,0:T(8,128)(2,1)S(1)}, u32[]{:S(2)}, u32[]{:S(2)}) collective-permute-start(bf16[1,64,256]{2,1,0:T(8,128)(2,1)S(1)} %get-tuple-element.39), channel_id=1, source_target_pairs={{0,16},{4,20},{8,24},{12,28},{16,0},{20,4},{24,8},{28,12},{1,17},{... | collective-permute-start | bytes 98312 | tf_op jit(solution)/shard_map/ppermute | solution.py:27
  39.8 5.4 %collective-permute-start.13 = (bf16[1,64,256]{2,1,0:T(8,128)(2,1)S(1)}, bf16[1,64,256]{2,1,0:T(8,128)(2,1)S(1)}, u32[]{:S(2)}, u32[]{:S(2)}) collective-permute-start(bf16[1,64,256]{2,1,0:T(8,128)(2,1)S(1)} %get-tuple-element.38), channel_id=1, source_target_pairs={{0,24},{4,28},{8,16},{12,20},{16,8},{20,12},{24,0},{28,4},{1,25},{... | collective-permute-start | bytes 98312 | tf_op jit(solution)/shard_map/ppermute | solution.py:27
  41.6 7.8 %collective-permute-start.6 = (bf16[1,256,256]{2,1,0:T(8,128)(2,1)S(1)}, bf16[1,256,256]{2,1,0:T(8,128)(2,1)S(1)}, u32[]{:S(2)}, u32[]{:S(2)}) collective-permute-start(bf16[1,256,256]{2,1,0:T(8,128)(2,1)S(1)} %bitcast.57), channel_id=1, source_target_pairs={{0,8},{4,12},{8,0},{12,4},{16,24},{20,28},{24,16},{28,20},{1,9},{5... | collective-permute-start | bytes 393224 | tf_op jit(solution)/shard_map/ppermute | solution.py:27
  41.7 9.7 %collective-permute-start.7 = (bf16[1,256,256]{2,1,0:T(8,128)(2,1)S(1)}, bf16[1,256,256]{2,1,0:T(8,128)(2,1)S(1)}, u32[]{:S(2)}, u32[]{:S(2)}) collective-permute-start(bf16[1,256,256]{2,1,0:T(8,128)(2,1)S(1)} %bitcast.58), channel_id=1, source_target_pairs={{0,16},{4,20},{8,24},{12,28},{16,0},{20,4},{24,8},{28,12},{1,17},{... | collective-permute-start | bytes 393224 | tf_op jit(solution)/shard_map/ppermute | solution.py:27
  43.3 8.2 %collective-permute-start.8 = (bf16[1,256,256]{2,1,0:T(8,128)(2,1)S(1)}, bf16[1,256,256]{2,1,0:T(8,128)(2,1)S(1)}, u32[]{:S(2)}, u32[]{:S(2)}) collective-permute-start(bf16[1,256,256]{2,1,0:T(8,128)(2,1)S(1)} %bitcast.59), channel_id=1, source_target_pairs={{0,24},{4,28},{8,16},{12,20},{16,8},{20,12},{24,0},{28,4},{1,25},{... | collective-permute-start | bytes 393224 | tf_op jit(solution)/shard_map/ppermute | solution.py:27
  45.2 6.4 %collective-permute-start.14 = (bf16[64,256]{1,0:T(8,128)(2,1)S(1)}, bf16[64,256]{1,0:T(8,128)(2,1)S(1)}, u32[]{:S(2)}, u32[]{:S(2)}) collective-permute-start(bf16[64,256]{1,0:T(8,128)(2,1)S(1)} %fusion.5), channel_id=1, source_target_pairs={{0,1},{1,0},{2,3},{3,2},{4,5},{5,4},{6,7},{7,6},{8,9},{9,8},{10,11... | collective-permute-start | bytes 98312 | tf_op jit(solution)/shard_map/ppermute | solution.py:27
  46.8 5.4 %collective-permute-start.15 = (bf16[64,256]{1,0:T(8,128)(2,1)S(1)}, bf16[64,256]{1,0:T(8,128)(2,1)S(1)}, u32[]{:S(2)}, u32[]{:S(2)}) collective-permute-start(bf16[64,256]{1,0:T(8,128)(2,1)S(1)} %fusion.5), channel_id=1, source_target_pairs={{0,2},{1,3},{2,0},{3,1},{4,6},{5,7},{6,4},{7,5},{8,10},{9,11},{10,... | collective-permute-start | bytes 98312 | tf_op jit(solution)/shard_map/ppermute | solution.py:27
  49.4 5.7 %collective-permute-start.16 = (bf16[64,256]{1,0:T(8,128)(2,1)S(1)}, bf16[64,256]{1,0:T(8,128)(2,1)S(1)}, u32[]{:S(2)}, u32[]{:S(2)}) collective-permute-start(bf16[64,256]{1,0:T(8,128)(2,1)S(1)} %fusion.5), channel_id=1, source_target_pairs={{0,3},{1,2},{2,1},{3,0},{4,7},{5,6},{6,5},{7,4},{8,11},{9,10},{10,... | collective-permute-start | bytes 98312 | tf_op jit(solution)/shard_map/ppermute | solution.py:27
  51.5 17.5 %collective-permute-start.9 = (bf16[4,256,256]{2,1,0:T(8,128)(2,1)S(1)}, bf16[4,256,256]{2,1,0:T(8,128)(2,1)S(1)}, u32[]{:S(2)}, u32[]{:S(2)}) collective-permute-start(bf16[4,256,256]{2,1,0:T(8,128)(2,1)S(1)} %pad_maximum_fusion.even_adj_ref), channel_id=1, source_target_pairs={{0,4},{4,0},{8,12},{12,8},{16,20},{20,16},{24,28},{28,24},{1,5},{5... | collective-permute-start | bytes 1572872 | tf_op jit(solution)/shard_map/ppermute | solution.py:27
  55.1 4.0 %collective-permute-start.17 = (bf16[1,64,256]{2,1,0:T(8,128)(2,1)S(1)}, bf16[1,64,256]{2,1,0:T(8,128)(2,1)S(1)}, u32[]{:S(2)}, u32[]{:S(2)}) collective-permute-start(bf16[1,64,256]{2,1,0:T(8,128)(2,1)S(1)} %fusion.4), channel_id=1, source_target_pairs={{0,8},{4,12},{8,0},{12,4},{16,24},{20,28},{24,16},{28,20},{1,9},{5... | collective-permute-start | bytes 98312 | tf_op jit(solution)/shard_map/ppermute | solution.py:27
  56.2 5.1 %collective-permute-start.18 = (bf16[1,64,256]{2,1,0:T(8,128)(2,1)S(1)}, bf16[1,64,256]{2,1,0:T(8,128)(2,1)S(1)}, u32[]{:S(2)}, u32[]{:S(2)}) collective-permute-start(bf16[1,64,256]{2,1,0:T(8,128)(2,1)S(1)} %fusion.4), channel_id=1, source_target_pairs={{0,16},{4,20},{8,24},{12,28},{16,0},{20,4},{24,8},{28,12},{1,17},{... | collective-permute-start | bytes 98312 | tf_op jit(solution)/shard_map/ppermute | solution.py:27
  57.4 5.7 %collective-permute-start.19 = (bf16[1,64,256]{2,1,0:T(8,128)(2,1)S(1)}, bf16[1,64,256]{2,1,0:T(8,128)(2,1)S(1)}, u32[]{:S(2)}, u32[]{:S(2)}) collective-permute-start(bf16[1,64,256]{2,1,0:T(8,128)(2,1)S(1)} %fusion.4), channel_id=1, source_target_pairs={{0,24},{4,28},{8,16},{12,20},{16,8},{20,12},{24,0},{28,4},{1,25},{... | collective-permute-start | bytes 98312 | tf_op jit(solution)/shard_map/ppermute | solution.py:27
  58.7 4.6 %collective-permute-start.21 = (bf16[128,256]{1,0:T(8,128)(2,1)S(1)}, bf16[128,256]{1,0:T(8,128)(2,1)S(1)}, u32[]{:S(2)}, u32[]{:S(2)}) collective-permute-start(bf16[128,256]{1,0:T(8,128)(2,1)S(1)} %convert_element_type.145), channel_id=1, source_target_pairs={{0,1},{1,0},{2,3},{3,2},{4,5},{5,4},{6,7},{7,6},{8,9},{9,8},{10,11... | collective-permute-start | bytes 196616 | tf_op jit(solution)/shard_map/ppermute | solution.py:27
  59.1 5.2 %collective-permute-start.22 = (bf16[128,256]{1,0:T(8,128)(2,1)S(1)}, bf16[128,256]{1,0:T(8,128)(2,1)S(1)}, u32[]{:S(2)}, u32[]{:S(2)}) collective-permute-start(bf16[128,256]{1,0:T(8,128)(2,1)S(1)} %convert_element_type.145), channel_id=1, source_target_pairs={{0,2},{1,3},{2,0},{3,1},{4,6},{5,7},{6,4},{7,5},{8,10},{9,11},{10,... | collective-permute-start | bytes 196616 | tf_op jit(solution)/shard_map/ppermute | solution.py:27
  61.3 6.1 %collective-permute-start.23 = (bf16[128,256]{1,0:T(8,128)(2,1)S(1)}, bf16[128,256]{1,0:T(8,128)(2,1)S(1)}, u32[]{:S(2)}, u32[]{:S(2)}) collective-permute-start(bf16[128,256]{1,0:T(8,128)(2,1)S(1)} %convert_element_type.145), channel_id=1, source_target_pairs={{0,3},{1,2},{2,1},{3,0},{4,7},{5,6},{6,5},{7,4},{8,11},{9,10},{10,... | collective-permute-start | bytes 196616 | tf_op jit(solution)/shard_map/ppermute | solution.py:27
  63.2 4.9 %collective-permute-start.20 = (bf16[256,256]{1,0:T(8,128)(2,1)S(1)}, bf16[256,256]{1,0:T(8,128)(2,1)S(1)}, u32[]{:S(2)}, u32[]{:S(2)}) collective-permute-start(bf16[256,256]{1,0:T(8,128)(2,1)S(1)} %bitcast.45), channel_id=1, source_target_pairs={{0,4},{4,0},{8,12},{12,8},{16,20},{20,16},{24,28},{28,24},{1,5},{5... | collective-permute-start | bytes 393224 | tf_op jit(solution)/shard_map/ppermute | solution.py:27
where the time goes:
time: 71.1 us; the launch traced here: 70.5 us
  starting transfers between devices  29 us (41%)
  waiting for transfers between devices  20.2 us (28%)
  Pallas kernels  12.6 us (18%)
  local copies, waits for them, and re-layouts  6.54 us (9%)
  other arithmetic  1.31 us (2%)
  between operations  0.88 us (1%)
    ppermute x22, starting transfers between devices, xor_permute(): lax.ppermute(value, axis, [(source, source ^ bits) for source in range(co...  25.4 us
    ppermute x22, waiting for transfers between devices, xor_permute(): lax.ppermute(value, axis, [(source, source ^ bits) for source in range(co...  20.2 us
    unnamed x27, local copies, waits for them, and re-layouts  6.44 us
    pallas_call x1, Pallas kernels, edge_rows(): pl.pallas_call(functools.partial(edge_kernel, block), name='edges', out_s...  5.19 us
    pallas_call x2, Pallas kernels, tables(): pl.pallas_call(functools.partial(tables_kernel, order), name='tables', ou...  3.99 us
    ppermute x2, starting transfers between devices, shifted(): lax.ppermute(value, axis, [(source, (source + steps) % count) for source...  3.59 us
    pallas_call x1, Pallas kernels, back_project(): pl.pallas_call(back_kernel, name='back', out_shape=jax.ShapeDtypeStruct((...  1.55 us
  transfers between devices with their start and end apart: 24, of which 9 were waited for; matrix products, arithmetic and copies ran while one was open for 2% of the time, Pallas kernels for 12%

commit v1 on v0

--- a/solution.py
+++ b/solution.py
@@ -8,6 +8,7 @@
 from jax.experimental.pallas import tpu as pltpu
 from jax.sharding import PartitionSpec as P
 
+
 cutoff_radius = 5.0
 f32, bf16 = jnp.float32, jnp.bfloat16
 
@@ -16,6 +17,7 @@
 
 VMEM = pl.BlockSpec(memory_space=pltpu.VMEM)
 SMEM = pl.BlockSpec(memory_space=pltpu.SMEM)
+HBM = pl.BlockSpec(memory_space=pltpu.HBM)
 
 
 def params():
@@ -48,69 +50,125 @@
     return total
 
 
+def halves(value):
+    high = value.astype(bf16)
+    return high, (value - high.astype(f32)).astype(bf16)
+
+
 def dot(left, right, left_dim=1, right_dim=0):
     return lax.dot_general(left, right, (((left_dim,), (right_dim,)), ((), ())), preferred_element_type=f32)
 
 
-def tables_kernel(order, slab_ref, kv_ref, pos_ref, rows_ref, cot_ref, table_ref, part_ref, k_rows, k_cols, p_rows):
+def table_blocks(order, slab, k_cols, positions, rows_ref, cot_ref, table_ref, part_ref):
     share = table_ref.shape[0] // (2 * len(order))
     channels = rows_ref.shape[1]
-    slab = slab_ref[0]
-    pos = pos_ref[...]
-    high = pos.astype(bf16).astype(f32)
-    middle = (pos - high).astype(bf16).astype(f32)
-    low = pos - high - middle
-    kv = kv_ref[...].astype(f32)
-    k_rows[...] = jnp.zeros_like(k_rows)
-    p_rows[...] = jnp.zeros_like(p_rows)
-    for i, piece in enumerate((high, middle, low)):
-        k_rows[3 * i : 3 * i + 3, :] = kv
-        p_rows[3 * i : 3 * i + 3, :] = piece
-    k_cols[...] = k_rows[...].T
-    positions = p_rows[...].astype(bf16)
-
-    def block(place, owner):
-        k_block = k_cols[pl.ds(pl.multiple_of(owner * share, 8), share), :].astype(bf16)
-        turns = dot(k_block, positions)
+    for place, offset in enumerate(order):
+        start = pl.multiple_of((slab ^ offset) * share, 8)
+        turns = dot(k_cols[pl.ds(start, share), :].astype(bf16), positions)
         r = turns - jnp.floor(turns + 0.5)
         z = r * r
         s = r * horner(sin_coefs, z)
         c = horner(cos_coefs, z)
-        cos = 1.0 - 2.0 * s * s
-        sin = 2.0 * s * c
-        table = jnp.concatenate([cos, sin], axis=0).astype(bf16)
+        table = jnp.concatenate([1.0 - 2.0 * s * s, 2.0 * s * c], axis=0).astype(bf16)
         at = pl.ds(place * 2 * share, 2 * share)
         table_ref[at, :] = table
-        part_ref[at, :channels] = dot(table, rows_ref[...]).astype(bf16)
-        part_ref[at, channels:] = dot(table, cot_ref[...]).astype(bf16)
-
-    for place, offset in enumerate(order):
-        block(place, slab ^ offset)
-
-
-def tables(order, slab, k_vectors, positions, rows, cotan, share):
-    atoms, channels = rows.shape
+        part_ref[at, :channels] = dot(table, rows_ref[...]).astype(part_ref.dtype)
+        part_ref[at, channels:] = dot(table, cot_ref[...]).astype(part_ref.dtype)
+
+
+def first_kernel(order, fetched, slab_ref, kv_hbm, pos_hbm, rows_hbm, cot_hbm, filter_hbm, *refs):
+    sources, refs = refs[:fetched], refs[fetched:]
+    table_ref, part_ref, k_cols, positions, rows_ref, cot_ref, filter_ref, *refs = refs
+    copies_to, (kv_ref, pos_ref, k_rows, p_rows, sems) = refs[:fetched], refs[fetched:]
+    slab = slab_ref[0]
+    share = filter_ref.shape[0]
+    filter_rows = pl.ds(pl.multiple_of(slab * share, 8), share)
+    pairs = [
+        (kv_hbm, kv_ref),
+        (pos_hbm.at[:, 0], pos_ref),
+        (rows_hbm.at[0], rows_ref),
+        (cot_hbm.at[0], cot_ref),
+        (filter_hbm.at[filter_rows, :], filter_ref),
+        *zip(sources, copies_to),
+    ]
+    copies = [pltpu.make_async_copy(source, target, sems.at[i]) for i, (source, target) in enumerate(pairs)]
+    for copy in copies:
+        copy.start()
+    k_rows[...] = jnp.zeros_like(k_rows)
+    p_rows[...] = jnp.zeros_like(p_rows)
+    copies[0].wait()
+    copies[1].wait()
+    pos = pos_ref[...]
+    high = pos.astype(bf16).astype(f32)
+    middle = (pos - high).astype(bf16).astype(f32)
+    kv = kv_ref[...].astype(f32)
+    for i, piece in enumerate((high, middle, pos - high - middle)):
+        k_rows[3 * i : 3 * i + 3, :] = kv
+        p_rows[3 * i : 3 * i + 3, :] = piece
+    k_cols[...] = k_rows[...].T
+    positions[...] = p_rows[...].astype(bf16)
+    copies[2].wait()
+    copies[3].wait()
+    table_blocks(order, slab, k_cols, positions[...], rows_ref, cot_ref, table_ref, part_ref)
+    for copy in copies[4:]:
+        copy.wait()
+
+
+def first_tables(order, slab, k_vectors, frac_pos, features, cotangent, k_filter, others, share):
+    _, atoms, channels = features.shape
     kcount = k_vectors.shape[1]
     height = 2 * share * len(order)
-    return pl.pallas_call(
-        functools.partial(tables_kernel, order),
-        name="tables",
+    operands = (k_vectors, frac_pos.transpose(1, 0, 2), features, cotangent, k_filter, *others)
+    shapes = [
+        ((height, atoms), bf16),
+        ((height, 2 * channels), bf16),
+        ((kcount, 16), f32),
+        ((16, atoms), bf16),
+        ((atoms, channels), bf16),
+        ((atoms, channels), bf16),
+        ((share, channels), f32),
+    ] + [(other.shape, other.dtype) for other in others]
+    return pl.pallas_call(
+        functools.partial(first_kernel, order, len(others)),
+        name="first",
+        out_shape=tuple(jax.ShapeDtypeStruct(shape, dtype) for shape, dtype in shapes),
+        in_specs=[SMEM] + [HBM] * (5 + len(others)),
+        out_specs=(VMEM,) * len(shapes),
+        scratch_shapes=[
+            pltpu.VMEM((3, kcount), jnp.int32),
+            pltpu.VMEM((3, atoms), f32),
+            pltpu.VMEM((16, kcount), f32),
+            pltpu.VMEM((16, atoms), f32),
+            pltpu.SemaphoreType.DMA((5 + len(others),)),
+        ],
+        compiler_params=params(),
+        cost_estimate=pl.CostEstimate(
+            flops=4 * height * atoms * channels, bytes_accessed=4 * height * atoms, transcendentals=0
+        ),
+    )(slab, *(pltpu.with_memory_space_constraint(value, pltpu.HBM) for value in operands))
+
+
+def second_kernel(order, slab_ref, k_cols, positions, rows_ref, cot_ref, table_ref, part_ref):
+    table_blocks(order, slab_ref[0], k_cols, positions[...], rows_ref, cot_ref, table_ref, part_ref)
+
+
+def second_tables(order, slab, k_cols, positions, rows, cotan, share):
+    atoms, channels = rows.shape
+    height = 2 * share * len(order)
+    return pl.pallas_call(
+        functools.partial(second_kernel, order),
+        name="second",
         out_shape=(
             jax.ShapeDtypeStruct((height, atoms), bf16),
-            jax.ShapeDtypeStruct((height, 2 * channels), bf16),
-        ),
-        in_specs=[SMEM, VMEM, VMEM, VMEM, VMEM],
+            jax.ShapeDtypeStruct((height, 2 * channels), f32),
+        ),
+        in_specs=[SMEM] + [VMEM] * 4,
         out_specs=(VMEM, VMEM),
-        scratch_shapes=[
-            pltpu.VMEM((16, kcount), f32),
-            pltpu.VMEM((kcount, 16), f32),
-            pltpu.VMEM((16, atoms), f32),
-        ],
-        compiler_params=params(),
-        cost_estimate=pl.CostEstimate(
-            flops=2 * height * atoms * 2 * channels, bytes_accessed=4 * height * atoms, transcendentals=0
-        ),
-    )(slab, k_vectors, positions, rows, cotan)
+        compiler_params=params(),
+        cost_estimate=pl.CostEstimate(
+            flops=4 * height * atoms * channels, bytes_accessed=4 * height * atoms, transcendentals=0
+        ),
+    )(slab, k_cols, positions, rows, cotan)
 
 
 def edge_kernel(block, src_ref, dst_ref, dist_ref, cot_ref, own_ref, low_ref, up_ref, total):
@@ -159,15 +217,17 @@
 
 def short_kernel(own_ref, above_ref, below_ref, lists_ref, rows_ref, cot_ref, w_ref, base_ref, grad_ref):
     atoms = own_ref.shape[0]
-    lists = lists_ref[...]
+    lists = lists_ref[0]
     shape = (atoms, lists.shape[1])
     row_at = lax.broadcasted_iota(jnp.int32, shape, 0)
     to_lower = (row_at == lists[0:1, :]).astype(f32).astype(bf16)
     to_upper = (row_at == lists[1:2, :]).astype(f32).astype(bf16)
     owned = own_ref[...] + dot(to_upper, above_ref[...]) + dot(to_lower, below_ref[...])
-    owned = owned.astype(bf16)
-    base_ref[...] = cot_ref[...].astype(f32) + dot(owned, w_ref[...], 1, 1)
-    grad_ref[...] = dot(rows_ref[...], owned, 0, 0)
+    high, low = halves(owned)
+    w = w_ref[...]
+    base_ref[...] = cot_ref[...].astype(f32) + (dot(high, w, 1, 1) + dot(low, w, 1, 1))
+    rows = rows_ref[...].T
+    grad_ref[...] = dot(rows, high) + dot(rows, low)
 
 
 def short_range(own, above, below, lists, rows, cotan, w_short):
@@ -197,12 +257,12 @@
     for part in parts:
         total = total + part[...].astype(f32)
     structure = total[:, :channels]
-    moved = total[:, channels:].astype(bf16)
-    response = dot(moved, w_ref[...], 1, 1)
+    moved, moved_low = halves(total[:, channels:])
+    response = dot(moved, w_ref[...], 1, 1) + dot(moved_low, w_ref[...], 1, 1)
     k_filter = filter_ref[...]
     double = jnp.concatenate([k_filter, k_filter], axis=0) * norm
-    filtered = (structure * double).astype(bf16)
-    full[:channels, :] = dot(filtered, moved, 0, 0)
+    filtered, filtered_low = halves((structure * double).T)
+    full[:channels, :] = dot(filtered, moved) + (dot(filtered, moved_low) + dot(filtered_low, moved))
     full[channels:, :] = short_ref[...]
     half = len(order) // 2
     for place, offset in enumerate(order):
@@ -219,25 +279,6 @@
 def own_share(order, norm, slab, k_filter, w_out, short_grad, own, parts):
     height, channels = own.shape[0], w_out.shape[0]
     share = height // 2
-    whole = lambda shape: pl.BlockSpec(shape, lambda i, slab_ref: (0, 0))
-    grid_spec = pltpu.PrefetchScalarGridSpec(
-        num_scalar_prefetch=1,
-        grid=(1,),
-        in_specs=[
-            pl.BlockSpec((share, channels), lambda i, slab_ref: (slab_ref[0], 0)),
-            whole(w_out.shape),
-            whole(short_grad.shape),
-            whole(own.shape),
-        ]
-        + [whole(own.shape)] * len(parts),
-        out_specs=(
-            whole((channels, height)),
-            whole((share, channels)),
-            whole((channels, channels)),
-            whole((channels, channels)),
-        ),
-        scratch_shapes=[pltpu.VMEM((2 * channels, channels), f32)],
-    )
     return pl.pallas_call(
         functools.partial(share_kernel, order, norm, len(parts)),
         name="share",
@@ -247,7 +288,9 @@
             jax.ShapeDtypeStruct((channels, channels), bf16),
             jax.ShapeDtypeStruct((channels, channels), f32),
         ),
-        grid_spec=grid_spec,
+        in_specs=[SMEM] + [VMEM] * (4 + len(parts)),
+        out_specs=(VMEM,) * 4,
+        scratch_shapes=[pltpu.VMEM((2 * channels, channels), f32)],
         compiler_params=params(),
         cost_estimate=pl.CostEstimate(
             flops=4 * height * channels * channels, bytes_accessed=16 * height * channels, transcendentals=0
@@ -314,7 +357,9 @@
             blocks = sum((part.astype(f32) for part in parts), blocks.astype(f32))
         width = len(group)
         split = blocks.reshape(-1, width, *blocks.shape[1:])
-        parts = [xor_permute(split[:, g].astype(bf16), "slab", group[g]) for g in range(1, width)]
+        parts = []
+        for g in range(1, width):
+            parts.append(xor_permute(split[:, g].astype(bf16), "slab", group[g]))
         blocks = split[:, 0]
     return blocks, parts
 
@@ -322,23 +367,30 @@
 def gather_blocks(block, groups):
     blocks, order = block[None], [0]
     for group in reversed(groups):
-        pieces = [blocks] + [xor_permute(blocks, "slab", offset) for offset in group[1:]]
+        pieces = [blocks]
+        for g in range(1, len(group)):
+            pieces.append(xor_permute(blocks, "slab", group[g]))
         blocks = jnp.concatenate(pieces, axis=0)
         order = [offset ^ held for offset in group for held in order]
-    return blocks, order
+    place_of = [order.index(offset) for offset in sorted(order)]
+    if place_of != list(range(len(order))):
+        blocks = jnp.stack([blocks[i] for i in place_of])
+    return blocks
 
 
 def sum_replicas(value):
     count = lax.axis_size("rep")
     sent = value.astype(bf16)
-    terms = [sent] + [xor_permute(sent, "rep", offset) for offset in range(1, count)]
+    terms = [sent]
+    for offset in range(1, count):
+        terms.append(xor_permute(sent, "rep", offset))
     terms = [term.astype(f32) for term in terms]
     while len(terms) > 1:
         terms = [terms[i] + terms[i + 1] for i in range(0, len(terms), 2)]
     return terms[0]
 
 
-def body(
+def block(
     features,
     cotangent,
     frac_pos,
@@ -351,9 +403,7 @@
     distance,
     halo_idx,
 ):
-    rows = features[0]
-    cotan = cotangent[0]
-    atoms, channels = rows.shape
+    _, atoms, channels = features.shape
     kcount = k_filter.shape[0]
     count = lax.axis_size("slab")
     replicas = lax.axis_size("rep")
@@ -361,56 +411,60 @@
     scale = 1.0 / math.sqrt(replicas * atoms * count)
     share = kcount // count
     slab = lax.axis_index("slab").astype(jnp.int32)[None]
-    pair, *rest = exchange_groups(count)
-
-    even = [0]
-    for group in reversed(rest):
-        even = [offset ^ held for offset in group for held in even]
-    keep_order = sorted(even)
-    odd = [offset ^ 1 for offset in keep_order]
-    order = odd + keep_order
-
-    odd_table, odd_part = tables(tuple(odd), slab, k_vectors, frac_pos[0], rows, cotan, share)
+    _, *rest = exchange_groups(count)
+
+    even = tuple(range(0, count, 2))
+    odd = tuple(offset + 1 for offset in even)
+    order = odd + even
+    half = count // 2
+
+    odd_table, odd_part, k_cols, positions, rows, cotan, own_filter, src, dst, dist, lists, w_out, w_short = (
+        first_tables(
+            odd,
+            slab,
+            k_vectors,
+            frac_pos,
+            features,
+            cotangent,
+            k_filter,
+            (edge_src, edge_dst, distance, halo_idx, w_out, w_short),
+            share,
+        )
+    )
     from_pair = xor_permute(odd_part, "slab", 1)
-    even_table, even_part = tables(tuple(keep_order), slab, k_vectors, frac_pos[0], rows, cotan, share)
-
-    own_rows, lower, upper = edge_rows(edge_src, edge_dst, distance, cotan, halo_idx.shape[2])
+    even_table, even_part = second_tables(even, slab, k_cols, positions, rows, cotan, share)
+    paired = even_part + from_pair.astype(f32)
+    own, parts = scatter_blocks(paired.reshape(half, 2 * share, 2 * channels), rest)
+
+    own_rows, lower, upper = edge_rows(src, dst, dist, cotan, lists.shape[2])
     from_above = shifted(lower, "slab", -1)
     from_below = shifted(upper, "slab", 1)
-    base, short_grad = short_range(own_rows, from_above, from_below, halo_idx[0], rows, cotan, w_short)
-
-    half = count // 2
-    paired = even_part.astype(f32) + from_pair.astype(f32)
-    own, parts = scatter_blocks(paired.reshape(half, 2 * share, 2 * channels), rest)
+    base, short_grad = short_range(own_rows, from_above, from_below, lists, rows, cotan, w_short)
+
     adj, gfilter, send, keep = own_share(
-        tuple(order), norm, slab, k_filter, w_out, short_grad, own[0], [part[0] for part in parts]
+        order, norm, slab, own_filter, w_out, short_grad, own[0], [part[0] for part in parts]
     )
 
-    summed = keep + xor_permute(send, "slab", 1).astype(f32)
+    from_pair = xor_permute(send, "slab", 1)
+    summed = keep + from_pair.astype(f32)
     own_grad, grad_parts = scatter_blocks(summed.reshape(half, -1, channels), rest)
     own_grad = sum((part.astype(f32) for part in grad_parts), own_grad)[0]
 
-    adj_even, held = gather_blocks(adj, rest)
-    place_of = [held.index(offset) for offset in keep_order]
-    if place_of != list(range(half)):
-        adj_even = jnp.stack([adj_even[i] for i in place_of])
+    adj_even = gather_blocks(adj, rest)
     adj_odd = xor_permute(adj_even, "slab", 1)
     grad_features = back_project(base, even_table, odd_table, adj_even, adj_odd)
 
     own_grad = sum_replicas(own_grad).astype(bf16)
     grad_filter = sum_replicas(gfilter) / replicas
-    grad_even, _ = gather_blocks(own_grad, rest)
-    if place_of != list(range(half)):
-        grad_even = jnp.stack([grad_even[i] for i in place_of])
-    grad_even = grad_even.reshape(-1, channels)
+    grad_even = gather_blocks(own_grad, rest).reshape(-1, channels)
     grad_odd = xor_permute(grad_even, "slab", 1)
-    grad_wout, grad_wshort = place_grads(tuple(order), scale, slab, grad_even, grad_odd)
+    grad_wout, grad_wshort = place_grads(order, scale, slab, grad_even, grad_odd)
     return (grad_features[None], grad_wout, grad_wshort, grad_filter)
 
 
 def solution(mesh):
     return jax.shard_map(
-        body,
+        block,
         mesh=mesh,
         in_specs=(
             P("rep", "slab", None),

time: 71.1 us -> 64 us (0.900)
  local copies, waits for them, and re-layouts: 6.54 us -> 0.1 us
  waiting for transfers between devices: 20.2 us -> 19.4 us
    unnamed x27 -> x0, local copies, waits for them, and re-layouts: 6.44 us -> none
    ppermute x22, waiting for transfers between devices: 20.2 us -> 19.3 us  [xor_permute(): lax.ppermute(value, axis, [(source, source ^ bits) for source in range(co...]
  transfers between devices with their start and end apart: 24 -> 24, of which waited for: 9 -> 8; matrix products, arithmetic and copies ran while one was open for 2% -> 2% of each run, Pallas kernels for 12% -> 13%
where the time goes in v1:
time: 64 us; the launch traced here: 63.8 us
  starting transfers between devices  28.9 us (45%)
  waiting for transfers between devices  19.4 us (30%)
  Pallas kernels  13.3 us (21%)
  other arithmetic  1.32 us (2%)
  between operations  0.79 us (1%)
    ppermute x22, starting transfers between devices, xor_permute(): lax.ppermute(value, axis, [(source, source ^ bits) for source in range(co...  25.3 us
    ppermute x22, waiting for transfers between devices, xor_permute(): lax.ppermute(value, axis, [(source, source ^ bits) for source in range(co...  19.3 us
    pallas_call x1, Pallas kernels, edge_rows(): pl.pallas_call(functools.partial(edge_kernel, block), name='edges', out_s...  5.19 us
    ppermute x2, starting transfers between devices, shifted(): lax.ppermute(value, axis, [(source, (source + steps) % count) for source...  3.6 us
    pallas_call x1, Pallas kernels, first_tables(): pl.pallas_call(functools.partial(first_kernel, order, len(others)), name=...  2.9 us
    pallas_call x1, Pallas kernels, second_tables(): pl.pallas_call(functools.partial(second_kernel, order), name='second', ou...  1.7 us
    pallas_call x1, Pallas kernels, back_project(): pl.pallas_call(back_kernel, name='back', out_shape=jax.ShapeDtypeStruct((...  1.55 us
  transfers between devices with their start and end apart: 24, of which 8 were waited for; matrix products, arithmetic and copies ran while one was open for 2% of the time, Pallas kernels for 13%

profile of v1, /device:TPU:0, one launch (start us, length us, event | category | flops | bytes accessed | tf_op | source)
XLA Modules:
  0.0 63.8 jit_solution(1118662402902822644)
XLA Ops:
  0.6 2.9 %first.1 = (bf16[1024,512]{1,0:T(8,128)(2,1)S(1)}, bf16[1024,512]{1,0:T(8,128)(2,1)S(1)}, f32[1024,16]{1,0:T(8,128)S(1)}, bf16[16,512]{1,0:T(8,128)(2,1)S(1)}, b...) custom-call(s32[1]{0:T(128)} %bitcast.slab_ref, ...), custom_call_target="tpu_custom_call" | custom-call | flops 536870912 | bytes 2097152 | tf_op jit(solution)/shard_map/first/pallas_call | solution.py:131
  3.5 0.6 collective-permute-start.2
  4.1 5.2 %edges.1 = (f32[512,256]{1,0:T(8,128)S(1)}, bf16[256,256]{1,0:T(8,128)(2,1)S(1)}, bf16[256,256]{1,0:T(8,128)(2,1)S(1)}) custom-call(s32[1,4096]{1,0:T(1,128)S(1)} %get-tuple-element.30.src_ref, s32[1,4096]{1,0:T(1,128)S(1)} %get-tuple-element.31.dst_ref, f32[1,4096]{1,0:T(1,128)S(1)} %get-tuple-element.32.dist_ref, ...), custom_call_target="tpu_custom_call" | custom-call | flops 3221225472 | bytes 49152 | tf_op jit(solution)/shard_map/edges/pallas_call | solution.py:200
  9.3 3.6 %collective-permute-start = (bf16[256,256]{1,0:T(8,128)(2,1)S(1)}, bf16[256,256]{1,0:T(8,128)(2,1)S(1)}, u32[]{:S(2)}, u32[]{:S(2)}) collective-permute-start(bf16[256,256]{1,0:T(8,128)(2,1)S(1)} %get-tuple-element.35), channel_id=1, source_target_pairs={{0,28},{4,0},{8,4},{12,8},{16,12},{20,16},{24,20},{28,24},{1,29},{... | collective-permute-start | bytes 393224 | tf_op jit(solution)/shard_map/ppermute | solution.py:34
  12.9 0.0 collective-permute-start.1
  12.9 1.7 %second.1 = (bf16[1024,512]{1,0:T(8,128)(2,1)S(1)}, f32[1024,512]{1,0:T(8,128)S(1)}) custom-call(s32[1]{0:T(128)} %bitcast.slab_ref, f32[1024,16]{1,0:T(8,128)S(1)} %get-tuple-element.41.k_cols, bf16[16,512]{1,0:T(8,128)(2,1)S(1)} %get-tuple-element.42.positions, bf16[512,256]{1,0:T(8,128)(2,1)S(1)} %get-tuple-element.38.rows_ref, ...), custom_call_target="tpu_custom_call" | custom-call | flops 536870912 | bytes 2097152 | tf_op jit(solution)/shard_map/second/pallas_call | solution.py:158
  14.6 0.0 collective-permute-done.2
  14.6 0.3 convert_add_fusion
  15.0 0.1 convert.10
  15.1 0.1 slice_bitcast_fusion.1
  15.2 0.6 collective-permute-start.5
  15.8 0.4 collective-permute-start.4
  16.2 2.5 %collective-permute-start.3 = (bf16[1,256,512]{2,1,0:T(8,128)(2,1)S(1)}, bf16[1,256,512]{2,1,0:T(8,128)(2,1)S(1)}, u32[]{:S(2)}, u32[]{:S(2)}) collective-permute-start(bf16[1,256,512]{2,1,0:T(8,128)(2,1)S(1)} %get-tuple-element.58), channel_id=1, source_target_pairs={{0,8},{4,12},{8,0},{12,4},{16,24},{20,28},{24,16},{28,20},{1,9},{5... | collective-permute-start | bytes 786440 | tf_op jit(solution)/shard_map/ppermute | solution.py:29
  18.7 0.0 collective-permute-done.above_ref
  18.7 0.0 collective-permute-done.1.below_ref
  18.7 0.6 short.1
  19.4 6.0 %collective-permute-done.5 = bf16[1,256,512]{2,1,0:T(8,128)(2,1)S(1)} collective-permute-done((bf16[1,256,512]{2,1,0:T(8,128)(2,1)S(1)}, bf16[1,256,512]{2,1,0:T(8,128)(2,1)S(1)}, u32[]{:S(2)}, u32[]{:S(2)}) %collective-permute-start.5) | collective-permute-done | bytes 262176 | tf_op jit(solution)/shard_map/ppermute | solution.py:29
  25.3 4.9 %collective-permute-done.4 = bf16[1,256,512]{2,1,0:T(8,128)(2,1)S(1)} collective-permute-done((bf16[1,256,512]{2,1,0:T(8,128)(2,1)S(1)}, bf16[1,256,512]{2,1,0:T(8,128)(2,1)S(1)}, u32[]{:S(2)}, u32[]{:S(2)}) %collective-permute-start.4) | collective-permute-done | bytes 262176 | tf_op jit(solution)/shard_map/ppermute | solution.py:29
  30.2 0.0 collective-permute-done.3
  30.3 0.5 share.1
  30.8 0.2 collective-permute-start.10
  31.0 1.2 %collective-permute-done.10 = bf16[256,256]{1,0:T(8,128)(2,1)S(1)} collective-permute-done((bf16[256,256]{1,0:T(8,128)(2,1)S(1)}, bf16[256,256]{1,0:T(8,128)(2,1)S(1)}, u32[]{:S(2)}, u32[]{:S(2)}) %collective-permute-start.10) | collective-permute-done | bytes 131104 | tf_op jit(solution)/shard_map/ppermute | solution.py:29
  32.3 0.3 collective-permute-start.11
  32.5 2.0 %collective-permute-start.13 = (bf16[1,64,256]{2,1,0:T(8,128)(2,1)S(1)}, bf16[1,64,256]{2,1,0:T(8,128)(2,1)S(1)}, u32[]{:S(2)}, u32[]{:S(2)}) collective-permute-start(bf16[1,64,256]{2,1,0:T(8,128)(2,1)S(1)} %get-tuple-element.60), channel_id=1, source_target_pairs={{0,24},{4,28},{8,16},{12,20},{16,8},{20,12},{24,0},{28,4},{1,25},{... | collective-permute-start | bytes 98312 | tf_op jit(solution)/shard_map/ppermute | solution.py:29
  34.5 1.3 %collective-permute-start.12 = (bf16[1,64,256]{2,1,0:T(8,128)(2,1)S(1)}, bf16[1,64,256]{2,1,0:T(8,128)(2,1)S(1)}, u32[]{:S(2)}, u32[]{:S(2)}) collective-permute-start(bf16[1,64,256]{2,1,0:T(8,128)(2,1)S(1)} %get-tuple-element.61), channel_id=1, source_target_pairs={{0,16},{4,20},{8,24},{12,28},{16,0},{20,4},{24,8},{28,12},{1,17},{... | collective-permute-start | bytes 98312 | tf_op jit(solution)/shard_map/ppermute | solution.py:29
  35.8 1.2 %collective-permute-start.8 = (bf16[1,256,256]{2,1,0:T(8,128)(2,1)S(1)}, bf16[1,256,256]{2,1,0:T(8,128)(2,1)S(1)}, u32[]{:S(2)}, u32[]{:S(2)}) collective-permute-start(bf16[1,256,256]{2,1,0:T(8,128)(2,1)S(1)} %bitcast.45), channel_id=1, source_target_pairs={{0,24},{4,28},{8,16},{12,20},{16,8},{20,12},{24,0},{28,4},{1,25},{... | collective-permute-start | bytes 393224 | tf_op jit(solution)/shard_map/ppermute | solution.py:29
  37.0 0.5 collective-permute-start.7
  37.5 0.0 collective-permute-done.11
  37.5 1.8 %collective-permute-start.6 = (bf16[1,256,256]{2,1,0:T(8,128)(2,1)S(1)}, bf16[1,256,256]{2,1,0:T(8,128)(2,1)S(1)}, u32[]{:S(2)}, u32[]{:S(2)}) collective-permute-start(bf16[1,256,256]{2,1,0:T(8,128)(2,1)S(1)} %bitcast.47), channel_id=1, source_target_pairs={{0,8},{4,12},{8,0},{12,4},{16,24},{20,28},{24,16},{28,20},{1,9},{5... | collective-permute-start | bytes 393224 | tf_op jit(solution)/shard_map/ppermute | solution.py:29
  39.3 0.0 collective-permute-done.13
  39.3 0.0 collective-permute-done.12
  39.3 3.7 %collective-permute-start.16 = (bf16[64,256]{1,0:T(8,128)(2,1)S(1)}, bf16[64,256]{1,0:T(8,128)(2,1)S(1)}, u32[]{:S(2)}, u32[]{:S(2)}) collective-permute-start(bf16[64,256]{1,0:T(8,128)(2,1)S(1)} %fusion.5), channel_id=1, source_target_pairs={{0,3},{1,2},{2,1},{3,0},{4,7},{5,6},{6,5},{7,4},{8,11},{9,10},{10,... | collective-permute-start | bytes 98312 | tf_op jit(solution)/shard_map/ppermute | solution.py:29
  43.0 0.0 collective-permute-start.15
  43.0 0.0 collective-permute-done.8
  43.0 1.4 %collective-permute-start.14 = (bf16[64,256]{1,0:T(8,128)(2,1)S(1)}, bf16[64,256]{1,0:T(8,128)(2,1)S(1)}, u32[]{:S(2)}, u32[]{:S(2)}) collective-permute-start(bf16[64,256]{1,0:T(8,128)(2,1)S(1)} %fusion.5), channel_id=1, source_target_pairs={{0,1},{1,0},{2,3},{3,2},{4,5},{5,4},{6,7},{7,6},{8,9},{9,8},{10,11... | collective-permute-start | bytes 98312 | tf_op jit(solution)/shard_map/ppermute | solution.py:29
  44.4 0.0 collective-permute-done.7
  44.4 0.0 collective-permute-done.6
  44.4 0.1 pad_maximum_fusion.even_adj_ref
  44.5 0.1 collective-permute-start.9
  44.6 0.7 %collective-permute-done.16 = bf16[64,256]{1,0:T(8,128)(2,1)S(1)} collective-permute-done((bf16[64,256]{1,0:T(8,128)(2,1)S(1)}, bf16[64,256]{1,0:T(8,128)(2,1)S(1)}, u32[]{:S(2)}, u32[]{:S(2)}) %collective-permute-start.16) | collective-permute-done | bytes 32800 | tf_op jit(solution)/shard_map/ppermute | solution.py:29
  45.2 2.6 %collective-permute-done.15 = bf16[64,256]{1,0:T(8,128)(2,1)S(1)} collective-permute-done((bf16[64,256]{1,0:T(8,128)(2,1)S(1)}, bf16[64,256]{1,0:T(8,128)(2,1)S(1)}, u32[]{:S(2)}, u32[]{:S(2)}) %collective-permute-start.15) | collective-permute-done | bytes 32800 | tf_op jit(solution)/shard_map/ppermute | solution.py:29
  47.8 0.0 collective-permute-done.14
  47.9 1.3 %collective-permute-start.19 = (bf16[1,64,256]{2,1,0:T(8,128)(2,1)S(1)}, bf16[1,64,256]{2,1,0:T(8,128)(2,1)S(1)}, u32[]{:S(2)}, u32[]{:S(2)}) collective-permute-start(bf16[1,64,256]{2,1,0:T(8,128)(2,1)S(1)} %fusion.4), channel_id=1, source_target_pairs={{0,24},{4,28},{8,16},{12,20},{16,8},{20,12},{24,0},{28,4},{1,25},{... | collective-permute-start | bytes 98312 | tf_op jit(solution)/shard_map/ppermute | solution.py:29
  49.1 3.0 %collective-permute-start.18 = (bf16[1,64,256]{2,1,0:T(8,128)(2,1)S(1)}, bf16[1,64,256]{2,1,0:T(8,128)(2,1)S(1)}, u32[]{:S(2)}, u32[]{:S(2)}) collective-permute-start(bf16[1,64,256]{2,1,0:T(8,128)(2,1)S(1)} %fusion.4), channel_id=1, source_target_pairs={{0,16},{4,20},{8,24},{12,28},{16,0},{20,4},{24,8},{28,12},{1,17},{... | collective-permute-start | bytes 98312 | tf_op jit(solution)/shard_map/ppermute | solution.py:29
  52.1 0.0 collective-permute-start.17
  52.1 2.1 %collective-permute-start.22 = (bf16[128,256]{1,0:T(8,128)(2,1)S(1)}, bf16[128,256]{1,0:T(8,128)(2,1)S(1)}, u32[]{:S(2)}, u32[]{:S(2)}) collective-permute-start(bf16[128,256]{1,0:T(8,128)(2,1)S(1)} %convert_element_type.141), channel_id=1, source_target_pairs={{0,2},{1,3},{2,0},{3,1},{4,6},{5,7},{6,4},{7,5},{8,10},{9,11},{10,... | collective-permute-start | bytes 196616 | tf_op jit(solution)/shard_map/ppermute | solution.py:29
  54.2 0.0 collective-permute-done.19
  54.2 0.3 collective-permute-start.21
  54.6 0.0 collective-permute-done.18
  54.6 2.0 %collective-permute-start.23 = (bf16[128,256]{1,0:T(8,128)(2,1)S(1)}, bf16[128,256]{1,0:T(8,128)(2,1)S(1)}, u32[]{:S(2)}, u32[]{:S(2)}) collective-permute-start(bf16[128,256]{1,0:T(8,128)(2,1)S(1)} %convert_element_type.141), channel_id=1, source_target_pairs={{0,3},{1,2},{2,1},{3,0},{4,7},{5,6},{6,5},{7,4},{8,11},{9,10},{10,... | collective-permute-start | bytes 196616 | tf_op jit(solution)/shard_map/ppermute | solution.py:29
  56.6 0.0 collective-permute-done.17
  56.6 0.1 collective-permute-start.20
  56.7 1.4 %collective-permute-done.22 = bf16[128,256]{1,0:T(8,128)(2,1)S(1)} collective-permute-done((bf16[128,256]{1,0:T(8,128)(2,1)S(1)}, bf16[128,256]{1,0:T(8,128)(2,1)S(1)}, u32[]{:S(2)}, u32[]{:S(2)}) %collective-permute-start.22) | collective-permute-done | bytes 65568 | tf_op jit(solution)/shard_map/ppermute | solution.py:29
  58.1 0.7 %collective-permute-done.21 = bf16[128,256]{1,0:T(8,128)(2,1)S(1)} collective-permute-done((bf16[128,256]{1,0:T(8,128)(2,1)S(1)}, bf16[128,256]{1,0:T(8,128)(2,1)S(1)}, u32[]{:S(2)}, u32[]{:S(2)}) %collective-permute-start.21) | collective-permute-done | bytes 65568 | tf_op jit(solution)/shard_map/ppermute | solution.py:29
  58.8 1.9 %collective-permute-done.23 = bf16[128,256]{1,0:T(8,128)(2,1)S(1)} collective-permute-done((bf16[128,256]{1,0:T(8,128)(2,1)S(1)}, bf16[128,256]{1,0:T(8,128)(2,1)S(1)}, u32[]{:S(2)}, u32[]{:S(2)}) %collective-permute-start.23) | collective-permute-done | bytes 65568 | tf_op jit(solution)/shard_map/ppermute | solution.py:29
  60.7 0.7 %add_multiply_fusion = f32[128,256]{1,0:T(8,128)} fusion(bf16[128,256]{1,0:T(8,128)(2,1)S(1)} %collective-permute-done.23, bf16[128,256]{1,0:T(8,128)(2,1)S(1)} %collective-permute-done.22, bf16[128,256]{1,0:T(8,128)(2,1)S(1)} %collective-permute-done.21, f32[128,256]{1,0:T(8,128)S(1)} %get-tuple-element.55), kind=kLoop, calls=%fused_computation.8 | loop fusion | flops 294912 | bytes 458752 | tf_op jit(solution)/shard_map/div | solution.py:458
  61.4 0.0 collective-permute-done.20.odd_ref
  61.4 0.8 %place.1 = (f32[256,256]{1,0:T(8,128)}, f32[256,256]{1,0:T(8,128)}) custom-call(s32[1]{0:T(128)} %bitcast.slab_ref, bf16[256,256]{1,0:T(8,128)(2,1)S(1)} %bitcast.41, bf16[256,256]{1,0:T(8,128)(2,1)S(1)} %collective-permute-done.20.odd_ref), custom_call_target="tpu_custom_call" | custom-call | tf_op jit(solution)/shard_map/place/pallas_call | solution.py:342
  62.2 0.0 collective-permute-done.9.odd_adj_ref
  62.2 1.5 %back.1 = bf16[512,256]{1,0:T(8,128)(2,1)} custom-call(f32[512,256]{1,0:T(8,128)S(1)} %get-tuple-element.40.base_ref, bf16[1024,512]{1,0:T(8,128)(2,1)S(1)} %get-tuple-element.43.even_ref, bf16[1024,512]{1,0:T(8,128)(2,1)S(1)} %get-tuple-element.44.odd_ref, bf16[4,256,256]{2,1,0:T(8,128)(2,1)S(1)} %pad_maximum_fusion.even_adj_ref, ...), custom_call_target="tpu_custom_call" | custom-call | flops 536870912 | bytes 2097152 | tf_op jit(solution)/shard_map/back/pallas_call | solution.py:313
  (8 shorter events, 0.1 us)
Async XLA Ops:
  3.5 11.1 %collective-permute-start.2 = (bf16[1024,512]{1,0:T(8,128)(2,1)S(1)}, bf16[1024,512]{1,0:T(8,128)(2,1)S(1)}, u32[]{:S(2)}, u32[]{:S(2)}) collective-permute-start(bf16[1024,512]{1,0:T(8,128)(2,1)S(1)} %get-tuple-element.49), channel_id=1, source_target_pairs={{0,4},{4,0},{8,12},{12,8},{16,20},{20,16},{24,28},{28,24},{1,5},{5... | collective-permute-start | bytes 3145736 | tf_op jit(solution)/shard_map/ppermute | solution.py:29
  9.3 9.4 %collective-permute-start = (bf16[256,256]{1,0:T(8,128)(2,1)S(1)}, bf16[256,256]{1,0:T(8,128)(2,1)S(1)}, u32[]{:S(2)}, u32[]{:S(2)}) collective-permute-start(bf16[256,256]{1,0:T(8,128)(2,1)S(1)} %get-tuple-element.35), channel_id=1, source_target_pairs={{0,28},{4,0},{8,4},{12,8},{16,12},{20,16},{24,20},{28,24},{1,29},{... | collective-permute-start | bytes 393224 | tf_op jit(solution)/shard_map/ppermute | solution.py:34
  12.9 5.8 %collective-permute-start.1 = (bf16[256,256]{1,0:T(8,128)(2,1)S(1)}, bf16[256,256]{1,0:T(8,128)(2,1)S(1)}, u32[]{:S(2)}, u32[]{:S(2)}) collective-permute-start(bf16[256,256]{1,0:T(8,128)(2,1)S(1)} %get-tuple-element.36), channel_id=1, source_target_pairs={{0,4},{4,8},{8,12},{12,16},{16,20},{20,24},{24,28},{28,0},{1,5},{5... | collective-permute-start | bytes 393224 | tf_op jit(solution)/shard_map/ppermute | solution.py:34
  15.2 10.2 %collective-permute-start.5 = (bf16[1,256,512]{2,1,0:T(8,128)(2,1)S(1)}, bf16[1,256,512]{2,1,0:T(8,128)(2,1)S(1)}, u32[]{:S(2)}, u32[]{:S(2)}) collective-permute-start(bf16[1,256,512]{2,1,0:T(8,128)(2,1)S(1)} %get-tuple-element.56), channel_id=1, source_target_pairs={{0,24},{4,28},{8,16},{12,20},{16,8},{20,12},{24,0},{28,4},{1,25},{... | collective-permute-start | bytes 786440 | tf_op jit(solution)/shard_map/ppermute | solution.py:29
  15.8 14.5 %collective-permute-start.4 = (bf16[1,256,512]{2,1,0:T(8,128)(2,1)S(1)}, bf16[1,256,512]{2,1,0:T(8,128)(2,1)S(1)}, u32[]{:S(2)}, u32[]{:S(2)}) collective-permute-start(bf16[1,256,512]{2,1,0:T(8,128)(2,1)S(1)} %get-tuple-element.57), channel_id=1, source_target_pairs={{0,16},{4,20},{8,24},{12,28},{16,0},{20,4},{24,8},{28,12},{1,17},{... | collective-permute-start | bytes 786440 | tf_op jit(solution)/shard_map/ppermute | solution.py:29
  16.2 14.1 %collective-permute-start.3 = (bf16[1,256,512]{2,1,0:T(8,128)(2,1)S(1)}, bf16[1,256,512]{2,1,0:T(8,128)(2,1)S(1)}, u32[]{:S(2)}, u32[]{:S(2)}) collective-permute-start(bf16[1,256,512]{2,1,0:T(8,128)(2,1)S(1)} %get-tuple-element.58), channel_id=1, source_target_pairs={{0,8},{4,12},{8,0},{12,4},{16,24},{20,28},{24,16},{28,20},{1,9},{5... | collective-permute-start | bytes 786440 | tf_op jit(solution)/shard_map/ppermute | solution.py:29
  30.8 1.4 %collective-permute-start.10 = (bf16[256,256]{1,0:T(8,128)(2,1)S(1)}, bf16[256,256]{1,0:T(8,128)(2,1)S(1)}, u32[]{:S(2)}, u32[]{:S(2)}) collective-permute-start(bf16[256,256]{1,0:T(8,128)(2,1)S(1)} %get-tuple-element.52), channel_id=1, source_target_pairs={{0,4},{4,0},{8,12},{12,8},{16,20},{20,16},{24,28},{28,24},{1,5},{5... | collective-permute-start | bytes 393224 | tf_op jit(solution)/shard_map/ppermute | solution.py:29
  32.3 5.2 %collective-permute-start.11 = (bf16[1,64,256]{2,1,0:T(8,128)(2,1)S(1)}, bf16[1,64,256]{2,1,0:T(8,128)(2,1)S(1)}, u32[]{:S(2)}, u32[]{:S(2)}) collective-permute-start(bf16[1,64,256]{2,1,0:T(8,128)(2,1)S(1)} %get-tuple-element.59), channel_id=1, source_target_pairs={{0,8},{4,12},{8,0},{12,4},{16,24},{20,28},{24,16},{28,20},{1,9},{5... | collective-permute-start | bytes 98312 | tf_op jit(solution)/shard_map/ppermute | solution.py:29
  32.5 6.8 %collective-permute-start.13 = (bf16[1,64,256]{2,1,0:T(8,128)(2,1)S(1)}, bf16[1,64,256]{2,1,0:T(8,128)(2,1)S(1)}, u32[]{:S(2)}, u32[]{:S(2)}) collective-permute-start(bf16[1,64,256]{2,1,0:T(8,128)(2,1)S(1)} %get-tuple-element.60), channel_id=1, source_target_pairs={{0,24},{4,28},{8,16},{12,20},{16,8},{20,12},{24,0},{28,4},{1,25},{... | collective-permute-start | bytes 98312 | tf_op jit(solution)/shard_map/ppermute | solution.py:29
  34.5 4.8 %collective-permute-start.12 = (bf16[1,64,256]{2,1,0:T(8,128)(2,1)S(1)}, bf16[1,64,256]{2,1,0:T(8,128)(2,1)S(1)}, u32[]{:S(2)}, u32[]{:S(2)}) collective-permute-start(bf16[1,64,256]{2,1,0:T(8,128)(2,1)S(1)} %get-tuple-element.61), channel_id=1, source_target_pairs={{0,16},{4,20},{8,24},{12,28},{16,0},{20,4},{24,8},{28,12},{1,17},{... | collective-permute-start | bytes 98312 | tf_op jit(solution)/shard_map/ppermute | solution.py:29
  35.8 7.2 %collective-permute-start.8 = (bf16[1,256,256]{2,1,0:T(8,128)(2,1)S(1)}, bf16[1,256,256]{2,1,0:T(8,128)(2,1)S(1)}, u32[]{:S(2)}, u32[]{:S(2)}) collective-permute-start(bf16[1,256,256]{2,1,0:T(8,128)(2,1)S(1)} %bitcast.45), channel_id=1, source_target_pairs={{0,24},{4,28},{8,16},{12,20},{16,8},{20,12},{24,0},{28,4},{1,25},{... | collective-permute-start | bytes 393224 | tf_op jit(solution)/shard_map/ppermute | solution.py:29
  37.0 7.4 %collective-permute-start.7 = (bf16[1,256,256]{2,1,0:T(8,128)(2,1)S(1)}, bf16[1,256,256]{2,1,0:T(8,128)(2,1)S(1)}, u32[]{:S(2)}, u32[]{:S(2)}) collective-permute-start(bf16[1,256,256]{2,1,0:T(8,128)(2,1)S(1)} %bitcast.46), channel_id=1, source_target_pairs={{0,16},{4,20},{8,24},{12,28},{16,0},{20,4},{24,8},{28,12},{1,17},{... | collective-permute-start | bytes 393224 | tf_op jit(solution)/shard_map/ppermute | solution.py:29
  37.5 6.9 %collective-permute-start.6 = (bf16[1,256,256]{2,1,0:T(8,128)(2,1)S(1)}, bf16[1,256,256]{2,1,0:T(8,128)(2,1)S(1)}, u32[]{:S(2)}, u32[]{:S(2)}) collective-permute-start(bf16[1,256,256]{2,1,0:T(8,128)(2,1)S(1)} %bitcast.47), channel_id=1, source_target_pairs={{0,8},{4,12},{8,0},{12,4},{16,24},{20,28},{24,16},{28,20},{1,9},{5... | collective-permute-start | bytes 393224 | tf_op jit(solution)/shard_map/ppermute | solution.py:29
  39.3 5.9 %collective-permute-start.16 = (bf16[64,256]{1,0:T(8,128)(2,1)S(1)}, bf16[64,256]{1,0:T(8,128)(2,1)S(1)}, u32[]{:S(2)}, u32[]{:S(2)}) collective-permute-start(bf16[64,256]{1,0:T(8,128)(2,1)S(1)} %fusion.5), channel_id=1, source_target_pairs={{0,3},{1,2},{2,1},{3,0},{4,7},{5,6},{6,5},{7,4},{8,11},{9,10},{10,... | collective-permute-start | bytes 98312 | tf_op jit(solution)/shard_map/ppermute | solution.py:29
  43.0 4.8 %collective-permute-start.15 = (bf16[64,256]{1,0:T(8,128)(2,1)S(1)}, bf16[64,256]{1,0:T(8,128)(2,1)S(1)}, u32[]{:S(2)}, u32[]{:S(2)}) collective-permute-start(bf16[64,256]{1,0:T(8,128)(2,1)S(1)} %fusion.5), channel_id=1, source_target_pairs={{0,2},{1,3},{2,0},{3,1},{4,6},{5,7},{6,4},{7,5},{8,10},{9,11},{10,... | collective-permute-start | bytes 98312 | tf_op jit(solution)/shard_map/ppermute | solution.py:29
  43.0 4.8 %collective-permute-start.14 = (bf16[64,256]{1,0:T(8,128)(2,1)S(1)}, bf16[64,256]{1,0:T(8,128)(2,1)S(1)}, u32[]{:S(2)}, u32[]{:S(2)}) collective-permute-start(bf16[64,256]{1,0:T(8,128)(2,1)S(1)} %fusion.5), channel_id=1, source_target_pairs={{0,1},{1,0},{2,3},{3,2},{4,5},{5,4},{6,7},{7,6},{8,9},{9,8},{10,11... | collective-permute-start | bytes 98312 | tf_op jit(solution)/shard_map/ppermute | solution.py:29
  44.5 17.7 %collective-permute-start.9 = (bf16[4,256,256]{2,1,0:T(8,128)(2,1)S(1)}, bf16[4,256,256]{2,1,0:T(8,128)(2,1)S(1)}, u32[]{:S(2)}, u32[]{:S(2)}) collective-permute-start(bf16[4,256,256]{2,1,0:T(8,128)(2,1)S(1)} %pad_maximum_fusion.even_adj_ref), channel_id=1, source_target_pairs={{0,4},{4,0},{8,12},{12,8},{16,20},{20,16},{24,28},{28,24},{1,5},{5... | collective-permute-start | bytes 1572872 | tf_op jit(solution)/shard_map/ppermute | solution.py:29
  47.9 6.4 %collective-permute-start.19 = (bf16[1,64,256]{2,1,0:T(8,128)(2,1)S(1)}, bf16[1,64,256]{2,1,0:T(8,128)(2,1)S(1)}, u32[]{:S(2)}, u32[]{:S(2)}) collective-permute-start(bf16[1,64,256]{2,1,0:T(8,128)(2,1)S(1)} %fusion.4), channel_id=1, source_target_pairs={{0,24},{4,28},{8,16},{12,20},{16,8},{20,12},{24,0},{28,4},{1,25},{... | collective-permute-start | bytes 98312 | tf_op jit(solution)/shard_map/ppermute | solution.py:29
  49.1 5.4 %collective-permute-start.18 = (bf16[1,64,256]{2,1,0:T(8,128)(2,1)S(1)}, bf16[1,64,256]{2,1,0:T(8,128)(2,1)S(1)}, u32[]{:S(2)}, u32[]{:S(2)}) collective-permute-start(bf16[1,64,256]{2,1,0:T(8,128)(2,1)S(1)} %fusion.4), channel_id=1, source_target_pairs={{0,16},{4,20},{8,24},{12,28},{16,0},{20,4},{24,8},{28,12},{1,17},{... | collective-permute-start | bytes 98312 | tf_op jit(solution)/shard_map/ppermute | solution.py:29
  52.1 4.5 %collective-permute-start.17 = (bf16[1,64,256]{2,1,0:T(8,128)(2,1)S(1)}, bf16[1,64,256]{2,1,0:T(8,128)(2,1)S(1)}, u32[]{:S(2)}, u32[]{:S(2)}) collective-permute-start(bf16[1,64,256]{2,1,0:T(8,128)(2,1)S(1)} %fusion.4), channel_id=1, source_target_pairs={{0,8},{4,12},{8,0},{12,4},{16,24},{20,28},{24,16},{28,20},{1,9},{5... | collective-permute-start | bytes 98312 | tf_op jit(solution)/shard_map/ppermute | solution.py:29
  52.1 6.0 %collective-permute-start.22 = (bf16[128,256]{1,0:T(8,128)(2,1)S(1)}, bf16[128,256]{1,0:T(8,128)(2,1)S(1)}, u32[]{:S(2)}, u32[]{:S(2)}) collective-permute-start(bf16[128,256]{1,0:T(8,128)(2,1)S(1)} %convert_element_type.141), channel_id=1, source_target_pairs={{0,2},{1,3},{2,0},{3,1},{4,6},{5,7},{6,4},{7,5},{8,10},{9,11},{10,... | collective-permute-start | bytes 196616 | tf_op jit(solution)/shard_map/ppermute | solution.py:29
  54.2 4.6 %collective-permute-start.21 = (bf16[128,256]{1,0:T(8,128)(2,1)S(1)}, bf16[128,256]{1,0:T(8,128)(2,1)S(1)}, u32[]{:S(2)}, u32[]{:S(2)}) collective-permute-start(bf16[128,256]{1,0:T(8,128)(2,1)S(1)} %convert_element_type.141), channel_id=1, source_target_pairs={{0,1},{1,0},{2,3},{3,2},{4,5},{5,4},{6,7},{7,6},{8,9},{9,8},{10,11... | collective-permute-start | bytes 196616 | tf_op jit(solution)/shard_map/ppermute | solution.py:29
  54.6 6.1 %collective-permute-start.23 = (bf16[128,256]{1,0:T(8,128)(2,1)S(1)}, bf16[128,256]{1,0:T(8,128)(2,1)S(1)}, u32[]{:S(2)}, u32[]{:S(2)}) collective-permute-start(bf16[128,256]{1,0:T(8,128)(2,1)S(1)} %convert_element_type.141), channel_id=1, source_target_pairs={{0,3},{1,2},{2,1},{3,0},{4,7},{5,6},{6,5},{7,4},{8,11},{9,10},{10,... | collective-permute-start | bytes 196616 | tf_op jit(solution)/shard_map/ppermute | solution.py:29
  56.6 4.7 %collective-permute-start.20 = (bf16[256,256]{1,0:T(8,128)(2,1)S(1)}, bf16[256,256]{1,0:T(8,128)(2,1)S(1)}, u32[]{:S(2)}, u32[]{:S(2)}) collective-permute-start(bf16[256,256]{1,0:T(8,128)(2,1)S(1)} %bitcast.40), channel_id=1, source_target_pairs={{0,4},{4,0},{8,12},{12,8},{16,20},{20,16},{24,28},{28,24},{1,5},{5... | collective-permute-start | bytes 393224 | tf_op jit(solution)/shard_map/ppermute | solution.py:29

commit v2 on v1

--- a/solution.py
+++ b/solution.py
@@ -34,13 +34,18 @@
     return lax.ppermute(value, axis, [(source, (source + steps) % count) for source in range(count)])
 
 
-def exchange_groups(count):
-    groups, base = [], 1
-    while base < count:
-        width = 2 if base == 1 else min(4, count // base)
-        groups.append([base * g for g in range(width)])
-        base *= width
-    return groups
+def halving_order(count):
+    order, bit = [0], count // 2
+    while bit > 1:
+        order = order + [offset | bit for offset in order]
+        bit //= 2
+    return tuple(order)
+
+
+def plane_order(count):
+    width = min(4, count // 2)
+    offsets = [[offset for offset in range(0, count, 2) if offset // 2 % width == g] for g in range(width)]
+    return offsets[: width // 2], offsets[width // 2 :]
 
 
 def horner(coefs, z):
@@ -152,15 +157,14 @@
     table_blocks(order, slab_ref[0], k_cols, positions[...], rows_ref, cot_ref, table_ref, part_ref)
 
 
-def second_tables(order, slab, k_cols, positions, rows, cotan, share):
+def next_tables(dtype, order, slab, k_cols, positions, rows, cotan, share):
     atoms, channels = rows.shape
     height = 2 * share * len(order)
     return pl.pallas_call(
         functools.partial(second_kernel, order),
-        name="second",
         out_shape=(
             jax.ShapeDtypeStruct((height, atoms), bf16),
-            jax.ShapeDtypeStruct((height, 2 * channels), f32),
+            jax.ShapeDtypeStruct((height, 2 * channels), dtype),
         ),
         in_specs=[SMEM] + [VMEM] * 4,
         out_specs=(VMEM, VMEM),
@@ -215,7 +219,18 @@
     )(sources, targets, lengths, cotan)
 
 
-def short_kernel(own_ref, above_ref, below_ref, lists_ref, rows_ref, cot_ref, w_ref, base_ref, grad_ref):
+def split_blocks(order, slab, value, send_ref, keep_ref, blocks):
+    count, height, _ = blocks.shape
+    for i in range(count):
+        blocks[i] = value[i * height : (i + 1) * height, :]
+    for place, offset in enumerate(order):
+        keep_ref[place] = blocks[slab ^ offset]
+        send_ref[place] = blocks[slab ^ offset ^ 1]
+
+
+def short_kernel(
+    order, slab_ref, own_ref, above_ref, below_ref, lists_ref, rows_ref, cot_ref, w_ref, base_ref, send_ref, keep_ref, blocks
+):
     atoms = own_ref.shape[0]
     lists = lists_ref[0]
     shape = (atoms, lists.shape[1])
@@ -227,34 +242,36 @@
     w = w_ref[...]
     base_ref[...] = cot_ref[...].astype(f32) + (dot(high, w, 1, 1) + dot(low, w, 1, 1))
     rows = rows_ref[...].T
-    grad_ref[...] = dot(rows, high) + dot(rows, low)
-
-
-def short_range(own, above, below, lists, rows, cotan, w_short):
+    split_blocks(order, slab_ref[0], dot(rows, high) + dot(rows, low), send_ref, keep_ref, blocks)
+
+
+def short_range(order, slab, own, above, below, lists, rows, cotan, w_short):
     atoms, channels = rows.shape
-    return pl.pallas_call(
-        short_kernel,
+    half = len(order)
+    height = channels // (2 * half)
+    return pl.pallas_call(
+        functools.partial(short_kernel, order),
         name="short",
         out_shape=(
             jax.ShapeDtypeStruct((atoms, channels), f32),
-            jax.ShapeDtypeStruct((channels, channels), f32),
-        ),
-        in_specs=[VMEM] * 7,
-        out_specs=(VMEM, VMEM),
+            jax.ShapeDtypeStruct((half, height, channels), f32),
+            jax.ShapeDtypeStruct((half, height, channels), f32),
+        ),
+        in_specs=[SMEM] + [VMEM] * 7,
+        out_specs=(VMEM,) * 3,
+        scratch_shapes=[pltpu.VMEM((2 * half, height, channels), f32)],
         compiler_params=params(),
         cost_estimate=pl.CostEstimate(
             flops=8 * atoms * channels * channels, bytes_accessed=8 * atoms * channels, transcendentals=0
         ),
-    )(own, above, below, lists, rows, cotan, w_short)
-
-
-def share_kernel(order, norm, count, slab_ref, filter_ref, w_ref, short_ref, own_ref, *refs):
-    parts, (adj_ref, gfilter_ref, send_ref, keep_ref, full) = refs[:count], refs[count:]
+    )(slab, own, above, below, lists, rows, cotan, w_short)
+
+
+def share_kernel(order, norm, count, slab_ref, filter_ref, w_ref, *refs):
+    parts, (adj_ref, gfilter_ref, send_ref, keep_ref, blocks) = refs[:count], refs[count:]
     channels = w_ref.shape[0]
-    height = 2 * channels // len(order)
-    slab = slab_ref[0]
-    total = own_ref[...].astype(f32)
-    for part in parts:
+    total = parts[0][...].astype(f32)
+    for part in parts[1:]:
         total = total + part[...].astype(f32)
     structure = total[:, :channels]
     moved, moved_low = halves(total[:, channels:])
@@ -262,132 +279,144 @@
     k_filter = filter_ref[...]
     double = jnp.concatenate([k_filter, k_filter], axis=0) * norm
     filtered, filtered_low = halves((structure * double).T)
-    full[:channels, :] = dot(filtered, moved) + (dot(filtered, moved_low) + dot(filtered_low, moved))
-    full[channels:, :] = short_ref[...]
-    half = len(order) // 2
-    for place, offset in enumerate(order):
-        ref = send_ref if place < half else keep_ref
-        at = (place % half) * height
-        rows = pl.ds(pl.multiple_of((slab ^ offset) * height, height), height)
-        ref[at : at + height, :] = full[rows, :].astype(ref.dtype)
+    wout = dot(filtered, moved) + (dot(filtered, moved_low) + dot(filtered_low, moved))
+    split_blocks(order, slab_ref[0], wout, send_ref, keep_ref, blocks)
     adj_ref[...] = (response * double).T.astype(bf16)
     product = structure * response
     share = k_filter.shape[0]
     gfilter_ref[...] = norm * (product[:share] + product[share:])
 
 
-def own_share(order, norm, slab, k_filter, w_out, short_grad, own, parts):
-    height, channels = own.shape[0], w_out.shape[0]
-    share = height // 2
+def own_share(order, norm, slab, k_filter, w_out, parts):
+    height, channels = parts[0].shape[0], w_out.shape[0]
+    half = len(order)
+    rows = channels // (2 * half)
     return pl.pallas_call(
         functools.partial(share_kernel, order, norm, len(parts)),
         name="share",
         out_shape=(
             jax.ShapeDtypeStruct((channels, height), bf16),
-            jax.ShapeDtypeStruct((share, channels), f32),
-            jax.ShapeDtypeStruct((channels, channels), bf16),
-            jax.ShapeDtypeStruct((channels, channels), f32),
-        ),
-        in_specs=[SMEM] + [VMEM] * (4 + len(parts)),
+            jax.ShapeDtypeStruct((height // 2, channels), f32),
+            jax.ShapeDtypeStruct((half, rows, channels), f32),
+            jax.ShapeDtypeStruct((half, rows, channels), f32),
+        ),
+        in_specs=[SMEM] + [VMEM] * (2 + len(parts)),
         out_specs=(VMEM,) * 4,
-        scratch_shapes=[pltpu.VMEM((2 * channels, channels), f32)],
+        scratch_shapes=[pltpu.VMEM((2 * half, rows, channels), f32)],
         compiler_params=params(),
         cost_estimate=pl.CostEstimate(
-            flops=4 * height * channels * channels, bytes_accessed=16 * height * channels, transcendentals=0
-        ),
-    )(slab, k_filter, w_out, short_grad, own, *parts)
-
-
-def back_kernel(base_ref, even_ref, odd_ref, even_adj_ref, odd_adj_ref, out_ref):
+            flops=8 * height * channels * channels, bytes_accessed=16 * height * channels, transcendentals=0
+        ),
+    )(slab, k_filter, w_out, *parts)
+
+
+def back_kernel(orders, order, base_ref, even_adj_ref, odd_adj_ref, *refs):
+    table_refs, out_ref = refs[:-1], refs[-1]
+    width = even_adj_ref.shape[2]
     total = None
-    for table_ref, adj_ref in ((even_ref, even_adj_ref), (odd_ref, odd_adj_ref)):
-        count, _, width = adj_ref.shape
-        for i in range(count):
-            part = dot(adj_ref[i], table_ref[i * width : (i + 1) * width, :])
+    for offsets, table_ref in zip(orders, table_refs):
+        for place, offset in enumerate(offsets):
+            adj = (odd_adj_ref if offset & 1 else even_adj_ref)[order.index(offset & ~1)]
+            part = dot(adj, table_ref[place * width : (place + 1) * width, :])
             total = part if total is None else total + part
     out_ref[...] = (base_ref[...] + total.T).astype(bf16)
 
 
-def back_project(base, even, odd, even_adj, odd_adj):
+def back_project(orders, order, base, even_adj, odd_adj, tables):
     atoms, channels = base.shape
-    return pl.pallas_call(
-        back_kernel,
+    height = sum(table.shape[0] for table in tables)
+    return pl.pallas_call(
+        functools.partial(back_kernel, orders, order),
         name="back",
         out_shape=jax.ShapeDtypeStruct((atoms, channels), bf16),
-        in_specs=[VMEM] * 5,
+        in_specs=[VMEM] * (3 + len(tables)),
         out_specs=VMEM,
         compiler_params=params(),
         cost_estimate=pl.CostEstimate(
-            flops=4 * even.shape[0] * atoms * channels, bytes_accessed=4 * even.shape[0] * atoms, transcendentals=0
-        ),
-    )(base, even, odd, even_adj, odd_adj)
-
-
-def place_kernel(order, scale, slab_ref, even_ref, odd_ref, wout_ref, wshort_ref, full):
-    channels = wout_ref.shape[0]
-    height = 2 * channels // len(order)
+            flops=2 * height * atoms * channels, bytes_accessed=2 * height * atoms, transcendentals=0
+        ),
+    )(base, even_adj, odd_adj, *tables)
+
+
+def place_kernel(order, scale, slab_ref, even_ref, odd_ref, wout_ref, wshort_ref, blocks):
+    count, height, _ = blocks.shape
+    half = height // 2
     slab = slab_ref[0]
-    half = len(order) // 2
     for place, offset in enumerate(order):
-        ref = odd_ref if place < half else even_ref
-        at = (place % half) * height
-        rows = pl.ds(pl.multiple_of((slab ^ offset) * height, height), height)
-        full[rows, :] = ref[at : at + height, :].astype(f32) * scale
-    wout_ref[...] = full[:channels, :]
-    wshort_ref[...] = full[channels:, :]
+        blocks[slab ^ offset] = even_ref[place].astype(f32) * scale
+        blocks[slab ^ offset ^ 1] = odd_ref[place].astype(f32) * scale
+    for i in range(count):
+        wout_ref[i * half : (i + 1) * half, :] = blocks[i, :half, :]
+        wshort_ref[i * half : (i + 1) * half, :] = blocks[i, half:, :]
 
 
 def place_grads(order, scale, slab, even, odd):
-    channels = even.shape[1]
+    half, height, channels = even.shape
     return pl.pallas_call(
         functools.partial(place_kernel, order, scale),
         name="place",
         out_shape=(jax.ShapeDtypeStruct((channels, channels), f32),) * 2,
         in_specs=[SMEM, VMEM, VMEM],
         out_specs=(VMEM, VMEM),
-        scratch_shapes=[pltpu.VMEM((2 * channels, channels), f32)],
+        scratch_shapes=[pltpu.VMEM((2 * half, height, channels), f32)],
         compiler_params=params(),
     )(slab, even, odd)
 
 
-def scatter_blocks(blocks, groups):
-    parts = []
-    for group in groups:
-        if parts:
-            blocks = sum((part.astype(f32) for part in parts), blocks.astype(f32))
-        width = len(group)
-        split = blocks.reshape(-1, width, *blocks.shape[1:])
-        parts = []
-        for g in range(1, width):
-            parts.append(xor_permute(split[:, g].astype(bf16), "slab", group[g]))
-        blocks = split[:, 0]
-    return blocks, parts
-
-
-def gather_blocks(block, groups):
-    blocks, order = block[None], [0]
-    for group in reversed(groups):
-        pieces = [blocks]
-        for g in range(1, len(group)):
-            pieces.append(xor_permute(blocks, "slab", group[g]))
-        blocks = jnp.concatenate(pieces, axis=0)
-        order = [offset ^ held for offset in group for held in order]
-    place_of = [order.index(offset) for offset in sorted(order)]
-    if place_of != list(range(len(order))):
-        blocks = jnp.stack([blocks[i] for i in place_of])
+def halving_sum(blocks):
+    bit = 2
+    while blocks.shape[0] > 1:
+        half = blocks.shape[0] // 2
+        moved = xor_permute(blocks[half:].astype(bf16), "slab", bit)
+        blocks = blocks[:half] + moved.astype(f32)
+        bit = 2 * bit
     return blocks
 
 
+def doubling_gather(blocks):
+    count = lax.axis_size("slab")
+    bit = count // 2
+    while bit > 1:
+        moved = xor_permute(blocks, "slab", bit)
+        blocks = jnp.concatenate([blocks, moved], axis=0)
+        bit = bit // 2
+    return blocks
+
+
 def sum_replicas(value):
-    count = lax.axis_size("rep")
-    sent = value.astype(bf16)
-    terms = [sent]
-    for offset in range(1, count):
-        terms.append(xor_permute(sent, "rep", offset))
-    terms = [term.astype(f32) for term in terms]
-    while len(terms) > 1:
-        terms = [terms[i] + terms[i + 1] for i in range(0, len(terms), 2)]
-    return terms[0]
+    bit = 1
+    while bit < lax.axis_size("rep"):
+        sent = value.astype(bf16)
+        moved = xor_permute(sent, "rep", bit)
+        value = sent.astype(f32) + moved.astype(f32)
+        bit = 2 * bit
+    return value
+
+
+def plane_sum(blocks):
+    count = lax.axis_size("slab")
+    bit = 2
+    terms = None
+    while bit < count:
+        width = min(4, count // bit)
+        sent = {g: [] for g in range(width)}
+        for offset in sorted(blocks):
+            sent[offset // bit % width].append(offset)
+        received = {offset: [] for offset in sent[0]}
+        for g in range(width - 1, 0, -1):
+            pieces = [blocks[offset].astype(bf16) for offset in sent[g]]
+            payload = pieces[0] if len(pieces) == 1 else jnp.concatenate(pieces, axis=0)
+            moved = xor_permute(payload, "slab", g * bit)
+            height = moved.shape[0] // len(pieces)
+            for i, offset in enumerate(sent[0]):
+                received[offset].append(moved[i * height : (i + 1) * height])
+        terms = [blocks[0], *received[0]]
+        blocks = {
+            offset: sum((piece.astype(f32) for piece in received[offset]), blocks[offset].astype(f32))
+            for offset in sent[0]
+        }
+        bit = bit * width
+    return terms
 
 
 def block(
@@ -403,7 +432,7 @@
     distance,
     halo_idx,
 ):
-    _, atoms, channels = features.shape
+    _, atoms, _ = features.shape
     kcount = k_filter.shape[0]
     count = lax.axis_size("slab")
     replicas = lax.axis_size("rep")
@@ -411,52 +440,57 @@
     scale = 1.0 / math.sqrt(replicas * atoms * count)
     share = kcount // count
     slab = lax.axis_index("slab").astype(jnp.int32)[None]
-    _, *rest = exchange_groups(count)
-
-    even = tuple(range(0, count, 2))
-    odd = tuple(offset + 1 for offset in even)
-    order = odd + even
-    half = count // 2
-
-    odd_table, odd_part, k_cols, positions, rows, cotan, own_filter, src, dst, dist, lists, w_out, w_short = (
-        first_tables(
-            odd,
-            slab,
-            k_vectors,
-            frac_pos,
-            features,
-            cotangent,
-            k_filter,
-            (edge_src, edge_dst, distance, halo_idx, w_out, w_short),
-            share,
-        )
+
+    near, far = plane_order(count)
+    near, far = (tuple(offset for group in groups for offset in group) for groups in (near, far))
+    flip = lambda offsets: tuple(offset ^ 1 for offset in offsets)
+    orders = (flip(far), far, flip(near), near)
+    order = halving_order(count)
+
+    odda, odda_part, k_cols, positions, rows, cotan, own_filter, src, dst, dist, lists, w_out, w_short = first_tables(
+        orders[0],
+        slab,
+        k_vectors,
+        frac_pos,
+        features,
+        cotangent,
+        k_filter,
+        (edge_src, edge_dst, distance, halo_idx, w_out, w_short),
+        share,
     )
-    from_pair = xor_permute(odd_part, "slab", 1)
-    even_table, even_part = second_tables(even, slab, k_cols, positions, rows, cotan, share)
-    paired = even_part + from_pair.astype(f32)
-    own, parts = scatter_blocks(paired.reshape(half, 2 * share, 2 * channels), rest)
+    moveda = xor_permute(odda_part, "slab", 1)
+    operands = (slab, k_cols, positions, rows, cotan, share)
+    evena, evena_part = next_tables(f32, orders[1], *operands)
+    oddb, oddb_part = next_tables(bf16, orders[2], *operands)
+    movedb = xor_permute(oddb_part, "slab", 1)
+    evenb, evenb_part = next_tables(f32, orders[3], *operands)
+    blocks = {}
+    for offsets, part, moved in ((far, evena_part, moveda), (near, evenb_part, movedb)):
+        paired = part + moved.astype(f32)
+        for i, offset in enumerate(offsets):
+            blocks[offset] = paired[i * 2 * share : (i + 1) * 2 * share]
+    parts = plane_sum(blocks)
 
     own_rows, lower, upper = edge_rows(src, dst, dist, cotan, lists.shape[2])
     from_above = shifted(lower, "slab", -1)
     from_below = shifted(upper, "slab", 1)
-    base, short_grad = short_range(own_rows, from_above, from_below, lists, rows, cotan, w_short)
-
-    adj, gfilter, send, keep = own_share(
-        order, norm, slab, own_filter, w_out, short_grad, own[0], [part[0] for part in parts]
+    adj, gfilter, wout_send, wout_keep = own_share(order, norm, slab, own_filter, w_out, parts)
+    wout_moved = xor_permute(wout_send, "slab", 1)
+    base, wshort_send, wshort_keep = short_range(
+        order, slab, own_rows, from_above, from_below, lists, rows, cotan, w_short
     )
-
-    from_pair = xor_permute(send, "slab", 1)
-    summed = keep + from_pair.astype(f32)
-    own_grad, grad_parts = scatter_blocks(summed.reshape(half, -1, channels), rest)
-    own_grad = sum((part.astype(f32) for part in grad_parts), own_grad)[0]
-
-    adj_even = gather_blocks(adj, rest)
+    wshort_moved = xor_permute(wshort_send, "slab", 1)
+    grads = jnp.concatenate([wout_keep + wout_moved, wshort_keep + wshort_moved], axis=1)
+    own_grad = halving_sum(grads)
+
+    adj_even = doubling_gather(adj[None])
     adj_odd = xor_permute(adj_even, "slab", 1)
-    grad_features = back_project(base, even_table, odd_table, adj_even, adj_odd)
+    grad_features = back_project(orders, order, base, adj_even, adj_odd, (odda, evena, oddb, evenb))
 
     own_grad = sum_replicas(own_grad).astype(bf16)
-    grad_filter = sum_replicas(gfilter) / replicas
-    grad_even = gather_blocks(own_grad, rest).reshape(-1, channels)
+    filter_sum = sum_replicas(gfilter)
+    grad_filter = filter_sum / replicas
+    grad_even = doubling_gather(own_grad)
     grad_odd = xor_permute(grad_even, "slab", 1)
     grad_wout, grad_wshort = place_grads(order, scale, slab, grad_even, grad_odd)
     return (grad_features[None], grad_wout, grad_wshort, grad_filter)

time: 64 us -> 61.3 us (0.958)
  starting transfers between devices: 28.9 us -> 25.8 us
    ppermute x22 -> x19, waiting for transfers between devices: 19.3 us -> 11.9 us  [xor_permute(): lax.ppermute(value, axis, [(source, source ^ bits) for source in range(co...]
    ppermute x2, waiting for transfers between devices: 0.01 us -> 7.42 us  [shifted(): lax.ppermute(value, axis, [(source, (source + steps) % count) for source...]
    ppermute x2, starting transfers between devices: 3.6 us -> 1.71 us  [shifted(): lax.ppermute(value, axis, [(source, (source + steps) % count) for source...]
    ppermute x22 -> x19, starting transfers between devices: 25.3 us -> 24.1 us  [xor_permute(): lax.ppermute(value, axis, [(source, source ^ bits) for source in range(co...]
    pallas_call x3 -> x5, Pallas kernels: 3.88 us -> 5.01 us  [the longest x3 2.81 us: next_tables(): pl.pallas_call(functools.partial(second_kernel, order), out_shape=(jax.Sh...]
    pallas_call x1, Pallas kernels: 2.9 us -> 2.13 us  [first_tables(): pl.pallas_call(functools.partial(first_kernel, order, len(others)), name=...]
  transfers between devices with their start and end apart: 24 -> 21, of which waited for: 8 -> 10; matrix products, arithmetic and copies ran while one was open for 2% -> 2% of each run, Pallas kernels for 13% -> 16%
where the time goes in v2:
time: 61.3 us; the launch traced here: 61 us
  starting transfers between devices  25.8 us (42%)
  waiting for transfers between devices  19.3 us (31%)
  Pallas kernels  13.7 us (22%)
  other arithmetic  1.21 us (2%)
  between operations  0.85 us (1%)
    ppermute x19, starting transfers between devices, xor_permute(): lax.ppermute(value, axis, [(source, source ^ bits) for source in range(co...  24.1 us
    ppermute x19, waiting for transfers between devices, xor_permute(): lax.ppermute(value, axis, [(source, source ^ bits) for source in range(co...  11.9 us
    ppermute x2, waiting for transfers between devices, shifted(): lax.ppermute(value, axis, [(source, (source + steps) % count) for source...  7.42 us
    pallas_call x1, Pallas kernels, edge_rows(): pl.pallas_call(functools.partial(edge_kernel, block), name='edges', out_s...  5.19 us
    pallas_call x3, Pallas kernels, next_tables(): pl.pallas_call(functools.partial(second_kernel, order), out_shape=(jax.Sh...  2.81 us
    pallas_call x1, Pallas kernels, first_tables(): pl.pallas_call(functools.partial(first_kernel, order, len(others)), name=...  2.13 us
    ppermute x2, starting transfers between devices, shifted(): lax.ppermute(value, axis, [(source, (source + steps) % count) for source...  1.71 us
    pallas_call x1, Pallas kernels, back_project(): pl.pallas_call(functools.partial(back_kernel, orders, order), name='back'...  1.55 us
  transfers between devices with their start and end apart: 21, of which 10 were waited for; matrix products, arithmetic and copies ran while one was open for 2% of the time, Pallas kernels for 16%

profile of v2, /device:TPU:0, one launch (start us, length us, event | category | flops | bytes accessed | tf_op | source)
XLA Modules:
  0.0 61.0 jit_solution(13606652576009785190)
XLA Ops:
  0.6 2.1 %first.1 = (bf16[512,512]{1,0:T(8,128)(2,1)S(1)}, bf16[512,512]{1,0:T(8,128)(2,1)S(1)}, f32[1024,16]{1,0:T(8,128)S(1)}, bf16[16,512]{1,0:T(8,128)(2,1)S(1)}, bf1...) custom-call(s32[1]{0:T(128)} %bitcast.slab_ref, ...), custom_call_target="tpu_custom_call" | custom-call | flops 268435456 | bytes 1048576 | tf_op jit(solution)/shard_map/first/pallas_call | solution.py:136
  2.8 0.6 collective-permute-start.3
  3.3 0.9 %shard_map.139 = (bf16[512,512]{1,0:T(8,128)(2,1)S(1)}, bf16[512,512]{1,0:T(8,128)(2,1)S(1)}) custom-call(s32[1]{0:T(128)} %bitcast.slab_ref, f32[1024,16]{1,0:T(8,128)S(1)} %get-tuple-element.48.k_cols, bf16[16,512]{1,0:T(8,128)(2,1)S(1)} %get-tuple-element.49.positions, bf16[512,256]{1,0:T(8,128)(2,1)S(1)} %get-tuple-element.43.rows_ref, ...), custom_call_target="tpu_custom_call" | custom-call | flops 268435456 | bytes 1048576 | tf_op jit(solution)/shard_map/pallas_call | solution.py:163
  4.3 0.1 collective-permute-start.2
  4.4 0.9 %shard_map.140 = (bf16[512,512]{1,0:T(8,128)(2,1)S(1)}, f32[512,512]{1,0:T(8,128)S(1)}) custom-call(s32[1]{0:T(128)} %bitcast.slab_ref, f32[1024,16]{1,0:T(8,128)S(1)} %get-tuple-element.48.k_cols, bf16[16,512]{1,0:T(8,128)(2,1)S(1)} %get-tuple-element.49.positions, bf16[512,256]{1,0:T(8,128)(2,1)S(1)} %get-tuple-element.43.rows_ref, ...), custom_call_target="tpu_custom_call" | custom-call | flops 268435456 | bytes 1048576 | tf_op jit(solution)/shard_map/pallas_call | solution.py:163
  5.3 0.9 %shard_map.138 = (bf16[512,512]{1,0:T(8,128)(2,1)S(1)}, f32[512,512]{1,0:T(8,128)S(1)}) custom-call(s32[1]{0:T(128)} %bitcast.slab_ref, f32[1024,16]{1,0:T(8,128)S(1)} %get-tuple-element.48.k_cols, bf16[16,512]{1,0:T(8,128)(2,1)S(1)} %get-tuple-element.49.positions, bf16[512,256]{1,0:T(8,128)(2,1)S(1)} %get-tuple-element.43.rows_ref, ...), custom_call_target="tpu_custom_call" | custom-call | flops 268435456 | bytes 1048576 | tf_op jit(solution)/shard_map/pallas_call | solution.py:163
  6.3 0.0 collective-permute-done.3
  6.3 0.2 add_convert_fusion
  6.5 3.0 %collective-permute-start.5 = (bf16[256,512]{1,0:T(8,128)(2,1)S(1)}, bf16[256,512]{1,0:T(8,128)(2,1)S(1)}, u32[]{:S(2)}, u32[]{:S(2)}) collective-permute-start(bf16[256,512]{1,0:T(8,128)(2,1)S(1)} %get-tuple-element.66), channel_id=1, source_target_pairs={{0,16},{4,20},{8,24},{12,28},{16,0},{20,4},{24,8},{28,12},{1,17},{... | collective-permute-start | bytes 786440 | tf_op jit(solution)/shard_map/ppermute | solution.py:29
  9.5 1.4 %collective-permute-start.4 = (bf16[256,512]{1,0:T(8,128)(2,1)S(1)}, bf16[256,512]{1,0:T(8,128)(2,1)S(1)}, u32[]{:S(2)}, u32[]{:S(2)}) collective-permute-start(bf16[256,512]{1,0:T(8,128)(2,1)S(1)} %get-tuple-element.67), channel_id=1, source_target_pairs={{0,24},{4,28},{8,16},{12,20},{16,8},{20,12},{24,0},{28,4},{1,25},{... | collective-permute-start | bytes 786440 | tf_op jit(solution)/shard_map/ppermute | solution.py:29
  11.0 0.0 collective-permute-done.2
  11.0 0.2 convert_add_fusion
  11.2 0.2 collective-permute-start.6
  11.3 5.2 %edges.1 = (f32[512,256]{1,0:T(8,128)S(1)}, bf16[256,256]{1,0:T(8,128)(2,1)S(1)}, bf16[256,256]{1,0:T(8,128)(2,1)S(1)}) custom-call(s32[1,4096]{1,0:T(1,128)S(1)} %get-tuple-element.35.src_ref, s32[1,4096]{1,0:T(1,128)S(1)} %get-tuple-element.36.dst_ref, f32[1,4096]{1,0:T(1,128)S(1)} %get-tuple-element.37.dist_ref, ...), custom_call_target="tpu_custom_call" | custom-call | flops 3221225472 | bytes 49152 | tf_op jit(solution)/shard_map/edges/pallas_call | solution.py:204
  16.5 1.7 %collective-permute-start = (bf16[256,256]{1,0:T(8,128)(2,1)S(1)}, bf16[256,256]{1,0:T(8,128)(2,1)S(1)}, u32[]{:S(2)}, u32[]{:S(2)}) collective-permute-start(bf16[256,256]{1,0:T(8,128)(2,1)S(1)} %get-tuple-element.40), channel_id=1, source_target_pairs={{0,28},{4,0},{8,4},{12,8},{16,12},{20,16},{24,20},{28,24},{1,29},{... | collective-permute-start | bytes 393224 | tf_op jit(solution)/shard_map/ppermute | solution.py:34
  18.2 0.0 collective-permute-start.1
  18.2 6.7 %collective-permute-done.above_ref = bf16[256,256]{1,0:T(8,128)(2,1)S(1)} collective-permute-done((bf16[256,256]{1,0:T(8,128)(2,1)S(1)}, bf16[256,256]{1,0:T(8,128)(2,1)S(1)}, u32[]{:S(2)}, u32[]{:S(2)}) %collective-permute-start) | collective-permute-done | bytes 131104 | tf_op jit(solution)/shard_map/ppermute | solution.py:34
  24.9 0.8 %collective-permute-done.1.below_ref = bf16[256,256]{1,0:T(8,128)(2,1)S(1)} collective-permute-done((bf16[256,256]{1,0:T(8,128)(2,1)S(1)}, bf16[256,256]{1,0:T(8,128)(2,1)S(1)}, u32[]{:S(2)}, u32[]{:S(2)}) %collective-permute-start.1) | collective-permute-done | bytes 131104 | tf_op jit(solution)/shard_map/ppermute | solution.py:34
  25.7 0.7 %short.1 = (f32[512,256]{1,0:T(8,128)S(1)}, f32[4,32,256]{2,1,0:T(8,128)S(1)}, f32[4,32,256]{2,1,0:T(8,128)S(1)}) custom-call(s32[1]{0:T(128)} %bitcast.slab_ref, f32[512,256]{1,0:T(8,128)S(1)} %get-tuple-element.39.own_ref, bf16[256,256]{1,0:T(8,128)(2,1)S(1)} %collective-permute-done.above_ref, bf16[256,256]{1,0:T(8,128)(2,1)S(1)} %collective-permute-done.1.below_ref, ...), custom_call_target="tpu_custom_call" | custom-call | flops 268435456 | bytes 1048576 | tf_op jit(solution)/shard_map/short/pallas_call | solution.py:252
  26.3 0.2 collective-permute-start.11
  26.6 0.0 collective-permute-done.5.refs_2_
  26.6 0.0 collective-permute-done.4.refs_1_
  26.6 0.0 collective-permute-done.6.refs_3_
  26.6 0.5 share.1
  27.1 0.5 collective-permute-start.10
  27.6 0.2 collective-permute-done.11
  27.8 0.8 %collective-permute-done.10 = f32[4,32,256]{2,1,0:T(8,128)S(1)} collective-permute-done((f32[4,32,256]{2,1,0:T(8,128)S(1)}, f32[4,32,256]{2,1,0:T(8,128)S(1)}, u32[]{:S(2)}, u32[]{:S(2)}) %collective-permute-start.10) | collective-permute-done | bytes 131104 | tf_op jit(solution)/shard_map/ppermute | solution.py:29
  28.6 2.4 %collective-permute-start.12 = (bf16[2,64,256]{2,1,0:T(8,128)(2,1)S(1)}, bf16[2,64,256]{2,1,0:T(8,128)(2,1)S(1)}, u32[]{:S(2)}, u32[]{:S(2)}) collective-permute-start(bf16[2,64,256]{2,1,0:T(8,128)(2,1)S(1)} %fusion.2), channel_id=1, source_target_pairs={{0,8},{4,12},{8,0},{12,4},{16,24},{20,28},{24,16},{28,20},{1,9},{5... | collective-permute-start | bytes 196616 | tf_op jit(solution)/shard_map/ppermute | solution.py:29
  31.0 2.4 %collective-permute-done.12 = bf16[2,64,256]{2,1,0:T(8,128)(2,1)S(1)} collective-permute-done((bf16[2,64,256]{2,1,0:T(8,128)(2,1)S(1)}, bf16[2,64,256]{2,1,0:T(8,128)(2,1)S(1)}, u32[]{:S(2)}, u32[]{:S(2)}) %collective-permute-start.12) | collective-permute-done | bytes 65568 | tf_op jit(solution)/shard_map/ppermute | solution.py:29
  33.4 1.0 %collective-permute-start.13 = (bf16[1,64,256]{2,1,0:T(8,128)(2,1)S(1)}, bf16[1,64,256]{2,1,0:T(8,128)(2,1)S(1)}, u32[]{:S(2)}, u32[]{:S(2)}) collective-permute-start(bf16[1,64,256]{2,1,0:T(8,128)(2,1)S(1)} %slice.59), channel_id=1, source_target_pairs={{0,16},{4,20},{8,24},{12,28},{16,0},{20,4},{24,8},{28,12},{1,17},{... | collective-permute-start | bytes 98312 | tf_op jit(solution)/shard_map/ppermute | solution.py:29
  34.4 3.0 %collective-permute-done.13 = bf16[1,64,256]{2,1,0:T(8,128)(2,1)S(1)} collective-permute-done((bf16[1,64,256]{2,1,0:T(8,128)(2,1)S(1)}, bf16[1,64,256]{2,1,0:T(8,128)(2,1)S(1)}, u32[]{:S(2)}, u32[]{:S(2)}) %collective-permute-start.13) | collective-permute-done | bytes 32800 | tf_op jit(solution)/shard_map/ppermute | solution.py:29
  37.4 1.7 %collective-permute-start.14 = (bf16[1,64,256]{2,1,0:T(8,128)(2,1)S(1)}, bf16[1,64,256]{2,1,0:T(8,128)(2,1)S(1)}, u32[]{:S(2)}, u32[]{:S(2)}) collective-permute-start(bf16[1,64,256]{2,1,0:T(8,128)(2,1)S(1)} %fusion.3), channel_id=1, source_target_pairs={{0,1},{1,0},{2,3},{3,2},{4,5},{5,4},{6,7},{7,6},{8,9},{9,8},{10,11... | collective-permute-start | bytes 98312 | tf_op jit(solution)/shard_map/ppermute | solution.py:29
  39.1 0.9 %collective-permute-start.7 = (bf16[1,256,256]{2,1,0:T(8,128)(2,1)S(1)}, bf16[1,256,256]{2,1,0:T(8,128)(2,1)S(1)}, u32[]{:S(2)}, u32[]{:S(2)}) collective-permute-start(bf16[1,256,256]{2,1,0:T(8,128)(2,1)S(1)} %bitcast.4), channel_id=1, source_target_pairs={{0,16},{4,20},{8,24},{12,28},{16,0},{20,4},{24,8},{28,12},{1,17},{... | collective-permute-start | bytes 393224 | tf_op jit(solution)/shard_map/ppermute | solution.py:29
  40.0 1.4 %collective-permute-done.14 = bf16[1,64,256]{2,1,0:T(8,128)(2,1)S(1)} collective-permute-done((bf16[1,64,256]{2,1,0:T(8,128)(2,1)S(1)}, bf16[1,64,256]{2,1,0:T(8,128)(2,1)S(1)}, u32[]{:S(2)}, u32[]{:S(2)}) %collective-permute-start.14) | collective-permute-done | bytes 32800 | tf_op jit(solution)/shard_map/ppermute | solution.py:29
  41.4 2.8 %collective-permute-start.15 = (bf16[1,64,256]{2,1,0:T(8,128)(2,1)S(1)}, bf16[1,64,256]{2,1,0:T(8,128)(2,1)S(1)}, u32[]{:S(2)}, u32[]{:S(2)}) collective-permute-start(bf16[1,64,256]{2,1,0:T(8,128)(2,1)S(1)} %add_convert_fusion.3), channel_id=1, source_target_pairs={{0,2},{1,3},{2,0},{3,1},{4,6},{5,7},{6,4},{7,5},{8,10},{9,11},{10,... | collective-permute-start | bytes 98312 | tf_op jit(solution)/shard_map/ppermute | solution.py:29
  44.2 0.0 collective-permute-done.7
  44.3 1.8 %collective-permute-start.8 = (bf16[2,256,256]{2,1,0:T(8,128)(2,1)S(1)}, bf16[2,256,256]{2,1,0:T(8,128)(2,1)S(1)}, u32[]{:S(2)}, u32[]{:S(2)}) collective-permute-start(bf16[2,256,256]{2,1,0:T(8,128)(2,1)S(1)} %pad_maximum_fusion.1), channel_id=1, source_target_pairs={{0,8},{4,12},{8,0},{12,4},{16,24},{20,28},{24,16},{28,20},{1,9},{5... | collective-permute-start | bytes 786440 | tf_op jit(solution)/shard_map/ppermute | solution.py:29
  46.0 0.3 collective-permute-done.15
  46.3 1.0 %collective-permute-start.16 = (bf16[1,64,256]{2,1,0:T(8,128)(2,1)S(1)}, bf16[1,64,256]{2,1,0:T(8,128)(2,1)S(1)}, u32[]{:S(2)}, u32[]{:S(2)}) collective-permute-start(bf16[1,64,256]{2,1,0:T(8,128)(2,1)S(1)} %add_convert_fusion.2), channel_id=1, source_target_pairs={{0,16},{4,20},{8,24},{12,28},{16,0},{20,4},{24,8},{28,12},{1,17},{... | collective-permute-start | bytes 98312 | tf_op jit(solution)/shard_map/ppermute | solution.py:29
  47.4 1.6 %collective-permute-start.19 = (bf16[128,256]{1,0:T(8,128)(2,1)S(1)}, bf16[128,256]{1,0:T(8,128)(2,1)S(1)}, u32[]{:S(2)}, u32[]{:S(2)}) collective-permute-start(bf16[128,256]{1,0:T(8,128)(2,1)S(1)} %convert_element_type.67), channel_id=1, source_target_pairs={{0,1},{1,0},{2,3},{3,2},{4,5},{5,4},{6,7},{7,6},{8,9},{9,8},{10,11... | collective-permute-start | bytes 196616 | tf_op jit(solution)/shard_map/ppermute | solution.py:29
  49.0 1.3 %collective-permute-done.16 = bf16[1,64,256]{2,1,0:T(8,128)(2,1)S(1)} collective-permute-done((bf16[1,64,256]{2,1,0:T(8,128)(2,1)S(1)}, bf16[1,64,256]{2,1,0:T(8,128)(2,1)S(1)}, u32[]{:S(2)}, u32[]{:S(2)}) %collective-permute-start.16) | collective-permute-done | bytes 32800 | tf_op jit(solution)/shard_map/ppermute | solution.py:29
  50.3 1.9 %collective-permute-start.17 = (bf16[2,64,256]{2,1,0:T(8,128)(2,1)S(1)}, bf16[2,64,256]{2,1,0:T(8,128)(2,1)S(1)}, u32[]{:S(2)}, u32[]{:S(2)}) collective-permute-start(bf16[2,64,256]{2,1,0:T(8,128)(2,1)S(1)} %pad_maximum_fusion.4), channel_id=1, source_target_pairs={{0,8},{4,12},{8,0},{12,4},{16,24},{20,28},{24,16},{28,20},{1,9},{5... | collective-permute-start | bytes 196616 | tf_op jit(solution)/shard_map/ppermute | solution.py:29
  52.2 0.0 collective-permute-done.8
  52.2 0.1 pad_maximum_fusion.even_adj_ref
  52.3 0.1 collective-permute-start.9
  52.4 0.0 collective-permute-done.19
  52.4 2.7 %collective-permute-start.20 = (bf16[128,256]{1,0:T(8,128)(2,1)S(1)}, bf16[128,256]{1,0:T(8,128)(2,1)S(1)}, u32[]{:S(2)}, u32[]{:S(2)}) collective-permute-start(bf16[128,256]{1,0:T(8,128)(2,1)S(1)} %add_convert_fusion.1), channel_id=1, source_target_pairs={{0,2},{1,3},{2,0},{3,1},{4,6},{5,7},{6,4},{7,5},{8,10},{9,11},{10,... | collective-permute-start | bytes 196616 | tf_op jit(solution)/shard_map/ppermute | solution.py:29
  55.1 0.0 collective-permute-done.17
  55.1 0.3 collective-permute-start.18
  55.4 2.5 %collective-permute-done.20 = bf16[128,256]{1,0:T(8,128)(2,1)S(1)} collective-permute-done((bf16[128,256]{1,0:T(8,128)(2,1)S(1)}, bf16[128,256]{1,0:T(8,128)(2,1)S(1)}, u32[]{:S(2)}, u32[]{:S(2)}) %collective-permute-start.20) | collective-permute-done | bytes 65568 | tf_op jit(solution)/shard_map/ppermute | solution.py:29
  57.9 0.7 %add_multiply_fusion = f32[128,256]{1,0:T(8,128)} fusion(bf16[128,256]{1,0:T(8,128)(2,1)S(1)} %collective-permute-done.20, bf16[128,256]{1,0:T(8,128)(2,1)S(1)} %add_convert_fusion.1), kind=kLoop, calls=%fused_computation.12 | loop fusion | flops 131072 | bytes 262144 | tf_op jit(solution)/shard_map/div | solution.py:492
  58.5 0.0 collective-permute-done.18.odd_ref
  58.5 0.9 %place.1 = (f32[256,256]{1,0:T(8,128)}, f32[256,256]{1,0:T(8,128)}) custom-call(s32[1]{0:T(128)} %bitcast.slab_ref, bf16[4,64,256]{2,1,0:T(8,128)(2,1)S(1)} %pad_maximum_fusion.3.even_ref, bf16[4,64,256]{2,1,0:T(8,128)(2,1)S(1)} %collective-permute-done.18.odd_ref), custom_call_target="tpu_custom_call" | custom-call | tf_op jit(solution)/shard_map/place/pallas_call | solution.py:355
  59.4 0.0 collective-permute-done.9.odd_adj_ref
  59.4 1.5 %back.1 = bf16[512,256]{1,0:T(8,128)(2,1)} custom-call(f32[512,256]{1,0:T(8,128)S(1)} %get-tuple-element.45.base_ref, bf16[4,256,256]{2,1,0:T(8,128)(2,1)S(1)} %pad_maximum_fusion.even_adj_ref, bf16[4,256,256]{2,1,0:T(8,128)(2,1)S(1)} %collective-permute-done.9.odd_adj_ref, bf16[512,512]{1,0:T(8,128)(2,1)S(1)} %get-tuple-element.55.refs_0_, ...), custom_call_target="tpu_custom_call" | custom-call | flops 536870912 | bytes 2097152 | tf_op jit(solution)/shard_map/back/pallas_call | solution.py:328
  (16 shorter events, 0.3 us)
Async XLA Ops:
  2.8 3.5 %collective-permute-start.3 = (bf16[512,512]{1,0:T(8,128)(2,1)S(1)}, bf16[512,512]{1,0:T(8,128)(2,1)S(1)}, u32[]{:S(2)}, u32[]{:S(2)}) collective-permute-start(bf16[512,512]{1,0:T(8,128)(2,1)S(1)} %get-tuple-element.53), channel_id=1, source_target_pairs={{0,4},{4,0},{8,12},{12,8},{16,20},{20,16},{24,28},{28,24},{1,5},{5... | collective-permute-start | bytes 1572872 | tf_op jit(solution)/shard_map/ppermute | solution.py:29
  4.3 6.7 %collective-permute-start.2 = (bf16[512,512]{1,0:T(8,128)(2,1)S(1)}, bf16[512,512]{1,0:T(8,128)(2,1)S(1)}, u32[]{:S(2)}, u32[]{:S(2)}) collective-permute-start(bf16[512,512]{1,0:T(8,128)(2,1)S(1)} %get-tuple-element.51), channel_id=1, source_target_pairs={{0,4},{4,0},{8,12},{12,8},{16,20},{20,16},{24,28},{28,24},{1,5},{5... | collective-permute-start | bytes 1572872 | tf_op jit(solution)/shard_map/ppermute | solution.py:29
  6.5 20.1 %collective-permute-start.5 = (bf16[256,512]{1,0:T(8,128)(2,1)S(1)}, bf16[256,512]{1,0:T(8,128)(2,1)S(1)}, u32[]{:S(2)}, u32[]{:S(2)}) collective-permute-start(bf16[256,512]{1,0:T(8,128)(2,1)S(1)} %get-tuple-element.66), channel_id=1, source_target_pairs={{0,16},{4,20},{8,24},{12,28},{16,0},{20,4},{24,8},{28,12},{1,17},{... | collective-permute-start | bytes 786440 | tf_op jit(solution)/shard_map/ppermute | solution.py:29
  9.5 17.0 %collective-permute-start.4 = (bf16[256,512]{1,0:T(8,128)(2,1)S(1)}, bf16[256,512]{1,0:T(8,128)(2,1)S(1)}, u32[]{:S(2)}, u32[]{:S(2)}) collective-permute-start(bf16[256,512]{1,0:T(8,128)(2,1)S(1)} %get-tuple-element.67), channel_id=1, source_target_pairs={{0,24},{4,28},{8,16},{12,20},{16,8},{20,12},{24,0},{28,4},{1,25},{... | collective-permute-start | bytes 786440 | tf_op jit(solution)/shard_map/ppermute | solution.py:29
  11.2 15.4 %collective-permute-start.6 = (bf16[256,512]{1,0:T(8,128)(2,1)S(1)}, bf16[256,512]{1,0:T(8,128)(2,1)S(1)}, u32[]{:S(2)}, u32[]{:S(2)}) collective-permute-start(bf16[256,512]{1,0:T(8,128)(2,1)S(1)} %slice.58), channel_id=1, source_target_pairs={{0,8},{4,12},{8,0},{12,4},{16,24},{20,28},{24,16},{28,20},{1,9},{5... | collective-permute-start | bytes 786440 | tf_op jit(solution)/shard_map/ppermute | solution.py:29
  16.5 8.4 %collective-permute-start = (bf16[256,256]{1,0:T(8,128)(2,1)S(1)}, bf16[256,256]{1,0:T(8,128)(2,1)S(1)}, u32[]{:S(2)}, u32[]{:S(2)}) collective-permute-start(bf16[256,256]{1,0:T(8,128)(2,1)S(1)} %get-tuple-element.40), channel_id=1, source_target_pairs={{0,28},{4,0},{8,4},{12,8},{16,12},{20,16},{24,20},{28,24},{1,29},{... | collective-permute-start | bytes 393224 | tf_op jit(solution)/shard_map/ppermute | solution.py:34
  18.2 7.4 %collective-permute-start.1 = (bf16[256,256]{1,0:T(8,128)(2,1)S(1)}, bf16[256,256]{1,0:T(8,128)(2,1)S(1)}, u32[]{:S(2)}, u32[]{:S(2)}) collective-permute-start(bf16[256,256]{1,0:T(8,128)(2,1)S(1)} %get-tuple-element.41), channel_id=1, source_target_pairs={{0,4},{4,8},{8,12},{12,16},{16,20},{20,24},{24,28},{28,0},{1,5},{5... | collective-permute-start | bytes 393224 | tf_op jit(solution)/shard_map/ppermute | solution.py:34
  26.3 1.4 %collective-permute-start.11 = (f32[4,32,256]{2,1,0:T(8,128)S(1)}, f32[4,32,256]{2,1,0:T(8,128)S(1)}, u32[]{:S(2)}, u32[]{:S(2)}) collective-permute-start(f32[4,32,256]{2,1,0:T(8,128)S(1)} %get-tuple-element.62), channel_id=1, source_target_pairs={{0,4},{4,0},{8,12},{12,8},{16,20},{20,16},{24,28},{28,24},{1,5},{5... | collective-permute-start | bytes 393224 | tf_op jit(solution)/shard_map/ppermute | solution.py:29
  27.1 1.4 %collective-permute-start.10 = (f32[4,32,256]{2,1,0:T(8,128)S(1)}, f32[4,32,256]{2,1,0:T(8,128)S(1)}, u32[]{:S(2)}, u32[]{:S(2)}) collective-permute-start(f32[4,32,256]{2,1,0:T(8,128)S(1)} %get-tuple-element.60), channel_id=1, source_target_pairs={{0,4},{4,0},{8,12},{12,8},{16,20},{20,16},{24,28},{28,24},{1,5},{5... | collective-permute-start | bytes 393224 | tf_op jit(solution)/shard_map/ppermute | solution.py:29
  28.6 4.8 %collective-permute-start.12 = (bf16[2,64,256]{2,1,0:T(8,128)(2,1)S(1)}, bf16[2,64,256]{2,1,0:T(8,128)(2,1)S(1)}, u32[]{:S(2)}, u32[]{:S(2)}) collective-permute-start(bf16[2,64,256]{2,1,0:T(8,128)(2,1)S(1)} %fusion.2), channel_id=1, source_target_pairs={{0,8},{4,12},{8,0},{12,4},{16,24},{20,28},{24,16},{28,20},{1,9},{5... | collective-permute-start | bytes 196616 | tf_op jit(solution)/shard_map/ppermute | solution.py:29
  33.4 4.0 %collective-permute-start.13 = (bf16[1,64,256]{2,1,0:T(8,128)(2,1)S(1)}, bf16[1,64,256]{2,1,0:T(8,128)(2,1)S(1)}, u32[]{:S(2)}, u32[]{:S(2)}) collective-permute-start(bf16[1,64,256]{2,1,0:T(8,128)(2,1)S(1)} %slice.59), channel_id=1, source_target_pairs={{0,16},{4,20},{8,24},{12,28},{16,0},{20,4},{24,8},{28,12},{1,17},{... | collective-permute-start | bytes 98312 | tf_op jit(solution)/shard_map/ppermute | solution.py:29
  37.4 4.0 %collective-permute-start.14 = (bf16[1,64,256]{2,1,0:T(8,128)(2,1)S(1)}, bf16[1,64,256]{2,1,0:T(8,128)(2,1)S(1)}, u32[]{:S(2)}, u32[]{:S(2)}) collective-permute-start(bf16[1,64,256]{2,1,0:T(8,128)(2,1)S(1)} %fusion.3), channel_id=1, source_target_pairs={{0,1},{1,0},{2,3},{3,2},{4,5},{5,4},{6,7},{7,6},{8,9},{9,8},{10,11... | collective-permute-start | bytes 98312 | tf_op jit(solution)/shard_map/ppermute | solution.py:29
  39.1 5.2 %collective-permute-start.7 = (bf16[1,256,256]{2,1,0:T(8,128)(2,1)S(1)}, bf16[1,256,256]{2,1,0:T(8,128)(2,1)S(1)}, u32[]{:S(2)}, u32[]{:S(2)}) collective-permute-start(bf16[1,256,256]{2,1,0:T(8,128)(2,1)S(1)} %bitcast.4), channel_id=1, source_target_pairs={{0,16},{4,20},{8,24},{12,28},{16,0},{20,4},{24,8},{28,12},{1,17},{... | collective-permute-start | bytes 393224 | tf_op jit(solution)/shard_map/ppermute | solution.py:29
  41.4 4.9 %collective-permute-start.15 = (bf16[1,64,256]{2,1,0:T(8,128)(2,1)S(1)}, bf16[1,64,256]{2,1,0:T(8,128)(2,1)S(1)}, u32[]{:S(2)}, u32[]{:S(2)}) collective-permute-start(bf16[1,64,256]{2,1,0:T(8,128)(2,1)S(1)} %add_convert_fusion.3), channel_id=1, source_target_pairs={{0,2},{1,3},{2,0},{3,1},{4,6},{5,7},{6,4},{7,5},{8,10},{9,11},{10,... | collective-permute-start | bytes 98312 | tf_op jit(solution)/shard_map/ppermute | solution.py:29
  44.3 8.0 %collective-permute-start.8 = (bf16[2,256,256]{2,1,0:T(8,128)(2,1)S(1)}, bf16[2,256,256]{2,1,0:T(8,128)(2,1)S(1)}, u32[]{:S(2)}, u32[]{:S(2)}) collective-permute-start(bf16[2,256,256]{2,1,0:T(8,128)(2,1)S(1)} %pad_maximum_fusion.1), channel_id=1, source_target_pairs={{0,8},{4,12},{8,0},{12,4},{16,24},{20,28},{24,16},{28,20},{1,9},{5... | collective-permute-start | bytes 786440 | tf_op jit(solution)/shard_map/ppermute | solution.py:29
  46.3 4.0 %collective-permute-start.16 = (bf16[1,64,256]{2,1,0:T(8,128)(2,1)S(1)}, bf16[1,64,256]{2,1,0:T(8,128)(2,1)S(1)}, u32[]{:S(2)}, u32[]{:S(2)}) collective-permute-start(bf16[1,64,256]{2,1,0:T(8,128)(2,1)S(1)} %add_convert_fusion.2), channel_id=1, source_target_pairs={{0,16},{4,20},{8,24},{12,28},{16,0},{20,4},{24,8},{28,12},{1,17},{... | collective-permute-start | bytes 98312 | tf_op jit(solution)/shard_map/ppermute | solution.py:29
  47.4 5.0 %collective-permute-start.19 = (bf16[128,256]{1,0:T(8,128)(2,1)S(1)}, bf16[128,256]{1,0:T(8,128)(2,1)S(1)}, u32[]{:S(2)}, u32[]{:S(2)}) collective-permute-start(bf16[128,256]{1,0:T(8,128)(2,1)S(1)} %convert_element_type.67), channel_id=1, source_target_pairs={{0,1},{1,0},{2,3},{3,2},{4,5},{5,4},{6,7},{7,6},{8,9},{9,8},{10,11... | collective-permute-start | bytes 196616 | tf_op jit(solution)/shard_map/ppermute | solution.py:29
  50.3 4.8 %collective-permute-start.17 = (bf16[2,64,256]{2,1,0:T(8,128)(2,1)S(1)}, bf16[2,64,256]{2,1,0:T(8,128)(2,1)S(1)}, u32[]{:S(2)}, u32[]{:S(2)}) collective-permute-start(bf16[2,64,256]{2,1,0:T(8,128)(2,1)S(1)} %pad_maximum_fusion.4), channel_id=1, source_target_pairs={{0,8},{4,12},{8,0},{12,4},{16,24},{20,28},{24,16},{28,20},{1,9},{5... | collective-permute-start | bytes 196616 | tf_op jit(solution)/shard_map/ppermute | solution.py:29
  52.3 7.1 %collective-permute-start.9 = (bf16[4,256,256]{2,1,0:T(8,128)(2,1)S(1)}, bf16[4,256,256]{2,1,0:T(8,128)(2,1)S(1)}, u32[]{:S(2)}, u32[]{:S(2)}) collective-permute-start(bf16[4,256,256]{2,1,0:T(8,128)(2,1)S(1)} %pad_maximum_fusion.even_adj_ref), channel_id=1, source_target_pairs={{0,4},{4,0},{8,12},{12,8},{16,20},{20,16},{24,28},{28,24},{1,5},{5... | collective-permute-start | bytes 1572872 | tf_op jit(solution)/shard_map/ppermute | solution.py:29
  52.4 5.5 %collective-permute-start.20 = (bf16[128,256]{1,0:T(8,128)(2,1)S(1)}, bf16[128,256]{1,0:T(8,128)(2,1)S(1)}, u32[]{:S(2)}, u32[]{:S(2)}) collective-permute-start(bf16[128,256]{1,0:T(8,128)(2,1)S(1)} %add_convert_fusion.1), channel_id=1, source_target_pairs={{0,2},{1,3},{2,0},{3,1},{4,6},{5,7},{6,4},{7,5},{8,10},{9,11},{10,... | collective-permute-start | bytes 196616 | tf_op jit(solution)/shard_map/ppermute | solution.py:29
  55.1 3.4 %collective-permute-start.18 = (bf16[4,64,256]{2,1,0:T(8,128)(2,1)S(1)}, bf16[4,64,256]{2,1,0:T(8,128)(2,1)S(1)}, u32[]{:S(2)}, u32[]{:S(2)}) collective-permute-start(bf16[4,64,256]{2,1,0:T(8,128)(2,1)S(1)} %pad_maximum_fusion.3.even_ref), channel_id=1, source_target_pairs={{0,4},{4,0},{8,12},{12,8},{16,20},{20,16},{24,28},{28,24},{1,5},{5... | collective-permute-start | bytes 393224 | tf_op jit(solution)/shard_map/ppermute | solution.py:29

commit v3 on v2

--- a/solution.py
+++ b/solution.py
@@ -363,16 +363,6 @@
     )(slab, even, odd)
 
 
-def halving_sum(blocks):
-    bit = 2
-    while blocks.shape[0] > 1:
-        half = blocks.shape[0] // 2
-        moved = xor_permute(blocks[half:].astype(bf16), "slab", bit)
-        blocks = blocks[:half] + moved.astype(f32)
-        bit = 2 * bit
-    return blocks
-
-
 def doubling_gather(blocks):
     count = lax.axis_size("slab")
     bit = count // 2
@@ -391,6 +381,23 @@
         value = sent.astype(f32) + moved.astype(f32)
         bit = 2 * bit
     return value
+
+
+def plane_gather(block, order):
+    count = lax.axis_size("slab")
+    planes, bit = [], 2
+    while bit < count:
+        planes.append((bit, min(4, count // bit)))
+        bit *= planes[-1][1]
+    held = {0: block}
+    for bit, width in reversed(planes):
+        offsets = sorted(held)
+        payload = held[0] if len(held) == 1 else jnp.stack([held[offset] for offset in offsets])
+        for g in range(width - 1, 0, -1):
+            moved = xor_permute(payload, "slab", g * bit)
+            for i, offset in enumerate(offsets):
+                held[offset ^ g * bit] = moved if len(offsets) == 1 else moved[i]
+    return jnp.stack([held[offset] for offset in order])
 
 
 def plane_sum(blocks):
@@ -481,7 +488,8 @@
     )
     wshort_moved = xor_permute(wshort_send, "slab", 1)
     grads = jnp.concatenate([wout_keep + wout_moved, wshort_keep + wshort_moved], axis=1)
-    own_grad = halving_sum(grads)
+    terms = plane_sum({offset: grads[i] for i, offset in enumerate(order)})
+    own_grad = sum((term.astype(f32) for term in terms[1:]), terms[0])
 
     adj_even = doubling_gather(adj[None])
     adj_odd = xor_permute(adj_even, "slab", 1)
@@ -490,7 +498,7 @@
     own_grad = sum_replicas(own_grad).astype(bf16)
     filter_sum = sum_replicas(gfilter)
     grad_filter = filter_sum / replicas
-    grad_even = doubling_gather(own_grad)
+    grad_even = plane_gather(own_grad, order)
     grad_odd = xor_permute(grad_even, "slab", 1)
     grad_wout, grad_wshort = place_grads(order, scale, slab, grad_even, grad_odd)
     return (grad_features[None], grad_wout, grad_wshort, grad_filter)

time: 61.3 us -> 58.7 us (0.958)
  waiting for transfers between devices: 19.3 us -> 15.6 us
  starting transfers between devices: 25.8 us -> 26.9 us
    ppermute x19 -> x21, waiting for transfers between devices: 11.9 us -> 8.17 us  [xor_permute(): lax.ppermute(value, axis, [(source, source ^ bits) for source in range(co...]
    ppermute x19 -> x21, starting transfers between devices: 24.1 us -> 25.2 us  [xor_permute(): lax.ppermute(value, axis, [(source, source ^ bits) for source in range(co...]
  transfers between devices with their start and end apart: 21 -> 23, of which waited for: 10 -> 10; matrix products, arithmetic and copies ran while one was open for 2% -> 2% of each run, Pallas kernels for 16% -> 17%
where the time goes in v3:
time: 58.7 us; the launch traced here: 58.4 us
  starting transfers between devices  26.9 us (46%)
  waiting for transfers between devices  15.6 us (27%)
  Pallas kernels  13.7 us (23%)
  other arithmetic  1.21 us (2%)
  between operations  0.85 us (1%)
    ppermute x21, starting transfers between devices, xor_permute(): lax.ppermute(value, axis, [(source, source ^ bits) for source in range(co...  25.2 us
    ppermute x21, waiting for transfers between devices, xor_permute(): lax.ppermute(value, axis, [(source, source ^ bits) for source in range(co...  8.17 us
    ppermute x2, waiting for transfers between devices, shifted(): lax.ppermute(value, axis, [(source, (source + steps) % count) for source...  7.42 us
    pallas_call x1, Pallas kernels, edge_rows(): pl.pallas_call(functools.partial(edge_kernel, block), name='edges', out_s...  5.19 us
    pallas_call x3, Pallas kernels, next_tables(): pl.pallas_call(functools.partial(second_kernel, order), out_shape=(jax.Sh...  2.81 us
    pallas_call x1, Pallas kernels, first_tables(): pl.pallas_call(functools.partial(first_kernel, order, len(others)), name=...  2.13 us
    ppermute x2, starting transfers between devices, shifted(): lax.ppermute(value, axis, [(source, (source + steps) % count) for source...  1.71 us
    pallas_call x1, Pallas kernels, back_project(): pl.pallas_call(functools.partial(back_kernel, orders, order), name='back'...  1.55 us
  transfers between devices with their start and end apart: 23, of which 10 were waited for; matrix products, arithmetic and copies ran while one was open for 2% of the time, Pallas kernels for 17%

profile of v3, /device:TPU:0, one launch (start us, length us, event | category | flops | bytes accessed | tf_op | source)
XLA Modules:
  0.0 58.4 jit_solution(11246455624505173920)
XLA Ops:
  0.6 2.1 %first.1 = (bf16[512,512]{1,0:T(8,128)(2,1)S(1)}, bf16[512,512]{1,0:T(8,128)(2,1)S(1)}, f32[1024,16]{1,0:T(8,128)S(1)}, bf16[16,512]{1,0:T(8,128)(2,1)S(1)}, bf1...) custom-call(s32[1]{0:T(128)} %bitcast.slab_ref, ...), custom_call_target="tpu_custom_call" | custom-call | flops 268435456 | bytes 1048576 | tf_op jit(solution)/shard_map/first/pallas_call | solution.py:136
  2.8 0.6 collective-permute-start.3
  3.3 0.9 %shard_map.139 = (bf16[512,512]{1,0:T(8,128)(2,1)S(1)}, bf16[512,512]{1,0:T(8,128)(2,1)S(1)}) custom-call(s32[1]{0:T(128)} %bitcast.slab_ref, f32[1024,16]{1,0:T(8,128)S(1)} %get-tuple-element.48.k_cols, bf16[16,512]{1,0:T(8,128)(2,1)S(1)} %get-tuple-element.49.positions, bf16[512,256]{1,0:T(8,128)(2,1)S(1)} %get-tuple-element.43.rows_ref, ...), custom_call_target="tpu_custom_call" | custom-call | flops 268435456 | bytes 1048576 | tf_op jit(solution)/shard_map/pallas_call | solution.py:163
  4.3 0.1 collective-permute-start.2
  4.4 0.9 %shard_map.140 = (bf16[512,512]{1,0:T(8,128)(2,1)S(1)}, f32[512,512]{1,0:T(8,128)S(1)}) custom-call(s32[1]{0:T(128)} %bitcast.slab_ref, f32[1024,16]{1,0:T(8,128)S(1)} %get-tuple-element.48.k_cols, bf16[16,512]{1,0:T(8,128)(2,1)S(1)} %get-tuple-element.49.positions, bf16[512,256]{1,0:T(8,128)(2,1)S(1)} %get-tuple-element.43.rows_ref, ...), custom_call_target="tpu_custom_call" | custom-call | flops 268435456 | bytes 1048576 | tf_op jit(solution)/shard_map/pallas_call | solution.py:163
  5.3 0.9 %shard_map.138 = (bf16[512,512]{1,0:T(8,128)(2,1)S(1)}, f32[512,512]{1,0:T(8,128)S(1)}) custom-call(s32[1]{0:T(128)} %bitcast.slab_ref, f32[1024,16]{1,0:T(8,128)S(1)} %get-tuple-element.48.k_cols, bf16[16,512]{1,0:T(8,128)(2,1)S(1)} %get-tuple-element.49.positions, bf16[512,256]{1,0:T(8,128)(2,1)S(1)} %get-tuple-element.43.rows_ref, ...), custom_call_target="tpu_custom_call" | custom-call | flops 268435456 | bytes 1048576 | tf_op jit(solution)/shard_map/pallas_call | solution.py:163
  6.3 0.0 collective-permute-done.3
  6.3 0.2 add_convert_fusion
  6.5 3.0 %collective-permute-start.5 = (bf16[256,512]{1,0:T(8,128)(2,1)S(1)}, bf16[256,512]{1,0:T(8,128)(2,1)S(1)}, u32[]{:S(2)}, u32[]{:S(2)}) collective-permute-start(bf16[256,512]{1,0:T(8,128)(2,1)S(1)} %get-tuple-element.66), channel_id=1, source_target_pairs={{0,16},{4,20},{8,24},{12,28},{16,0},{20,4},{24,8},{28,12},{1,17},{... | collective-permute-start | bytes 786440 | tf_op jit(solution)/shard_map/ppermute | solution.py:29
  9.5 1.4 %collective-permute-start.4 = (bf16[256,512]{1,0:T(8,128)(2,1)S(1)}, bf16[256,512]{1,0:T(8,128)(2,1)S(1)}, u32[]{:S(2)}, u32[]{:S(2)}) collective-permute-start(bf16[256,512]{1,0:T(8,128)(2,1)S(1)} %get-tuple-element.67), channel_id=1, source_target_pairs={{0,24},{4,28},{8,16},{12,20},{16,8},{20,12},{24,0},{28,4},{1,25},{... | collective-permute-start | bytes 786440 | tf_op jit(solution)/shard_map/ppermute | solution.py:29
  11.0 0.0 collective-permute-done.2
  11.0 0.2 convert_add_fusion
  11.2 0.2 collective-permute-start.6
  11.3 5.2 %edges.1 = (f32[512,256]{1,0:T(8,128)S(1)}, bf16[256,256]{1,0:T(8,128)(2,1)S(1)}, bf16[256,256]{1,0:T(8,128)(2,1)S(1)}) custom-call(s32[1,4096]{1,0:T(1,128)S(1)} %get-tuple-element.35.src_ref, s32[1,4096]{1,0:T(1,128)S(1)} %get-tuple-element.36.dst_ref, f32[1,4096]{1,0:T(1,128)S(1)} %get-tuple-element.37.dist_ref, ...), custom_call_target="tpu_custom_call" | custom-call | flops 3221225472 | bytes 49152 | tf_op jit(solution)/shard_map/edges/pallas_call | solution.py:204
  16.5 1.7 %collective-permute-start = (bf16[256,256]{1,0:T(8,128)(2,1)S(1)}, bf16[256,256]{1,0:T(8,128)(2,1)S(1)}, u32[]{:S(2)}, u32[]{:S(2)}) collective-permute-start(bf16[256,256]{1,0:T(8,128)(2,1)S(1)} %get-tuple-element.40), channel_id=1, source_target_pairs={{0,28},{4,0},{8,4},{12,8},{16,12},{20,16},{24,20},{28,24},{1,29},{... | collective-permute-start | bytes 393224 | tf_op jit(solution)/shard_map/ppermute | solution.py:34
  18.2 0.0 collective-permute-start.1
  18.2 6.7 %collective-permute-done.above_ref = bf16[256,256]{1,0:T(8,128)(2,1)S(1)} collective-permute-done((bf16[256,256]{1,0:T(8,128)(2,1)S(1)}, bf16[256,256]{1,0:T(8,128)(2,1)S(1)}, u32[]{:S(2)}, u32[]{:S(2)}) %collective-permute-start) | collective-permute-done | bytes 131104 | tf_op jit(solution)/shard_map/ppermute | solution.py:34
  24.9 0.8 %collective-permute-done.1.below_ref = bf16[256,256]{1,0:T(8,128)(2,1)S(1)} collective-permute-done((bf16[256,256]{1,0:T(8,128)(2,1)S(1)}, bf16[256,256]{1,0:T(8,128)(2,1)S(1)}, u32[]{:S(2)}, u32[]{:S(2)}) %collective-permute-start.1) | collective-permute-done | bytes 131104 | tf_op jit(solution)/shard_map/ppermute | solution.py:34
  25.7 0.7 %short.1 = (f32[512,256]{1,0:T(8,128)S(1)}, f32[4,32,256]{2,1,0:T(8,128)S(1)}, f32[4,32,256]{2,1,0:T(8,128)S(1)}) custom-call(s32[1]{0:T(128)} %bitcast.slab_ref, f32[512,256]{1,0:T(8,128)S(1)} %get-tuple-element.39.own_ref, bf16[256,256]{1,0:T(8,128)(2,1)S(1)} %collective-permute-done.above_ref, bf16[256,256]{1,0:T(8,128)(2,1)S(1)} %collective-permute-done.1.below_ref, ...), custom_call_target="tpu_custom_call" | custom-call | flops 268435456 | bytes 1048576 | tf_op jit(solution)/shard_map/short/pallas_call | solution.py:252
  26.3 0.2 collective-permute-start.11
  26.6 0.0 collective-permute-done.5.refs_2_
  26.6 0.0 collective-permute-done.4.refs_1_
  26.6 0.0 collective-permute-done.6.refs_3_
  26.6 0.5 share.1
  27.1 0.5 collective-permute-start.10
  27.6 0.2 collective-permute-done.11
  27.8 0.8 %collective-permute-done.10 = f32[4,32,256]{2,1,0:T(8,128)S(1)} collective-permute-done((f32[4,32,256]{2,1,0:T(8,128)S(1)}, f32[4,32,256]{2,1,0:T(8,128)S(1)}, u32[]{:S(2)}, u32[]{:S(2)}) %collective-permute-start.10) | collective-permute-done | bytes 131104 | tf_op jit(solution)/shard_map/ppermute | solution.py:29
  28.6 2.4 %collective-permute-start.12 = (bf16[64,256]{1,0:T(8,128)(2,1)S(1)}, bf16[64,256]{1,0:T(8,128)(2,1)S(1)}, u32[]{:S(2)}, u32[]{:S(2)}) collective-permute-start(bf16[64,256]{1,0:T(8,128)(2,1)S(1)} %get-tuple-element.68), channel_id=1, source_target_pairs={{0,24},{4,28},{8,16},{12,20},{16,8},{20,12},{24,0},{28,4},{1,25},{... | collective-permute-start | bytes 98312 | tf_op jit(solution)/shard_map/ppermute | solution.py:29
  31.0 0.6 %collective-permute-start.14 = (bf16[64,256]{1,0:T(8,128)(2,1)S(1)}, bf16[64,256]{1,0:T(8,128)(2,1)S(1)}, u32[]{:S(2)}, u32[]{:S(2)}) collective-permute-start(bf16[64,256]{1,0:T(8,128)(2,1)S(1)} %get-tuple-element.69), channel_id=1, source_target_pairs={{0,8},{4,12},{8,0},{12,4},{16,24},{20,28},{24,16},{28,20},{1,9},{5... | collective-permute-start | bytes 98312 | tf_op jit(solution)/shard_map/ppermute | solution.py:29
  31.6 0.9 %collective-permute-start.13 = (bf16[64,256]{1,0:T(8,128)(2,1)S(1)}, bf16[64,256]{1,0:T(8,128)(2,1)S(1)}, u32[]{:S(2)}, u32[]{:S(2)}) collective-permute-start(bf16[64,256]{1,0:T(8,128)(2,1)S(1)} %get-tuple-element.70), channel_id=1, source_target_pairs={{0,16},{4,20},{8,24},{12,28},{16,0},{20,4},{24,8},{28,12},{1,17},{... | collective-permute-start | bytes 98312 | tf_op jit(solution)/shard_map/ppermute | solution.py:29
  32.5 1.1 %collective-permute-start.7 = (bf16[1,256,256]{2,1,0:T(8,128)(2,1)S(1)}, bf16[1,256,256]{2,1,0:T(8,128)(2,1)S(1)}, u32[]{:S(2)}, u32[]{:S(2)}) collective-permute-start(bf16[1,256,256]{2,1,0:T(8,128)(2,1)S(1)} %bitcast.24), channel_id=1, source_target_pairs={{0,16},{4,20},{8,24},{12,28},{16,0},{20,4},{24,8},{28,12},{1,17},{... | collective-permute-start | bytes 393224 | tf_op jit(solution)/shard_map/ppermute | solution.py:29
  33.6 0.0 collective-permute-done.12
  33.6 1.3 %collective-permute-done.14 = bf16[64,256]{1,0:T(8,128)(2,1)S(1)} collective-permute-done((bf16[64,256]{1,0:T(8,128)(2,1)S(1)}, bf16[64,256]{1,0:T(8,128)(2,1)S(1)}, u32[]{:S(2)}, u32[]{:S(2)}) %collective-permute-start.14) | collective-permute-done | bytes 32800 | tf_op jit(solution)/shard_map/ppermute | solution.py:29
  34.9 0.9 %collective-permute-done.13 = bf16[64,256]{1,0:T(8,128)(2,1)S(1)} collective-permute-done((bf16[64,256]{1,0:T(8,128)(2,1)S(1)}, bf16[64,256]{1,0:T(8,128)(2,1)S(1)}, u32[]{:S(2)}, u32[]{:S(2)}) %collective-permute-start.13) | collective-permute-done | bytes 32800 | tf_op jit(solution)/shard_map/ppermute | solution.py:29
  35.9 1.6 %collective-permute-start.15 = (bf16[64,256]{1,0:T(8,128)(2,1)S(1)}, bf16[64,256]{1,0:T(8,128)(2,1)S(1)}, u32[]{:S(2)}, u32[]{:S(2)}) collective-permute-start(bf16[64,256]{1,0:T(8,128)(2,1)S(1)} %fusion.6), channel_id=1, source_target_pairs={{0,1},{1,0},{2,3},{3,2},{4,5},{5,4},{6,7},{7,6},{8,9},{9,8},{10,11... | collective-permute-start | bytes 98312 | tf_op jit(solution)/shard_map/ppermute | solution.py:29
  37.5 0.3 collective-permute-done.7
  37.9 1.8 %collective-permute-start.8 = (bf16[2,256,256]{2,1,0:T(8,128)(2,1)S(1)}, bf16[2,256,256]{2,1,0:T(8,128)(2,1)S(1)}, u32[]{:S(2)}, u32[]{:S(2)}) collective-permute-start(bf16[2,256,256]{2,1,0:T(8,128)(2,1)S(1)} %pad_maximum_fusion.2), channel_id=1, source_target_pairs={{0,8},{4,12},{8,0},{12,4},{16,24},{20,28},{24,16},{28,20},{1,9},{5... | collective-permute-start | bytes 786440 | tf_op jit(solution)/shard_map/ppermute | solution.py:29
  39.7 0.2 collective-permute-done.15
  39.8 2.7 %collective-permute-start.16 = (bf16[64,256]{1,0:T(8,128)(2,1)S(1)}, bf16[64,256]{1,0:T(8,128)(2,1)S(1)}, u32[]{:S(2)}, u32[]{:S(2)}) collective-permute-start(bf16[64,256]{1,0:T(8,128)(2,1)S(1)} %add_convert_fusion.3), channel_id=1, source_target_pairs={{0,2},{1,3},{2,0},{3,1},{4,6},{5,7},{6,4},{7,5},{8,10},{9,11},{10,... | collective-permute-start | bytes 98312 | tf_op jit(solution)/shard_map/ppermute | solution.py:29
  42.5 1.6 %collective-permute-start.21 = (bf16[128,256]{1,0:T(8,128)(2,1)S(1)}, bf16[128,256]{1,0:T(8,128)(2,1)S(1)}, u32[]{:S(2)}, u32[]{:S(2)}) collective-permute-start(bf16[128,256]{1,0:T(8,128)(2,1)S(1)} %convert_element_type.84), channel_id=1, source_target_pairs={{0,1},{1,0},{2,3},{3,2},{4,5},{5,4},{6,7},{7,6},{8,9},{9,8},{10,11... | collective-permute-start | bytes 196616 | tf_op jit(solution)/shard_map/ppermute | solution.py:29
  44.2 0.6 collective-permute-done.16
  44.7 2.4 %collective-permute-start.19 = (bf16[64,256]{1,0:T(8,128)(2,1)S(1)}, bf16[64,256]{1,0:T(8,128)(2,1)S(1)}, u32[]{:S(2)}, u32[]{:S(2)}) collective-permute-start(bf16[64,256]{1,0:T(8,128)(2,1)S(1)} %add_convert_fusion.2), channel_id=1, source_target_pairs={{0,24},{4,28},{8,16},{12,20},{16,8},{20,12},{24,0},{28,4},{1,25},{... | collective-permute-start | bytes 98312 | tf_op jit(solution)/shard_map/ppermute | solution.py:29
  47.2 0.0 collective-permute-start.18
  47.2 1.1 %collective-permute-start.17 = (bf16[64,256]{1,0:T(8,128)(2,1)S(1)}, bf16[64,256]{1,0:T(8,128)(2,1)S(1)}, u32[]{:S(2)}, u32[]{:S(2)}) collective-permute-start(bf16[64,256]{1,0:T(8,128)(2,1)S(1)} %add_convert_fusion.2), channel_id=1, source_target_pairs={{0,16},{4,20},{8,24},{12,28},{16,0},{20,4},{24,8},{28,12},{1,17},{... | collective-permute-start | bytes 98312 | tf_op jit(solution)/shard_map/ppermute | solution.py:29
  48.3 0.0 collective-permute-done.8
  48.3 0.1 pad_maximum_fusion.even_adj_ref
  48.4 0.1 collective-permute-start.9
  48.4 0.0 collective-permute-done.21
  48.5 2.7 %collective-permute-start.22 = (bf16[128,256]{1,0:T(8,128)(2,1)S(1)}, bf16[128,256]{1,0:T(8,128)(2,1)S(1)}, u32[]{:S(2)}, u32[]{:S(2)}) collective-permute-start(bf16[128,256]{1,0:T(8,128)(2,1)S(1)} %add_convert_fusion.1), channel_id=1, source_target_pairs={{0,2},{1,3},{2,0},{3,1},{4,6},{5,7},{6,4},{7,5},{8,10},{9,11},{10,... | collective-permute-start | bytes 196616 | tf_op jit(solution)/shard_map/ppermute | solution.py:29
  51.1 0.0 collective-permute-done.19
  51.1 0.0 collective-permute-done.18
  51.1 0.0 collective-permute-done.17
  51.2 0.3 collective-permute-start.20
  51.5 3.9 %collective-permute-done.22 = bf16[128,256]{1,0:T(8,128)(2,1)S(1)} collective-permute-done((bf16[128,256]{1,0:T(8,128)(2,1)S(1)}, bf16[128,256]{1,0:T(8,128)(2,1)S(1)}, u32[]{:S(2)}, u32[]{:S(2)}) %collective-permute-start.22) | collective-permute-done | bytes 65568 | tf_op jit(solution)/shard_map/ppermute | solution.py:29
  55.3 0.7 %add_multiply_fusion = f32[128,256]{1,0:T(8,128)} fusion(bf16[128,256]{1,0:T(8,128)(2,1)S(1)} %collective-permute-done.22, bf16[128,256]{1,0:T(8,128)(2,1)S(1)} %add_convert_fusion.1), kind=kLoop, calls=%fused_computation.10 | loop fusion | flops 131072 | bytes 262144 | tf_op jit(solution)/shard_map/div | solution.py:500
  56.0 0.0 collective-permute-done.20.odd_ref
  56.0 0.9 %place.1 = (f32[256,256]{1,0:T(8,128)}, f32[256,256]{1,0:T(8,128)}) custom-call(s32[1]{0:T(128)} %bitcast.slab_ref, bf16[4,64,256]{2,1,0:T(8,128)(2,1)S(1)} %pad_maximum_fusion.3.even_ref, bf16[4,64,256]{2,1,0:T(8,128)(2,1)S(1)} %collective-permute-done.20.odd_ref), custom_call_target="tpu_custom_call" | custom-call | tf_op jit(solution)/shard_map/place/pallas_call | solution.py:355
  56.9 0.0 collective-permute-done.9.odd_adj_ref
  56.9 1.5 %back.1 = bf16[512,256]{1,0:T(8,128)(2,1)} custom-call(f32[512,256]{1,0:T(8,128)S(1)} %get-tuple-element.45.base_ref, bf16[4,256,256]{2,1,0:T(8,128)(2,1)S(1)} %pad_maximum_fusion.even_adj_ref, bf16[4,256,256]{2,1,0:T(8,128)(2,1)S(1)} %collective-permute-done.9.odd_adj_ref, bf16[512,512]{1,0:T(8,128)(2,1)S(1)} %get-tuple-element.55.refs_0_, ...), custom_call_target="tpu_custom_call" | custom-call | flops 536870912 | bytes 2097152 | tf_op jit(solution)/shard_map/back/pallas_call | solution.py:328
  (14 shorter events, 0.3 us)
Async XLA Ops:
  2.8 3.5 %collective-permute-start.3 = (bf16[512,512]{1,0:T(8,128)(2,1)S(1)}, bf16[512,512]{1,0:T(8,128)(2,1)S(1)}, u32[]{:S(2)}, u32[]{:S(2)}) collective-permute-start(bf16[512,512]{1,0:T(8,128)(2,1)S(1)} %get-tuple-element.53), channel_id=1, source_target_pairs={{0,4},{4,0},{8,12},{12,8},{16,20},{20,16},{24,28},{28,24},{1,5},{5... | collective-permute-start | bytes 1572872 | tf_op jit(solution)/shard_map/ppermute | solution.py:29
  4.3 6.7 %collective-permute-start.2 = (bf16[512,512]{1,0:T(8,128)(2,1)S(1)}, bf16[512,512]{1,0:T(8,128)(2,1)S(1)}, u32[]{:S(2)}, u32[]{:S(2)}) collective-permute-start(bf16[512,512]{1,0:T(8,128)(2,1)S(1)} %get-tuple-element.51), channel_id=1, source_target_pairs={{0,4},{4,0},{8,12},{12,8},{16,20},{20,16},{24,28},{28,24},{1,5},{5... | collective-permute-start | bytes 1572872 | tf_op jit(solution)/shard_map/ppermute | solution.py:29
  6.5 20.1 %collective-permute-start.5 = (bf16[256,512]{1,0:T(8,128)(2,1)S(1)}, bf16[256,512]{1,0:T(8,128)(2,1)S(1)}, u32[]{:S(2)}, u32[]{:S(2)}) collective-permute-start(bf16[256,512]{1,0:T(8,128)(2,1)S(1)} %get-tuple-element.66), channel_id=1, source_target_pairs={{0,16},{4,20},{8,24},{12,28},{16,0},{20,4},{24,8},{28,12},{1,17},{... | collective-permute-start | bytes 786440 | tf_op jit(solution)/shard_map/ppermute | solution.py:29
  9.5 17.0 %collective-permute-start.4 = (bf16[256,512]{1,0:T(8,128)(2,1)S(1)}, bf16[256,512]{1,0:T(8,128)(2,1)S(1)}, u32[]{:S(2)}, u32[]{:S(2)}) collective-permute-start(bf16[256,512]{1,0:T(8,128)(2,1)S(1)} %get-tuple-element.67), channel_id=1, source_target_pairs={{0,24},{4,28},{8,16},{12,20},{16,8},{20,12},{24,0},{28,4},{1,25},{... | collective-permute-start | bytes 786440 | tf_op jit(solution)/shard_map/ppermute | solution.py:29
  11.2 15.4 %collective-permute-start.6 = (bf16[256,512]{1,0:T(8,128)(2,1)S(1)}, bf16[256,512]{1,0:T(8,128)(2,1)S(1)}, u32[]{:S(2)}, u32[]{:S(2)}) collective-permute-start(bf16[256,512]{1,0:T(8,128)(2,1)S(1)} %slice.67), channel_id=1, source_target_pairs={{0,8},{4,12},{8,0},{12,4},{16,24},{20,28},{24,16},{28,20},{1,9},{5... | collective-permute-start | bytes 786440 | tf_op jit(solution)/shard_map/ppermute | solution.py:29
  16.5 8.4 %collective-permute-start = (bf16[256,256]{1,0:T(8,128)(2,1)S(1)}, bf16[256,256]{1,0:T(8,128)(2,1)S(1)}, u32[]{:S(2)}, u32[]{:S(2)}) collective-permute-start(bf16[256,256]{1,0:T(8,128)(2,1)S(1)} %get-tuple-element.40), channel_id=1, source_target_pairs={{0,28},{4,0},{8,4},{12,8},{16,12},{20,16},{24,20},{28,24},{1,29},{... | collective-permute-start | bytes 393224 | tf_op jit(solution)/shard_map/ppermute | solution.py:34
  18.2 7.4 %collective-permute-start.1 = (bf16[256,256]{1,0:T(8,128)(2,1)S(1)}, bf16[256,256]{1,0:T(8,128)(2,1)S(1)}, u32[]{:S(2)}, u32[]{:S(2)}) collective-permute-start(bf16[256,256]{1,0:T(8,128)(2,1)S(1)} %get-tuple-element.41), channel_id=1, source_target_pairs={{0,4},{4,8},{8,12},{12,16},{16,20},{20,24},{24,28},{28,0},{1,5},{5... | collective-permute-start | bytes 393224 | tf_op jit(solution)/shard_map/ppermute | solution.py:34
  26.3 1.4 %collective-permute-start.11 = (f32[4,32,256]{2,1,0:T(8,128)S(1)}, f32[4,32,256]{2,1,0:T(8,128)S(1)}, u32[]{:S(2)}, u32[]{:S(2)}) collective-permute-start(f32[4,32,256]{2,1,0:T(8,128)S(1)} %get-tuple-element.62), channel_id=1, source_target_pairs={{0,4},{4,0},{8,12},{12,8},{16,20},{20,16},{24,28},{28,24},{1,5},{5... | collective-permute-start | bytes 393224 | tf_op jit(solution)/shard_map/ppermute | solution.py:29
  27.1 1.4 %collective-permute-start.10 = (f32[4,32,256]{2,1,0:T(8,128)S(1)}, f32[4,32,256]{2,1,0:T(8,128)S(1)}, u32[]{:S(2)}, u32[]{:S(2)}) collective-permute-start(f32[4,32,256]{2,1,0:T(8,128)S(1)} %get-tuple-element.60), channel_id=1, source_target_pairs={{0,4},{4,0},{8,12},{12,8},{16,20},{20,16},{24,28},{28,24},{1,5},{5... | collective-permute-start | bytes 393224 | tf_op jit(solution)/shard_map/ppermute | solution.py:29
  28.6 5.0 %collective-permute-start.12 = (bf16[64,256]{1,0:T(8,128)(2,1)S(1)}, bf16[64,256]{1,0:T(8,128)(2,1)S(1)}, u32[]{:S(2)}, u32[]{:S(2)}) collective-permute-start(bf16[64,256]{1,0:T(8,128)(2,1)S(1)} %get-tuple-element.68), channel_id=1, source_target_pairs={{0,24},{4,28},{8,16},{12,20},{16,8},{20,12},{24,0},{28,4},{1,25},{... | collective-permute-start | bytes 98312 | tf_op jit(solution)/shard_map/ppermute | solution.py:29
  31.0 3.9 %collective-permute-start.14 = (bf16[64,256]{1,0:T(8,128)(2,1)S(1)}, bf16[64,256]{1,0:T(8,128)(2,1)S(1)}, u32[]{:S(2)}, u32[]{:S(2)}) collective-permute-start(bf16[64,256]{1,0:T(8,128)(2,1)S(1)} %get-tuple-element.69), channel_id=1, source_target_pairs={{0,8},{4,12},{8,0},{12,4},{16,24},{20,28},{24,16},{28,20},{1,9},{5... | collective-permute-start | bytes 98312 | tf_op jit(solution)/shard_map/ppermute | solution.py:29
  31.6 4.3 %collective-permute-start.13 = (bf16[64,256]{1,0:T(8,128)(2,1)S(1)}, bf16[64,256]{1,0:T(8,128)(2,1)S(1)}, u32[]{:S(2)}, u32[]{:S(2)}) collective-permute-start(bf16[64,256]{1,0:T(8,128)(2,1)S(1)} %get-tuple-element.70), channel_id=1, source_target_pairs={{0,16},{4,20},{8,24},{12,28},{16,0},{20,4},{24,8},{28,12},{1,17},{... | collective-permute-start | bytes 98312 | tf_op jit(solution)/shard_map/ppermute | solution.py:29
  32.5 5.3 %collective-permute-start.7 = (bf16[1,256,256]{2,1,0:T(8,128)(2,1)S(1)}, bf16[1,256,256]{2,1,0:T(8,128)(2,1)S(1)}, u32[]{:S(2)}, u32[]{:S(2)}) collective-permute-start(bf16[1,256,256]{2,1,0:T(8,128)(2,1)S(1)} %bitcast.24), channel_id=1, source_target_pairs={{0,16},{4,20},{8,24},{12,28},{16,0},{20,4},{24,8},{28,12},{1,17},{... | collective-permute-start | bytes 393224 | tf_op jit(solution)/shard_map/ppermute | solution.py:29
  35.9 4.0 %collective-permute-start.15 = (bf16[64,256]{1,0:T(8,128)(2,1)S(1)}, bf16[64,256]{1,0:T(8,128)(2,1)S(1)}, u32[]{:S(2)}, u32[]{:S(2)}) collective-permute-start(bf16[64,256]{1,0:T(8,128)(2,1)S(1)} %fusion.6), channel_id=1, source_target_pairs={{0,1},{1,0},{2,3},{3,2},{4,5},{5,4},{6,7},{7,6},{8,9},{9,8},{10,11... | collective-permute-start | bytes 98312 | tf_op jit(solution)/shard_map/ppermute | solution.py:29
  37.9 10.4 %collective-permute-start.8 = (bf16[2,256,256]{2,1,0:T(8,128)(2,1)S(1)}, bf16[2,256,256]{2,1,0:T(8,128)(2,1)S(1)}, u32[]{:S(2)}, u32[]{:S(2)}) collective-permute-start(bf16[2,256,256]{2,1,0:T(8,128)(2,1)S(1)} %pad_maximum_fusion.2), channel_id=1, source_target_pairs={{0,8},{4,12},{8,0},{12,4},{16,24},{20,28},{24,16},{28,20},{1,9},{5... | collective-permute-start | bytes 786440 | tf_op jit(solution)/shard_map/ppermute | solution.py:29
  39.8 4.9 %collective-permute-start.16 = (bf16[64,256]{1,0:T(8,128)(2,1)S(1)}, bf16[64,256]{1,0:T(8,128)(2,1)S(1)}, u32[]{:S(2)}, u32[]{:S(2)}) collective-permute-start(bf16[64,256]{1,0:T(8,128)(2,1)S(1)} %add_convert_fusion.3), channel_id=1, source_target_pairs={{0,2},{1,3},{2,0},{3,1},{4,6},{5,7},{6,4},{7,5},{8,10},{9,11},{10,... | collective-permute-start | bytes 98312 | tf_op jit(solution)/shard_map/ppermute | solution.py:29
  42.5 5.9 %collective-permute-start.21 = (bf16[128,256]{1,0:T(8,128)(2,1)S(1)}, bf16[128,256]{1,0:T(8,128)(2,1)S(1)}, u32[]{:S(2)}, u32[]{:S(2)}) collective-permute-start(bf16[128,256]{1,0:T(8,128)(2,1)S(1)} %convert_element_type.84), channel_id=1, source_target_pairs={{0,1},{1,0},{2,3},{3,2},{4,5},{5,4},{6,7},{7,6},{8,9},{9,8},{10,11... | collective-permute-start | bytes 196616 | tf_op jit(solution)/shard_map/ppermute | solution.py:29
  44.7 6.4 %collective-permute-start.19 = (bf16[64,256]{1,0:T(8,128)(2,1)S(1)}, bf16[64,256]{1,0:T(8,128)(2,1)S(1)}, u32[]{:S(2)}, u32[]{:S(2)}) collective-permute-start(bf16[64,256]{1,0:T(8,128)(2,1)S(1)} %add_convert_fusion.2), channel_id=1, source_target_pairs={{0,24},{4,28},{8,16},{12,20},{16,8},{20,12},{24,0},{28,4},{1,25},{... | collective-permute-start | bytes 98312 | tf_op jit(solution)/shard_map/ppermute | solution.py:29
  47.2 4.0 %collective-permute-start.18 = (bf16[64,256]{1,0:T(8,128)(2,1)S(1)}, bf16[64,256]{1,0:T(8,128)(2,1)S(1)}, u32[]{:S(2)}, u32[]{:S(2)}) collective-permute-start(bf16[64,256]{1,0:T(8,128)(2,1)S(1)} %add_convert_fusion.2), channel_id=1, source_target_pairs={{0,8},{4,12},{8,0},{12,4},{16,24},{20,28},{24,16},{28,20},{1,9},{5... | collective-permute-start | bytes 98312 | tf_op jit(solution)/shard_map/ppermute | solution.py:29
  47.2 4.0 %collective-permute-start.17 = (bf16[64,256]{1,0:T(8,128)(2,1)S(1)}, bf16[64,256]{1,0:T(8,128)(2,1)S(1)}, u32[]{:S(2)}, u32[]{:S(2)}) collective-permute-start(bf16[64,256]{1,0:T(8,128)(2,1)S(1)} %add_convert_fusion.2), channel_id=1, source_target_pairs={{0,16},{4,20},{8,24},{12,28},{16,0},{20,4},{24,8},{28,12},{1,17},{... | collective-permute-start | bytes 98312 | tf_op jit(solution)/shard_map/ppermute | solution.py:29
  48.4 8.5 %collective-permute-start.9 = (bf16[4,256,256]{2,1,0:T(8,128)(2,1)S(1)}, bf16[4,256,256]{2,1,0:T(8,128)(2,1)S(1)}, u32[]{:S(2)}, u32[]{:S(2)}) collective-permute-start(bf16[4,256,256]{2,1,0:T(8,128)(2,1)S(1)} %pad_maximum_fusion.even_adj_ref), channel_id=1, source_target_pairs={{0,4},{4,0},{8,12},{12,8},{16,20},{20,16},{24,28},{28,24},{1,5},{5... | collective-permute-start | bytes 1572872 | tf_op jit(solution)/shard_map/ppermute | solution.py:29
  48.5 6.9 %collective-permute-start.22 = (bf16[128,256]{1,0:T(8,128)(2,1)S(1)}, bf16[128,256]{1,0:T(8,128)(2,1)S(1)}, u32[]{:S(2)}, u32[]{:S(2)}) collective-permute-start(bf16[128,256]{1,0:T(8,128)(2,1)S(1)} %add_convert_fusion.1), channel_id=1, source_target_pairs={{0,2},{1,3},{2,0},{3,1},{4,6},{5,7},{6,4},{7,5},{8,10},{9,11},{10,... | collective-permute-start | bytes 196616 | tf_op jit(solution)/shard_map/ppermute | solution.py:29
  51.2 4.8 %collective-permute-start.20 = (bf16[4,64,256]{2,1,0:T(8,128)(2,1)S(1)}, bf16[4,64,256]{2,1,0:T(8,128)(2,1)S(1)}, u32[]{:S(2)}, u32[]{:S(2)}) collective-permute-start(bf16[4,64,256]{2,1,0:T(8,128)(2,1)S(1)} %pad_maximum_fusion.3.even_ref), channel_id=1, source_target_pairs={{0,4},{4,0},{8,12},{12,8},{16,20},{20,16},{24,28},{28,24},{1,5},{5... | collective-permute-start | bytes 393224 | tf_op jit(solution)/shard_map/ppermute | solution.py:29

commit v4 on v3

--- a/solution.py
+++ b/solution.py
@@ -175,28 +175,62 @@
     )(slab, k_cols, positions, rows, cotan)
 
 
-def edge_kernel(block, src_ref, dst_ref, dist_ref, cot_ref, own_ref, low_ref, up_ref, total):
+def one_hot(row_count, indices):
+    rows = lax.broadcasted_iota(jnp.int32, (row_count, indices.shape[1]), 0)
+    return (rows == indices).astype(f32).astype(bf16)
+
+
+def rims_kernel(rows_ref, lists_ref, rows_t_ref, prev_ref, next_ref):
+    atoms = rows_ref.shape[0]
+    lists = lists_ref[0]
+    rows_t = rows_ref[...].T
+    rows_t_ref[...] = rows_t
+    prev_ref[...] = dot(rows_t, one_hot(atoms, lists[0:1, :])).astype(bf16)
+    next_ref[...] = dot(rows_t, one_hot(atoms, lists[1:2, :])).astype(bf16)
+
+
+def rim_features(rows, lists):
+    atoms, channels = rows.shape
+    rim = lists.shape[2]
+    return pl.pallas_call(
+        rims_kernel,
+        name="rims",
+        out_shape=(
+            jax.ShapeDtypeStruct((channels, atoms), bf16),
+            jax.ShapeDtypeStruct((channels, rim), bf16),
+            jax.ShapeDtypeStruct((channels, rim), bf16),
+        ),
+        in_specs=[VMEM] * 2,
+        out_specs=(VMEM,) * 3,
+        compiler_params=params(),
+        cost_estimate=pl.CostEstimate(
+            flops=4 * atoms * channels * rim, bytes_accessed=4 * atoms * channels, transcendentals=0
+        ),
+    )(rows, lists)
+
+
+def edge_kernel(block, src_ref, dst_ref, dist_ref, cot_ref, rows_t_ref, own_ref, low_ref, up_ref, grad_ref, total):
     atoms, _ = cot_ref.shape
     rim = low_ref.shape[0]
     edges = src_ref.shape[1]
     cot_t = cot_ref[...].T
     for start in range(0, edges, block):
         at = slice(start, start + block)
-        source, target = src_ref[:, at], dst_ref[:, at]
         weight = jnp.maximum(1.0 - dist_ref[:, at] / cutoff_radius, 0.0)
         weight = weight * weight
-        pick = lax.broadcasted_iota(jnp.int32, (atoms, block), 0) == target
-        taken = dot(cot_t, pick.astype(f32).astype(bf16))
+        taken = dot(cot_t, one_hot(atoms, dst_ref[:, at]))
         weighted = (taken * weight).astype(bf16)
-        put = lax.broadcasted_iota(jnp.int32, (total.shape[0], block), 0) == source
-        part = dot(put.astype(f32).astype(bf16), weighted, 1, 1)
+        part = dot(one_hot(total.shape[0], src_ref[:, at]), weighted, 1, 1)
         total[...] = part if start == 0 else total[...] + part
-    own_ref[...] = total[:atoms, :]
+    own = total[:atoms, :]
+    own_ref[...] = own
     low_ref[...] = total[atoms : atoms + rim, :].astype(bf16)
     up_ref[...] = total[atoms + rim :, :].astype(bf16)
-
-
-def edge_rows(sources, targets, lengths, cotan, rim):
+    high, low = halves(own)
+    grad_ref[...] = dot(rows_t_ref[...], high) + dot(rows_t_ref[...], low)
+
+
+def edge_rows(sources, targets, lengths, cotan, rows_t, rim):
     atoms, channels = cotan.shape
     edges = sources.shape[1]
     rows = atoms + 2 * rim
@@ -208,66 +242,57 @@
             jax.ShapeDtypeStruct((atoms, channels), f32),
             jax.ShapeDtypeStruct((rim, channels), bf16),
             jax.ShapeDtypeStruct((rim, channels), bf16),
-        ),
-        in_specs=[VMEM] * 4,
-        out_specs=(VMEM,) * 3,
+            jax.ShapeDtypeStruct((channels, channels), f32),
+        ),
+        in_specs=[VMEM] * 5,
+        out_specs=(VMEM,) * 4,
         scratch_shapes=[pltpu.VMEM((rows, channels), f32)],
         compiler_params=params(),
         cost_estimate=pl.CostEstimate(
             flops=2 * edges * (rows + atoms) * channels, bytes_accessed=edges * 12, transcendentals=0
         ),
-    )(sources, targets, lengths, cotan)
-
-
-def split_blocks(order, slab, value, send_ref, keep_ref, blocks):
+    )(sources, targets, lengths, cotan, rows_t)
+
+
+def split_blocks(order, slab, values, send_ref, keep_ref, blocks):
     count, height, _ = blocks.shape
+    height = height // len(values)
     for i in range(count):
-        blocks[i] = value[i * height : (i + 1) * height, :]
+        for j, value in enumerate(values):
+            blocks[i, j * height : (j + 1) * height] = value[i * height : (i + 1) * height, :]
     for place, offset in enumerate(order):
         keep_ref[place] = blocks[slab ^ offset]
         send_ref[place] = blocks[slab ^ offset ^ 1]
 
 
-def short_kernel(
-    order, slab_ref, own_ref, above_ref, below_ref, lists_ref, rows_ref, cot_ref, w_ref, base_ref, send_ref, keep_ref, blocks
-):
+def short_kernel(own_ref, above_ref, below_ref, lists_ref, cot_ref, w_ref, base_ref):
     atoms = own_ref.shape[0]
     lists = lists_ref[0]
-    shape = (atoms, lists.shape[1])
-    row_at = lax.broadcasted_iota(jnp.int32, shape, 0)
-    to_lower = (row_at == lists[0:1, :]).astype(f32).astype(bf16)
-    to_upper = (row_at == lists[1:2, :]).astype(f32).astype(bf16)
-    owned = own_ref[...] + dot(to_upper, above_ref[...]) + dot(to_lower, below_ref[...])
+    owned = own_ref[...] + dot(one_hot(atoms, lists[1:2, :]), above_ref[...])
+    owned = owned + dot(one_hot(atoms, lists[0:1, :]), below_ref[...])
     high, low = halves(owned)
     w = w_ref[...]
     base_ref[...] = cot_ref[...].astype(f32) + (dot(high, w, 1, 1) + dot(low, w, 1, 1))
-    rows = rows_ref[...].T
-    split_blocks(order, slab_ref[0], dot(rows, high) + dot(rows, low), send_ref, keep_ref, blocks)
-
-
-def short_range(order, slab, own, above, below, lists, rows, cotan, w_short):
-    atoms, channels = rows.shape
-    half = len(order)
-    height = channels // (2 * half)
-    return pl.pallas_call(
-        functools.partial(short_kernel, order),
+
+
+def short_range(own, above, below, lists, cotan, w_short):
+    atoms, channels = cotan.shape
+    return pl.pallas_call(
+        short_kernel,
         name="short",
-        out_shape=(
-            jax.ShapeDtypeStruct((atoms, channels), f32),
-            jax.ShapeDtypeStruct((half, height, channels), f32),
-            jax.ShapeDtypeStruct((half, height, channels), f32),
-        ),
-        in_specs=[SMEM] + [VMEM] * 7,
-        out_specs=(VMEM,) * 3,
-        scratch_shapes=[pltpu.VMEM((2 * half, height, channels), f32)],
+        out_shape=jax.ShapeDtypeStruct((atoms, channels), f32),
+        in_specs=[VMEM] * 6,
+        out_specs=VMEM,
         compiler_params=params(),
         cost_estimate=pl.CostEstimate(
             flops=8 * atoms * channels * channels, bytes_accessed=8 * atoms * channels, transcendentals=0
         ),
-    )(slab, own, above, below, lists, rows, cotan, w_short)
-
-
-def share_kernel(order, norm, count, slab_ref, filter_ref, w_ref, *refs):
+    )(own, above, below, lists, cotan, w_short)
+
+
+def share_kernel(
+    order, norm, count, slab_ref, filter_ref, w_ref, grad_ref, lower_t, upper_t, low_ref, up_ref, *refs
+):
     parts, (adj_ref, gfilter_ref, send_ref, keep_ref, blocks) = refs[:count], refs[count:]
     channels = w_ref.shape[0]
     total = parts[0][...].astype(f32)
@@ -280,17 +305,18 @@
     double = jnp.concatenate([k_filter, k_filter], axis=0) * norm
     filtered, filtered_low = halves((structure * double).T)
     wout = dot(filtered, moved) + (dot(filtered, moved_low) + dot(filtered_low, moved))
-    split_blocks(order, slab_ref[0], wout, send_ref, keep_ref, blocks)
+    wshort = grad_ref[...] + (dot(lower_t[...], low_ref[...]) + dot(upper_t[...], up_ref[...]))
+    split_blocks(order, slab_ref[0], (wout, wshort), send_ref, keep_ref, blocks)
     adj_ref[...] = (response * double).T.astype(bf16)
     product = structure * response
     share = k_filter.shape[0]
     gfilter_ref[...] = norm * (product[:share] + product[share:])
 
 
-def own_share(order, norm, slab, k_filter, w_out, parts):
+def own_share(order, norm, slab, k_filter, w_out, short_terms, parts):
     height, channels = parts[0].shape[0], w_out.shape[0]
     half = len(order)
-    rows = channels // (2 * half)
+    rows = 2 * channels // (2 * half)
     return pl.pallas_call(
         functools.partial(share_kernel, order, norm, len(parts)),
         name="share",
@@ -300,14 +326,14 @@
             jax.ShapeDtypeStruct((half, rows, channels), f32),
             jax.ShapeDtypeStruct((half, rows, channels), f32),
         ),
-        in_specs=[SMEM] + [VMEM] * (2 + len(parts)),
+        in_specs=[SMEM] + [VMEM] * (2 + len(short_terms) + len(parts)),
         out_specs=(VMEM,) * 4,
         scratch_shapes=[pltpu.VMEM((2 * half, rows, channels), f32)],
         compiler_params=params(),
         cost_estimate=pl.CostEstimate(
             flops=8 * height * channels * channels, bytes_accessed=16 * height * channels, transcendentals=0
         ),
-    )(slab, k_filter, w_out, *parts)
+    )(slab, k_filter, w_out, *short_terms, *parts)
 
 
 def back_kernel(orders, order, base_ref, even_adj_ref, odd_adj_ref, *refs):
@@ -478,16 +504,18 @@
             blocks[offset] = paired[i * 2 * share : (i + 1) * 2 * share]
     parts = plane_sum(blocks)
 
-    own_rows, lower, upper = edge_rows(src, dst, dist, cotan, lists.shape[2])
-    from_above = shifted(lower, "slab", -1)
-    from_below = shifted(upper, "slab", 1)
-    adj, gfilter, wout_send, wout_keep = own_share(order, norm, slab, own_filter, w_out, parts)
-    wout_moved = xor_permute(wout_send, "slab", 1)
-    base, wshort_send, wshort_keep = short_range(
-        order, slab, own_rows, from_above, from_below, lists, rows, cotan, w_short
-    )
-    wshort_moved = xor_permute(wshort_send, "slab", 1)
-    grads = jnp.concatenate([wout_keep + wout_moved, wshort_keep + wshort_moved], axis=1)
+    rows_t, to_prev, to_next = rim_features(rows, lists)
+    lower_t = shifted(to_next, "slab", 1)
+    upper_t = shifted(to_prev, "slab", -1)
+    own_rows, low, up, wshort = edge_rows(src, dst, dist, cotan, rows_t, lists.shape[2])
+    short_terms = (wshort, lower_t, upper_t, low, up)
+    adj, gfilter, send, keep = own_share(order, norm, slab, own_filter, w_out, short_terms, parts)
+    grads = keep + xor_permute(send, "slab", 1)
+
+    from_above = shifted(low, "slab", -1)
+    from_below = shifted(up, "slab", 1)
+    base = short_range(own_rows, from_above, from_below, lists, cotan, w_short)
+
     terms = plane_sum({offset: grads[i] for i, offset in enumerate(order)})
     own_grad = sum((term.astype(f32) for term in terms[1:]), terms[0])
 

time: 58.7 us -> 60 us (1.022)
  Pallas kernels: 13.7 us -> 14.4 us
    ppermute x21 -> x20, waiting for transfers between devices: 8.17 us -> 16.2 us  [xor_permute(): lax.ppermute(value, axis, [(source, source ^ bits) for source in range(co...]
    ppermute x2 -> x4, waiting for transfers between devices: 7.42 us -> 0.01 us  [shifted(): lax.ppermute(value, axis, [(source, (source + steps) % count) for source...]
    ppermute x21 -> x20, starting transfers between devices: 25.2 us -> 22.7 us  [xor_permute(): lax.ppermute(value, axis, [(source, source ^ bits) for source in range(co...]
    ppermute x2 -> x4, starting transfers between devices: 1.71 us -> 4.16 us  [shifted(): lax.ppermute(value, axis, [(source, (source + steps) % count) for source...]
  transfers between devices with their start and end apart: 23 -> 24, of which waited for: 10 -> 9; matrix products, arithmetic and copies ran while one was open for 2% -> 2% of each run, Pallas kernels for 17% -> 17%
where the time goes in v4:
time: 60 us; the launch traced here: 59.8 us
  starting transfers between devices  26.9 us (45%)
  waiting for transfers between devices  16.2 us (27%)
  Pallas kernels  14.4 us (24%)
  other arithmetic  1.2 us (2%)
  between operations  0.86 us (1%)
    ppermute x20, starting transfers between devices, xor_permute(): lax.ppermute(value, axis, [(source, source ^ bits) for source in range(co...  22.7 us
    ppermute x20, waiting for transfers between devices, xor_permute(): lax.ppermute(value, axis, [(source, source ^ bits) for source in range(co...  16.2 us
    pallas_call x1, Pallas kernels, edge_rows(): pl.pallas_call(functools.partial(edge_kernel, block), name='edges', out_s...  5.51 us
    ppermute x4, starting transfers between devices, shifted(): lax.ppermute(value, axis, [(source, (source + steps) % count) for source...  4.16 us
    pallas_call x3, Pallas kernels, next_tables(): pl.pallas_call(functools.partial(second_kernel, order), out_shape=(jax.Sh...  2.81 us
    pallas_call x1, Pallas kernels, first_tables(): pl.pallas_call(functools.partial(first_kernel, order, len(others)), name=...  2.13 us
    pallas_call x1, Pallas kernels, back_project(): pl.pallas_call(functools.partial(back_kernel, orders, order), name='back'...  1.55 us
  transfers between devices with their start and end apart: 24, of which 9 were waited for; matrix products, arithmetic and copies ran while one was open for 2% of the time, Pallas kernels for 17%

profile of v4, /device:TPU:0, one launch (start us, length us, event | category | flops | bytes accessed | tf_op | source)
XLA Modules:
  0.0 59.8 jit_solution(14851790453742576330)
XLA Ops:
  0.6 2.1 %first.1 = (bf16[512,512]{1,0:T(8,128)(2,1)S(1)}, bf16[512,512]{1,0:T(8,128)(2,1)S(1)}, f32[1024,16]{1,0:T(8,128)S(1)}, bf16[16,512]{1,0:T(8,128)(2,1)S(1)}, bf1...) custom-call(s32[1]{0:T(128)} %bitcast.slab_ref, ...), custom_call_target="tpu_custom_call" | custom-call | flops 268435456 | bytes 1048576 | tf_op jit(solution)/shard_map/first/pallas_call | solution.py:136
  2.8 0.6 collective-permute-start.5
  3.3 0.3 rims.1
  3.7 0.1 collective-permute-start.2
  3.7 3.6 %collective-permute-start.3 = (bf16[256,256]{1,0:T(8,128)(2,1)S(1)}, bf16[256,256]{1,0:T(8,128)(2,1)S(1)}, u32[]{:S(2)}, u32[]{:S(2)}) collective-permute-start(bf16[256,256]{1,0:T(8,128)(2,1)S(1)} %get-tuple-element.51), channel_id=1, source_target_pairs={{0,28},{4,0},{8,4},{12,8},{16,12},{20,16},{24,20},{28,24},{1,29},{... | collective-permute-start | bytes 393224 | tf_op jit(solution)/shard_map/ppermute | solution.py:34
  7.3 0.9 %shard_map.139 = (bf16[512,512]{1,0:T(8,128)(2,1)S(1)}, bf16[512,512]{1,0:T(8,128)(2,1)S(1)}) custom-call(s32[1]{0:T(128)} %bitcast.slab_ref, f32[1024,16]{1,0:T(8,128)S(1)} %get-tuple-element.52.k_cols, bf16[16,512]{1,0:T(8,128)(2,1)S(1)} %get-tuple-element.53.positions, bf16[512,256]{1,0:T(8,128)(2,1)S(1)} %get-tuple-element.40.rows_ref, ...), custom_call_target="tpu_custom_call" | custom-call | flops 268435456 | bytes 1048576 | tf_op jit(solution)/shard_map/pallas_call | solution.py:163
  8.3 0.1 collective-permute-start.4
  8.3 0.9 %shard_map.140 = (bf16[512,512]{1,0:T(8,128)(2,1)S(1)}, f32[512,512]{1,0:T(8,128)S(1)}) custom-call(s32[1]{0:T(128)} %bitcast.slab_ref, f32[1024,16]{1,0:T(8,128)S(1)} %get-tuple-element.52.k_cols, bf16[16,512]{1,0:T(8,128)(2,1)S(1)} %get-tuple-element.53.positions, bf16[512,256]{1,0:T(8,128)(2,1)S(1)} %get-tuple-element.40.rows_ref, ...), custom_call_target="tpu_custom_call" | custom-call | flops 268435456 | bytes 1048576 | tf_op jit(solution)/shard_map/pallas_call | solution.py:163
  9.3 0.9 %shard_map.138 = (bf16[512,512]{1,0:T(8,128)(2,1)S(1)}, f32[512,512]{1,0:T(8,128)S(1)}) custom-call(s32[1]{0:T(128)} %bitcast.slab_ref, f32[1024,16]{1,0:T(8,128)S(1)} %get-tuple-element.52.k_cols, bf16[16,512]{1,0:T(8,128)(2,1)S(1)} %get-tuple-element.53.positions, bf16[512,256]{1,0:T(8,128)(2,1)S(1)} %get-tuple-element.40.rows_ref, ...), custom_call_target="tpu_custom_call" | custom-call | flops 268435456 | bytes 1048576 | tf_op jit(solution)/shard_map/pallas_call | solution.py:163
  10.2 0.0 collective-permute-done.5
  10.2 0.2 add_convert_fusion
  10.5 1.6 %collective-permute-start.7 = (bf16[256,512]{1,0:T(8,128)(2,1)S(1)}, bf16[256,512]{1,0:T(8,128)(2,1)S(1)}, u32[]{:S(2)}, u32[]{:S(2)}) collective-permute-start(bf16[256,512]{1,0:T(8,128)(2,1)S(1)} %get-tuple-element.70), channel_id=1, source_target_pairs={{0,16},{4,20},{8,24},{12,28},{16,0},{20,4},{24,8},{28,12},{1,17},{... | collective-permute-start | bytes 786440 | tf_op jit(solution)/shard_map/ppermute | solution.py:29
  12.1 0.5 collective-permute-start.6
  12.6 0.0 collective-permute-done.4
  12.6 0.2 convert_add_fusion
  12.8 1.5 %collective-permute-start.8 = (bf16[256,512]{1,0:T(8,128)(2,1)S(1)}, bf16[256,512]{1,0:T(8,128)(2,1)S(1)}, u32[]{:S(2)}, u32[]{:S(2)}) collective-permute-start(bf16[256,512]{1,0:T(8,128)(2,1)S(1)} %slice.59), channel_id=1, source_target_pairs={{0,8},{4,12},{8,0},{12,4},{16,24},{20,28},{24,16},{28,20},{1,9},{5... | collective-permute-start | bytes 786440 | tf_op jit(solution)/shard_map/ppermute | solution.py:29
  14.3 5.5 %edges.1 = (f32[512,256]{1,0:T(8,128)S(1)}, bf16[256,256]{1,0:T(8,128)(2,1)S(1)}, bf16[256,256]{1,0:T(8,128)(2,1)S(1)}, f32[256,256]{1,0:T(8,128)S(1)}) custom-call(s32[1,4096]{1,0:T(1,128)S(1)} %get-tuple-element.36.src_ref, s32[1,4096]{1,0:T(1,128)S(1)} %get-tuple-element.37.dst_ref, f32[1,4096]{1,0:T(1,128)S(1)} %get-tuple-element.38.dist_ref, ...), custom_call_target="tpu_custom_call" | custom-call | flops 3221225472 | bytes 49152 | tf_op jit(solution)/shard_map/edges/pallas_call | solution.py:238
  19.9 0.0 collective-permute-done.2.lower_t
  19.9 0.0 collective-permute-done.3.upper_t
  19.9 5.0 %collective-permute-done.7.refs_2_ = bf16[256,512]{1,0:T(8,128)(2,1)S(1)} collective-permute-done((bf16[256,512]{1,0:T(8,128)(2,1)S(1)}, bf16[256,512]{1,0:T(8,128)(2,1)S(1)}, u32[]{:S(2)}, u32[]{:S(2)}) %collective-permute-start.7) | collective-permute-done | bytes 262176 | tf_op jit(solution)/shard_map/ppermute | solution.py:29
  24.8 0.0 collective-permute-done.6.refs_1_
  24.9 1.2 %collective-permute-done.8.refs_3_ = bf16[256,512]{1,0:T(8,128)(2,1)S(1)} collective-permute-done((bf16[256,512]{1,0:T(8,128)(2,1)S(1)}, bf16[256,512]{1,0:T(8,128)(2,1)S(1)}, u32[]{:S(2)}, u32[]{:S(2)}) %collective-permute-start.8) | collective-permute-done | bytes 262176 | tf_op jit(solution)/shard_map/ppermute | solution.py:29
  26.1 0.6 share.1
  26.7 0.1 collective-permute-start.12
  26.7 1.5 %collective-permute-done.12 = f32[4,64,256]{2,1,0:T(8,128)S(1)} collective-permute-done((f32[4,64,256]{2,1,0:T(8,128)S(1)}, f32[4,64,256]{2,1,0:T(8,128)S(1)}, u32[]{:S(2)}, u32[]{:S(2)}) %collective-permute-start.12) | collective-permute-done | bytes 262176 | tf_op jit(solution)/shard_map/ppermute | solution.py:29
  28.3 1.6 %collective-permute-start.13 = (bf16[64,256]{1,0:T(8,128)(2,1)S(1)}, bf16[64,256]{1,0:T(8,128)(2,1)S(1)}, u32[]{:S(2)}, u32[]{:S(2)}) collective-permute-start(bf16[64,256]{1,0:T(8,128)(2,1)S(1)} %get-tuple-element.72), channel_id=1, source_target_pairs={{0,24},{4,28},{8,16},{12,20},{16,8},{20,12},{24,0},{28,4},{1,25},{... | collective-permute-start | bytes 98312 | tf_op jit(solution)/shard_map/ppermute | solution.py:29
  30.0 1.4 %collective-permute-start.15 = (bf16[64,256]{1,0:T(8,128)(2,1)S(1)}, bf16[64,256]{1,0:T(8,128)(2,1)S(1)}, u32[]{:S(2)}, u32[]{:S(2)}) collective-permute-start(bf16[64,256]{1,0:T(8,128)(2,1)S(1)} %get-tuple-element.73), channel_id=1, source_target_pairs={{0,8},{4,12},{8,0},{12,4},{16,24},{20,28},{24,16},{28,20},{1,9},{5... | collective-permute-start | bytes 98312 | tf_op jit(solution)/shard_map/ppermute | solution.py:29
  31.4 0.5 collective-permute-start.14
  31.9 0.5 collective-permute-start
  32.4 0.0 collective-permute-start.1
  32.4 0.8 %collective-permute-done.13 = bf16[64,256]{1,0:T(8,128)(2,1)S(1)} collective-permute-done((bf16[64,256]{1,0:T(8,128)(2,1)S(1)}, bf16[64,256]{1,0:T(8,128)(2,1)S(1)}, u32[]{:S(2)}, u32[]{:S(2)}) %collective-permute-start.13) | collective-permute-done | bytes 32800 | tf_op jit(solution)/shard_map/ppermute | solution.py:29
  33.2 1.5 %collective-permute-start.9 = (bf16[1,256,256]{2,1,0:T(8,128)(2,1)S(1)}, bf16[1,256,256]{2,1,0:T(8,128)(2,1)S(1)}, u32[]{:S(2)}, u32[]{:S(2)}) collective-permute-start(bf16[1,256,256]{2,1,0:T(8,128)(2,1)S(1)} %bitcast.24), channel_id=1, source_target_pairs={{0,16},{4,20},{8,24},{12,28},{16,0},{20,4},{24,8},{28,12},{1,17},{... | collective-permute-start | bytes 393224 | tf_op jit(solution)/shard_map/ppermute | solution.py:29
  34.8 0.0 collective-permute-done.15
  34.8 0.6 collective-permute-done.14
  35.3 1.7 %collective-permute-start.16 = (bf16[64,256]{1,0:T(8,128)(2,1)S(1)}, bf16[64,256]{1,0:T(8,128)(2,1)S(1)}, u32[]{:S(2)}, u32[]{:S(2)}) collective-permute-start(bf16[64,256]{1,0:T(8,128)(2,1)S(1)} %fusion.3), channel_id=1, source_target_pairs={{0,1},{1,0},{2,3},{3,2},{4,5},{5,4},{6,7},{7,6},{8,9},{9,8},{10,11... | collective-permute-start | bytes 98312 | tf_op jit(solution)/shard_map/ppermute | solution.py:29
  37.0 2.7 %collective-permute-done.9 = bf16[1,256,256]{2,1,0:T(8,128)(2,1)S(1)} collective-permute-done((bf16[1,256,256]{2,1,0:T(8,128)(2,1)S(1)}, bf16[1,256,256]{2,1,0:T(8,128)(2,1)S(1)}, u32[]{:S(2)}, u32[]{:S(2)}) %collective-permute-start.9) | collective-permute-done | bytes 131104 | tf_op jit(solution)/shard_map/ppermute | solution.py:29
  39.8 1.2 %collective-permute-start.10 = (bf16[2,256,256]{2,1,0:T(8,128)(2,1)S(1)}, bf16[2,256,256]{2,1,0:T(8,128)(2,1)S(1)}, u32[]{:S(2)}, u32[]{:S(2)}) collective-permute-start(bf16[2,256,256]{2,1,0:T(8,128)(2,1)S(1)} %pad_maximum_fusion.1), channel_id=1, source_target_pairs={{0,8},{4,12},{8,0},{12,4},{16,24},{20,28},{24,16},{28,20},{1,9},{5... | collective-permute-start | bytes 786440 | tf_op jit(solution)/shard_map/ppermute | solution.py:29
  41.0 0.0 collective-permute-done.16
  41.0 2.6 %collective-permute-start.17 = (bf16[64,256]{1,0:T(8,128)(2,1)S(1)}, bf16[64,256]{1,0:T(8,128)(2,1)S(1)}, u32[]{:S(2)}, u32[]{:S(2)}) collective-permute-start(bf16[64,256]{1,0:T(8,128)(2,1)S(1)} %add_convert_fusion.3), channel_id=1, source_target_pairs={{0,2},{1,3},{2,0},{3,1},{4,6},{5,7},{6,4},{7,5},{8,10},{9,11},{10,... | collective-permute-start | bytes 98312 | tf_op jit(solution)/shard_map/ppermute | solution.py:29
  43.7 0.0 collective-permute-done.above_ref
  43.7 0.0 collective-permute-done.1.below_ref
  43.7 0.7 %short.1.base_ref = f32[512,256]{1,0:T(8,128)S(1)} custom-call(f32[512,256]{1,0:T(8,128)S(1)} %get-tuple-element.43.own_ref, bf16[256,256]{1,0:T(8,128)(2,1)S(1)} %collective-permute-done.above_ref, bf16[256,256]{1,0:T(8,128)(2,1)S(1)} %collective-permute-done.1.below_ref, s32[1,2,256]{2,1,0:T(2,128)S(1)} %get-tuple-element.41.lists_ref, ...), custom_call_target="tpu_custom_call" | custom-call | flops 268435456 | bytes 1048576 | tf_op jit(solution)/shard_map/short/pallas_call | solution.py:280
  44.4 1.6 %collective-permute-start.22 = (bf16[128,256]{1,0:T(8,128)(2,1)S(1)}, bf16[128,256]{1,0:T(8,128)(2,1)S(1)}, u32[]{:S(2)}, u32[]{:S(2)}) collective-permute-start(bf16[128,256]{1,0:T(8,128)(2,1)S(1)} %convert_element_type.84), channel_id=1, source_target_pairs={{0,1},{1,0},{2,3},{3,2},{4,5},{5,4},{6,7},{7,6},{8,9},{9,8},{10,11... | collective-permute-start | bytes 196616 | tf_op jit(solution)/shard_map/ppermute | solution.py:29
  46.0 0.1 collective-permute-done.17
  46.1 1.9 %collective-permute-start.20 = (bf16[64,256]{1,0:T(8,128)(2,1)S(1)}, bf16[64,256]{1,0:T(8,128)(2,1)S(1)}, u32[]{:S(2)}, u32[]{:S(2)}) collective-permute-start(bf16[64,256]{1,0:T(8,128)(2,1)S(1)} %add_convert_fusion.2), channel_id=1, source_target_pairs={{0,24},{4,28},{8,16},{12,20},{16,8},{20,12},{24,0},{28,4},{1,25},{... | collective-permute-start | bytes 98312 | tf_op jit(solution)/shard_map/ppermute | solution.py:29
  48.0 0.9 %collective-permute-start.19 = (bf16[64,256]{1,0:T(8,128)(2,1)S(1)}, bf16[64,256]{1,0:T(8,128)(2,1)S(1)}, u32[]{:S(2)}, u32[]{:S(2)}) collective-permute-start(bf16[64,256]{1,0:T(8,128)(2,1)S(1)} %add_convert_fusion.2), channel_id=1, source_target_pairs={{0,8},{4,12},{8,0},{12,4},{16,24},{20,28},{24,16},{28,20},{1,9},{5... | collective-permute-start | bytes 98312 | tf_op jit(solution)/shard_map/ppermute | solution.py:29
  48.9 0.8 %collective-permute-start.18 = (bf16[64,256]{1,0:T(8,128)(2,1)S(1)}, bf16[64,256]{1,0:T(8,128)(2,1)S(1)}, u32[]{:S(2)}, u32[]{:S(2)}) collective-permute-start(bf16[64,256]{1,0:T(8,128)(2,1)S(1)} %add_convert_fusion.2), channel_id=1, source_target_pairs={{0,16},{4,20},{8,24},{12,28},{16,0},{20,4},{24,8},{28,12},{1,17},{... | collective-permute-start | bytes 98312 | tf_op jit(solution)/shard_map/ppermute | solution.py:29
  49.7 0.0 collective-permute-done.10
  49.7 0.1 pad_maximum_fusion.even_adj_ref
  49.7 0.1 collective-permute-start.11
  49.8 0.0 collective-permute-done.22
  49.8 2.5 %collective-permute-start.23 = (bf16[128,256]{1,0:T(8,128)(2,1)S(1)}, bf16[128,256]{1,0:T(8,128)(2,1)S(1)}, u32[]{:S(2)}, u32[]{:S(2)}) collective-permute-start(bf16[128,256]{1,0:T(8,128)(2,1)S(1)} %add_convert_fusion.1), channel_id=1, source_target_pairs={{0,2},{1,3},{2,0},{3,1},{4,6},{5,7},{6,4},{7,5},{8,10},{9,11},{10,... | collective-permute-start | bytes 196616 | tf_op jit(solution)/shard_map/ppermute | solution.py:29
  52.3 0.0 collective-permute-done.20
  52.3 0.0 collective-permute-done.19
  52.3 0.5 collective-permute-done.18
  52.8 0.1 collective-permute-start.21
  52.9 3.8 %collective-permute-done.23 = bf16[128,256]{1,0:T(8,128)(2,1)S(1)} collective-permute-done((bf16[128,256]{1,0:T(8,128)(2,1)S(1)}, bf16[128,256]{1,0:T(8,128)(2,1)S(1)}, u32[]{:S(2)}, u32[]{:S(2)}) %collective-permute-start.23) | collective-permute-done | bytes 65568 | tf_op jit(solution)/shard_map/ppermute | solution.py:29
  56.7 0.7 %add_multiply_fusion = f32[128,256]{1,0:T(8,128)} fusion(bf16[128,256]{1,0:T(8,128)(2,1)S(1)} %collective-permute-done.23, bf16[128,256]{1,0:T(8,128)(2,1)S(1)} %add_convert_fusion.1), kind=kLoop, calls=%fused_computation.6 | loop fusion | flops 131072 | bytes 262144 | tf_op jit(solution)/shard_map/div | solution.py:528
  57.4 0.0 collective-permute-done.21.odd_ref
  57.4 0.9 %place.1 = (f32[256,256]{1,0:T(8,128)}, f32[256,256]{1,0:T(8,128)}) custom-call(s32[1]{0:T(128)} %bitcast.slab_ref, bf16[4,64,256]{2,1,0:T(8,128)(2,1)S(1)} %pad_maximum_fusion.2.even_ref, bf16[4,64,256]{2,1,0:T(8,128)(2,1)S(1)} %collective-permute-done.21.odd_ref), custom_call_target="tpu_custom_call" | custom-call | tf_op jit(solution)/shard_map/place/pallas_call | solution.py:381
  58.2 0.0 collective-permute-done.11.odd_adj_ref
  58.2 1.5 %back.1 = bf16[512,256]{1,0:T(8,128)(2,1)} custom-call(f32[512,256]{1,0:T(8,128)S(1)} %short.1.base_ref, bf16[4,256,256]{2,1,0:T(8,128)(2,1)S(1)} %pad_maximum_fusion.even_adj_ref, bf16[4,256,256]{2,1,0:T(8,128)(2,1)S(1)} %collective-permute-done.11.odd_adj_ref, bf16[512,512]{1,0:T(8,128)(2,1)S(1)} %get-tuple-element.59.refs_0_, ...), custom_call_target="tpu_custom_call" | custom-call | flops 536870912 | bytes 2097152 | tf_op jit(solution)/shard_map/back/pallas_call | solution.py:354
  (12 shorter events, 0.3 us)
Async XLA Ops:
  2.8 7.5 %collective-permute-start.5 = (bf16[512,512]{1,0:T(8,128)(2,1)S(1)}, bf16[512,512]{1,0:T(8,128)(2,1)S(1)}, u32[]{:S(2)}, u32[]{:S(2)}) collective-permute-start(bf16[512,512]{1,0:T(8,128)(2,1)S(1)} %get-tuple-element.57), channel_id=1, source_target_pairs={{0,4},{4,0},{8,12},{12,8},{16,20},{20,16},{24,28},{28,24},{1,5},{5... | collective-permute-start | bytes 1572872 | tf_op jit(solution)/shard_map/ppermute | solution.py:29
  3.7 16.2 %collective-permute-start.2 = (bf16[256,256]{1,0:T(8,128)(2,1)S(1)}, bf16[256,256]{1,0:T(8,128)(2,1)S(1)}, u32[]{:S(2)}, u32[]{:S(2)}) collective-permute-start(bf16[256,256]{1,0:T(8,128)(2,1)S(1)} %get-tuple-element.50), channel_id=1, source_target_pairs={{0,4},{4,8},{8,12},{12,16},{16,20},{20,24},{24,28},{28,0},{1,5},{5... | collective-permute-start | bytes 393224 | tf_op jit(solution)/shard_map/ppermute | solution.py:34
  3.7 16.1 %collective-permute-start.3 = (bf16[256,256]{1,0:T(8,128)(2,1)S(1)}, bf16[256,256]{1,0:T(8,128)(2,1)S(1)}, u32[]{:S(2)}, u32[]{:S(2)}) collective-permute-start(bf16[256,256]{1,0:T(8,128)(2,1)S(1)} %get-tuple-element.51), channel_id=1, source_target_pairs={{0,28},{4,0},{8,4},{12,8},{16,12},{20,16},{24,20},{28,24},{1,29},{... | collective-permute-start | bytes 393224 | tf_op jit(solution)/shard_map/ppermute | solution.py:34
  8.3 4.4 %collective-permute-start.4 = (bf16[512,512]{1,0:T(8,128)(2,1)S(1)}, bf16[512,512]{1,0:T(8,128)(2,1)S(1)}, u32[]{:S(2)}, u32[]{:S(2)}) collective-permute-start(bf16[512,512]{1,0:T(8,128)(2,1)S(1)} %get-tuple-element.55), channel_id=1, source_target_pairs={{0,4},{4,0},{8,12},{12,8},{16,20},{20,16},{24,28},{28,24},{1,5},{5... | collective-permute-start | bytes 1572872 | tf_op jit(solution)/shard_map/ppermute | solution.py:29
  10.5 14.4 %collective-permute-start.7 = (bf16[256,512]{1,0:T(8,128)(2,1)S(1)}, bf16[256,512]{1,0:T(8,128)(2,1)S(1)}, u32[]{:S(2)}, u32[]{:S(2)}) collective-permute-start(bf16[256,512]{1,0:T(8,128)(2,1)S(1)} %get-tuple-element.70), channel_id=1, source_target_pairs={{0,16},{4,20},{8,24},{12,28},{16,0},{20,4},{24,8},{28,12},{1,17},{... | collective-permute-start | bytes 786440 | tf_op jit(solution)/shard_map/ppermute | solution.py:29
  12.1 12.8 %collective-permute-start.6 = (bf16[256,512]{1,0:T(8,128)(2,1)S(1)}, bf16[256,512]{1,0:T(8,128)(2,1)S(1)}, u32[]{:S(2)}, u32[]{:S(2)}) collective-permute-start(bf16[256,512]{1,0:T(8,128)(2,1)S(1)} %get-tuple-element.71), channel_id=1, source_target_pairs={{0,24},{4,28},{8,16},{12,20},{16,8},{20,12},{24,0},{28,4},{1,25},{... | collective-permute-start | bytes 786440 | tf_op jit(solution)/shard_map/ppermute | solution.py:29
  12.8 13.2 %collective-permute-start.8 = (bf16[256,512]{1,0:T(8,128)(2,1)S(1)}, bf16[256,512]{1,0:T(8,128)(2,1)S(1)}, u32[]{:S(2)}, u32[]{:S(2)}) collective-permute-start(bf16[256,512]{1,0:T(8,128)(2,1)S(1)} %slice.59), channel_id=1, source_target_pairs={{0,8},{4,12},{8,0},{12,4},{16,24},{20,28},{24,16},{28,20},{1,9},{5... | collective-permute-start | bytes 786440 | tf_op jit(solution)/shard_map/ppermute | solution.py:29
  26.7 1.6 %collective-permute-start.12 = (f32[4,64,256]{2,1,0:T(8,128)S(1)}, f32[4,64,256]{2,1,0:T(8,128)S(1)}, u32[]{:S(2)}, u32[]{:S(2)}) collective-permute-start(f32[4,64,256]{2,1,0:T(8,128)S(1)} %get-tuple-element.64), channel_id=1, source_target_pairs={{0,4},{4,0},{8,12},{12,8},{16,20},{20,16},{24,28},{28,24},{1,5},{5... | collective-permute-start | bytes 786440 | tf_op jit(solution)/shard_map/ppermute | solution.py:29
  28.3 4.9 %collective-permute-start.13 = (bf16[64,256]{1,0:T(8,128)(2,1)S(1)}, bf16[64,256]{1,0:T(8,128)(2,1)S(1)}, u32[]{:S(2)}, u32[]{:S(2)}) collective-permute-start(bf16[64,256]{1,0:T(8,128)(2,1)S(1)} %get-tuple-element.72), channel_id=1, source_target_pairs={{0,24},{4,28},{8,16},{12,20},{16,8},{20,12},{24,0},{28,4},{1,25},{... | collective-permute-start | bytes 98312 | tf_op jit(solution)/shard_map/ppermute | solution.py:29
  30.0 4.8 %collective-permute-start.15 = (bf16[64,256]{1,0:T(8,128)(2,1)S(1)}, bf16[64,256]{1,0:T(8,128)(2,1)S(1)}, u32[]{:S(2)}, u32[]{:S(2)}) collective-permute-start(bf16[64,256]{1,0:T(8,128)(2,1)S(1)} %get-tuple-element.73), channel_id=1, source_target_pairs={{0,8},{4,12},{8,0},{12,4},{16,24},{20,28},{24,16},{28,20},{1,9},{5... | collective-permute-start | bytes 98312 | tf_op jit(solution)/shard_map/ppermute | solution.py:29
  31.4 3.9 %collective-permute-start.14 = (bf16[64,256]{1,0:T(8,128)(2,1)S(1)}, bf16[64,256]{1,0:T(8,128)(2,1)S(1)}, u32[]{:S(2)}, u32[]{:S(2)}) collective-permute-start(bf16[64,256]{1,0:T(8,128)(2,1)S(1)} %get-tuple-element.74), channel_id=1, source_target_pairs={{0,16},{4,20},{8,24},{12,28},{16,0},{20,4},{24,8},{28,12},{1,17},{... | collective-permute-start | bytes 98312 | tf_op jit(solution)/shard_map/ppermute | solution.py:29
  31.9 11.8 %collective-permute-start = (bf16[256,256]{1,0:T(8,128)(2,1)S(1)}, bf16[256,256]{1,0:T(8,128)(2,1)S(1)}, u32[]{:S(2)}, u32[]{:S(2)}) collective-permute-start(bf16[256,256]{1,0:T(8,128)(2,1)S(1)} %get-tuple-element.44.low_ref), channel_id=1, source_target_pairs={{0,28},{4,0},{8,4},{12,8},{16,12},{20,16},{24,20},{28,24},{1,29},{... | collective-permute-start | bytes 393224 | tf_op jit(solution)/shard_map/ppermute | solution.py:34
  32.4 11.3 %collective-permute-start.1 = (bf16[256,256]{1,0:T(8,128)(2,1)S(1)}, bf16[256,256]{1,0:T(8,128)(2,1)S(1)}, u32[]{:S(2)}, u32[]{:S(2)}) collective-permute-start(bf16[256,256]{1,0:T(8,128)(2,1)S(1)} %get-tuple-element.45.up_ref), channel_id=1, source_target_pairs={{0,4},{4,8},{8,12},{12,16},{16,20},{20,24},{24,28},{28,0},{1,5},{5... | collective-permute-start | bytes 393224 | tf_op jit(solution)/shard_map/ppermute | solution.py:34
  33.2 6.5 %collective-permute-start.9 = (bf16[1,256,256]{2,1,0:T(8,128)(2,1)S(1)}, bf16[1,256,256]{2,1,0:T(8,128)(2,1)S(1)}, u32[]{:S(2)}, u32[]{:S(2)}) collective-permute-start(bf16[1,256,256]{2,1,0:T(8,128)(2,1)S(1)} %bitcast.24), channel_id=1, source_target_pairs={{0,16},{4,20},{8,24},{12,28},{16,0},{20,4},{24,8},{28,12},{1,17},{... | collective-permute-start | bytes 393224 | tf_op jit(solution)/shard_map/ppermute | solution.py:29
  35.3 5.7 %collective-permute-start.16 = (bf16[64,256]{1,0:T(8,128)(2,1)S(1)}, bf16[64,256]{1,0:T(8,128)(2,1)S(1)}, u32[]{:S(2)}, u32[]{:S(2)}) collective-permute-start(bf16[64,256]{1,0:T(8,128)(2,1)S(1)} %fusion.3), channel_id=1, source_target_pairs={{0,1},{1,0},{2,3},{3,2},{4,5},{5,4},{6,7},{7,6},{8,9},{9,8},{10,11... | collective-permute-start | bytes 98312 | tf_op jit(solution)/shard_map/ppermute | solution.py:29
  39.8 9.9 %collective-permute-start.10 = (bf16[2,256,256]{2,1,0:T(8,128)(2,1)S(1)}, bf16[2,256,256]{2,1,0:T(8,128)(2,1)S(1)}, u32[]{:S(2)}, u32[]{:S(2)}) collective-permute-start(bf16[2,256,256]{2,1,0:T(8,128)(2,1)S(1)} %pad_maximum_fusion.1), channel_id=1, source_target_pairs={{0,8},{4,12},{8,0},{12,4},{16,24},{20,28},{24,16},{28,20},{1,9},{5... | collective-permute-start | bytes 786440 | tf_op jit(solution)/shard_map/ppermute | solution.py:29
  41.0 5.1 %collective-permute-start.17 = (bf16[64,256]{1,0:T(8,128)(2,1)S(1)}, bf16[64,256]{1,0:T(8,128)(2,1)S(1)}, u32[]{:S(2)}, u32[]{:S(2)}) collective-permute-start(bf16[64,256]{1,0:T(8,128)(2,1)S(1)} %add_convert_fusion.3), channel_id=1, source_target_pairs={{0,2},{1,3},{2,0},{3,1},{4,6},{5,7},{6,4},{7,5},{8,10},{9,11},{10,... | collective-permute-start | bytes 98312 | tf_op jit(solution)/shard_map/ppermute | solution.py:29
  44.4 5.4 %collective-permute-start.22 = (bf16[128,256]{1,0:T(8,128)(2,1)S(1)}, bf16[128,256]{1,0:T(8,128)(2,1)S(1)}, u32[]{:S(2)}, u32[]{:S(2)}) collective-permute-start(bf16[128,256]{1,0:T(8,128)(2,1)S(1)} %convert_element_type.84), channel_id=1, source_target_pairs={{0,1},{1,0},{2,3},{3,2},{4,5},{5,4},{6,7},{7,6},{8,9},{9,8},{10,11... | collective-permute-start | bytes 196616 | tf_op jit(solution)/shard_map/ppermute | solution.py:29
  46.1 6.2 %collective-permute-start.20 = (bf16[64,256]{1,0:T(8,128)(2,1)S(1)}, bf16[64,256]{1,0:T(8,128)(2,1)S(1)}, u32[]{:S(2)}, u32[]{:S(2)}) collective-permute-start(bf16[64,256]{1,0:T(8,128)(2,1)S(1)} %add_convert_fusion.2), channel_id=1, source_target_pairs={{0,24},{4,28},{8,16},{12,20},{16,8},{20,12},{24,0},{28,4},{1,25},{... | collective-permute-start | bytes 98312 | tf_op jit(solution)/shard_map/ppermute | solution.py:29
  48.0 4.3 %collective-permute-start.19 = (bf16[64,256]{1,0:T(8,128)(2,1)S(1)}, bf16[64,256]{1,0:T(8,128)(2,1)S(1)}, u32[]{:S(2)}, u32[]{:S(2)}) collective-permute-start(bf16[64,256]{1,0:T(8,128)(2,1)S(1)} %add_convert_fusion.2), channel_id=1, source_target_pairs={{0,8},{4,12},{8,0},{12,4},{16,24},{20,28},{24,16},{28,20},{1,9},{5... | collective-permute-start | bytes 98312 | tf_op jit(solution)/shard_map/ppermute | solution.py:29
  48.9 3.9 %collective-permute-start.18 = (bf16[64,256]{1,0:T(8,128)(2,1)S(1)}, bf16[64,256]{1,0:T(8,128)(2,1)S(1)}, u32[]{:S(2)}, u32[]{:S(2)}) collective-permute-start(bf16[64,256]{1,0:T(8,128)(2,1)S(1)} %add_convert_fusion.2), channel_id=1, source_target_pairs={{0,16},{4,20},{8,24},{12,28},{16,0},{20,4},{24,8},{28,12},{1,17},{... | collective-permute-start | bytes 98312 | tf_op jit(solution)/shard_map/ppermute | solution.py:29
  49.7 8.5 %collective-permute-start.11 = (bf16[4,256,256]{2,1,0:T(8,128)(2,1)S(1)}, bf16[4,256,256]{2,1,0:T(8,128)(2,1)S(1)}, u32[]{:S(2)}, u32[]{:S(2)}) collective-permute-start(bf16[4,256,256]{2,1,0:T(8,128)(2,1)S(1)} %pad_maximum_fusion.even_adj_ref), channel_id=1, source_target_pairs={{0,4},{4,0},{8,12},{12,8},{16,20},{20,16},{24,28},{28,24},{1,5},{5... | collective-permute-start | bytes 1572872 | tf_op jit(solution)/shard_map/ppermute | solution.py:29
  49.8 6.9 %collective-permute-start.23 = (bf16[128,256]{1,0:T(8,128)(2,1)S(1)}, bf16[128,256]{1,0:T(8,128)(2,1)S(1)}, u32[]{:S(2)}, u32[]{:S(2)}) collective-permute-start(bf16[128,256]{1,0:T(8,128)(2,1)S(1)} %add_convert_fusion.1), channel_id=1, source_target_pairs={{0,2},{1,3},{2,0},{3,1},{4,6},{5,7},{6,4},{7,5},{8,10},{9,11},{10,... | collective-permute-start | bytes 196616 | tf_op jit(solution)/shard_map/ppermute | solution.py:29
  52.8 4.6 %collective-permute-start.21 = (bf16[4,64,256]{2,1,0:T(8,128)(2,1)S(1)}, bf16[4,64,256]{2,1,0:T(8,128)(2,1)S(1)}, u32[]{:S(2)}, u32[]{:S(2)}) collective-permute-start(bf16[4,64,256]{2,1,0:T(8,128)(2,1)S(1)} %pad_maximum_fusion.2.even_ref), channel_id=1, source_target_pairs={{0,4},{4,0},{8,12},{12,8},{16,20},{20,16},{24,28},{28,24},{1,5},{5... | collective-permute-start | bytes 393224 | tf_op jit(solution)/shard_map/ppermute | solution.py:29

commit v5 on v3

--- a/solution.py
+++ b/solution.py
@@ -383,6 +383,17 @@
     return value
 
 
+def sum_replicas_direct(value):
+    count = lax.axis_size("rep")
+    terms = [value.astype(bf16)]
+    for offset in range(count - 1, 0, -1):
+        terms.insert(1, xor_permute(terms[0], "rep", offset))
+    terms = [term.astype(f32) for term in terms]
+    while len(terms) > 1:
+        terms = [terms[i] + terms[i + 1] for i in range(0, len(terms), 2)]
+    return terms[0]
+
+
 def plane_gather(block, order):
     count = lax.axis_size("slab")
     planes, bit = [], 2
@@ -495,7 +506,7 @@
     adj_odd = xor_permute(adj_even, "slab", 1)
     grad_features = back_project(orders, order, base, adj_even, adj_odd, (odda, evena, oddb, evenb))
 
-    own_grad = sum_replicas(own_grad).astype(bf16)
+    own_grad = sum_replicas_direct(own_grad).astype(bf16)
     filter_sum = sum_replicas(gfilter)
     grad_filter = filter_sum / replicas
     grad_even = plane_gather(own_grad, order)

time: 58.7 us -> 58.7 us (level)
    ppermute x21 -> x22, waiting for transfers between devices: 8.17 us -> 8.33 us  [xor_permute(): lax.ppermute(value, axis, [(source, source ^ bits) for source in range(co...]
    ppermute x21 -> x22, starting transfers between devices: 25.2 us -> 25.1 us  [xor_permute(): lax.ppermute(value, axis, [(source, source ^ bits) for source in range(co...]
  transfers between devices with their start and end apart: 23 -> 24, of which waited for: 10 -> 7; matrix products, arithmetic and copies ran while one was open for 2% -> 2% of each run, Pallas kernels for 17% -> 17%
where the time goes in v5:
time: 58.7 us; the launch traced here: 58.4 us
  starting transfers between devices  26.8 us (46%)
  waiting for transfers between devices  15.7 us (27%)
  Pallas kernels  13.7 us (23%)
  other arithmetic  1.21 us (2%)
  between operations  0.85 us (1%)
    ppermute x22, starting transfers between devices, xor_permute(): lax.ppermute(value, axis, [(source, source ^ bits) for source in range(co...  25.1 us
    ppermute x22, waiting for transfers between devices, xor_permute(): lax.ppermute(value, axis, [(source, source ^ bits) for source in range(co...  8.33 us
    ppermute x2, waiting for transfers between devices, shifted(): lax.ppermute(value, axis, [(source, (source + steps) % count) for source...  7.42 us
    pallas_call x1, Pallas kernels, edge_rows(): pl.pallas_call(functools.partial(edge_kernel, block), name='edges', out_s...  5.19 us
    pallas_call x3, Pallas kernels, next_tables(): pl.pallas_call(functools.partial(second_kernel, order), out_shape=(jax.Sh...  2.81 us
    pallas_call x1, Pallas kernels, first_tables(): pl.pallas_call(functools.partial(first_kernel, order, len(others)), name=...  2.13 us
    ppermute x2, starting transfers between devices, shifted(): lax.ppermute(value, axis, [(source, (source + steps) % count) for source...  1.71 us
    pallas_call x1, Pallas kernels, back_project(): pl.pallas_call(functools.partial(back_kernel, orders, order), name='back'...  1.55 us
  transfers between devices with their start and end apart: 24, of which 7 were waited for; matrix products, arithmetic and copies ran while one was open for 2% of the time, Pallas kernels for 17%

profile of v5, /device:TPU:0, one launch (start us, length us, event | category | flops | bytes accessed | tf_op | source)
XLA Modules:
  0.0 58.4 jit_solution(2440095709929431214)
XLA Ops:
  0.6 2.1 %first.1 = (bf16[512,512]{1,0:T(8,128)(2,1)S(1)}, bf16[512,512]{1,0:T(8,128)(2,1)S(1)}, f32[1024,16]{1,0:T(8,128)S(1)}, bf16[16,512]{1,0:T(8,128)(2,1)S(1)}, bf1...) custom-call(s32[1]{0:T(128)} %bitcast.slab_ref, ...), custom_call_target="tpu_custom_call" | custom-call | flops 268435456 | bytes 1048576 | tf_op jit(solution)/shard_map/first/pallas_call | solution.py:136
  2.8 0.6 collective-permute-start.3
  3.3 0.9 %shard_map.139 = (bf16[512,512]{1,0:T(8,128)(2,1)S(1)}, bf16[512,512]{1,0:T(8,128)(2,1)S(1)}) custom-call(s32[1]{0:T(128)} %bitcast.slab_ref, f32[1024,16]{1,0:T(8,128)S(1)} %get-tuple-element.48.k_cols, bf16[16,512]{1,0:T(8,128)(2,1)S(1)} %get-tuple-element.49.positions, bf16[512,256]{1,0:T(8,128)(2,1)S(1)} %get-tuple-element.43.rows_ref, ...), custom_call_target="tpu_custom_call" | custom-call | flops 268435456 | bytes 1048576 | tf_op jit(solution)/shard_map/pallas_call | solution.py:163
  4.3 0.1 collective-permute-start.2
  4.4 0.9 %shard_map.140 = (bf16[512,512]{1,0:T(8,128)(2,1)S(1)}, f32[512,512]{1,0:T(8,128)S(1)}) custom-call(s32[1]{0:T(128)} %bitcast.slab_ref, f32[1024,16]{1,0:T(8,128)S(1)} %get-tuple-element.48.k_cols, bf16[16,512]{1,0:T(8,128)(2,1)S(1)} %get-tuple-element.49.positions, bf16[512,256]{1,0:T(8,128)(2,1)S(1)} %get-tuple-element.43.rows_ref, ...), custom_call_target="tpu_custom_call" | custom-call | flops 268435456 | bytes 1048576 | tf_op jit(solution)/shard_map/pallas_call | solution.py:163
  5.3 0.9 %shard_map.138 = (bf16[512,512]{1,0:T(8,128)(2,1)S(1)}, f32[512,512]{1,0:T(8,128)S(1)}) custom-call(s32[1]{0:T(128)} %bitcast.slab_ref, f32[1024,16]{1,0:T(8,128)S(1)} %get-tuple-element.48.k_cols, bf16[16,512]{1,0:T(8,128)(2,1)S(1)} %get-tuple-element.49.positions, bf16[512,256]{1,0:T(8,128)(2,1)S(1)} %get-tuple-element.43.rows_ref, ...), custom_call_target="tpu_custom_call" | custom-call | flops 268435456 | bytes 1048576 | tf_op jit(solution)/shard_map/pallas_call | solution.py:163
  6.3 0.0 collective-permute-done.3
  6.3 0.2 add_convert_fusion
  6.5 3.0 %collective-permute-start.5 = (bf16[256,512]{1,0:T(8,128)(2,1)S(1)}, bf16[256,512]{1,0:T(8,128)(2,1)S(1)}, u32[]{:S(2)}, u32[]{:S(2)}) collective-permute-start(bf16[256,512]{1,0:T(8,128)(2,1)S(1)} %get-tuple-element.66), channel_id=1, source_target_pairs={{0,16},{4,20},{8,24},{12,28},{16,0},{20,4},{24,8},{28,12},{1,17},{... | collective-permute-start | bytes 786440 | tf_op jit(solution)/shard_map/ppermute | solution.py:29
  9.5 1.4 %collective-permute-start.4 = (bf16[256,512]{1,0:T(8,128)(2,1)S(1)}, bf16[256,512]{1,0:T(8,128)(2,1)S(1)}, u32[]{:S(2)}, u32[]{:S(2)}) collective-permute-start(bf16[256,512]{1,0:T(8,128)(2,1)S(1)} %get-tuple-element.67), channel_id=1, source_target_pairs={{0,24},{4,28},{8,16},{12,20},{16,8},{20,12},{24,0},{28,4},{1,25},{... | collective-permute-start | bytes 786440 | tf_op jit(solution)/shard_map/ppermute | solution.py:29
  11.0 0.0 collective-permute-done.2
  11.0 0.2 convert_add_fusion
  11.2 0.2 collective-permute-start.6
  11.3 5.2 %edges.1 = (f32[512,256]{1,0:T(8,128)S(1)}, bf16[256,256]{1,0:T(8,128)(2,1)S(1)}, bf16[256,256]{1,0:T(8,128)(2,1)S(1)}) custom-call(s32[1,4096]{1,0:T(1,128)S(1)} %get-tuple-element.35.src_ref, s32[1,4096]{1,0:T(1,128)S(1)} %get-tuple-element.36.dst_ref, f32[1,4096]{1,0:T(1,128)S(1)} %get-tuple-element.37.dist_ref, ...), custom_call_target="tpu_custom_call" | custom-call | flops 3221225472 | bytes 49152 | tf_op jit(solution)/shard_map/edges/pallas_call | solution.py:204
  16.5 1.7 %collective-permute-start = (bf16[256,256]{1,0:T(8,128)(2,1)S(1)}, bf16[256,256]{1,0:T(8,128)(2,1)S(1)}, u32[]{:S(2)}, u32[]{:S(2)}) collective-permute-start(bf16[256,256]{1,0:T(8,128)(2,1)S(1)} %get-tuple-element.40), channel_id=1, source_target_pairs={{0,28},{4,0},{8,4},{12,8},{16,12},{20,16},{24,20},{28,24},{1,29},{... | collective-permute-start | bytes 393224 | tf_op jit(solution)/shard_map/ppermute | solution.py:34
  18.2 0.0 collective-permute-start.1
  18.2 6.7 %collective-permute-done.above_ref = bf16[256,256]{1,0:T(8,128)(2,1)S(1)} collective-permute-done((bf16[256,256]{1,0:T(8,128)(2,1)S(1)}, bf16[256,256]{1,0:T(8,128)(2,1)S(1)}, u32[]{:S(2)}, u32[]{:S(2)}) %collective-permute-start) | collective-permute-done | bytes 131104 | tf_op jit(solution)/shard_map/ppermute | solution.py:34
  24.9 0.8 %collective-permute-done.1.below_ref = bf16[256,256]{1,0:T(8,128)(2,1)S(1)} collective-permute-done((bf16[256,256]{1,0:T(8,128)(2,1)S(1)}, bf16[256,256]{1,0:T(8,128)(2,1)S(1)}, u32[]{:S(2)}, u32[]{:S(2)}) %collective-permute-start.1) | collective-permute-done | bytes 131104 | tf_op jit(solution)/shard_map/ppermute | solution.py:34
  25.7 0.7 %short.1 = (f32[512,256]{1,0:T(8,128)S(1)}, f32[4,32,256]{2,1,0:T(8,128)S(1)}, f32[4,32,256]{2,1,0:T(8,128)S(1)}) custom-call(s32[1]{0:T(128)} %bitcast.slab_ref, f32[512,256]{1,0:T(8,128)S(1)} %get-tuple-element.39.own_ref, bf16[256,256]{1,0:T(8,128)(2,1)S(1)} %collective-permute-done.above_ref, bf16[256,256]{1,0:T(8,128)(2,1)S(1)} %collective-permute-done.1.below_ref, ...), custom_call_target="tpu_custom_call" | custom-call | flops 268435456 | bytes 1048576 | tf_op jit(solution)/shard_map/short/pallas_call | solution.py:252
  26.3 0.2 collective-permute-start.11
  26.6 0.0 collective-permute-done.5.refs_2_
  26.6 0.0 collective-permute-done.4.refs_1_
  26.6 0.0 collective-permute-done.6.refs_3_
  26.6 0.5 share.1
  27.1 0.5 collective-permute-start.10
  27.6 0.2 collective-permute-done.11
  27.8 1.3 %collective-permute-start.7 = (bf16[1,256,256]{2,1,0:T(8,128)(2,1)S(1)}, bf16[1,256,256]{2,1,0:T(8,128)(2,1)S(1)}, u32[]{:S(2)}, u32[]{:S(2)}) collective-permute-start(bf16[1,256,256]{2,1,0:T(8,128)(2,1)S(1)} %bitcast.24), channel_id=1, source_target_pairs={{0,16},{4,20},{8,24},{12,28},{16,0},{20,4},{24,8},{28,12},{1,17},{... | collective-permute-start | bytes 393224 | tf_op jit(solution)/shard_map/ppermute | solution.py:29
  29.0 0.0 collective-permute-done.10
  29.1 2.5 %collective-permute-start.12 = (bf16[64,256]{1,0:T(8,128)(2,1)S(1)}, bf16[64,256]{1,0:T(8,128)(2,1)S(1)}, u32[]{:S(2)}, u32[]{:S(2)}) collective-permute-start(bf16[64,256]{1,0:T(8,128)(2,1)S(1)} %get-tuple-element.68), channel_id=1, source_target_pairs={{0,24},{4,28},{8,16},{12,20},{16,8},{20,12},{24,0},{28,4},{1,25},{... | collective-permute-start | bytes 98312 | tf_op jit(solution)/shard_map/ppermute | solution.py:29
  31.6 0.0 collective-permute-start.14
  31.6 1.1 %collective-permute-start.13 = (bf16[64,256]{1,0:T(8,128)(2,1)S(1)}, bf16[64,256]{1,0:T(8,128)(2,1)S(1)}, u32[]{:S(2)}, u32[]{:S(2)}) collective-permute-start(bf16[64,256]{1,0:T(8,128)(2,1)S(1)} %get-tuple-element.70), channel_id=1, source_target_pairs={{0,16},{4,20},{8,24},{12,28},{16,0},{20,4},{24,8},{28,12},{1,17},{... | collective-permute-start | bytes 98312 | tf_op jit(solution)/shard_map/ppermute | solution.py:29
  32.7 1.5 %collective-permute-done.7 = bf16[1,256,256]{2,1,0:T(8,128)(2,1)S(1)} collective-permute-done((bf16[1,256,256]{2,1,0:T(8,128)(2,1)S(1)}, bf16[1,256,256]{2,1,0:T(8,128)(2,1)S(1)}, u32[]{:S(2)}, u32[]{:S(2)}) %collective-permute-start.7) | collective-permute-done | bytes 131104 | tf_op jit(solution)/shard_map/ppermute | solution.py:29
  34.2 2.7 %collective-permute-start.8 = (bf16[2,256,256]{2,1,0:T(8,128)(2,1)S(1)}, bf16[2,256,256]{2,1,0:T(8,128)(2,1)S(1)}, u32[]{:S(2)}, u32[]{:S(2)}) collective-permute-start(bf16[2,256,256]{2,1,0:T(8,128)(2,1)S(1)} %pad_maximum_fusion.2), channel_id=1, source_target_pairs={{0,8},{4,12},{8,0},{12,4},{16,24},{20,28},{24,16},{28,20},{1,9},{5... | collective-permute-start | bytes 786440 | tf_op jit(solution)/shard_map/ppermute | solution.py:29
  36.9 0.0 collective-permute-done.12
  36.9 0.0 collective-permute-done.14
  36.9 0.0 collective-permute-done.13
  36.9 3.7 %collective-permute-start.17 = (bf16[64,256]{1,0:T(8,128)(2,1)S(1)}, bf16[64,256]{1,0:T(8,128)(2,1)S(1)}, u32[]{:S(2)}, u32[]{:S(2)}) collective-permute-start(bf16[64,256]{1,0:T(8,128)(2,1)S(1)} %fusion.6), channel_id=1, source_target_pairs={{0,3},{1,2},{2,1},{3,0},{4,7},{5,6},{6,5},{7,4},{8,11},{9,10},{10,... | collective-permute-start | bytes 98312 | tf_op jit(solution)/shard_map/ppermute | solution.py:29
  40.6 0.0 collective-permute-start.16
  40.6 0.8 %collective-permute-start.15 = (bf16[64,256]{1,0:T(8,128)(2,1)S(1)}, bf16[64,256]{1,0:T(8,128)(2,1)S(1)}, u32[]{:S(2)}, u32[]{:S(2)}) collective-permute-start(bf16[64,256]{1,0:T(8,128)(2,1)S(1)} %fusion.6), channel_id=1, source_target_pairs={{0,1},{1,0},{2,3},{3,2},{4,5},{5,4},{6,7},{7,6},{8,9},{9,8},{10,11... | collective-permute-start | bytes 98312 | tf_op jit(solution)/shard_map/ppermute | solution.py:29
  41.4 1.3 %collective-permute-start.22 = (bf16[128,256]{1,0:T(8,128)(2,1)S(1)}, bf16[128,256]{1,0:T(8,128)(2,1)S(1)}, u32[]{:S(2)}, u32[]{:S(2)}) collective-permute-start(bf16[128,256]{1,0:T(8,128)(2,1)S(1)} %convert_element_type.80), channel_id=1, source_target_pairs={{0,1},{1,0},{2,3},{3,2},{4,5},{5,4},{6,7},{7,6},{8,9},{9,8},{10,11... | collective-permute-start | bytes 196616 | tf_op jit(solution)/shard_map/ppermute | solution.py:29
  42.7 0.2 collective-permute-done.17
  42.9 2.6 %collective-permute-done.16 = bf16[64,256]{1,0:T(8,128)(2,1)S(1)} collective-permute-done((bf16[64,256]{1,0:T(8,128)(2,1)S(1)}, bf16[64,256]{1,0:T(8,128)(2,1)S(1)}, u32[]{:S(2)}, u32[]{:S(2)}) %collective-permute-start.16) | collective-permute-done | bytes 32800 | tf_op jit(solution)/shard_map/ppermute | solution.py:29
  45.5 0.0 collective-permute-done.15
  45.5 1.0 %collective-permute-start.20 = (bf16[64,256]{1,0:T(8,128)(2,1)S(1)}, bf16[64,256]{1,0:T(8,128)(2,1)S(1)}, u32[]{:S(2)}, u32[]{:S(2)}) collective-permute-start(bf16[64,256]{1,0:T(8,128)(2,1)S(1)} %add_convert_fusion.2), channel_id=1, source_target_pairs={{0,24},{4,28},{8,16},{12,20},{16,8},{20,12},{24,0},{28,4},{1,25},{... | collective-permute-start | bytes 98312 | tf_op jit(solution)/shard_map/ppermute | solution.py:29
  46.6 0.2 collective-permute-start.19
  46.8 2.3 %collective-permute-start.18 = (bf16[64,256]{1,0:T(8,128)(2,1)S(1)}, bf16[64,256]{1,0:T(8,128)(2,1)S(1)}, u32[]{:S(2)}, u32[]{:S(2)}) collective-permute-start(bf16[64,256]{1,0:T(8,128)(2,1)S(1)} %add_convert_fusion.2), channel_id=1, source_target_pairs={{0,16},{4,20},{8,24},{12,28},{16,0},{20,4},{24,8},{28,12},{1,17},{... | collective-permute-start | bytes 98312 | tf_op jit(solution)/shard_map/ppermute | solution.py:29
  49.1 0.0 collective-permute-done.8
  49.1 0.1 pad_maximum_fusion.even_adj_ref
  49.2 0.1 collective-permute-start.9
  49.2 0.0 collective-permute-done.22
  49.3 2.0 %collective-permute-start.23 = (bf16[128,256]{1,0:T(8,128)(2,1)S(1)}, bf16[128,256]{1,0:T(8,128)(2,1)S(1)}, u32[]{:S(2)}, u32[]{:S(2)}) collective-permute-start(bf16[128,256]{1,0:T(8,128)(2,1)S(1)} %add_convert_fusion.1), channel_id=1, source_target_pairs={{0,2},{1,3},{2,0},{3,1},{4,6},{5,7},{6,4},{7,5},{8,10},{9,11},{10,... | collective-permute-start | bytes 196616 | tf_op jit(solution)/shard_map/ppermute | solution.py:29
  51.3 0.0 collective-permute-done.20
  51.3 0.0 collective-permute-done.19
  51.3 0.0 collective-permute-done.18
  51.3 0.3 collective-permute-start.21
  51.6 3.8 %collective-permute-done.23 = bf16[128,256]{1,0:T(8,128)(2,1)S(1)} collective-permute-done((bf16[128,256]{1,0:T(8,128)(2,1)S(1)}, bf16[128,256]{1,0:T(8,128)(2,1)S(1)}, u32[]{:S(2)}, u32[]{:S(2)}) %collective-permute-start.23) | collective-permute-done | bytes 65568 | tf_op jit(solution)/shard_map/ppermute | solution.py:29
  55.3 0.7 %add_multiply_fusion = f32[128,256]{1,0:T(8,128)} fusion(bf16[128,256]{1,0:T(8,128)(2,1)S(1)} %collective-permute-done.23, bf16[128,256]{1,0:T(8,128)(2,1)S(1)} %add_convert_fusion.1), kind=kLoop, calls=%fused_computation.10 | loop fusion | flops 131072 | bytes 262144 | tf_op jit(solution)/shard_map/div | solution.py:511
  56.0 0.0 collective-permute-done.21.odd_ref
  56.0 0.9 %place.1 = (f32[256,256]{1,0:T(8,128)}, f32[256,256]{1,0:T(8,128)}) custom-call(s32[1]{0:T(128)} %bitcast.slab_ref, bf16[4,64,256]{2,1,0:T(8,128)(2,1)S(1)} %pad_maximum_fusion.3.even_ref, bf16[4,64,256]{2,1,0:T(8,128)(2,1)S(1)} %collective-permute-done.21.odd_ref), custom_call_target="tpu_custom_call" | custom-call | tf_op jit(solution)/shard_map/place/pallas_call | solution.py:355
  56.9 0.0 collective-permute-done.9.odd_adj_ref
  56.9 1.5 %back.1 = bf16[512,256]{1,0:T(8,128)(2,1)} custom-call(f32[512,256]{1,0:T(8,128)S(1)} %get-tuple-element.45.base_ref, bf16[4,256,256]{2,1,0:T(8,128)(2,1)S(1)} %pad_maximum_fusion.even_adj_ref, bf16[4,256,256]{2,1,0:T(8,128)(2,1)S(1)} %collective-permute-done.9.odd_adj_ref, bf16[512,512]{1,0:T(8,128)(2,1)S(1)} %get-tuple-element.55.refs_0_, ...), custom_call_target="tpu_custom_call" | custom-call | flops 536870912 | bytes 2097152 | tf_op jit(solution)/shard_map/back/pallas_call | solution.py:328
  (13 shorter events, 0.3 us)
Async XLA Ops:
  2.8 3.5 %collective-permute-start.3 = (bf16[512,512]{1,0:T(8,128)(2,1)S(1)}, bf16[512,512]{1,0:T(8,128)(2,1)S(1)}, u32[]{:S(2)}, u32[]{:S(2)}) collective-permute-start(bf16[512,512]{1,0:T(8,128)(2,1)S(1)} %get-tuple-element.53), channel_id=1, source_target_pairs={{0,4},{4,0},{8,12},{12,8},{16,20},{20,16},{24,28},{28,24},{1,5},{5... | collective-permute-start | bytes 1572872 | tf_op jit(solution)/shard_map/ppermute | solution.py:29
  4.3 6.7 %collective-permute-start.2 = (bf16[512,512]{1,0:T(8,128)(2,1)S(1)}, bf16[512,512]{1,0:T(8,128)(2,1)S(1)}, u32[]{:S(2)}, u32[]{:S(2)}) collective-permute-start(bf16[512,512]{1,0:T(8,128)(2,1)S(1)} %get-tuple-element.51), channel_id=1, source_target_pairs={{0,4},{4,0},{8,12},{12,8},{16,20},{20,16},{24,28},{28,24},{1,5},{5... | collective-permute-start | bytes 1572872 | tf_op jit(solution)/shard_map/ppermute | solution.py:29
  6.5 20.1 %collective-permute-start.5 = (bf16[256,512]{1,0:T(8,128)(2,1)S(1)}, bf16[256,512]{1,0:T(8,128)(2,1)S(1)}, u32[]{:S(2)}, u32[]{:S(2)}) collective-permute-start(bf16[256,512]{1,0:T(8,128)(2,1)S(1)} %get-tuple-element.66), channel_id=1, source_target_pairs={{0,16},{4,20},{8,24},{12,28},{16,0},{20,4},{24,8},{28,12},{1,17},{... | collective-permute-start | bytes 786440 | tf_op jit(solution)/shard_map/ppermute | solution.py:29
  9.5 17.0 %collective-permute-start.4 = (bf16[256,512]{1,0:T(8,128)(2,1)S(1)}, bf16[256,512]{1,0:T(8,128)(2,1)S(1)}, u32[]{:S(2)}, u32[]{:S(2)}) collective-permute-start(bf16[256,512]{1,0:T(8,128)(2,1)S(1)} %get-tuple-element.67), channel_id=1, source_target_pairs={{0,24},{4,28},{8,16},{12,20},{16,8},{20,12},{24,0},{28,4},{1,25},{... | collective-permute-start | bytes 786440 | tf_op jit(solution)/shard_map/ppermute | solution.py:29
  11.2 15.4 %collective-permute-start.6 = (bf16[256,512]{1,0:T(8,128)(2,1)S(1)}, bf16[256,512]{1,0:T(8,128)(2,1)S(1)}, u32[]{:S(2)}, u32[]{:S(2)}) collective-permute-start(bf16[256,512]{1,0:T(8,128)(2,1)S(1)} %slice.67), channel_id=1, source_target_pairs={{0,8},{4,12},{8,0},{12,4},{16,24},{20,28},{24,16},{28,20},{1,9},{5... | collective-permute-start | bytes 786440 | tf_op jit(solution)/shard_map/ppermute | solution.py:29
  16.5 8.4 %collective-permute-start = (bf16[256,256]{1,0:T(8,128)(2,1)S(1)}, bf16[256,256]{1,0:T(8,128)(2,1)S(1)}, u32[]{:S(2)}, u32[]{:S(2)}) collective-permute-start(bf16[256,256]{1,0:T(8,128)(2,1)S(1)} %get-tuple-element.40), channel_id=1, source_target_pairs={{0,28},{4,0},{8,4},{12,8},{16,12},{20,16},{24,20},{28,24},{1,29},{... | collective-permute-start | bytes 393224 | tf_op jit(solution)/shard_map/ppermute | solution.py:34
  18.2 7.4 %collective-permute-start.1 = (bf16[256,256]{1,0:T(8,128)(2,1)S(1)}, bf16[256,256]{1,0:T(8,128)(2,1)S(1)}, u32[]{:S(2)}, u32[]{:S(2)}) collective-permute-start(bf16[256,256]{1,0:T(8,128)(2,1)S(1)} %get-tuple-element.41), channel_id=1, source_target_pairs={{0,4},{4,8},{8,12},{12,16},{16,20},{20,24},{24,28},{28,0},{1,5},{5... | collective-permute-start | bytes 393224 | tf_op jit(solution)/shard_map/ppermute | solution.py:34
  26.3 1.4 %collective-permute-start.11 = (f32[4,32,256]{2,1,0:T(8,128)S(1)}, f32[4,32,256]{2,1,0:T(8,128)S(1)}, u32[]{:S(2)}, u32[]{:S(2)}) collective-permute-start(f32[4,32,256]{2,1,0:T(8,128)S(1)} %get-tuple-element.62), channel_id=1, source_target_pairs={{0,4},{4,0},{8,12},{12,8},{16,20},{20,16},{24,28},{28,24},{1,5},{5... | collective-permute-start | bytes 393224 | tf_op jit(solution)/shard_map/ppermute | solution.py:29
  27.1 1.9 %collective-permute-start.10 = (f32[4,32,256]{2,1,0:T(8,128)S(1)}, f32[4,32,256]{2,1,0:T(8,128)S(1)}, u32[]{:S(2)}, u32[]{:S(2)}) collective-permute-start(f32[4,32,256]{2,1,0:T(8,128)S(1)} %get-tuple-element.60), channel_id=1, source_target_pairs={{0,4},{4,0},{8,12},{12,8},{16,20},{20,16},{24,28},{28,24},{1,5},{5... | collective-permute-start | bytes 393224 | tf_op jit(solution)/shard_map/ppermute | solution.py:29
  27.8 6.4 %collective-permute-start.7 = (bf16[1,256,256]{2,1,0:T(8,128)(2,1)S(1)}, bf16[1,256,256]{2,1,0:T(8,128)(2,1)S(1)}, u32[]{:S(2)}, u32[]{:S(2)}) collective-permute-start(bf16[1,256,256]{2,1,0:T(8,128)(2,1)S(1)} %bitcast.24), channel_id=1, source_target_pairs={{0,16},{4,20},{8,24},{12,28},{16,0},{20,4},{24,8},{28,12},{1,17},{... | collective-permute-start | bytes 393224 | tf_op jit(solution)/shard_map/ppermute | solution.py:29
  29.1 7.8 %collective-permute-start.12 = (bf16[64,256]{1,0:T(8,128)(2,1)S(1)}, bf16[64,256]{1,0:T(8,128)(2,1)S(1)}, u32[]{:S(2)}, u32[]{:S(2)}) collective-permute-start(bf16[64,256]{1,0:T(8,128)(2,1)S(1)} %get-tuple-element.68), channel_id=1, source_target_pairs={{0,24},{4,28},{8,16},{12,20},{16,8},{20,12},{24,0},{28,4},{1,25},{... | collective-permute-start | bytes 98312 | tf_op jit(solution)/shard_map/ppermute | solution.py:29
  31.6 5.3 %collective-permute-start.14 = (bf16[64,256]{1,0:T(8,128)(2,1)S(1)}, bf16[64,256]{1,0:T(8,128)(2,1)S(1)}, u32[]{:S(2)}, u32[]{:S(2)}) collective-permute-start(bf16[64,256]{1,0:T(8,128)(2,1)S(1)} %get-tuple-element.69), channel_id=1, source_target_pairs={{0,8},{4,12},{8,0},{12,4},{16,24},{20,28},{24,16},{28,20},{1,9},{5... | collective-permute-start | bytes 98312 | tf_op jit(solution)/shard_map/ppermute | solution.py:29
  31.6 5.3 %collective-permute-start.13 = (bf16[64,256]{1,0:T(8,128)(2,1)S(1)}, bf16[64,256]{1,0:T(8,128)(2,1)S(1)}, u32[]{:S(2)}, u32[]{:S(2)}) collective-permute-start(bf16[64,256]{1,0:T(8,128)(2,1)S(1)} %get-tuple-element.70), channel_id=1, source_target_pairs={{0,16},{4,20},{8,24},{12,28},{16,0},{20,4},{24,8},{28,12},{1,17},{... | collective-permute-start | bytes 98312 | tf_op jit(solution)/shard_map/ppermute | solution.py:29
  34.2 14.9 %collective-permute-start.8 = (bf16[2,256,256]{2,1,0:T(8,128)(2,1)S(1)}, bf16[2,256,256]{2,1,0:T(8,128)(2,1)S(1)}, u32[]{:S(2)}, u32[]{:S(2)}) collective-permute-start(bf16[2,256,256]{2,1,0:T(8,128)(2,1)S(1)} %pad_maximum_fusion.2), channel_id=1, source_target_pairs={{0,8},{4,12},{8,0},{12,4},{16,24},{20,28},{24,16},{28,20},{1,9},{5... | collective-permute-start | bytes 786440 | tf_op jit(solution)/shard_map/ppermute | solution.py:29
  36.9 6.0 %collective-permute-start.17 = (bf16[64,256]{1,0:T(8,128)(2,1)S(1)}, bf16[64,256]{1,0:T(8,128)(2,1)S(1)}, u32[]{:S(2)}, u32[]{:S(2)}) collective-permute-start(bf16[64,256]{1,0:T(8,128)(2,1)S(1)} %fusion.6), channel_id=1, source_target_pairs={{0,3},{1,2},{2,1},{3,0},{4,7},{5,6},{6,5},{7,4},{8,11},{9,10},{10,... | collective-permute-start | bytes 98312 | tf_op jit(solution)/shard_map/ppermute | solution.py:29
  40.6 4.9 %collective-permute-start.16 = (bf16[64,256]{1,0:T(8,128)(2,1)S(1)}, bf16[64,256]{1,0:T(8,128)(2,1)S(1)}, u32[]{:S(2)}, u32[]{:S(2)}) collective-permute-start(bf16[64,256]{1,0:T(8,128)(2,1)S(1)} %fusion.6), channel_id=1, source_target_pairs={{0,2},{1,3},{2,0},{3,1},{4,6},{5,7},{6,4},{7,5},{8,10},{9,11},{10,... | collective-permute-start | bytes 98312 | tf_op jit(solution)/shard_map/ppermute | solution.py:29
  40.6 4.9 %collective-permute-start.15 = (bf16[64,256]{1,0:T(8,128)(2,1)S(1)}, bf16[64,256]{1,0:T(8,128)(2,1)S(1)}, u32[]{:S(2)}, u32[]{:S(2)}) collective-permute-start(bf16[64,256]{1,0:T(8,128)(2,1)S(1)} %fusion.6), channel_id=1, source_target_pairs={{0,1},{1,0},{2,3},{3,2},{4,5},{5,4},{6,7},{7,6},{8,9},{9,8},{10,11... | collective-permute-start | bytes 98312 | tf_op jit(solution)/shard_map/ppermute | solution.py:29
  41.4 7.9 %collective-permute-start.22 = (bf16[128,256]{1,0:T(8,128)(2,1)S(1)}, bf16[128,256]{1,0:T(8,128)(2,1)S(1)}, u32[]{:S(2)}, u32[]{:S(2)}) collective-permute-start(bf16[128,256]{1,0:T(8,128)(2,1)S(1)} %convert_element_type.80), channel_id=1, source_target_pairs={{0,1},{1,0},{2,3},{3,2},{4,5},{5,4},{6,7},{7,6},{8,9},{9,8},{10,11... | collective-permute-start | bytes 196616 | tf_op jit(solution)/shard_map/ppermute | solution.py:29
  45.5 5.7 %collective-permute-start.20 = (bf16[64,256]{1,0:T(8,128)(2,1)S(1)}, bf16[64,256]{1,0:T(8,128)(2,1)S(1)}, u32[]{:S(2)}, u32[]{:S(2)}) collective-permute-start(bf16[64,256]{1,0:T(8,128)(2,1)S(1)} %add_convert_fusion.2), channel_id=1, source_target_pairs={{0,24},{4,28},{8,16},{12,20},{16,8},{20,12},{24,0},{28,4},{1,25},{... | collective-permute-start | bytes 98312 | tf_op jit(solution)/shard_map/ppermute | solution.py:29
  46.6 4.7 %collective-permute-start.19 = (bf16[64,256]{1,0:T(8,128)(2,1)S(1)}, bf16[64,256]{1,0:T(8,128)(2,1)S(1)}, u32[]{:S(2)}, u32[]{:S(2)}) collective-permute-start(bf16[64,256]{1,0:T(8,128)(2,1)S(1)} %add_convert_fusion.2), channel_id=1, source_target_pairs={{0,8},{4,12},{8,0},{12,4},{16,24},{20,28},{24,16},{28,20},{1,9},{5... | collective-permute-start | bytes 98312 | tf_op jit(solution)/shard_map/ppermute | solution.py:29
  46.8 4.5 %collective-permute-start.18 = (bf16[64,256]{1,0:T(8,128)(2,1)S(1)}, bf16[64,256]{1,0:T(8,128)(2,1)S(1)}, u32[]{:S(2)}, u32[]{:S(2)}) collective-permute-start(bf16[64,256]{1,0:T(8,128)(2,1)S(1)} %add_convert_fusion.2), channel_id=1, source_target_pairs={{0,16},{4,20},{8,24},{12,28},{16,0},{20,4},{24,8},{28,12},{1,17},{... | collective-permute-start | bytes 98312 | tf_op jit(solution)/shard_map/ppermute | solution.py:29
  49.2 7.7 %collective-permute-start.9 = (bf16[4,256,256]{2,1,0:T(8,128)(2,1)S(1)}, bf16[4,256,256]{2,1,0:T(8,128)(2,1)S(1)}, u32[]{:S(2)}, u32[]{:S(2)}) collective-permute-start(bf16[4,256,256]{2,1,0:T(8,128)(2,1)S(1)} %pad_maximum_fusion.even_adj_ref), channel_id=1, source_target_pairs={{0,4},{4,0},{8,12},{12,8},{16,20},{20,16},{24,28},{28,24},{1,5},{5... | collective-permute-start | bytes 1572872 | tf_op jit(solution)/shard_map/ppermute | solution.py:29
  49.3 6.1 %collective-permute-start.23 = (bf16[128,256]{1,0:T(8,128)(2,1)S(1)}, bf16[128,256]{1,0:T(8,128)(2,1)S(1)}, u32[]{:S(2)}, u32[]{:S(2)}) collective-permute-start(bf16[128,256]{1,0:T(8,128)(2,1)S(1)} %add_convert_fusion.1), channel_id=1, source_target_pairs={{0,2},{1,3},{2,0},{3,1},{4,6},{5,7},{6,4},{7,5},{8,10},{9,11},{10,... | collective-permute-start | bytes 196616 | tf_op jit(solution)/shard_map/ppermute | solution.py:29
  51.3 4.7 %collective-permute-start.21 = (bf16[4,64,256]{2,1,0:T(8,128)(2,1)S(1)}, bf16[4,64,256]{2,1,0:T(8,128)(2,1)S(1)}, u32[]{:S(2)}, u32[]{:S(2)}) collective-permute-start(bf16[4,64,256]{2,1,0:T(8,128)(2,1)S(1)} %pad_maximum_fusion.3.even_ref), channel_id=1, source_target_pairs={{0,4},{4,0},{8,12},{12,8},{16,20},{20,16},{24,28},{28,24},{1,5},{5... | collective-permute-start | bytes 393224 | tf_op jit(solution)/shard_map/ppermute | solution.py:29

commit v6 on v4

--- a/solution.py
+++ b/solution.py
@@ -45,7 +45,7 @@
 def plane_order(count):
     width = min(4, count // 2)
     offsets = [[offset for offset in range(0, count, 2) if offset // 2 % width == g] for g in range(width)]
-    return offsets[: width // 2], offsets[width // 2 :]
+    return offsets[:-1], offsets[-1:]
 
 
 def horner(coefs, z):
@@ -234,7 +234,7 @@
     atoms, channels = cotan.shape
     edges = sources.shape[1]
     rows = atoms + 2 * rim
-    block = math.gcd(edges, 512)
+    block = math.gcd(edges, 2048)
     return pl.pallas_call(
         functools.partial(edge_kernel, block),
         name="edges",
@@ -407,6 +407,50 @@
         value = sent.astype(f32) + moved.astype(f32)
         bit = 2 * bit
     return value
+
+
+def sum_replicas_direct(value):
+    count = lax.axis_size("rep")
+    terms = [value.astype(bf16)]
+    for offset in range(count - 1, 0, -1):
+        terms.insert(1, xor_permute(terms[0], "rep", offset))
+    terms = [term.astype(f32) for term in terms]
+    while len(terms) > 1:
+        terms = [terms[i] + terms[i + 1] for i in range(0, len(terms), 2)]
+    return terms[0]
+
+
+def folded_sum(blocks):
+    count = lax.axis_size("slab")
+    bit = 2
+    terms = None
+    while bit < count:
+        width = min(4, count // bit)
+        sent = [[offset for offset in sorted(blocks) if offset // bit % width == g] for g in range(width)]
+        half = blocks[0].shape[1] // 2
+
+        def move(g, pieces):
+            payload = pieces[0] if len(pieces) == 1 else jnp.concatenate(pieces, axis=0)
+            moved = xor_permute(payload, "slab", g * bit)
+            return jnp.split(moved, len(pieces), axis=0)
+
+        if width == 4:
+            first = move(1, [blocks[offset][:, :half].astype(bf16) for offset in sent[3]])
+            second = move(2, [blocks[offset][:, half:].astype(bf16) for offset in sent[3]])
+            for i, offset in enumerate(sent[2]):
+                left = blocks[offset][:, :half] + first[i].astype(f32)
+                blocks[offset] = jnp.concatenate([left, blocks[offset][:, half:]], axis=1)
+            for i, offset in enumerate(sent[1]):
+                right = blocks[offset][:, half:] + second[i].astype(f32)
+                blocks[offset] = jnp.concatenate([blocks[offset][:, :half], right], axis=1)
+        received = [move(g, [blocks[offset].astype(bf16) for offset in sent[g]]) for g in range(1, min(width, 3))]
+        terms = [blocks[0], *(moved[0] for moved in received)]
+        blocks = {
+            offset: sum((moved[i].astype(f32) for moved in received), blocks[offset])
+            for i, offset in enumerate(sent[0])
+        }
+        bit = bit * width
+    return terms
 
 
 def plane_gather(block, order):
@@ -502,7 +546,7 @@
         paired = part + moved.astype(f32)
         for i, offset in enumerate(offsets):
             blocks[offset] = paired[i * 2 * share : (i + 1) * 2 * share]
-    parts = plane_sum(blocks)
+    parts = folded_sum(blocks)
 
     rows_t, to_prev, to_next = rim_features(rows, lists)
     lower_t = shifted(to_next, "slab", 1)
@@ -523,7 +567,7 @@
     adj_odd = xor_permute(adj_even, "slab", 1)
     grad_features = back_project(orders, order, base, adj_even, adj_odd, (odda, evena, oddb, evenb))
 
-    own_grad = sum_replicas(own_grad).astype(bf16)
+    own_grad = sum_replicas_direct(own_grad).astype(bf16)
     filter_sum = sum_replicas(gfilter)
     grad_filter = filter_sum / replicas
     grad_even = plane_gather(own_grad, order)

time: 60 us -> 62 us (1.033)
  waiting for transfers between devices: 16.2 us -> 20.7 us
  starting transfers between devices: 26.9 us -> 24.9 us
    ppermute x20 -> x22, starting transfers between devices: 22.7 us -> 18.2 us  [xor_permute(): lax.ppermute(value, axis, [(source, source ^ bits) for source in range(co...]
    ppermute x20 -> x22, waiting for transfers between devices: 16.2 us -> 20.7 us  [xor_permute(): lax.ppermute(value, axis, [(source, source ^ bits) for source in range(co...]
    ppermute x4, starting transfers between devices: 4.16 us -> 6.67 us  [shifted(): lax.ppermute(value, axis, [(source, (source + steps) % count) for source...]
  transfers between devices with their start and end apart: 24 -> 26, of which waited for: 9 -> 12; matrix products, arithmetic and copies ran while one was open for 2% -> 2% of each run, Pallas kernels for 17% -> 14%
where the time goes in v6:
time: 62 us; the launch traced here: 61.7 us
  starting transfers between devices  24.9 us (40%)
  waiting for transfers between devices  20.7 us (33%)
  Pallas kernels  13.8 us (22%)
  other arithmetic  1.36 us (2%)
  between operations  0.89 us (1%)
    ppermute x22, waiting for transfers between devices, xor_permute(): lax.ppermute(value, axis, [(source, source ^ bits) for source in range(co...  20.7 us
    ppermute x22, starting transfers between devices, xor_permute(): lax.ppermute(value, axis, [(source, source ^ bits) for source in range(co...  18.2 us
    ppermute x4, starting transfers between devices, shifted(): lax.ppermute(value, axis, [(source, (source + steps) % count) for source...  6.67 us
    pallas_call x1, Pallas kernels, edge_rows(): pl.pallas_call(functools.partial(edge_kernel, block), name='edges', out_s...  4.95 us
    pallas_call x3, Pallas kernels, next_tables(): pl.pallas_call(functools.partial(second_kernel, order), out_shape=(jax.Sh...  3.19 us
    pallas_call x1, Pallas kernels, first_tables(): pl.pallas_call(functools.partial(first_kernel, order, len(others)), name=...  1.73 us
    pallas_call x1, Pallas kernels, back_project(): pl.pallas_call(functools.partial(back_kernel, orders, order), name='back'...  1.55 us
  transfers between devices with their start and end apart: 26, of which 12 were waited for; matrix products, arithmetic and copies ran while one was open for 2% of the time, Pallas kernels for 14%

profile of v6, /device:TPU:0, one launch (start us, length us, event | category | flops | bytes accessed | tf_op | source)
XLA Modules:
  0.0 61.7 jit_solution(15771014165790335955)
XLA Ops:
  0.6 1.7 %first.1 = (bf16[256,512]{1,0:T(8,128)(2,1)S(1)}, bf16[256,512]{1,0:T(8,128)(2,1)S(1)}, f32[1024,16]{1,0:T(8,128)S(1)}, bf16[16,512]{1,0:T(8,128)(2,1)S(1)}, bf1...) custom-call(s32[1]{0:T(128)} %bitcast.slab_ref, ...), custom_call_target="tpu_custom_call" | custom-call | flops 134217728 | bytes 524288 | tf_op jit(solution)/shard_map/first/pallas_call | solution.py:136
  2.4 1.3 %shard_map.139 = (bf16[768,512]{1,0:T(8,128)(2,1)S(1)}, bf16[768,512]{1,0:T(8,128)(2,1)S(1)}) custom-call(s32[1]{0:T(128)} %bitcast.slab_ref, f32[1024,16]{1,0:T(8,128)S(1)} %get-tuple-element.52.k_cols, bf16[16,512]{1,0:T(8,128)(2,1)S(1)} %get-tuple-element.53.positions, bf16[512,256]{1,0:T(8,128)(2,1)S(1)} %get-tuple-element.40.rows_ref, ...), custom_call_target="tpu_custom_call" | custom-call | flops 402653184 | bytes 1572864 | tf_op jit(solution)/shard_map/pallas_call | solution.py:163
  3.7 0.6 collective-permute-start.4
  4.3 0.1 collective-permute-start.5
  4.4 0.3 rims.1
  4.7 0.5 collective-permute-start.2
  5.2 3.2 %collective-permute-start.3 = (bf16[256,256]{1,0:T(8,128)(2,1)S(1)}, bf16[256,256]{1,0:T(8,128)(2,1)S(1)}, u32[]{:S(2)}, u32[]{:S(2)}) collective-permute-start(bf16[256,256]{1,0:T(8,128)(2,1)S(1)} %get-tuple-element.51), channel_id=1, source_target_pairs={{0,28},{4,0},{8,4},{12,8},{16,12},{20,16},{24,20},{28,24},{1,29},{... | collective-permute-start | bytes 393224 | tf_op jit(solution)/shard_map/ppermute | solution.py:34
  8.3 0.5 shard_map.140
  8.9 1.3 %shard_map.138 = (bf16[768,512]{1,0:T(8,128)(2,1)S(1)}, f32[768,512]{1,0:T(8,128)S(1)}) custom-call(s32[1]{0:T(128)} %bitcast.slab_ref, f32[1024,16]{1,0:T(8,128)S(1)} %get-tuple-element.52.k_cols, bf16[16,512]{1,0:T(8,128)(2,1)S(1)} %get-tuple-element.53.positions, bf16[512,256]{1,0:T(8,128)(2,1)S(1)} %get-tuple-element.40.rows_ref, ...), custom_call_target="tpu_custom_call" | custom-call | flops 402653184 | bytes 1572864 | tf_op jit(solution)/shard_map/pallas_call | solution.py:163
  10.2 0.0 collective-permute-done.5
  10.2 0.1 add_convert_fusion
  10.3 2.0 %collective-permute-start.6 = (bf16[256,256]{1,0:T(8,128)(2,1)S(1)}, bf16[256,256]{1,0:T(8,128)(2,1)S(1)}, u32[]{:S(2)}, u32[]{:S(2)}) collective-permute-start(bf16[256,256]{1,0:T(8,128)(2,1)S(1)} %get-tuple-element.77), channel_id=1, source_target_pairs={{0,16},{4,20},{8,24},{12,28},{16,0},{20,4},{24,8},{28,12},{1,17},{... | collective-permute-start | bytes 393224 | tf_op jit(solution)/shard_map/ppermute | solution.py:29
  12.4 0.6 collective-permute-start.8
  13.0 0.0 collective-permute-done.4
  13.0 0.3 fusion.7
  13.3 2.1 %collective-permute-done.6 = bf16[256,256]{1,0:T(8,128)(2,1)S(1)} collective-permute-done((bf16[256,256]{1,0:T(8,128)(2,1)S(1)}, bf16[256,256]{1,0:T(8,128)(2,1)S(1)}, u32[]{:S(2)}, u32[]{:S(2)}) %collective-permute-start.6) | collective-permute-done | bytes 131104 | tf_op jit(solution)/shard_map/ppermute | solution.py:29
  15.4 2.0 %collective-permute-done.8 = bf16[256,256]{1,0:T(8,128)(2,1)S(1)} collective-permute-done((bf16[256,256]{1,0:T(8,128)(2,1)S(1)}, bf16[256,256]{1,0:T(8,128)(2,1)S(1)}, u32[]{:S(2)}, u32[]{:S(2)}) %collective-permute-start.8) | collective-permute-done | bytes 131104 | tf_op jit(solution)/shard_map/ppermute | solution.py:29
  17.3 0.1 fusion
  17.4 0.1 collective-permute-start.9
  17.6 1.1 %collective-permute-start.7 = (bf16[256,512]{1,0:T(8,128)(2,1)S(1)}, bf16[256,512]{1,0:T(8,128)(2,1)S(1)}, u32[]{:S(2)}, u32[]{:S(2)}) collective-permute-start(bf16[256,512]{1,0:T(8,128)(2,1)S(1)} %pad_maximum_fusion.1), channel_id=1, source_target_pairs={{0,8},{4,12},{8,0},{12,4},{16,24},{20,28},{24,16},{28,20},{1,9},{5... | collective-permute-start | bytes 786440 | tf_op jit(solution)/shard_map/ppermute | solution.py:29
  18.7 5.0 %edges.1 = (f32[512,256]{1,0:T(8,128)S(1)}, bf16[256,256]{1,0:T(8,128)(2,1)S(1)}, bf16[256,256]{1,0:T(8,128)(2,1)S(1)}, f32[256,256]{1,0:T(8,128)S(1)}) custom-call(s32[1,4096]{1,0:T(1,128)S(1)} %get-tuple-element.36.src_ref, s32[1,4096]{1,0:T(1,128)S(1)} %get-tuple-element.37.dst_ref, f32[1,4096]{1,0:T(1,128)S(1)} %get-tuple-element.38.dist_ref, ...), custom_call_target="tpu_custom_call" | custom-call | flops 3221225472 | bytes 49152 | tf_op jit(solution)/shard_map/edges/pallas_call | solution.py:238
  23.7 0.0 collective-permute-done.3.upper_t
  23.7 0.1 collective-permute-done.9.refs_2_
  23.9 0.2 collective-permute-done.7.refs_1_
  24.1 0.5 share.1
  24.6 0.1 collective-permute-start.13
  24.7 3.0 %collective-permute-start = (bf16[256,256]{1,0:T(8,128)(2,1)S(1)}, bf16[256,256]{1,0:T(8,128)(2,1)S(1)}, u32[]{:S(2)}, u32[]{:S(2)}) collective-permute-start(bf16[256,256]{1,0:T(8,128)(2,1)S(1)} %get-tuple-element.44.low_ref), channel_id=1, source_target_pairs={{0,28},{4,0},{8,4},{12,8},{16,12},{20,16},{24,20},{28,24},{1,29},{... | collective-permute-start | bytes 393224 | tf_op jit(solution)/shard_map/ppermute | solution.py:34
  27.7 0.0 collective-permute-start.1
  27.7 0.3 collective-permute-start.10
  28.1 1.2 %collective-permute-start.14 = (bf16[64,256]{1,0:T(8,128)(2,1)S(1)}, bf16[64,256]{1,0:T(8,128)(2,1)S(1)}, u32[]{:S(2)}, u32[]{:S(2)}) collective-permute-start(bf16[64,256]{1,0:T(8,128)(2,1)S(1)} %get-tuple-element.78), channel_id=1, source_target_pairs={{0,24},{4,28},{8,16},{12,20},{16,8},{20,12},{24,0},{28,4},{1,25},{... | collective-permute-start | bytes 98312 | tf_op jit(solution)/shard_map/ppermute | solution.py:29
  29.3 1.1 %collective-permute-start.15 = (bf16[64,256]{1,0:T(8,128)(2,1)S(1)}, bf16[64,256]{1,0:T(8,128)(2,1)S(1)}, u32[]{:S(2)}, u32[]{:S(2)}) collective-permute-start(bf16[64,256]{1,0:T(8,128)(2,1)S(1)} %get-tuple-element.80), channel_id=1, source_target_pairs={{0,16},{4,20},{8,24},{12,28},{16,0},{20,4},{24,8},{28,12},{1,17},{... | collective-permute-start | bytes 98312 | tf_op jit(solution)/shard_map/ppermute | solution.py:29
  30.3 4.8 %collective-permute-done.10 = bf16[1,256,256]{2,1,0:T(8,128)(2,1)S(1)} collective-permute-done((bf16[1,256,256]{2,1,0:T(8,128)(2,1)S(1)}, bf16[1,256,256]{2,1,0:T(8,128)(2,1)S(1)}, u32[]{:S(2)}, u32[]{:S(2)}) %collective-permute-start.10) | collective-permute-done | bytes 131104 | tf_op jit(solution)/shard_map/ppermute | solution.py:29
  35.1 0.0 collective-permute-start.16
  35.2 0.0 collective-permute-done.14
  35.2 2.1 %collective-permute-start.11 = (bf16[2,256,256]{2,1,0:T(8,128)(2,1)S(1)}, bf16[2,256,256]{2,1,0:T(8,128)(2,1)S(1)}, u32[]{:S(2)}, u32[]{:S(2)}) collective-permute-start(bf16[2,256,256]{2,1,0:T(8,128)(2,1)S(1)} %pad_maximum_fusion.3), channel_id=1, source_target_pairs={{0,8},{4,12},{8,0},{12,4},{16,24},{20,28},{24,16},{28,20},{1,9},{5... | collective-permute-start | bytes 786440 | tf_op jit(solution)/shard_map/ppermute | solution.py:29
  37.3 0.0 collective-permute-done.15
  37.3 2.1 %collective-permute-done.16 = bf16[64,256]{1,0:T(8,128)(2,1)S(1)} collective-permute-done((bf16[64,256]{1,0:T(8,128)(2,1)S(1)}, bf16[64,256]{1,0:T(8,128)(2,1)S(1)}, u32[]{:S(2)}, u32[]{:S(2)}) %collective-permute-start.16) | collective-permute-done | bytes 32800 | tf_op jit(solution)/shard_map/ppermute | solution.py:29
  39.4 1.7 %collective-permute-start.17 = (bf16[64,256]{1,0:T(8,128)(2,1)S(1)}, bf16[64,256]{1,0:T(8,128)(2,1)S(1)}, u32[]{:S(2)}, u32[]{:S(2)}) collective-permute-start(bf16[64,256]{1,0:T(8,128)(2,1)S(1)} %fusion.5), channel_id=1, source_target_pairs={{0,1},{1,0},{2,3},{3,2},{4,5},{5,4},{6,7},{7,6},{8,9},{9,8},{10,11... | collective-permute-start | bytes 98312 | tf_op jit(solution)/shard_map/ppermute | solution.py:29
  41.1 2.6 %collective-permute-start.18 = (bf16[64,256]{1,0:T(8,128)(2,1)S(1)}, bf16[64,256]{1,0:T(8,128)(2,1)S(1)}, u32[]{:S(2)}, u32[]{:S(2)}) collective-permute-start(bf16[64,256]{1,0:T(8,128)(2,1)S(1)} %fusion.5), channel_id=1, source_target_pairs={{0,2},{1,3},{2,0},{3,1},{4,6},{5,7},{6,4},{7,5},{8,10},{9,11},{10,... | collective-permute-start | bytes 98312 | tf_op jit(solution)/shard_map/ppermute | solution.py:29
  43.7 0.2 collective-permute-start.19
  43.9 0.0 collective-permute-done.1.below_ref
  43.9 0.7 %short.1.base_ref = f32[512,256]{1,0:T(8,128)S(1)} custom-call(f32[512,256]{1,0:T(8,128)S(1)} %get-tuple-element.43.own_ref, bf16[256,256]{1,0:T(8,128)(2,1)S(1)} %collective-permute-done.above_ref, bf16[256,256]{1,0:T(8,128)(2,1)S(1)} %collective-permute-done.1.below_ref, s32[1,2,256]{2,1,0:T(2,128)S(1)} %get-tuple-element.41.lists_ref, ...), custom_call_target="tpu_custom_call" | custom-call | flops 268435456 | bytes 1048576 | tf_op jit(solution)/shard_map/short/pallas_call | solution.py:280
  44.6 0.8 %collective-permute-start.24 = (bf16[128,256]{1,0:T(8,128)(2,1)S(1)}, bf16[128,256]{1,0:T(8,128)(2,1)S(1)}, u32[]{:S(2)}, u32[]{:S(2)}) collective-permute-start(bf16[128,256]{1,0:T(8,128)(2,1)S(1)} %convert_element_type.89), channel_id=1, source_target_pairs={{0,1},{1,0},{2,3},{3,2},{4,5},{5,4},{6,7},{7,6},{8,9},{9,8},{10,11... | collective-permute-start | bytes 196616 | tf_op jit(solution)/shard_map/ppermute | solution.py:29
  45.4 0.0 collective-permute-done.17
  45.4 0.9 %collective-permute-done.18 = bf16[64,256]{1,0:T(8,128)(2,1)S(1)} collective-permute-done((bf16[64,256]{1,0:T(8,128)(2,1)S(1)}, bf16[64,256]{1,0:T(8,128)(2,1)S(1)}, u32[]{:S(2)}, u32[]{:S(2)}) %collective-permute-start.18) | collective-permute-done | bytes 32800 | tf_op jit(solution)/shard_map/ppermute | solution.py:29
  46.3 3.2 %collective-permute-done.19 = bf16[64,256]{1,0:T(8,128)(2,1)S(1)} collective-permute-done((bf16[64,256]{1,0:T(8,128)(2,1)S(1)}, bf16[64,256]{1,0:T(8,128)(2,1)S(1)}, u32[]{:S(2)}, u32[]{:S(2)}) %collective-permute-start.19) | collective-permute-done | bytes 32800 | tf_op jit(solution)/shard_map/ppermute | solution.py:29
  49.4 0.1 collective-permute-start.21
  49.5 2.8 %collective-permute-start.22 = (bf16[64,256]{1,0:T(8,128)(2,1)S(1)}, bf16[64,256]{1,0:T(8,128)(2,1)S(1)}, u32[]{:S(2)}, u32[]{:S(2)}) collective-permute-start(bf16[64,256]{1,0:T(8,128)(2,1)S(1)} %add_convert_fusion.2), channel_id=1, source_target_pairs={{0,24},{4,28},{8,16},{12,20},{16,8},{20,12},{24,0},{28,4},{1,25},{... | collective-permute-start | bytes 98312 | tf_op jit(solution)/shard_map/ppermute | solution.py:29
  52.3 0.7 %collective-permute-start.20 = (bf16[64,256]{1,0:T(8,128)(2,1)S(1)}, bf16[64,256]{1,0:T(8,128)(2,1)S(1)}, u32[]{:S(2)}, u32[]{:S(2)}) collective-permute-start(bf16[64,256]{1,0:T(8,128)(2,1)S(1)} %add_convert_fusion.2), channel_id=1, source_target_pairs={{0,16},{4,20},{8,24},{12,28},{16,0},{20,4},{24,8},{28,12},{1,17},{... | collective-permute-start | bytes 98312 | tf_op jit(solution)/shard_map/ppermute | solution.py:29
  53.0 0.0 collective-permute-done.11
  53.0 0.1 pad_maximum_fusion.even_adj_ref
  53.1 0.1 collective-permute-start.12
  53.1 0.0 collective-permute-done.24
  53.2 0.1 collective-permute-start.25
  53.2 0.2 collective-permute-done.21
  53.4 1.1 %collective-permute-done.22 = bf16[64,256]{1,0:T(8,128)(2,1)S(1)} collective-permute-done((bf16[64,256]{1,0:T(8,128)(2,1)S(1)}, bf16[64,256]{1,0:T(8,128)(2,1)S(1)}, u32[]{:S(2)}, u32[]{:S(2)}) %collective-permute-start.22) | collective-permute-done | bytes 32800 | tf_op jit(solution)/shard_map/ppermute | solution.py:29
  54.5 1.7 %collective-permute-done.20 = bf16[64,256]{1,0:T(8,128)(2,1)S(1)} collective-permute-done((bf16[64,256]{1,0:T(8,128)(2,1)S(1)}, bf16[64,256]{1,0:T(8,128)(2,1)S(1)}, u32[]{:S(2)}, u32[]{:S(2)}) %collective-permute-start.20) | collective-permute-done | bytes 32800 | tf_op jit(solution)/shard_map/ppermute | solution.py:29
  56.2 0.1 collective-permute-start.23
  56.3 2.3 %collective-permute-done.25 = bf16[128,256]{1,0:T(8,128)(2,1)S(1)} collective-permute-done((bf16[128,256]{1,0:T(8,128)(2,1)S(1)}, bf16[128,256]{1,0:T(8,128)(2,1)S(1)}, u32[]{:S(2)}, u32[]{:S(2)}) %collective-permute-start.25) | collective-permute-done | bytes 65568 | tf_op jit(solution)/shard_map/ppermute | solution.py:29
  58.6 0.7 %add_multiply_fusion = f32[128,256]{1,0:T(8,128)} fusion(bf16[128,256]{1,0:T(8,128)(2,1)S(1)} %collective-permute-done.25, bf16[128,256]{1,0:T(8,128)(2,1)S(1)} %add_convert_fusion.1), kind=kLoop, calls=%fused_computation.11 | loop fusion | flops 131072 | bytes 262144 | tf_op jit(solution)/shard_map/div | solution.py:572
  59.3 0.0 collective-permute-done.23.odd_ref
  59.3 0.9 %place.1 = (f32[256,256]{1,0:T(8,128)}, f32[256,256]{1,0:T(8,128)}) custom-call(s32[1]{0:T(128)} %bitcast.slab_ref, bf16[4,64,256]{2,1,0:T(8,128)(2,1)S(1)} %pad_maximum_fusion.4.even_ref, bf16[4,64,256]{2,1,0:T(8,128)(2,1)S(1)} %collective-permute-done.23.odd_ref), custom_call_target="tpu_custom_call" | custom-call | tf_op jit(solution)/shard_map/place/pallas_call | solution.py:381
  60.2 0.0 collective-permute-done.12.odd_adj_ref
  60.2 1.5 %back.1 = bf16[512,256]{1,0:T(8,128)(2,1)} custom-call(f32[512,256]{1,0:T(8,128)S(1)} %short.1.base_ref, bf16[4,256,256]{2,1,0:T(8,128)(2,1)S(1)} %pad_maximum_fusion.even_adj_ref, bf16[4,256,256]{2,1,0:T(8,128)(2,1)S(1)} %collective-permute-done.12.odd_adj_ref, bf16[256,512]{1,0:T(8,128)(2,1)S(1)} %get-tuple-element.59.refs_0_, ...), custom_call_target="tpu_custom_call" | custom-call | flops 536870912 | bytes 2097152 | tf_op jit(solution)/shard_map/back/pallas_call | solution.py:354
  (16 shorter events, 0.3 us)
Async XLA Ops:
  3.7 9.2 %collective-permute-start.4 = (bf16[768,512]{1,0:T(8,128)(2,1)S(1)}, bf16[768,512]{1,0:T(8,128)(2,1)S(1)}, u32[]{:S(2)}, u32[]{:S(2)}) collective-permute-start(bf16[768,512]{1,0:T(8,128)(2,1)S(1)} %get-tuple-element.55), channel_id=1, source_target_pairs={{0,4},{4,0},{8,12},{12,8},{16,20},{20,16},{24,28},{28,24},{1,5},{5... | collective-permute-start | bytes 2359304 | tf_op jit(solution)/shard_map/ppermute | solution.py:29
  4.3 5.9 %collective-permute-start.5 = (bf16[256,512]{1,0:T(8,128)(2,1)S(1)}, bf16[256,512]{1,0:T(8,128)(2,1)S(1)}, u32[]{:S(2)}, u32[]{:S(2)}) collective-permute-start(bf16[256,512]{1,0:T(8,128)(2,1)S(1)} %get-tuple-element.57), channel_id=1, source_target_pairs={{0,4},{4,0},{8,12},{12,8},{16,20},{20,16},{24,28},{28,24},{1,5},{5... | collective-permute-start | bytes 786440 | tf_op jit(solution)/shard_map/ppermute | solution.py:29
  4.7 19.0 %collective-permute-start.2 = (bf16[256,256]{1,0:T(8,128)(2,1)S(1)}, bf16[256,256]{1,0:T(8,128)(2,1)S(1)}, u32[]{:S(2)}, u32[]{:S(2)}) collective-permute-start(bf16[256,256]{1,0:T(8,128)(2,1)S(1)} %get-tuple-element.50), channel_id=1, source_target_pairs={{0,4},{4,8},{8,12},{12,16},{16,20},{20,24},{24,28},{28,0},{1,5},{5... | collective-permute-start | bytes 393224 | tf_op jit(solution)/shard_map/ppermute | solution.py:34
  5.2 18.5 %collective-permute-start.3 = (bf16[256,256]{1,0:T(8,128)(2,1)S(1)}, bf16[256,256]{1,0:T(8,128)(2,1)S(1)}, u32[]{:S(2)}, u32[]{:S(2)}) collective-permute-start(bf16[256,256]{1,0:T(8,128)(2,1)S(1)} %get-tuple-element.51), channel_id=1, source_target_pairs={{0,28},{4,0},{8,4},{12,8},{16,12},{20,16},{24,20},{28,24},{1,29},{... | collective-permute-start | bytes 393224 | tf_op jit(solution)/shard_map/ppermute | solution.py:34
  10.3 5.0 %collective-permute-start.6 = (bf16[256,256]{1,0:T(8,128)(2,1)S(1)}, bf16[256,256]{1,0:T(8,128)(2,1)S(1)}, u32[]{:S(2)}, u32[]{:S(2)}) collective-permute-start(bf16[256,256]{1,0:T(8,128)(2,1)S(1)} %get-tuple-element.77), channel_id=1, source_target_pairs={{0,16},{4,20},{8,24},{12,28},{16,0},{20,4},{24,8},{28,12},{1,17},{... | collective-permute-start | bytes 393224 | tf_op jit(solution)/shard_map/ppermute | solution.py:29
  12.4 5.0 %collective-permute-start.8 = (bf16[256,256]{1,0:T(8,128)(2,1)S(1)}, bf16[256,256]{1,0:T(8,128)(2,1)S(1)}, u32[]{:S(2)}, u32[]{:S(2)}) collective-permute-start(bf16[256,256]{1,0:T(8,128)(2,1)S(1)} %get-tuple-element.76), channel_id=1, source_target_pairs={{0,8},{4,12},{8,0},{12,4},{16,24},{20,28},{24,16},{28,20},{1,9},{5... | collective-permute-start | bytes 393224 | tf_op jit(solution)/shard_map/ppermute | solution.py:29
  17.4 6.4 %collective-permute-start.9 = (bf16[256,512]{1,0:T(8,128)(2,1)S(1)}, bf16[256,512]{1,0:T(8,128)(2,1)S(1)}, u32[]{:S(2)}, u32[]{:S(2)}) collective-permute-start(bf16[256,512]{1,0:T(8,128)(2,1)S(1)} %pad_maximum_fusion.2), channel_id=1, source_target_pairs={{0,16},{4,20},{8,24},{12,28},{16,0},{20,4},{24,8},{28,12},{1,17},{... | collective-permute-start | bytes 786440 | tf_op jit(solution)/shard_map/ppermute | solution.py:29
  17.6 6.5 %collective-permute-start.7 = (bf16[256,512]{1,0:T(8,128)(2,1)S(1)}, bf16[256,512]{1,0:T(8,128)(2,1)S(1)}, u32[]{:S(2)}, u32[]{:S(2)}) collective-permute-start(bf16[256,512]{1,0:T(8,128)(2,1)S(1)} %pad_maximum_fusion.1), channel_id=1, source_target_pairs={{0,8},{4,12},{8,0},{12,4},{16,24},{20,28},{24,16},{28,20},{1,9},{5... | collective-permute-start | bytes 786440 | tf_op jit(solution)/shard_map/ppermute | solution.py:29
  24.6 3.4 %collective-permute-start.13 = (f32[4,64,256]{2,1,0:T(8,128)S(1)}, f32[4,64,256]{2,1,0:T(8,128)S(1)}, u32[]{:S(2)}, u32[]{:S(2)}) collective-permute-start(f32[4,64,256]{2,1,0:T(8,128)S(1)} %get-tuple-element.64), channel_id=1, source_target_pairs={{0,4},{4,0},{8,12},{12,8},{16,20},{20,16},{24,28},{28,24},{1,5},{5... | collective-permute-start | bytes 786440 | tf_op jit(solution)/shard_map/ppermute | solution.py:29
  24.7 19.0 %collective-permute-start = (bf16[256,256]{1,0:T(8,128)(2,1)S(1)}, bf16[256,256]{1,0:T(8,128)(2,1)S(1)}, u32[]{:S(2)}, u32[]{:S(2)}) collective-permute-start(bf16[256,256]{1,0:T(8,128)(2,1)S(1)} %get-tuple-element.44.low_ref), channel_id=1, source_target_pairs={{0,28},{4,0},{8,4},{12,8},{16,12},{20,16},{24,20},{28,24},{1,29},{... | collective-permute-start | bytes 393224 | tf_op jit(solution)/shard_map/ppermute | solution.py:34
  27.7 16.2 %collective-permute-start.1 = (bf16[256,256]{1,0:T(8,128)(2,1)S(1)}, bf16[256,256]{1,0:T(8,128)(2,1)S(1)}, u32[]{:S(2)}, u32[]{:S(2)}) collective-permute-start(bf16[256,256]{1,0:T(8,128)(2,1)S(1)} %get-tuple-element.45.up_ref), channel_id=1, source_target_pairs={{0,4},{4,8},{8,12},{12,16},{16,20},{20,24},{24,28},{28,0},{1,5},{5... | collective-permute-start | bytes 393224 | tf_op jit(solution)/shard_map/ppermute | solution.py:34
  27.7 7.4 %collective-permute-start.10 = (bf16[1,256,256]{2,1,0:T(8,128)(2,1)S(1)}, bf16[1,256,256]{2,1,0:T(8,128)(2,1)S(1)}, u32[]{:S(2)}, u32[]{:S(2)}) collective-permute-start(bf16[1,256,256]{2,1,0:T(8,128)(2,1)S(1)} %bitcast.24), channel_id=1, source_target_pairs={{0,16},{4,20},{8,24},{12,28},{16,0},{20,4},{24,8},{28,12},{1,17},{... | collective-permute-start | bytes 393224 | tf_op jit(solution)/shard_map/ppermute | solution.py:29
  28.1 7.1 %collective-permute-start.14 = (bf16[64,256]{1,0:T(8,128)(2,1)S(1)}, bf16[64,256]{1,0:T(8,128)(2,1)S(1)}, u32[]{:S(2)}, u32[]{:S(2)}) collective-permute-start(bf16[64,256]{1,0:T(8,128)(2,1)S(1)} %get-tuple-element.78), channel_id=1, source_target_pairs={{0,24},{4,28},{8,16},{12,20},{16,8},{20,12},{24,0},{28,4},{1,25},{... | collective-permute-start | bytes 98312 | tf_op jit(solution)/shard_map/ppermute | solution.py:29
  29.3 8.0 %collective-permute-start.15 = (bf16[64,256]{1,0:T(8,128)(2,1)S(1)}, bf16[64,256]{1,0:T(8,128)(2,1)S(1)}, u32[]{:S(2)}, u32[]{:S(2)}) collective-permute-start(bf16[64,256]{1,0:T(8,128)(2,1)S(1)} %get-tuple-element.80), channel_id=1, source_target_pairs={{0,16},{4,20},{8,24},{12,28},{16,0},{20,4},{24,8},{28,12},{1,17},{... | collective-permute-start | bytes 98312 | tf_op jit(solution)/shard_map/ppermute | solution.py:29
  35.1 4.3 %collective-permute-start.16 = (bf16[64,256]{1,0:T(8,128)(2,1)S(1)}, bf16[64,256]{1,0:T(8,128)(2,1)S(1)}, u32[]{:S(2)}, u32[]{:S(2)}) collective-permute-start(bf16[64,256]{1,0:T(8,128)(2,1)S(1)} %get-tuple-element.79), channel_id=1, source_target_pairs={{0,8},{4,12},{8,0},{12,4},{16,24},{20,28},{24,16},{28,20},{1,9},{5... | collective-permute-start | bytes 98312 | tf_op jit(solution)/shard_map/ppermute | solution.py:29
  35.2 17.8 %collective-permute-start.11 = (bf16[2,256,256]{2,1,0:T(8,128)(2,1)S(1)}, bf16[2,256,256]{2,1,0:T(8,128)(2,1)S(1)}, u32[]{:S(2)}, u32[]{:S(2)}) collective-permute-start(bf16[2,256,256]{2,1,0:T(8,128)(2,1)S(1)} %pad_maximum_fusion.3), channel_id=1, source_target_pairs={{0,8},{4,12},{8,0},{12,4},{16,24},{20,28},{24,16},{28,20},{1,9},{5... | collective-permute-start | bytes 786440 | tf_op jit(solution)/shard_map/ppermute | solution.py:29
  39.4 5.9 %collective-permute-start.17 = (bf16[64,256]{1,0:T(8,128)(2,1)S(1)}, bf16[64,256]{1,0:T(8,128)(2,1)S(1)}, u32[]{:S(2)}, u32[]{:S(2)}) collective-permute-start(bf16[64,256]{1,0:T(8,128)(2,1)S(1)} %fusion.5), channel_id=1, source_target_pairs={{0,1},{1,0},{2,3},{3,2},{4,5},{5,4},{6,7},{7,6},{8,9},{9,8},{10,11... | collective-permute-start | bytes 98312 | tf_op jit(solution)/shard_map/ppermute | solution.py:29
  41.1 5.2 %collective-permute-start.18 = (bf16[64,256]{1,0:T(8,128)(2,1)S(1)}, bf16[64,256]{1,0:T(8,128)(2,1)S(1)}, u32[]{:S(2)}, u32[]{:S(2)}) collective-permute-start(bf16[64,256]{1,0:T(8,128)(2,1)S(1)} %fusion.5), channel_id=1, source_target_pairs={{0,2},{1,3},{2,0},{3,1},{4,6},{5,7},{6,4},{7,5},{8,10},{9,11},{10,... | collective-permute-start | bytes 98312 | tf_op jit(solution)/shard_map/ppermute | solution.py:29
  43.7 5.7 %collective-permute-start.19 = (bf16[64,256]{1,0:T(8,128)(2,1)S(1)}, bf16[64,256]{1,0:T(8,128)(2,1)S(1)}, u32[]{:S(2)}, u32[]{:S(2)}) collective-permute-start(bf16[64,256]{1,0:T(8,128)(2,1)S(1)} %fusion.5), channel_id=1, source_target_pairs={{0,3},{1,2},{2,1},{3,0},{4,7},{5,6},{6,5},{7,4},{8,11},{9,10},{10,... | collective-permute-start | bytes 98312 | tf_op jit(solution)/shard_map/ppermute | solution.py:29
  44.6 8.5 %collective-permute-start.24 = (bf16[128,256]{1,0:T(8,128)(2,1)S(1)}, bf16[128,256]{1,0:T(8,128)(2,1)S(1)}, u32[]{:S(2)}, u32[]{:S(2)}) collective-permute-start(bf16[128,256]{1,0:T(8,128)(2,1)S(1)} %convert_element_type.89), channel_id=1, source_target_pairs={{0,1},{1,0},{2,3},{3,2},{4,5},{5,4},{6,7},{7,6},{8,9},{9,8},{10,11... | collective-permute-start | bytes 196616 | tf_op jit(solution)/shard_map/ppermute | solution.py:29
  49.4 4.0 %collective-permute-start.21 = (bf16[64,256]{1,0:T(8,128)(2,1)S(1)}, bf16[64,256]{1,0:T(8,128)(2,1)S(1)}, u32[]{:S(2)}, u32[]{:S(2)}) collective-permute-start(bf16[64,256]{1,0:T(8,128)(2,1)S(1)} %add_convert_fusion.2), channel_id=1, source_target_pairs={{0,8},{4,12},{8,0},{12,4},{16,24},{20,28},{24,16},{28,20},{1,9},{5... | collective-permute-start | bytes 98312 | tf_op jit(solution)/shard_map/ppermute | solution.py:29
  49.5 5.0 %collective-permute-start.22 = (bf16[64,256]{1,0:T(8,128)(2,1)S(1)}, bf16[64,256]{1,0:T(8,128)(2,1)S(1)}, u32[]{:S(2)}, u32[]{:S(2)}) collective-permute-start(bf16[64,256]{1,0:T(8,128)(2,1)S(1)} %add_convert_fusion.2), channel_id=1, source_target_pairs={{0,24},{4,28},{8,16},{12,20},{16,8},{20,12},{24,0},{28,4},{1,25},{... | collective-permute-start | bytes 98312 | tf_op jit(solution)/shard_map/ppermute | solution.py:29
  52.3 3.9 %collective-permute-start.20 = (bf16[64,256]{1,0:T(8,128)(2,1)S(1)}, bf16[64,256]{1,0:T(8,128)(2,1)S(1)}, u32[]{:S(2)}, u32[]{:S(2)}) collective-permute-start(bf16[64,256]{1,0:T(8,128)(2,1)S(1)} %add_convert_fusion.2), channel_id=1, source_target_pairs={{0,16},{4,20},{8,24},{12,28},{16,0},{20,4},{24,8},{28,12},{1,17},{... | collective-permute-start | bytes 98312 | tf_op jit(solution)/shard_map/ppermute | solution.py:29
  53.1 7.1 %collective-permute-start.12 = (bf16[4,256,256]{2,1,0:T(8,128)(2,1)S(1)}, bf16[4,256,256]{2,1,0:T(8,128)(2,1)S(1)}, u32[]{:S(2)}, u32[]{:S(2)}) collective-permute-start(bf16[4,256,256]{2,1,0:T(8,128)(2,1)S(1)} %pad_maximum_fusion.even_adj_ref), channel_id=1, source_target_pairs={{0,4},{4,0},{8,12},{12,8},{16,20},{20,16},{24,28},{28,24},{1,5},{5... | collective-permute-start | bytes 1572872 | tf_op jit(solution)/shard_map/ppermute | solution.py:29
  53.2 5.4 %collective-permute-start.25 = (bf16[128,256]{1,0:T(8,128)(2,1)S(1)}, bf16[128,256]{1,0:T(8,128)(2,1)S(1)}, u32[]{:S(2)}, u32[]{:S(2)}) collective-permute-start(bf16[128,256]{1,0:T(8,128)(2,1)S(1)} %add_convert_fusion.1), channel_id=1, source_target_pairs={{0,2},{1,3},{2,0},{3,1},{4,6},{5,7},{6,4},{7,5},{8,10},{9,11},{10,... | collective-permute-start | bytes 196616 | tf_op jit(solution)/shard_map/ppermute | solution.py:29
  56.2 3.1 %collective-permute-start.23 = (bf16[4,64,256]{2,1,0:T(8,128)(2,1)S(1)}, bf16[4,64,256]{2,1,0:T(8,128)(2,1)S(1)}, u32[]{:S(2)}, u32[]{:S(2)}) collective-permute-start(bf16[4,64,256]{2,1,0:T(8,128)(2,1)S(1)} %pad_maximum_fusion.4.even_ref), channel_id=1, source_target_pairs={{0,4},{4,0},{8,12},{12,8},{16,20},{20,16},{24,28},{28,24},{1,5},{5... | collective-permute-start | bytes 393224 | tf_op jit(solution)/shard_map/ppermute | solution.py:29

commit v7 on v6

--- a/solution.py
+++ b/solution.py
@@ -389,16 +389,6 @@
     )(slab, even, odd)
 
 
-def doubling_gather(blocks):
-    count = lax.axis_size("slab")
-    bit = count // 2
-    while bit > 1:
-        moved = xor_permute(blocks, "slab", bit)
-        blocks = jnp.concatenate([blocks, moved], axis=0)
-        bit = bit // 2
-    return blocks
-
-
 def sum_replicas(value):
     bit = 1
     while bit < lax.axis_size("rep"):
@@ -563,7 +553,7 @@
     terms = plane_sum({offset: grads[i] for i, offset in enumerate(order)})
     own_grad = sum((term.astype(f32) for term in terms[1:]), terms[0])
 
-    adj_even = doubling_gather(adj[None])
+    adj_even = plane_gather(adj, order)
     adj_odd = xor_permute(adj_even, "slab", 1)
     grad_features = back_project(orders, order, base, adj_even, adj_odd, (odda, evena, oddb, evenb))
 

time: 62 us -> 61 us (0.984)
  waiting for transfers between devices: 20.7 us -> 16.4 us
  starting transfers between devices: 24.9 us -> 28.2 us
    ppermute x22 -> x23, waiting for transfers between devices: 20.7 us -> 14.3 us  [xor_permute(): lax.ppermute(value, axis, [(source, source ^ bits) for source in range(co...]
    ppermute x22 -> x23, starting transfers between devices: 18.2 us -> 21.5 us  [xor_permute(): lax.ppermute(value, axis, [(source, source ^ bits) for source in range(co...]
    ppermute x4, waiting for transfers between devices: 0.01 us -> 2.08 us  [shifted(): lax.ppermute(value, axis, [(source, (source + steps) % count) for source...]
  transfers between devices with their start and end apart: 26 -> 27, of which waited for: 12 -> 12; matrix products, arithmetic and copies ran while one was open for 2% -> 2% of each run, Pallas kernels for 14% -> 14%
where the time goes in v7:
time: 61 us; the launch traced here: 60.8 us
  starting transfers between devices  28.2 us (46%)
  waiting for transfers between devices  16.4 us (27%)
  Pallas kernels  13.8 us (23%)
  other arithmetic  1.35 us (2%)
  between operations  0.88 us (1%)
    ppermute x23, starting transfers between devices, xor_permute(): lax.ppermute(value, axis, [(source, source ^ bits) for source in range(co...  21.5 us
    ppermute x23, waiting for transfers between devices, xor_permute(): lax.ppermute(value, axis, [(source, source ^ bits) for source in range(co...  14.3 us
    ppermute x4, starting transfers between devices, shifted(): lax.ppermute(value, axis, [(source, (source + steps) % count) for source...  6.67 us
    pallas_call x1, Pallas kernels, edge_rows(): pl.pallas_call(functools.partial(edge_kernel, block), name='edges', out_s...  4.95 us
    pallas_call x3, Pallas kernels, next_tables(): pl.pallas_call(functools.partial(second_kernel, order), out_shape=(jax.Sh...  3.19 us
    ppermute x4, waiting for transfers between devices, shifted(): lax.ppermute(value, axis, [(source, (source + steps) % count) for source...  2.08 us
    pallas_call x1, Pallas kernels, first_tables(): pl.pallas_call(functools.partial(first_kernel, order, len(others)), name=...  1.73 us
    pallas_call x1, Pallas kernels, back_project(): pl.pallas_call(functools.partial(back_kernel, orders, order), name='back'...  1.55 us
  transfers between devices with their start and end apart: 27, of which 12 were waited for; matrix products, arithmetic and copies ran while one was open for 2% of the time, Pallas kernels for 14%

profile of v7, /device:TPU:0, one launch (start us, length us, event | category | flops | bytes accessed | tf_op | source)
XLA Modules:
  0.0 60.8 jit_solution(4612199732031347104)
XLA Ops:
  0.6 1.7 %first.1 = (bf16[256,512]{1,0:T(8,128)(2,1)S(1)}, bf16[256,512]{1,0:T(8,128)(2,1)S(1)}, f32[1024,16]{1,0:T(8,128)S(1)}, bf16[16,512]{1,0:T(8,128)(2,1)S(1)}, bf1...) custom-call(s32[1]{0:T(128)} %bitcast.slab_ref, ...), custom_call_target="tpu_custom_call" | custom-call | flops 134217728 | bytes 524288 | tf_op jit(solution)/shard_map/first/pallas_call | solution.py:136
  2.4 1.3 %shard_map.139 = (bf16[768,512]{1,0:T(8,128)(2,1)S(1)}, bf16[768,512]{1,0:T(8,128)(2,1)S(1)}) custom-call(s32[1]{0:T(128)} %bitcast.slab_ref, f32[1024,16]{1,0:T(8,128)S(1)} %get-tuple-element.52.k_cols, bf16[16,512]{1,0:T(8,128)(2,1)S(1)} %get-tuple-element.53.positions, bf16[512,256]{1,0:T(8,128)(2,1)S(1)} %get-tuple-element.40.rows_ref, ...), custom_call_target="tpu_custom_call" | custom-call | flops 402653184 | bytes 1572864 | tf_op jit(solution)/shard_map/pallas_call | solution.py:163
  3.7 0.6 collective-permute-start.4
  4.3 0.1 collective-permute-start.5
  4.4 0.3 rims.1
  4.7 0.5 collective-permute-start.2
  5.2 3.2 %collective-permute-start.3 = (bf16[256,256]{1,0:T(8,128)(2,1)S(1)}, bf16[256,256]{1,0:T(8,128)(2,1)S(1)}, u32[]{:S(2)}, u32[]{:S(2)}) collective-permute-start(bf16[256,256]{1,0:T(8,128)(2,1)S(1)} %get-tuple-element.51), channel_id=1, source_target_pairs={{0,28},{4,0},{8,4},{12,8},{16,12},{20,16},{24,20},{28,24},{1,29},{... | collective-permute-start | bytes 393224 | tf_op jit(solution)/shard_map/ppermute | solution.py:34
  8.3 0.5 shard_map.140
  8.9 1.3 %shard_map.138 = (bf16[768,512]{1,0:T(8,128)(2,1)S(1)}, f32[768,512]{1,0:T(8,128)S(1)}) custom-call(s32[1]{0:T(128)} %bitcast.slab_ref, f32[1024,16]{1,0:T(8,128)S(1)} %get-tuple-element.52.k_cols, bf16[16,512]{1,0:T(8,128)(2,1)S(1)} %get-tuple-element.53.positions, bf16[512,256]{1,0:T(8,128)(2,1)S(1)} %get-tuple-element.40.rows_ref, ...), custom_call_target="tpu_custom_call" | custom-call | flops 402653184 | bytes 1572864 | tf_op jit(solution)/shard_map/pallas_call | solution.py:163
  10.2 0.0 collective-permute-done.5
  10.2 0.1 add_convert_fusion
  10.3 2.0 %collective-permute-start.6 = (bf16[256,256]{1,0:T(8,128)(2,1)S(1)}, bf16[256,256]{1,0:T(8,128)(2,1)S(1)}, u32[]{:S(2)}, u32[]{:S(2)}) collective-permute-start(bf16[256,256]{1,0:T(8,128)(2,1)S(1)} %get-tuple-element.77), channel_id=1, source_target_pairs={{0,16},{4,20},{8,24},{12,28},{16,0},{20,4},{24,8},{28,12},{1,17},{... | collective-permute-start | bytes 393224 | tf_op jit(solution)/shard_map/ppermute | solution.py:29
  12.4 0.6 collective-permute-start.8
  13.0 0.3 fusion.7
  13.3 2.1 %collective-permute-done.6 = bf16[256,256]{1,0:T(8,128)(2,1)S(1)} collective-permute-done((bf16[256,256]{1,0:T(8,128)(2,1)S(1)}, bf16[256,256]{1,0:T(8,128)(2,1)S(1)}, u32[]{:S(2)}, u32[]{:S(2)}) %collective-permute-start.6) | collective-permute-done | bytes 131104 | tf_op jit(solution)/shard_map/ppermute | solution.py:29
  15.4 2.0 %collective-permute-done.8 = bf16[256,256]{1,0:T(8,128)(2,1)S(1)} collective-permute-done((bf16[256,256]{1,0:T(8,128)(2,1)S(1)}, bf16[256,256]{1,0:T(8,128)(2,1)S(1)}, u32[]{:S(2)}, u32[]{:S(2)}) %collective-permute-start.8) | collective-permute-done | bytes 131104 | tf_op jit(solution)/shard_map/ppermute | solution.py:29
  17.3 0.1 fusion
  17.4 0.1 collective-permute-start.9
  17.6 1.1 %collective-permute-start.7 = (bf16[256,512]{1,0:T(8,128)(2,1)S(1)}, bf16[256,512]{1,0:T(8,128)(2,1)S(1)}, u32[]{:S(2)}, u32[]{:S(2)}) collective-permute-start(bf16[256,512]{1,0:T(8,128)(2,1)S(1)} %pad_maximum_fusion.1), channel_id=1, source_target_pairs={{0,8},{4,12},{8,0},{12,4},{16,24},{20,28},{24,16},{28,20},{1,9},{5... | collective-permute-start | bytes 786440 | tf_op jit(solution)/shard_map/ppermute | solution.py:29
  18.7 5.0 %edges.1 = (f32[512,256]{1,0:T(8,128)S(1)}, bf16[256,256]{1,0:T(8,128)(2,1)S(1)}, bf16[256,256]{1,0:T(8,128)(2,1)S(1)}, f32[256,256]{1,0:T(8,128)S(1)}) custom-call(s32[1,4096]{1,0:T(1,128)S(1)} %get-tuple-element.36.src_ref, s32[1,4096]{1,0:T(1,128)S(1)} %get-tuple-element.37.dst_ref, f32[1,4096]{1,0:T(1,128)S(1)} %get-tuple-element.38.dist_ref, ...), custom_call_target="tpu_custom_call" | custom-call | flops 3221225472 | bytes 49152 | tf_op jit(solution)/shard_map/edges/pallas_call | solution.py:238
  23.7 0.0 collective-permute-done.3.upper_t
  23.7 0.1 collective-permute-done.9.refs_2_
  23.9 0.2 collective-permute-done.7.refs_1_
  24.1 0.5 share.1
  24.6 0.1 collective-permute-start.14
  24.7 3.0 %collective-permute-start = (bf16[256,256]{1,0:T(8,128)(2,1)S(1)}, bf16[256,256]{1,0:T(8,128)(2,1)S(1)}, u32[]{:S(2)}, u32[]{:S(2)}) collective-permute-start(bf16[256,256]{1,0:T(8,128)(2,1)S(1)} %get-tuple-element.44.low_ref), channel_id=1, source_target_pairs={{0,28},{4,0},{8,4},{12,8},{16,12},{20,16},{24,20},{28,24},{1,29},{... | collective-permute-start | bytes 393224 | tf_op jit(solution)/shard_map/ppermute | solution.py:34
  27.7 0.0 collective-permute-start.1
  27.7 0.0 collective-permute-done.14
  27.8 1.5 %collective-permute-start.15 = (bf16[64,256]{1,0:T(8,128)(2,1)S(1)}, bf16[64,256]{1,0:T(8,128)(2,1)S(1)}, u32[]{:S(2)}, u32[]{:S(2)}) collective-permute-start(bf16[64,256]{1,0:T(8,128)(2,1)S(1)} %get-tuple-element.78), channel_id=1, source_target_pairs={{0,24},{4,28},{8,16},{12,20},{16,8},{20,12},{24,0},{28,4},{1,25},{... | collective-permute-start | bytes 98312 | tf_op jit(solution)/shard_map/ppermute | solution.py:29
  29.3 0.3 collective-permute-start.16
  29.6 1.8 %collective-permute-start.17 = (bf16[64,256]{1,0:T(8,128)(2,1)S(1)}, bf16[64,256]{1,0:T(8,128)(2,1)S(1)}, u32[]{:S(2)}, u32[]{:S(2)}) collective-permute-start(bf16[64,256]{1,0:T(8,128)(2,1)S(1)} %get-tuple-element.79), channel_id=1, source_target_pairs={{0,8},{4,12},{8,0},{12,4},{16,24},{20,28},{24,16},{28,20},{1,9},{5... | collective-permute-start | bytes 98312 | tf_op jit(solution)/shard_map/ppermute | solution.py:29
  31.3 2.1 %collective-permute-done.1.below_ref = bf16[256,256]{1,0:T(8,128)(2,1)S(1)} collective-permute-done((bf16[256,256]{1,0:T(8,128)(2,1)S(1)}, bf16[256,256]{1,0:T(8,128)(2,1)S(1)}, u32[]{:S(2)}, u32[]{:S(2)}) %collective-permute-start.1) | collective-permute-done | bytes 131104 | tf_op jit(solution)/shard_map/ppermute | solution.py:34
  33.4 0.7 %short.1.base_ref = f32[512,256]{1,0:T(8,128)S(1)} custom-call(f32[512,256]{1,0:T(8,128)S(1)} %get-tuple-element.43.own_ref, bf16[256,256]{1,0:T(8,128)(2,1)S(1)} %collective-permute-done.above_ref, bf16[256,256]{1,0:T(8,128)(2,1)S(1)} %collective-permute-done.1.below_ref, s32[1,2,256]{2,1,0:T(2,128)S(1)} %get-tuple-element.41.lists_ref, ...), custom_call_target="tpu_custom_call" | custom-call | flops 268435456 | bytes 1048576 | tf_op jit(solution)/shard_map/short/pallas_call | solution.py:280
  34.1 0.4 collective-permute-start.10
  34.5 0.8 %collective-permute-start.11 = (bf16[256,256]{1,0:T(8,128)(2,1)S(1)}, bf16[256,256]{1,0:T(8,128)(2,1)S(1)}, u32[]{:S(2)}, u32[]{:S(2)}) collective-permute-start(bf16[256,256]{1,0:T(8,128)(2,1)S(1)} %get-tuple-element.58), channel_id=1, source_target_pairs={{0,8},{4,12},{8,0},{12,4},{16,24},{20,28},{24,16},{28,20},{1,9},{5... | collective-permute-start | bytes 393224 | tf_op jit(solution)/shard_map/ppermute | solution.py:29
  35.3 0.0 collective-permute-done.15
  35.3 2.5 %collective-permute-start.12 = (bf16[256,256]{1,0:T(8,128)(2,1)S(1)}, bf16[256,256]{1,0:T(8,128)(2,1)S(1)}, u32[]{:S(2)}, u32[]{:S(2)}) collective-permute-start(bf16[256,256]{1,0:T(8,128)(2,1)S(1)} %get-tuple-element.58), channel_id=1, source_target_pairs={{0,24},{4,28},{8,16},{12,20},{16,8},{20,12},{24,0},{28,4},{1,25},{... | collective-permute-start | bytes 393224 | tf_op jit(solution)/shard_map/ppermute | solution.py:29
  37.7 0.0 collective-permute-done.16
  37.7 1.6 %collective-permute-start.25 = (bf16[128,256]{1,0:T(8,128)(2,1)S(1)}, bf16[128,256]{1,0:T(8,128)(2,1)S(1)}, u32[]{:S(2)}, u32[]{:S(2)}) collective-permute-start(bf16[128,256]{1,0:T(8,128)(2,1)S(1)} %convert_element_type.89), channel_id=1, source_target_pairs={{0,1},{1,0},{2,3},{3,2},{4,5},{5,4},{6,7},{7,6},{8,9},{9,8},{10,11... | collective-permute-start | bytes 196616 | tf_op jit(solution)/shard_map/ppermute | solution.py:29
  39.3 0.0 collective-permute-done.17
  39.3 0.5 collective-permute-start.18
  39.9 0.7 %collective-permute-done.10 = bf16[256,256]{1,0:T(8,128)(2,1)S(1)} collective-permute-done((bf16[256,256]{1,0:T(8,128)(2,1)S(1)}, bf16[256,256]{1,0:T(8,128)(2,1)S(1)}, u32[]{:S(2)}, u32[]{:S(2)}) %collective-permute-start.10) | collective-permute-done | bytes 131104 | tf_op jit(solution)/shard_map/ppermute | solution.py:29
  40.5 2.6 %collective-permute-start.19 = (bf16[64,256]{1,0:T(8,128)(2,1)S(1)}, bf16[64,256]{1,0:T(8,128)(2,1)S(1)}, u32[]{:S(2)}, u32[]{:S(2)}) collective-permute-start(bf16[64,256]{1,0:T(8,128)(2,1)S(1)} %fusion.5), channel_id=1, source_target_pairs={{0,2},{1,3},{2,0},{3,1},{4,6},{5,7},{6,4},{7,5},{8,10},{9,11},{10,... | collective-permute-start | bytes 98312 | tf_op jit(solution)/shard_map/ppermute | solution.py:29
  43.1 0.0 collective-permute-done.11
  43.1 1.3 %collective-permute-start.20 = (bf16[64,256]{1,0:T(8,128)(2,1)S(1)}, bf16[64,256]{1,0:T(8,128)(2,1)S(1)}, u32[]{:S(2)}, u32[]{:S(2)}) collective-permute-start(bf16[64,256]{1,0:T(8,128)(2,1)S(1)} %fusion.5), channel_id=1, source_target_pairs={{0,3},{1,2},{2,1},{3,0},{4,7},{5,6},{6,5},{7,4},{8,11},{9,10},{10,... | collective-permute-start | bytes 98312 | tf_op jit(solution)/shard_map/ppermute | solution.py:29
  44.5 0.0 collective-permute-done.12
  44.5 0.1 pad_maximum_fusion.even_adj_ref
  44.5 0.1 collective-permute-start.13
  44.6 0.0 collective-permute-done.18
  44.6 0.7 %collective-permute-done.19 = bf16[64,256]{1,0:T(8,128)(2,1)S(1)} collective-permute-done((bf16[64,256]{1,0:T(8,128)(2,1)S(1)}, bf16[64,256]{1,0:T(8,128)(2,1)S(1)}, u32[]{:S(2)}, u32[]{:S(2)}) %collective-permute-start.19) | collective-permute-done | bytes 32800 | tf_op jit(solution)/shard_map/ppermute | solution.py:29
  45.3 3.5 %collective-permute-done.20 = bf16[64,256]{1,0:T(8,128)(2,1)S(1)} collective-permute-done((bf16[64,256]{1,0:T(8,128)(2,1)S(1)}, bf16[64,256]{1,0:T(8,128)(2,1)S(1)}, u32[]{:S(2)}, u32[]{:S(2)}) %collective-permute-start.20) | collective-permute-done | bytes 32800 | tf_op jit(solution)/shard_map/ppermute | solution.py:29
  48.9 0.1 collective-permute-start.21
  48.9 0.4 collective-permute-start.22
  49.4 3.1 %collective-permute-start.23 = (bf16[64,256]{1,0:T(8,128)(2,1)S(1)}, bf16[64,256]{1,0:T(8,128)(2,1)S(1)}, u32[]{:S(2)}, u32[]{:S(2)}) collective-permute-start(bf16[64,256]{1,0:T(8,128)(2,1)S(1)} %add_convert_fusion.2), channel_id=1, source_target_pairs={{0,24},{4,28},{8,16},{12,20},{16,8},{20,12},{24,0},{28,4},{1,25},{... | collective-permute-start | bytes 98312 | tf_op jit(solution)/shard_map/ppermute | solution.py:29
  52.4 0.0 collective-permute-done.25
  52.4 0.1 collective-permute-start.26
  52.5 0.3 collective-permute-done.21
  52.8 0.1 collective-permute-done.22
  52.9 1.7 %collective-permute-done.23 = bf16[64,256]{1,0:T(8,128)(2,1)S(1)} collective-permute-done((bf16[64,256]{1,0:T(8,128)(2,1)S(1)}, bf16[64,256]{1,0:T(8,128)(2,1)S(1)}, u32[]{:S(2)}, u32[]{:S(2)}) %collective-permute-start.23) | collective-permute-done | bytes 32800 | tf_op jit(solution)/shard_map/ppermute | solution.py:29
  54.7 0.1 collective-permute-start.24
  54.8 2.9 %collective-permute-done.26 = bf16[128,256]{1,0:T(8,128)(2,1)S(1)} collective-permute-done((bf16[128,256]{1,0:T(8,128)(2,1)S(1)}, bf16[128,256]{1,0:T(8,128)(2,1)S(1)}, u32[]{:S(2)}, u32[]{:S(2)}) %collective-permute-start.26) | collective-permute-done | bytes 65568 | tf_op jit(solution)/shard_map/ppermute | solution.py:29
  57.7 0.7 %add_multiply_fusion = f32[128,256]{1,0:T(8,128)} fusion(bf16[128,256]{1,0:T(8,128)(2,1)S(1)} %collective-permute-done.26, bf16[128,256]{1,0:T(8,128)(2,1)S(1)} %add_convert_fusion.1), kind=kLoop, calls=%fused_computation.10 | loop fusion | flops 131072 | bytes 262144 | tf_op jit(solution)/shard_map/div | solution.py:562
  58.4 0.9 %place.1 = (f32[256,256]{1,0:T(8,128)}, f32[256,256]{1,0:T(8,128)}) custom-call(s32[1]{0:T(128)} %bitcast.slab_ref, bf16[4,64,256]{2,1,0:T(8,128)(2,1)S(1)} %pad_maximum_fusion.3.even_ref, bf16[4,64,256]{2,1,0:T(8,128)(2,1)S(1)} %collective-permute-done.24.odd_ref), custom_call_target="tpu_custom_call" | custom-call | tf_op jit(solution)/shard_map/place/pallas_call | solution.py:381
  59.2 1.5 %back.1 = bf16[512,256]{1,0:T(8,128)(2,1)} custom-call(f32[512,256]{1,0:T(8,128)S(1)} %short.1.base_ref, bf16[4,256,256]{2,1,0:T(8,128)(2,1)S(1)} %pad_maximum_fusion.even_adj_ref, bf16[4,256,256]{2,1,0:T(8,128)(2,1)S(1)} %collective-permute-done.13.odd_adj_ref, bf16[256,512]{1,0:T(8,128)(2,1)S(1)} %get-tuple-element.59.refs_0_, ...), custom_call_target="tpu_custom_call" | custom-call | flops 536870912 | bytes 2097152 | tf_op jit(solution)/shard_map/back/pallas_call | solution.py:354
  (17 shorter events, 0.3 us)
Async XLA Ops:
  3.7 9.2 %collective-permute-start.4 = (bf16[768,512]{1,0:T(8,128)(2,1)S(1)}, bf16[768,512]{1,0:T(8,128)(2,1)S(1)}, u32[]{:S(2)}, u32[]{:S(2)}) collective-permute-start(bf16[768,512]{1,0:T(8,128)(2,1)S(1)} %get-tuple-element.55), channel_id=1, source_target_pairs={{0,4},{4,0},{8,12},{12,8},{16,20},{20,16},{24,28},{28,24},{1,5},{5... | collective-permute-start | bytes 2359304 | tf_op jit(solution)/shard_map/ppermute | solution.py:29
  4.3 5.9 %collective-permute-start.5 = (bf16[256,512]{1,0:T(8,128)(2,1)S(1)}, bf16[256,512]{1,0:T(8,128)(2,1)S(1)}, u32[]{:S(2)}, u32[]{:S(2)}) collective-permute-start(bf16[256,512]{1,0:T(8,128)(2,1)S(1)} %get-tuple-element.57), channel_id=1, source_target_pairs={{0,4},{4,0},{8,12},{12,8},{16,20},{20,16},{24,28},{28,24},{1,5},{5... | collective-permute-start | bytes 786440 | tf_op jit(solution)/shard_map/ppermute | solution.py:29
  4.7 19.0 %collective-permute-start.2 = (bf16[256,256]{1,0:T(8,128)(2,1)S(1)}, bf16[256,256]{1,0:T(8,128)(2,1)S(1)}, u32[]{:S(2)}, u32[]{:S(2)}) collective-permute-start(bf16[256,256]{1,0:T(8,128)(2,1)S(1)} %get-tuple-element.50), channel_id=1, source_target_pairs={{0,4},{4,8},{8,12},{12,16},{16,20},{20,24},{24,28},{28,0},{1,5},{5... | collective-permute-start | bytes 393224 | tf_op jit(solution)/shard_map/ppermute | solution.py:34
  5.2 18.5 %collective-permute-start.3 = (bf16[256,256]{1,0:T(8,128)(2,1)S(1)}, bf16[256,256]{1,0:T(8,128)(2,1)S(1)}, u32[]{:S(2)}, u32[]{:S(2)}) collective-permute-start(bf16[256,256]{1,0:T(8,128)(2,1)S(1)} %get-tuple-element.51), channel_id=1, source_target_pairs={{0,28},{4,0},{8,4},{12,8},{16,12},{20,16},{24,20},{28,24},{1,29},{... | collective-permute-start | bytes 393224 | tf_op jit(solution)/shard_map/ppermute | solution.py:34
  10.3 5.0 %collective-permute-start.6 = (bf16[256,256]{1,0:T(8,128)(2,1)S(1)}, bf16[256,256]{1,0:T(8,128)(2,1)S(1)}, u32[]{:S(2)}, u32[]{:S(2)}) collective-permute-start(bf16[256,256]{1,0:T(8,128)(2,1)S(1)} %get-tuple-element.77), channel_id=1, source_target_pairs={{0,16},{4,20},{8,24},{12,28},{16,0},{20,4},{24,8},{28,12},{1,17},{... | collective-permute-start | bytes 393224 | tf_op jit(solution)/shard_map/ppermute | solution.py:29
  12.4 5.0 %collective-permute-start.8 = (bf16[256,256]{1,0:T(8,128)(2,1)S(1)}, bf16[256,256]{1,0:T(8,128)(2,1)S(1)}, u32[]{:S(2)}, u32[]{:S(2)}) collective-permute-start(bf16[256,256]{1,0:T(8,128)(2,1)S(1)} %get-tuple-element.76), channel_id=1, source_target_pairs={{0,8},{4,12},{8,0},{12,4},{16,24},{20,28},{24,16},{28,20},{1,9},{5... | collective-permute-start | bytes 393224 | tf_op jit(solution)/shard_map/ppermute | solution.py:29
  17.4 6.4 %collective-permute-start.9 = (bf16[256,512]{1,0:T(8,128)(2,1)S(1)}, bf16[256,512]{1,0:T(8,128)(2,1)S(1)}, u32[]{:S(2)}, u32[]{:S(2)}) collective-permute-start(bf16[256,512]{1,0:T(8,128)(2,1)S(1)} %pad_maximum_fusion.2), channel_id=1, source_target_pairs={{0,16},{4,20},{8,24},{12,28},{16,0},{20,4},{24,8},{28,12},{1,17},{... | collective-permute-start | bytes 786440 | tf_op jit(solution)/shard_map/ppermute | solution.py:29
  17.6 6.5 %collective-permute-start.7 = (bf16[256,512]{1,0:T(8,128)(2,1)S(1)}, bf16[256,512]{1,0:T(8,128)(2,1)S(1)}, u32[]{:S(2)}, u32[]{:S(2)}) collective-permute-start(bf16[256,512]{1,0:T(8,128)(2,1)S(1)} %pad_maximum_fusion.1), channel_id=1, source_target_pairs={{0,8},{4,12},{8,0},{12,4},{16,24},{20,28},{24,16},{28,20},{1,9},{5... | collective-permute-start | bytes 786440 | tf_op jit(solution)/shard_map/ppermute | solution.py:29
  24.6 3.1 %collective-permute-start.14 = (f32[4,64,256]{2,1,0:T(8,128)S(1)}, f32[4,64,256]{2,1,0:T(8,128)S(1)}, u32[]{:S(2)}, u32[]{:S(2)}) collective-permute-start(f32[4,64,256]{2,1,0:T(8,128)S(1)} %get-tuple-element.64), channel_id=1, source_target_pairs={{0,4},{4,0},{8,12},{12,8},{16,20},{20,16},{24,28},{28,24},{1,5},{5... | collective-permute-start | bytes 786440 | tf_op jit(solution)/shard_map/ppermute | solution.py:29
  24.7 6.6 %collective-permute-start = (bf16[256,256]{1,0:T(8,128)(2,1)S(1)}, bf16[256,256]{1,0:T(8,128)(2,1)S(1)}, u32[]{:S(2)}, u32[]{:S(2)}) collective-permute-start(bf16[256,256]{1,0:T(8,128)(2,1)S(1)} %get-tuple-element.44.low_ref), channel_id=1, source_target_pairs={{0,28},{4,0},{8,4},{12,8},{16,12},{20,16},{24,20},{28,24},{1,29},{... | collective-permute-start | bytes 393224 | tf_op jit(solution)/shard_map/ppermute | solution.py:34
  27.7 5.7 %collective-permute-start.1 = (bf16[256,256]{1,0:T(8,128)(2,1)S(1)}, bf16[256,256]{1,0:T(8,128)(2,1)S(1)}, u32[]{:S(2)}, u32[]{:S(2)}) collective-permute-start(bf16[256,256]{1,0:T(8,128)(2,1)S(1)} %get-tuple-element.45.up_ref), channel_id=1, source_target_pairs={{0,4},{4,8},{8,12},{12,16},{16,20},{20,24},{24,28},{28,0},{1,5},{5... | collective-permute-start | bytes 393224 | tf_op jit(solution)/shard_map/ppermute | solution.py:34
  27.8 7.5 %collective-permute-start.15 = (bf16[64,256]{1,0:T(8,128)(2,1)S(1)}, bf16[64,256]{1,0:T(8,128)(2,1)S(1)}, u32[]{:S(2)}, u32[]{:S(2)}) collective-permute-start(bf16[64,256]{1,0:T(8,128)(2,1)S(1)} %get-tuple-element.78), channel_id=1, source_target_pairs={{0,24},{4,28},{8,16},{12,20},{16,8},{20,12},{24,0},{28,4},{1,25},{... | collective-permute-start | bytes 98312 | tf_op jit(solution)/shard_map/ppermute | solution.py:29
  29.3 8.5 %collective-permute-start.16 = (bf16[64,256]{1,0:T(8,128)(2,1)S(1)}, bf16[64,256]{1,0:T(8,128)(2,1)S(1)}, u32[]{:S(2)}, u32[]{:S(2)}) collective-permute-start(bf16[64,256]{1,0:T(8,128)(2,1)S(1)} %get-tuple-element.80), channel_id=1, source_target_pairs={{0,16},{4,20},{8,24},{12,28},{16,0},{20,4},{24,8},{28,12},{1,17},{... | collective-permute-start | bytes 98312 | tf_op jit(solution)/shard_map/ppermute | solution.py:29
  29.6 9.8 %collective-permute-start.17 = (bf16[64,256]{1,0:T(8,128)(2,1)S(1)}, bf16[64,256]{1,0:T(8,128)(2,1)S(1)}, u32[]{:S(2)}, u32[]{:S(2)}) collective-permute-start(bf16[64,256]{1,0:T(8,128)(2,1)S(1)} %get-tuple-element.79), channel_id=1, source_target_pairs={{0,8},{4,12},{8,0},{12,4},{16,24},{20,28},{24,16},{28,20},{1,9},{5... | collective-permute-start | bytes 98312 | tf_op jit(solution)/shard_map/ppermute | solution.py:29
  34.1 6.4 %collective-permute-start.10 = (bf16[256,256]{1,0:T(8,128)(2,1)S(1)}, bf16[256,256]{1,0:T(8,128)(2,1)S(1)}, u32[]{:S(2)}, u32[]{:S(2)}) collective-permute-start(bf16[256,256]{1,0:T(8,128)(2,1)S(1)} %get-tuple-element.58), channel_id=1, source_target_pairs={{0,16},{4,20},{8,24},{12,28},{16,0},{20,4},{24,8},{28,12},{1,17},{... | collective-permute-start | bytes 393224 | tf_op jit(solution)/shard_map/ppermute | solution.py:29
  34.5 8.7 %collective-permute-start.11 = (bf16[256,256]{1,0:T(8,128)(2,1)S(1)}, bf16[256,256]{1,0:T(8,128)(2,1)S(1)}, u32[]{:S(2)}, u32[]{:S(2)}) collective-permute-start(bf16[256,256]{1,0:T(8,128)(2,1)S(1)} %get-tuple-element.58), channel_id=1, source_target_pairs={{0,8},{4,12},{8,0},{12,4},{16,24},{20,28},{24,16},{28,20},{1,9},{5... | collective-permute-start | bytes 393224 | tf_op jit(solution)/shard_map/ppermute | solution.py:29
  35.3 9.2 %collective-permute-start.12 = (bf16[256,256]{1,0:T(8,128)(2,1)S(1)}, bf16[256,256]{1,0:T(8,128)(2,1)S(1)}, u32[]{:S(2)}, u32[]{:S(2)}) collective-permute-start(bf16[256,256]{1,0:T(8,128)(2,1)S(1)} %get-tuple-element.58), channel_id=1, source_target_pairs={{0,24},{4,28},{8,16},{12,20},{16,8},{20,12},{24,0},{28,4},{1,25},{... | collective-permute-start | bytes 393224 | tf_op jit(solution)/shard_map/ppermute | solution.py:29
  37.7 14.7 %collective-permute-start.25 = (bf16[128,256]{1,0:T(8,128)(2,1)S(1)}, bf16[128,256]{1,0:T(8,128)(2,1)S(1)}, u32[]{:S(2)}, u32[]{:S(2)}) collective-permute-start(bf16[128,256]{1,0:T(8,128)(2,1)S(1)} %convert_element_type.89), channel_id=1, source_target_pairs={{0,1},{1,0},{2,3},{3,2},{4,5},{5,4},{6,7},{7,6},{8,9},{9,8},{10,11... | collective-permute-start | bytes 196616 | tf_op jit(solution)/shard_map/ppermute | solution.py:29
  39.3 5.3 %collective-permute-start.18 = (bf16[64,256]{1,0:T(8,128)(2,1)S(1)}, bf16[64,256]{1,0:T(8,128)(2,1)S(1)}, u32[]{:S(2)}, u32[]{:S(2)}) collective-permute-start(bf16[64,256]{1,0:T(8,128)(2,1)S(1)} %fusion.5), channel_id=1, source_target_pairs={{0,1},{1,0},{2,3},{3,2},{4,5},{5,4},{6,7},{7,6},{8,9},{9,8},{10,11... | collective-permute-start | bytes 98312 | tf_op jit(solution)/shard_map/ppermute | solution.py:29
  40.5 4.8 %collective-permute-start.19 = (bf16[64,256]{1,0:T(8,128)(2,1)S(1)}, bf16[64,256]{1,0:T(8,128)(2,1)S(1)}, u32[]{:S(2)}, u32[]{:S(2)}) collective-permute-start(bf16[64,256]{1,0:T(8,128)(2,1)S(1)} %fusion.5), channel_id=1, source_target_pairs={{0,2},{1,3},{2,0},{3,1},{4,6},{5,7},{6,4},{7,5},{8,10},{9,11},{10,... | collective-permute-start | bytes 98312 | tf_op jit(solution)/shard_map/ppermute | solution.py:29
  43.1 5.7 %collective-permute-start.20 = (bf16[64,256]{1,0:T(8,128)(2,1)S(1)}, bf16[64,256]{1,0:T(8,128)(2,1)S(1)}, u32[]{:S(2)}, u32[]{:S(2)}) collective-permute-start(bf16[64,256]{1,0:T(8,128)(2,1)S(1)} %fusion.5), channel_id=1, source_target_pairs={{0,3},{1,2},{2,1},{3,0},{4,7},{5,6},{6,5},{7,4},{8,11},{9,10},{10,... | collective-permute-start | bytes 98312 | tf_op jit(solution)/shard_map/ppermute | solution.py:29
  44.5 14.7 %collective-permute-start.13 = (bf16[4,256,256]{2,1,0:T(8,128)(2,1)S(1)}, bf16[4,256,256]{2,1,0:T(8,128)(2,1)S(1)}, u32[]{:S(2)}, u32[]{:S(2)}) collective-permute-start(bf16[4,256,256]{2,1,0:T(8,128)(2,1)S(1)} %pad_maximum_fusion.even_adj_ref), channel_id=1, source_target_pairs={{0,4},{4,0},{8,12},{12,8},{16,20},{20,16},{24,28},{28,24},{1,5},{5... | collective-permute-start | bytes 1572872 | tf_op jit(solution)/shard_map/ppermute | solution.py:29
  48.9 4.0 %collective-permute-start.21 = (bf16[64,256]{1,0:T(8,128)(2,1)S(1)}, bf16[64,256]{1,0:T(8,128)(2,1)S(1)}, u32[]{:S(2)}, u32[]{:S(2)}) collective-permute-start(bf16[64,256]{1,0:T(8,128)(2,1)S(1)} %add_convert_fusion.2), channel_id=1, source_target_pairs={{0,16},{4,20},{8,24},{12,28},{16,0},{20,4},{24,8},{28,12},{1,17},{... | collective-permute-start | bytes 98312 | tf_op jit(solution)/shard_map/ppermute | solution.py:29
  48.9 4.0 %collective-permute-start.22 = (bf16[64,256]{1,0:T(8,128)(2,1)S(1)}, bf16[64,256]{1,0:T(8,128)(2,1)S(1)}, u32[]{:S(2)}, u32[]{:S(2)}) collective-permute-start(bf16[64,256]{1,0:T(8,128)(2,1)S(1)} %add_convert_fusion.2), channel_id=1, source_target_pairs={{0,8},{4,12},{8,0},{12,4},{16,24},{20,28},{24,16},{28,20},{1,9},{5... | collective-permute-start | bytes 98312 | tf_op jit(solution)/shard_map/ppermute | solution.py:29
  49.4 5.3 %collective-permute-start.23 = (bf16[64,256]{1,0:T(8,128)(2,1)S(1)}, bf16[64,256]{1,0:T(8,128)(2,1)S(1)}, u32[]{:S(2)}, u32[]{:S(2)}) collective-permute-start(bf16[64,256]{1,0:T(8,128)(2,1)S(1)} %add_convert_fusion.2), channel_id=1, source_target_pairs={{0,24},{4,28},{8,16},{12,20},{16,8},{20,12},{24,0},{28,4},{1,25},{... | collective-permute-start | bytes 98312 | tf_op jit(solution)/shard_map/ppermute | solution.py:29
  52.4 5.2 %collective-permute-start.26 = (bf16[128,256]{1,0:T(8,128)(2,1)S(1)}, bf16[128,256]{1,0:T(8,128)(2,1)S(1)}, u32[]{:S(2)}, u32[]{:S(2)}) collective-permute-start(bf16[128,256]{1,0:T(8,128)(2,1)S(1)} %add_convert_fusion.1), channel_id=1, source_target_pairs={{0,2},{1,3},{2,0},{3,1},{4,6},{5,7},{6,4},{7,5},{8,10},{9,11},{10,... | collective-permute-start | bytes 196616 | tf_op jit(solution)/shard_map/ppermute | solution.py:29
  54.7 3.7 %collective-permute-start.24 = (bf16[4,64,256]{2,1,0:T(8,128)(2,1)S(1)}, bf16[4,64,256]{2,1,0:T(8,128)(2,1)S(1)}, u32[]{:S(2)}, u32[]{:S(2)}) collective-permute-start(bf16[4,64,256]{2,1,0:T(8,128)(2,1)S(1)} %pad_maximum_fusion.3.even_ref), channel_id=1, source_target_pairs={{0,4},{4,0},{8,12},{12,8},{16,20},{20,16},{24,28},{28,24},{1,5},{5... | collective-permute-start | bytes 393224 | tf_op jit(solution)/shard_map/ppermute | solution.py:29

commit v8 on v7

--- a/solution.py
+++ b/solution.py
@@ -29,9 +29,9 @@
     return lax.ppermute(value, axis, [(source, source ^ bits) for source in range(count)])
 
 
-def shifted(value, axis, steps):
-    count = lax.axis_size(axis)
-    return lax.ppermute(value, axis, [(source, (source + steps) % count) for source in range(count)])
+def across_chips(value):
+    count = lax.axis_size("slab")
+    return lax.ppermute(value, "slab", [(source, (source + 2 * (source % 2) - 1) % count) for source in range(count)])
 
 
 def halving_order(count):
@@ -180,16 +180,23 @@
     return (rows == indices).astype(f32).astype(bf16)
 
 
-def rims_kernel(rows_ref, lists_ref, rows_t_ref, prev_ref, next_ref):
+def rim_lists(slab_ref, lists_ref):
+    core = slab_ref[0] & 1
+    lists = lists_ref[0]
+    before, after = lists[0:1, :], lists[1:2, :]
+    return jnp.where(core == 0, after, before), jnp.where(core == 0, before, after)
+
+
+def rims_kernel(slab_ref, rows_ref, lists_ref, rows_t_ref, pair_ref, cross_ref):
     atoms = rows_ref.shape[0]
-    lists = lists_ref[0]
+    pair, cross = rim_lists(slab_ref, lists_ref)
     rows_t = rows_ref[...].T
     rows_t_ref[...] = rows_t
-    prev_ref[...] = dot(rows_t, one_hot(atoms, lists[0:1, :])).astype(bf16)
-    next_ref[...] = dot(rows_t, one_hot(atoms, lists[1:2, :])).astype(bf16)
-
-
-def rim_features(rows, lists):
+    pair_ref[...] = dot(rows_t, one_hot(atoms, pair)).astype(bf16)
+    cross_ref[...] = dot(rows_t, one_hot(atoms, cross)).astype(bf16)
+
+
+def rim_features(slab, rows, lists):
     atoms, channels = rows.shape
     rim = lists.shape[2]
     return pl.pallas_call(
@@ -200,18 +207,21 @@
             jax.ShapeDtypeStruct((channels, rim), bf16),
             jax.ShapeDtypeStruct((channels, rim), bf16),
         ),
-        in_specs=[VMEM] * 2,
+        in_specs=[SMEM] + [VMEM] * 2,
         out_specs=(VMEM,) * 3,
         compiler_params=params(),
         cost_estimate=pl.CostEstimate(
             flops=4 * atoms * channels * rim, bytes_accessed=4 * atoms * channels, transcendentals=0
         ),
-    )(rows, lists)
-
-
-def edge_kernel(block, src_ref, dst_ref, dist_ref, cot_ref, rows_t_ref, own_ref, low_ref, up_ref, grad_ref, total):
+    )(slab, rows, lists)
+
+
+def edge_kernel(
+    block, slab_ref, src_ref, dst_ref, dist_ref, cot_ref, rows_t_ref, own_ref, pair_ref, cross_ref, grad_ref, total
+):
     atoms, _ = cot_ref.shape
-    rim = low_ref.shape[0]
+    rim = pair_ref.shape[0]
+    core = slab_ref[0] & 1
     edges = src_ref.shape[1]
     cot_t = cot_ref[...].T
     for start in range(0, edges, block):
@@ -224,13 +234,13 @@
         total[...] = part if start == 0 else total[...] + part
     own = total[:atoms, :]
     own_ref[...] = own
-    low_ref[...] = total[atoms : atoms + rim, :].astype(bf16)
-    up_ref[...] = total[atoms + rim :, :].astype(bf16)
+    pair_ref[...] = total[pl.ds(pl.multiple_of(atoms + (1 - core) * rim, 8), rim), :].astype(bf16)
+    cross_ref[...] = total[pl.ds(pl.multiple_of(atoms + core * rim, 8), rim), :].astype(bf16)
     high, low = halves(own)
     grad_ref[...] = dot(rows_t_ref[...], high) + dot(rows_t_ref[...], low)
 
 
-def edge_rows(sources, targets, lengths, cotan, rows_t, rim):
+def edge_rows(slab, sources, targets, lengths, cotan, rows_t, rim):
     atoms, channels = cotan.shape
     edges = sources.shape[1]
     rows = atoms + 2 * rim
@@ -244,14 +254,14 @@
             jax.ShapeDtypeStruct((rim, channels), bf16),
             jax.ShapeDtypeStruct((channels, channels), f32),
         ),
-        in_specs=[VMEM] * 5,
+        in_specs=[SMEM] + [VMEM] * 5,
         out_specs=(VMEM,) * 4,
         scratch_shapes=[pltpu.VMEM((rows, channels), f32)],
         compiler_params=params(),
         cost_estimate=pl.CostEstimate(
             flops=2 * edges * (rows + atoms) * channels, bytes_accessed=edges * 12, transcendentals=0
         ),
-    )(sources, targets, lengths, cotan, rows_t)
+    )(slab, sources, targets, lengths, cotan, rows_t)
 
 
 def split_blocks(order, slab, values, send_ref, keep_ref, blocks):
@@ -265,33 +275,33 @@
         send_ref[place] = blocks[slab ^ offset ^ 1]
 
 
-def short_kernel(own_ref, above_ref, below_ref, lists_ref, cot_ref, w_ref, base_ref):
+def short_kernel(slab_ref, own_ref, pair_ref, cross_ref, lists_ref, cot_ref, w_ref, base_ref):
     atoms = own_ref.shape[0]
-    lists = lists_ref[0]
-    owned = own_ref[...] + dot(one_hot(atoms, lists[1:2, :]), above_ref[...])
-    owned = owned + dot(one_hot(atoms, lists[0:1, :]), below_ref[...])
+    pair, cross = rim_lists(slab_ref, lists_ref)
+    owned = own_ref[...] + dot(one_hot(atoms, pair), pair_ref[...])
+    owned = owned + dot(one_hot(atoms, cross), cross_ref[...])
     high, low = halves(owned)
     w = w_ref[...]
     base_ref[...] = cot_ref[...].astype(f32) + (dot(high, w, 1, 1) + dot(low, w, 1, 1))
 
 
-def short_range(own, above, below, lists, cotan, w_short):
+def short_range(slab, own, pair, cross, lists, cotan, w_short):
     atoms, channels = cotan.shape
     return pl.pallas_call(
         short_kernel,
         name="short",
         out_shape=jax.ShapeDtypeStruct((atoms, channels), f32),
-        in_specs=[VMEM] * 6,
+        in_specs=[SMEM] + [VMEM] * 6,
         out_specs=VMEM,
         compiler_params=params(),
         cost_estimate=pl.CostEstimate(
             flops=8 * atoms * channels * channels, bytes_accessed=8 * atoms * channels, transcendentals=0
         ),
-    )(own, above, below, lists, cotan, w_short)
+    )(slab, own, pair, cross, lists, cotan, w_short)
 
 
 def share_kernel(
-    order, norm, count, slab_ref, filter_ref, w_ref, grad_ref, lower_t, upper_t, low_ref, up_ref, *refs
+    order, norm, count, slab_ref, filter_ref, w_ref, grad_ref, pair_t, cross_t, pair_ref, cross_ref, *refs
 ):
     parts, (adj_ref, gfilter_ref, send_ref, keep_ref, blocks) = refs[:count], refs[count:]
     channels = w_ref.shape[0]
@@ -305,7 +315,7 @@
     double = jnp.concatenate([k_filter, k_filter], axis=0) * norm
     filtered, filtered_low = halves((structure * double).T)
     wout = dot(filtered, moved) + (dot(filtered, moved_low) + dot(filtered_low, moved))
-    wshort = grad_ref[...] + (dot(lower_t[...], low_ref[...]) + dot(upper_t[...], up_ref[...]))
+    wshort = grad_ref[...] + (dot(pair_t[...], pair_ref[...]) + dot(cross_t[...], cross_ref[...]))
     split_blocks(order, slab_ref[0], (wout, wshort), send_ref, keep_ref, blocks)
     adj_ref[...] = (response * double).T.astype(bf16)
     product = structure * response
@@ -538,17 +548,17 @@
             blocks[offset] = paired[i * 2 * share : (i + 1) * 2 * share]
     parts = folded_sum(blocks)
 
-    rows_t, to_prev, to_next = rim_features(rows, lists)
-    lower_t = shifted(to_next, "slab", 1)
-    upper_t = shifted(to_prev, "slab", -1)
-    own_rows, low, up, wshort = edge_rows(src, dst, dist, cotan, rows_t, lists.shape[2])
-    short_terms = (wshort, lower_t, upper_t, low, up)
+    rows_t, to_pair, to_cross = rim_features(slab, rows, lists)
+    cross_t = across_chips(to_cross)
+    pair_t = xor_permute(to_pair, "slab", 1)
+    own_rows, pair_rows, cross_rows, wshort = edge_rows(slab, src, dst, dist, cotan, rows_t, lists.shape[2])
+    short_terms = (wshort, pair_t, cross_t, pair_rows, cross_rows)
     adj, gfilter, send, keep = own_share(order, norm, slab, own_filter, w_out, short_terms, parts)
     grads = keep + xor_permute(send, "slab", 1)
 
-    from_above = shifted(low, "slab", -1)
-    from_below = shifted(up, "slab", 1)
-    base = short_range(own_rows, from_above, from_below, lists, cotan, w_short)
+    from_cross = across_chips(cross_rows)
+    from_pair = xor_permute(pair_rows, "slab", 1)
+    base = short_range(slab, own_rows, from_pair, from_cross, lists, cotan, w_short)
 
     terms = plane_sum({offset: grads[i] for i, offset in enumerate(order)})
     own_grad = sum((term.astype(f32) for term in terms[1:]), terms[0])

time: 61 us -> 59.3 us (0.972)
  waiting for transfers between devices: 16.4 us -> 14.4 us
    ppermute x23 -> x25, starting transfers between devices: 21.5 us -> 23.1 us  [xor_permute(): lax.ppermute(value, axis, [(source, source ^ bits) for source in range(co...]
    ppermute x4 -> x2, starting transfers between devices: 6.67 us -> 5.4 us  [across_chips(): lax.ppermute(value, 'slab', [(source, (source + 2 * (source % 2) - 1) % c...]
    ppermute x23 -> x25, waiting for transfers between devices: 14.3 us -> 13.3 us  [xor_permute(): lax.ppermute(value, axis, [(source, source ^ bits) for source in range(co...]
    ppermute x4 -> x2, waiting for transfers between devices: 2.08 us -> 1.14 us  [across_chips(): lax.ppermute(value, 'slab', [(source, (source + 2 * (source % 2) - 1) % c...]
  transfers between devices with their start and end apart: 27 -> 27, of which waited for: 12 -> 9; matrix products, arithmetic and copies ran while one was open for 2% -> 2% of each run, Pallas kernels for 14% -> 15%
where the time goes in v8:
time: 59.3 us; the launch traced here: 59.1 us
  starting transfers between devices  28.5 us (48%)
  waiting for transfers between devices  14.4 us (24%)
  Pallas kernels  13.9 us (23%)
  other arithmetic  1.31 us (2%)
  between operations  0.87 us (1%)
    ppermute x25, starting transfers between devices, xor_permute(): lax.ppermute(value, axis, [(source, source ^ bits) for source in range(co...  23.1 us
    ppermute x25, waiting for transfers between devices, xor_permute(): lax.ppermute(value, axis, [(source, source ^ bits) for source in range(co...  13.3 us
    ppermute x2, starting transfers between devices, across_chips(): lax.ppermute(value, 'slab', [(source, (source + 2 * (source % 2) - 1) % c...  5.4 us
    pallas_call x1, Pallas kernels, edge_rows(): pl.pallas_call(functools.partial(edge_kernel, block), name='edges', out_s...  5.02 us
    pallas_call x3, Pallas kernels, next_tables(): pl.pallas_call(functools.partial(second_kernel, order), out_shape=(jax.Sh...  3.21 us
    pallas_call x1, Pallas kernels, first_tables(): pl.pallas_call(functools.partial(first_kernel, order, len(others)), name=...  1.72 us
    pallas_call x1, Pallas kernels, back_project(): pl.pallas_call(functools.partial(back_kernel, orders, order), name='back'...  1.55 us
  transfers between devices with their start and end apart: 27, of which 9 were waited for; matrix products, arithmetic and copies ran while one was open for 2% of the time, Pallas kernels for 15%

profile of v8, /device:TPU:0, one launch (start us, length us, event | category | flops | bytes accessed | tf_op | source)
XLA Modules:
  0.0 59.1 jit_solution(16257154199352660964)
XLA Ops:
  0.6 1.7 %first.1 = (bf16[256,512]{1,0:T(8,128)(2,1)S(1)}, bf16[256,512]{1,0:T(8,128)(2,1)S(1)}, f32[1024,16]{1,0:T(8,128)S(1)}, bf16[16,512]{1,0:T(8,128)(2,1)S(1)}, bf1...) custom-call(s32[1]{0:T(128)} %bitcast.slab_ref, ...), custom_call_target="tpu_custom_call" | custom-call | flops 134217728 | bytes 524288 | tf_op jit(solution)/shard_map/first/pallas_call | solution.py:136
  2.4 1.3 %shard_map.139 = (bf16[768,512]{1,0:T(8,128)(2,1)S(1)}, bf16[768,512]{1,0:T(8,128)(2,1)S(1)}) custom-call(s32[1]{0:T(128)} %bitcast.slab_ref, f32[1024,16]{1,0:T(8,128)S(1)} %get-tuple-element.52.k_cols, bf16[16,512]{1,0:T(8,128)(2,1)S(1)} %get-tuple-element.53.positions, bf16[512,256]{1,0:T(8,128)(2,1)S(1)} %get-tuple-element.40.rows_ref, ...), custom_call_target="tpu_custom_call" | custom-call | flops 402653184 | bytes 1572864 | tf_op jit(solution)/shard_map/pallas_call | solution.py:163
  3.7 0.6 collective-permute-start.4
  4.3 0.1 collective-permute-start.5
  4.4 0.3 rims.1
  4.7 0.5 collective-permute-start.2
  5.2 3.5 %collective-permute-start.3 = (bf16[256,256]{1,0:T(8,128)(2,1)S(1)}, bf16[256,256]{1,0:T(8,128)(2,1)S(1)}, u32[]{:S(2)}, u32[]{:S(2)}) collective-permute-start(bf16[256,256]{1,0:T(8,128)(2,1)S(1)} %get-tuple-element.51), channel_id=1, source_target_pairs={{0,28},{4,8},{8,4},{12,16},{16,12},{20,24},{24,20},{28,0},{1,29},{... | collective-permute-start | bytes 393224 | tf_op jit(solution)/shard_map/ppermute | solution.py:34
  8.7 0.5 shard_map.140
  9.3 1.3 %shard_map.138 = (bf16[768,512]{1,0:T(8,128)(2,1)S(1)}, f32[768,512]{1,0:T(8,128)S(1)}) custom-call(s32[1]{0:T(128)} %bitcast.slab_ref, f32[1024,16]{1,0:T(8,128)S(1)} %get-tuple-element.52.k_cols, bf16[16,512]{1,0:T(8,128)(2,1)S(1)} %get-tuple-element.53.positions, bf16[512,256]{1,0:T(8,128)(2,1)S(1)} %get-tuple-element.40.rows_ref, ...), custom_call_target="tpu_custom_call" | custom-call | flops 402653184 | bytes 1572864 | tf_op jit(solution)/shard_map/pallas_call | solution.py:163
  10.6 0.0 collective-permute-done.5
  10.6 0.1 add_convert_fusion
  10.7 0.6 collective-permute-start.6
  11.3 0.6 collective-permute-start.8
  11.9 0.0 collective-permute-done.4
  11.9 0.3 fusion.7
  12.2 3.6 %collective-permute-done.6 = bf16[256,256]{1,0:T(8,128)(2,1)S(1)} collective-permute-done((bf16[256,256]{1,0:T(8,128)(2,1)S(1)}, bf16[256,256]{1,0:T(8,128)(2,1)S(1)}, u32[]{:S(2)}, u32[]{:S(2)}) %collective-permute-start.6) | collective-permute-done | bytes 131104 | tf_op jit(solution)/shard_map/ppermute | solution.py:29
  15.7 0.8 %collective-permute-done.8 = bf16[256,256]{1,0:T(8,128)(2,1)S(1)} collective-permute-done((bf16[256,256]{1,0:T(8,128)(2,1)S(1)}, bf16[256,256]{1,0:T(8,128)(2,1)S(1)}, u32[]{:S(2)}, u32[]{:S(2)}) %collective-permute-start.8) | collective-permute-done | bytes 131104 | tf_op jit(solution)/shard_map/ppermute | solution.py:29
  16.5 0.1 fusion
  16.6 1.3 %collective-permute-start.9 = (bf16[256,512]{1,0:T(8,128)(2,1)S(1)}, bf16[256,512]{1,0:T(8,128)(2,1)S(1)}, u32[]{:S(2)}, u32[]{:S(2)}) collective-permute-start(bf16[256,512]{1,0:T(8,128)(2,1)S(1)} %pad_maximum_fusion.2), channel_id=1, source_target_pairs={{0,16},{4,20},{8,24},{12,28},{16,0},{20,4},{24,8},{28,12},{1,17},{... | collective-permute-start | bytes 786440 | tf_op jit(solution)/shard_map/ppermute | solution.py:29
  17.9 0.8 %collective-permute-start.7 = (bf16[256,512]{1,0:T(8,128)(2,1)S(1)}, bf16[256,512]{1,0:T(8,128)(2,1)S(1)}, u32[]{:S(2)}, u32[]{:S(2)}) collective-permute-start(bf16[256,512]{1,0:T(8,128)(2,1)S(1)} %pad_maximum_fusion.1), channel_id=1, source_target_pairs={{0,8},{4,12},{8,0},{12,4},{16,24},{20,28},{24,16},{28,20},{1,9},{5... | collective-permute-start | bytes 786440 | tf_op jit(solution)/shard_map/ppermute | solution.py:29
  18.8 5.0 %edges.1 = (f32[512,256]{1,0:T(8,128)S(1)}, bf16[256,256]{1,0:T(8,128)(2,1)S(1)}, bf16[256,256]{1,0:T(8,128)(2,1)S(1)}, f32[256,256]{1,0:T(8,128)S(1)}) custom-call(s32[1]{0:T(128)} %bitcast.slab_ref, s32[1,4096]{1,0:T(1,128)S(1)} %get-tuple-element.36.src_ref, s32[1,4096]{1,0:T(1,128)S(1)} %get-tuple-element.37.dst_ref, ...), custom_call_target="tpu_custom_call" | custom-call | flops 3221225472 | bytes 49152 | tf_op jit(solution)/shard_map/edges/pallas_call | solution.py:248
  23.9 0.0 collective-permute-done.2.pair_t
  23.9 0.0 collective-permute-done.3.cross_t
  23.9 0.0 collective-permute-done.9.refs_2_
  23.9 0.5 collective-permute-done.7.refs_1_
  24.5 0.5 share.1
  25.0 0.1 collective-permute-start.14
  25.1 0.5 collective-permute-start
  25.6 1.9 %collective-permute-start.1 = (bf16[256,256]{1,0:T(8,128)(2,1)S(1)}, bf16[256,256]{1,0:T(8,128)(2,1)S(1)}, u32[]{:S(2)}, u32[]{:S(2)}) collective-permute-start(bf16[256,256]{1,0:T(8,128)(2,1)S(1)} %get-tuple-element.45.cross_ref), channel_id=1, source_target_pairs={{0,28},{4,8},{8,4},{12,16},{16,12},{20,24},{24,20},{28,0},{1,29},{... | collective-permute-start | bytes 393224 | tf_op jit(solution)/shard_map/ppermute | solution.py:34
  27.4 0.0 collective-permute-done.14
  27.5 1.4 %collective-permute-start.15 = (bf16[64,256]{1,0:T(8,128)(2,1)S(1)}, bf16[64,256]{1,0:T(8,128)(2,1)S(1)}, u32[]{:S(2)}, u32[]{:S(2)}) collective-permute-start(bf16[64,256]{1,0:T(8,128)(2,1)S(1)} %get-tuple-element.78), channel_id=1, source_target_pairs={{0,24},{4,28},{8,16},{12,20},{16,8},{20,12},{24,0},{28,4},{1,25},{... | collective-permute-start | bytes 98312 | tf_op jit(solution)/shard_map/ppermute | solution.py:29
  28.9 1.0 %collective-permute-start.16 = (bf16[64,256]{1,0:T(8,128)(2,1)S(1)}, bf16[64,256]{1,0:T(8,128)(2,1)S(1)}, u32[]{:S(2)}, u32[]{:S(2)}) collective-permute-start(bf16[64,256]{1,0:T(8,128)(2,1)S(1)} %get-tuple-element.80), channel_id=1, source_target_pairs={{0,16},{4,20},{8,24},{12,28},{16,0},{20,4},{24,8},{28,12},{1,17},{... | collective-permute-start | bytes 98312 | tf_op jit(solution)/shard_map/ppermute | solution.py:29
  29.9 1.1 %collective-permute-start.17 = (bf16[64,256]{1,0:T(8,128)(2,1)S(1)}, bf16[64,256]{1,0:T(8,128)(2,1)S(1)}, u32[]{:S(2)}, u32[]{:S(2)}) collective-permute-start(bf16[64,256]{1,0:T(8,128)(2,1)S(1)} %get-tuple-element.79), channel_id=1, source_target_pairs={{0,8},{4,12},{8,0},{12,4},{16,24},{20,28},{24,16},{28,20},{1,9},{5... | collective-permute-start | bytes 98312 | tf_op jit(solution)/shard_map/ppermute | solution.py:29
  31.0 0.0 collective-permute-done.pair_ref
  31.1 1.1 %collective-permute-done.1.cross_ref = bf16[256,256]{1,0:T(8,128)(2,1)S(1)} collective-permute-done((bf16[256,256]{1,0:T(8,128)(2,1)S(1)}, bf16[256,256]{1,0:T(8,128)(2,1)S(1)}, u32[]{:S(2)}, u32[]{:S(2)}) %collective-permute-start.1) | collective-permute-done | bytes 131104 | tf_op jit(solution)/shard_map/ppermute | solution.py:34
  32.2 0.7 %short.1.base_ref = f32[512,256]{1,0:T(8,128)S(1)} custom-call(s32[1]{0:T(128)} %bitcast.slab_ref, f32[512,256]{1,0:T(8,128)S(1)} %get-tuple-element.43.own_ref, bf16[256,256]{1,0:T(8,128)(2,1)S(1)} %collective-permute-done.pair_ref, bf16[256,256]{1,0:T(8,128)(2,1)S(1)} %collective-permute-done.1.cross_ref, s32[1,2,256]{2,1,0:T(2,128)S(1)} %get-tuple-element.41.lists_ref, ...), custom_call_target="tpu_custom_call" | custom-call | flops 268435456 | bytes 1048576 | tf_op jit(solution)/shard_map/short/pallas_call | solution.py:290
  32.9 1.2 %collective-permute-start.10 = (bf16[256,256]{1,0:T(8,128)(2,1)S(1)}, bf16[256,256]{1,0:T(8,128)(2,1)S(1)}, u32[]{:S(2)}, u32[]{:S(2)}) collective-permute-start(bf16[256,256]{1,0:T(8,128)(2,1)S(1)} %get-tuple-element.58), channel_id=1, source_target_pairs={{0,16},{4,20},{8,24},{12,28},{16,0},{20,4},{24,8},{28,12},{1,17},{... | collective-permute-start | bytes 393224 | tf_op jit(solution)/shard_map/ppermute | solution.py:29
  34.1 0.1 collective-permute-start.11
  34.2 2.4 %collective-permute-start.12 = (bf16[256,256]{1,0:T(8,128)(2,1)S(1)}, bf16[256,256]{1,0:T(8,128)(2,1)S(1)}, u32[]{:S(2)}, u32[]{:S(2)}) collective-permute-start(bf16[256,256]{1,0:T(8,128)(2,1)S(1)} %get-tuple-element.58), channel_id=1, source_target_pairs={{0,24},{4,28},{8,16},{12,20},{16,8},{20,12},{24,0},{28,4},{1,25},{... | collective-permute-start | bytes 393224 | tf_op jit(solution)/shard_map/ppermute | solution.py:29
  36.5 1.5 %collective-permute-start.25 = (bf16[128,256]{1,0:T(8,128)(2,1)S(1)}, bf16[128,256]{1,0:T(8,128)(2,1)S(1)}, u32[]{:S(2)}, u32[]{:S(2)}) collective-permute-start(bf16[128,256]{1,0:T(8,128)(2,1)S(1)} %convert_element_type.89), channel_id=1, source_target_pairs={{0,1},{1,0},{2,3},{3,2},{4,5},{5,4},{6,7},{7,6},{8,9},{9,8},{10,11... | collective-permute-start | bytes 196616 | tf_op jit(solution)/shard_map/ppermute | solution.py:29
  38.1 0.6 collective-permute-start.18
  38.6 2.5 %collective-permute-start.19 = (bf16[64,256]{1,0:T(8,128)(2,1)S(1)}, bf16[64,256]{1,0:T(8,128)(2,1)S(1)}, u32[]{:S(2)}, u32[]{:S(2)}) collective-permute-start(bf16[64,256]{1,0:T(8,128)(2,1)S(1)} %fusion.5), channel_id=1, source_target_pairs={{0,2},{1,3},{2,0},{3,1},{4,6},{5,7},{6,4},{7,5},{8,10},{9,11},{10,... | collective-permute-start | bytes 98312 | tf_op jit(solution)/shard_map/ppermute | solution.py:29
  41.2 0.0 collective-permute-done.11
  41.2 2.5 %collective-permute-start.20 = (bf16[64,256]{1,0:T(8,128)(2,1)S(1)}, bf16[64,256]{1,0:T(8,128)(2,1)S(1)}, u32[]{:S(2)}, u32[]{:S(2)}) collective-permute-start(bf16[64,256]{1,0:T(8,128)(2,1)S(1)} %fusion.5), channel_id=1, source_target_pairs={{0,3},{1,2},{2,1},{3,0},{4,7},{5,6},{6,5},{7,4},{8,11},{9,10},{10,... | collective-permute-start | bytes 98312 | tf_op jit(solution)/shard_map/ppermute | solution.py:29
  43.7 0.0 collective-permute-done.12
  43.7 0.1 pad_maximum_fusion.even_adj_ref
  43.7 0.1 collective-permute-start.13
  43.8 0.0 collective-permute-done.19
  43.8 3.0 %collective-permute-done.20 = bf16[64,256]{1,0:T(8,128)(2,1)S(1)} collective-permute-done((bf16[64,256]{1,0:T(8,128)(2,1)S(1)}, bf16[64,256]{1,0:T(8,128)(2,1)S(1)}, u32[]{:S(2)}, u32[]{:S(2)}) %collective-permute-start.20) | collective-permute-done | bytes 32800 | tf_op jit(solution)/shard_map/ppermute | solution.py:29
  46.9 1.2 %collective-permute-start.21 = (bf16[64,256]{1,0:T(8,128)(2,1)S(1)}, bf16[64,256]{1,0:T(8,128)(2,1)S(1)}, u32[]{:S(2)}, u32[]{:S(2)}) collective-permute-start(bf16[64,256]{1,0:T(8,128)(2,1)S(1)} %add_convert_fusion.2), channel_id=1, source_target_pairs={{0,16},{4,20},{8,24},{12,28},{16,0},{20,4},{24,8},{28,12},{1,17},{... | collective-permute-start | bytes 98312 | tf_op jit(solution)/shard_map/ppermute | solution.py:29
  48.1 1.5 %collective-permute-start.22 = (bf16[64,256]{1,0:T(8,128)(2,1)S(1)}, bf16[64,256]{1,0:T(8,128)(2,1)S(1)}, u32[]{:S(2)}, u32[]{:S(2)}) collective-permute-start(bf16[64,256]{1,0:T(8,128)(2,1)S(1)} %add_convert_fusion.2), channel_id=1, source_target_pairs={{0,8},{4,12},{8,0},{12,4},{16,24},{20,28},{24,16},{28,20},{1,9},{5... | collective-permute-start | bytes 98312 | tf_op jit(solution)/shard_map/ppermute | solution.py:29
  49.6 0.8 %collective-permute-start.23 = (bf16[64,256]{1,0:T(8,128)(2,1)S(1)}, bf16[64,256]{1,0:T(8,128)(2,1)S(1)}, u32[]{:S(2)}, u32[]{:S(2)}) collective-permute-start(bf16[64,256]{1,0:T(8,128)(2,1)S(1)} %add_convert_fusion.2), channel_id=1, source_target_pairs={{0,24},{4,28},{8,16},{12,20},{16,8},{20,12},{24,0},{28,4},{1,25},{... | collective-permute-start | bytes 98312 | tf_op jit(solution)/shard_map/ppermute | solution.py:29
  50.5 0.0 collective-permute-done.25
  50.5 0.1 collective-permute-start.26
  50.6 0.3 collective-permute-done.21
  50.9 1.2 %collective-permute-done.22 = bf16[64,256]{1,0:T(8,128)(2,1)S(1)} collective-permute-done((bf16[64,256]{1,0:T(8,128)(2,1)S(1)}, bf16[64,256]{1,0:T(8,128)(2,1)S(1)}, u32[]{:S(2)}, u32[]{:S(2)}) %collective-permute-start.22) | collective-permute-done | bytes 32800 | tf_op jit(solution)/shard_map/ppermute | solution.py:29
  52.1 2.4 %collective-permute-done.23 = bf16[64,256]{1,0:T(8,128)(2,1)S(1)} collective-permute-done((bf16[64,256]{1,0:T(8,128)(2,1)S(1)}, bf16[64,256]{1,0:T(8,128)(2,1)S(1)}, u32[]{:S(2)}, u32[]{:S(2)}) %collective-permute-start.23) | collective-permute-done | bytes 32800 | tf_op jit(solution)/shard_map/ppermute | solution.py:29
  54.5 0.1 collective-permute-start.24
  54.5 1.5 %collective-permute-done.26 = bf16[128,256]{1,0:T(8,128)(2,1)S(1)} collective-permute-done((bf16[128,256]{1,0:T(8,128)(2,1)S(1)}, bf16[128,256]{1,0:T(8,128)(2,1)S(1)}, u32[]{:S(2)}, u32[]{:S(2)}) %collective-permute-start.26) | collective-permute-done | bytes 65568 | tf_op jit(solution)/shard_map/ppermute | solution.py:29
  56.0 0.7 %add_multiply_fusion = f32[128,256]{1,0:T(8,128)} fusion(bf16[128,256]{1,0:T(8,128)(2,1)S(1)} %collective-permute-done.26, bf16[128,256]{1,0:T(8,128)(2,1)S(1)} %add_convert_fusion.1), kind=kLoop, calls=%fused_computation.10 | loop fusion | flops 131072 | bytes 262144 | tf_op jit(solution)/shard_map/div | solution.py:572
  56.7 0.0 collective-permute-done.24.odd_ref
  56.7 0.9 %place.1 = (f32[256,256]{1,0:T(8,128)}, f32[256,256]{1,0:T(8,128)}) custom-call(s32[1]{0:T(128)} %bitcast.slab_ref, bf16[4,64,256]{2,1,0:T(8,128)(2,1)S(1)} %pad_maximum_fusion.3.even_ref, bf16[4,64,256]{2,1,0:T(8,128)(2,1)S(1)} %collective-permute-done.24.odd_ref), custom_call_target="tpu_custom_call" | custom-call | tf_op jit(solution)/shard_map/place/pallas_call | solution.py:391
  57.5 0.0 collective-permute-done.13.odd_adj_ref
  57.5 1.5 %back.1 = bf16[512,256]{1,0:T(8,128)(2,1)} custom-call(f32[512,256]{1,0:T(8,128)S(1)} %short.1.base_ref, bf16[4,256,256]{2,1,0:T(8,128)(2,1)S(1)} %pad_maximum_fusion.even_adj_ref, bf16[4,256,256]{2,1,0:T(8,128)(2,1)S(1)} %collective-permute-done.13.odd_adj_ref, bf16[256,512]{1,0:T(8,128)(2,1)S(1)} %get-tuple-element.59.refs_0_, ...), custom_call_target="tpu_custom_call" | custom-call | flops 536870912 | bytes 2097152 | tf_op jit(solution)/shard_map/back/pallas_call | solution.py:364
  (17 shorter events, 0.3 us)
Async XLA Ops:
  3.7 8.2 %collective-permute-start.4 = (bf16[768,512]{1,0:T(8,128)(2,1)S(1)}, bf16[768,512]{1,0:T(8,128)(2,1)S(1)}, u32[]{:S(2)}, u32[]{:S(2)}) collective-permute-start(bf16[768,512]{1,0:T(8,128)(2,1)S(1)} %get-tuple-element.55), channel_id=1, source_target_pairs={{0,4},{4,0},{8,12},{12,8},{16,20},{20,16},{24,28},{28,24},{1,5},{5... | collective-permute-start | bytes 2359304 | tf_op jit(solution)/shard_map/ppermute | solution.py:29
  4.3 6.3 %collective-permute-start.5 = (bf16[256,512]{1,0:T(8,128)(2,1)S(1)}, bf16[256,512]{1,0:T(8,128)(2,1)S(1)}, u32[]{:S(2)}, u32[]{:S(2)}) collective-permute-start(bf16[256,512]{1,0:T(8,128)(2,1)S(1)} %get-tuple-element.57), channel_id=1, source_target_pairs={{0,4},{4,0},{8,12},{12,8},{16,20},{20,16},{24,28},{28,24},{1,5},{5... | collective-permute-start | bytes 786440 | tf_op jit(solution)/shard_map/ppermute | solution.py:29
  4.7 19.2 %collective-permute-start.2 = (bf16[256,256]{1,0:T(8,128)(2,1)S(1)}, bf16[256,256]{1,0:T(8,128)(2,1)S(1)}, u32[]{:S(2)}, u32[]{:S(2)}) collective-permute-start(bf16[256,256]{1,0:T(8,128)(2,1)S(1)} %get-tuple-element.50), channel_id=1, source_target_pairs={{0,4},{4,0},{8,12},{12,8},{16,20},{20,16},{24,28},{28,24},{1,5},{5... | collective-permute-start | bytes 393224 | tf_op jit(solution)/shard_map/ppermute | solution.py:29
  5.2 18.7 %collective-permute-start.3 = (bf16[256,256]{1,0:T(8,128)(2,1)S(1)}, bf16[256,256]{1,0:T(8,128)(2,1)S(1)}, u32[]{:S(2)}, u32[]{:S(2)}) collective-permute-start(bf16[256,256]{1,0:T(8,128)(2,1)S(1)} %get-tuple-element.51), channel_id=1, source_target_pairs={{0,28},{4,8},{8,4},{12,16},{16,12},{20,24},{24,20},{28,0},{1,29},{... | collective-permute-start | bytes 393224 | tf_op jit(solution)/shard_map/ppermute | solution.py:34
  10.7 5.0 %collective-permute-start.6 = (bf16[256,256]{1,0:T(8,128)(2,1)S(1)}, bf16[256,256]{1,0:T(8,128)(2,1)S(1)}, u32[]{:S(2)}, u32[]{:S(2)}) collective-permute-start(bf16[256,256]{1,0:T(8,128)(2,1)S(1)} %get-tuple-element.77), channel_id=1, source_target_pairs={{0,16},{4,20},{8,24},{12,28},{16,0},{20,4},{24,8},{28,12},{1,17},{... | collective-permute-start | bytes 393224 | tf_op jit(solution)/shard_map/ppermute | solution.py:29
  11.3 5.3 %collective-permute-start.8 = (bf16[256,256]{1,0:T(8,128)(2,1)S(1)}, bf16[256,256]{1,0:T(8,128)(2,1)S(1)}, u32[]{:S(2)}, u32[]{:S(2)}) collective-permute-start(bf16[256,256]{1,0:T(8,128)(2,1)S(1)} %get-tuple-element.76), channel_id=1, source_target_pairs={{0,8},{4,12},{8,0},{12,4},{16,24},{20,28},{24,16},{28,20},{1,9},{5... | collective-permute-start | bytes 393224 | tf_op jit(solution)/shard_map/ppermute | solution.py:29
  16.6 7.3 %collective-permute-start.9 = (bf16[256,512]{1,0:T(8,128)(2,1)S(1)}, bf16[256,512]{1,0:T(8,128)(2,1)S(1)}, u32[]{:S(2)}, u32[]{:S(2)}) collective-permute-start(bf16[256,512]{1,0:T(8,128)(2,1)S(1)} %pad_maximum_fusion.2), channel_id=1, source_target_pairs={{0,16},{4,20},{8,24},{12,28},{16,0},{20,4},{24,8},{28,12},{1,17},{... | collective-permute-start | bytes 786440 | tf_op jit(solution)/shard_map/ppermute | solution.py:29
  17.9 6.5 %collective-permute-start.7 = (bf16[256,512]{1,0:T(8,128)(2,1)S(1)}, bf16[256,512]{1,0:T(8,128)(2,1)S(1)}, u32[]{:S(2)}, u32[]{:S(2)}) collective-permute-start(bf16[256,512]{1,0:T(8,128)(2,1)S(1)} %pad_maximum_fusion.1), channel_id=1, source_target_pairs={{0,8},{4,12},{8,0},{12,4},{16,24},{20,28},{24,16},{28,20},{1,9},{5... | collective-permute-start | bytes 786440 | tf_op jit(solution)/shard_map/ppermute | solution.py:29
  25.0 2.4 %collective-permute-start.14 = (f32[4,64,256]{2,1,0:T(8,128)S(1)}, f32[4,64,256]{2,1,0:T(8,128)S(1)}, u32[]{:S(2)}, u32[]{:S(2)}) collective-permute-start(f32[4,64,256]{2,1,0:T(8,128)S(1)} %get-tuple-element.64), channel_id=1, source_target_pairs={{0,4},{4,0},{8,12},{12,8},{16,20},{20,16},{24,28},{28,24},{1,5},{5... | collective-permute-start | bytes 786440 | tf_op jit(solution)/shard_map/ppermute | solution.py:29
  25.1 6.0 %collective-permute-start = (bf16[256,256]{1,0:T(8,128)(2,1)S(1)}, bf16[256,256]{1,0:T(8,128)(2,1)S(1)}, u32[]{:S(2)}, u32[]{:S(2)}) collective-permute-start(bf16[256,256]{1,0:T(8,128)(2,1)S(1)} %get-tuple-element.44.pair_ref), channel_id=1, source_target_pairs={{0,4},{4,0},{8,12},{12,8},{16,20},{20,16},{24,28},{28,24},{1,5},{5... | collective-permute-start | bytes 393224 | tf_op jit(solution)/shard_map/ppermute | solution.py:29
  25.6 6.6 %collective-permute-start.1 = (bf16[256,256]{1,0:T(8,128)(2,1)S(1)}, bf16[256,256]{1,0:T(8,128)(2,1)S(1)}, u32[]{:S(2)}, u32[]{:S(2)}) collective-permute-start(bf16[256,256]{1,0:T(8,128)(2,1)S(1)} %get-tuple-element.45.cross_ref), channel_id=1, source_target_pairs={{0,28},{4,8},{8,4},{12,16},{16,12},{20,24},{24,20},{28,0},{1,29},{... | collective-permute-start | bytes 393224 | tf_op jit(solution)/shard_map/ppermute | solution.py:34
  27.5 6.7 %collective-permute-start.15 = (bf16[64,256]{1,0:T(8,128)(2,1)S(1)}, bf16[64,256]{1,0:T(8,128)(2,1)S(1)}, u32[]{:S(2)}, u32[]{:S(2)}) collective-permute-start(bf16[64,256]{1,0:T(8,128)(2,1)S(1)} %get-tuple-element.78), channel_id=1, source_target_pairs={{0,24},{4,28},{8,16},{12,20},{16,8},{20,12},{24,0},{28,4},{1,25},{... | collective-permute-start | bytes 98312 | tf_op jit(solution)/shard_map/ppermute | solution.py:29
  28.9 7.6 %collective-permute-start.16 = (bf16[64,256]{1,0:T(8,128)(2,1)S(1)}, bf16[64,256]{1,0:T(8,128)(2,1)S(1)}, u32[]{:S(2)}, u32[]{:S(2)}) collective-permute-start(bf16[64,256]{1,0:T(8,128)(2,1)S(1)} %get-tuple-element.80), channel_id=1, source_target_pairs={{0,16},{4,20},{8,24},{12,28},{16,0},{20,4},{24,8},{28,12},{1,17},{... | collective-permute-start | bytes 98312 | tf_op jit(solution)/shard_map/ppermute | solution.py:29
  29.9 8.1 %collective-permute-start.17 = (bf16[64,256]{1,0:T(8,128)(2,1)S(1)}, bf16[64,256]{1,0:T(8,128)(2,1)S(1)}, u32[]{:S(2)}, u32[]{:S(2)}) collective-permute-start(bf16[64,256]{1,0:T(8,128)(2,1)S(1)} %get-tuple-element.79), channel_id=1, source_target_pairs={{0,8},{4,12},{8,0},{12,4},{16,24},{20,28},{24,16},{28,20},{1,9},{5... | collective-permute-start | bytes 98312 | tf_op jit(solution)/shard_map/ppermute | solution.py:29
  32.9 5.8 %collective-permute-start.10 = (bf16[256,256]{1,0:T(8,128)(2,1)S(1)}, bf16[256,256]{1,0:T(8,128)(2,1)S(1)}, u32[]{:S(2)}, u32[]{:S(2)}) collective-permute-start(bf16[256,256]{1,0:T(8,128)(2,1)S(1)} %get-tuple-element.58), channel_id=1, source_target_pairs={{0,16},{4,20},{8,24},{12,28},{16,0},{20,4},{24,8},{28,12},{1,17},{... | collective-permute-start | bytes 393224 | tf_op jit(solution)/shard_map/ppermute | solution.py:29
  34.1 7.1 %collective-permute-start.11 = (bf16[256,256]{1,0:T(8,128)(2,1)S(1)}, bf16[256,256]{1,0:T(8,128)(2,1)S(1)}, u32[]{:S(2)}, u32[]{:S(2)}) collective-permute-start(bf16[256,256]{1,0:T(8,128)(2,1)S(1)} %get-tuple-element.58), channel_id=1, source_target_pairs={{0,8},{4,12},{8,0},{12,4},{16,24},{20,28},{24,16},{28,20},{1,9},{5... | collective-permute-start | bytes 393224 | tf_op jit(solution)/shard_map/ppermute | solution.py:29
  34.2 9.5 %collective-permute-start.12 = (bf16[256,256]{1,0:T(8,128)(2,1)S(1)}, bf16[256,256]{1,0:T(8,128)(2,1)S(1)}, u32[]{:S(2)}, u32[]{:S(2)}) collective-permute-start(bf16[256,256]{1,0:T(8,128)(2,1)S(1)} %get-tuple-element.58), channel_id=1, source_target_pairs={{0,24},{4,28},{8,16},{12,20},{16,8},{20,12},{24,0},{28,4},{1,25},{... | collective-permute-start | bytes 393224 | tf_op jit(solution)/shard_map/ppermute | solution.py:29
  36.5 13.9 %collective-permute-start.25 = (bf16[128,256]{1,0:T(8,128)(2,1)S(1)}, bf16[128,256]{1,0:T(8,128)(2,1)S(1)}, u32[]{:S(2)}, u32[]{:S(2)}) collective-permute-start(bf16[128,256]{1,0:T(8,128)(2,1)S(1)} %convert_element_type.89), channel_id=1, source_target_pairs={{0,1},{1,0},{2,3},{3,2},{4,5},{5,4},{6,7},{7,6},{8,9},{9,8},{10,11... | collective-permute-start | bytes 196616 | tf_op jit(solution)/shard_map/ppermute | solution.py:29
  38.1 5.7 %collective-permute-start.18 = (bf16[64,256]{1,0:T(8,128)(2,1)S(1)}, bf16[64,256]{1,0:T(8,128)(2,1)S(1)}, u32[]{:S(2)}, u32[]{:S(2)}) collective-permute-start(bf16[64,256]{1,0:T(8,128)(2,1)S(1)} %fusion.5), channel_id=1, source_target_pairs={{0,1},{1,0},{2,3},{3,2},{4,5},{5,4},{6,7},{7,6},{8,9},{9,8},{10,11... | collective-permute-start | bytes 98312 | tf_op jit(solution)/shard_map/ppermute | solution.py:29
  38.6 5.2 %collective-permute-start.19 = (bf16[64,256]{1,0:T(8,128)(2,1)S(1)}, bf16[64,256]{1,0:T(8,128)(2,1)S(1)}, u32[]{:S(2)}, u32[]{:S(2)}) collective-permute-start(bf16[64,256]{1,0:T(8,128)(2,1)S(1)} %fusion.5), channel_id=1, source_target_pairs={{0,2},{1,3},{2,0},{3,1},{4,6},{5,7},{6,4},{7,5},{8,10},{9,11},{10,... | collective-permute-start | bytes 98312 | tf_op jit(solution)/shard_map/ppermute | solution.py:29
  41.2 5.7 %collective-permute-start.20 = (bf16[64,256]{1,0:T(8,128)(2,1)S(1)}, bf16[64,256]{1,0:T(8,128)(2,1)S(1)}, u32[]{:S(2)}, u32[]{:S(2)}) collective-permute-start(bf16[64,256]{1,0:T(8,128)(2,1)S(1)} %fusion.5), channel_id=1, source_target_pairs={{0,3},{1,2},{2,1},{3,0},{4,7},{5,6},{6,5},{7,4},{8,11},{9,10},{10,... | collective-permute-start | bytes 98312 | tf_op jit(solution)/shard_map/ppermute | solution.py:29
  43.7 13.8 %collective-permute-start.13 = (bf16[4,256,256]{2,1,0:T(8,128)(2,1)S(1)}, bf16[4,256,256]{2,1,0:T(8,128)(2,1)S(1)}, u32[]{:S(2)}, u32[]{:S(2)}) collective-permute-start(bf16[4,256,256]{2,1,0:T(8,128)(2,1)S(1)} %pad_maximum_fusion.even_adj_ref), channel_id=1, source_target_pairs={{0,4},{4,0},{8,12},{12,8},{16,20},{20,16},{24,28},{28,24},{1,5},{5... | collective-permute-start | bytes 1572872 | tf_op jit(solution)/shard_map/ppermute | solution.py:29
  46.9 4.0 %collective-permute-start.21 = (bf16[64,256]{1,0:T(8,128)(2,1)S(1)}, bf16[64,256]{1,0:T(8,128)(2,1)S(1)}, u32[]{:S(2)}, u32[]{:S(2)}) collective-permute-start(bf16[64,256]{1,0:T(8,128)(2,1)S(1)} %add_convert_fusion.2), channel_id=1, source_target_pairs={{0,16},{4,20},{8,24},{12,28},{16,0},{20,4},{24,8},{28,12},{1,17},{... | collective-permute-start | bytes 98312 | tf_op jit(solution)/shard_map/ppermute | solution.py:29
  48.1 3.9 %collective-permute-start.22 = (bf16[64,256]{1,0:T(8,128)(2,1)S(1)}, bf16[64,256]{1,0:T(8,128)(2,1)S(1)}, u32[]{:S(2)}, u32[]{:S(2)}) collective-permute-start(bf16[64,256]{1,0:T(8,128)(2,1)S(1)} %add_convert_fusion.2), channel_id=1, source_target_pairs={{0,8},{4,12},{8,0},{12,4},{16,24},{20,28},{24,16},{28,20},{1,9},{5... | collective-permute-start | bytes 98312 | tf_op jit(solution)/shard_map/ppermute | solution.py:29
  49.6 4.8 %collective-permute-start.23 = (bf16[64,256]{1,0:T(8,128)(2,1)S(1)}, bf16[64,256]{1,0:T(8,128)(2,1)S(1)}, u32[]{:S(2)}, u32[]{:S(2)}) collective-permute-start(bf16[64,256]{1,0:T(8,128)(2,1)S(1)} %add_convert_fusion.2), channel_id=1, source_target_pairs={{0,24},{4,28},{8,16},{12,20},{16,8},{20,12},{24,0},{28,4},{1,25},{... | collective-permute-start | bytes 98312 | tf_op jit(solution)/shard_map/ppermute | solution.py:29
  50.5 5.5 %collective-permute-start.26 = (bf16[128,256]{1,0:T(8,128)(2,1)S(1)}, bf16[128,256]{1,0:T(8,128)(2,1)S(1)}, u32[]{:S(2)}, u32[]{:S(2)}) collective-permute-start(bf16[128,256]{1,0:T(8,128)(2,1)S(1)} %add_convert_fusion.1), channel_id=1, source_target_pairs={{0,2},{1,3},{2,0},{3,1},{4,6},{5,7},{6,4},{7,5},{8,10},{9,11},{10,... | collective-permute-start | bytes 196616 | tf_op jit(solution)/shard_map/ppermute | solution.py:29
  54.5 2.2 %collective-permute-start.24 = (bf16[4,64,256]{2,1,0:T(8,128)(2,1)S(1)}, bf16[4,64,256]{2,1,0:T(8,128)(2,1)S(1)}, u32[]{:S(2)}, u32[]{:S(2)}) collective-permute-start(bf16[4,64,256]{2,1,0:T(8,128)(2,1)S(1)} %pad_maximum_fusion.3.even_ref), channel_id=1, source_target_pairs={{0,4},{4,0},{8,12},{12,8},{16,20},{20,16},{24,28},{28,24},{1,5},{5... | collective-permute-start | bytes 393224 | tf_op jit(solution)/shard_map/ppermute | solution.py:29
